TPU v7x, 256 devices: a whole 4x4x8 slice. The times are simulated.
256 devices in a mesh: dp: 16 (over x, y), tensor: 8 (over z), side: 2 (over core).
Axes of the slice: x: 4, y: 4, z: 8, core: 2. Of those that a mesh axis runs over, the one named last changes fastest.
Arguments:
- q_new: bfloat16 [1024, 6144], P(('dp', 'side'), 'tensor'), may hold values from -6 to 6
- k_new: bfloat16 [1024, 1024], P(('dp', 'side'), 'tensor'), may hold values from -6 to 6
- v_new: bfloat16 [1024, 1024], P(('dp', 'side'), 'tensor'), may hold values from -6 to 6
- k_cache: bfloat16 [1024, 192, 1024], P(('dp', 'side'), None, 'tensor'), may hold values from -6 to 6
- v_cache: bfloat16 [1024, 192, 1024], P(('dp', 'side'), None, 'tensor'), may hold values from -6 to 6
- lengths: int32 [1024], P(('dp', 'side')), may hold values from 24 to 192, as said below
- attn_out_weight: bfloat16 [6144, 6144], P('tensor', ('dp', 'side')), may hold values from -0.078125 to 0.078125
- residual: bfloat16 [1024, 6144], P('tensor', ('dp', 'side')), may hold values from -1.5 to 1.5
- norm_gain: float32 [6144], replicated, may hold values from 0.1 to 1.9
- router_weight: bfloat16 [6144, 8], replicated, may hold values from -0.02734375 to 0.02734375
- expert_ids: int32 [1024, 2], replicated, may hold values from 0 to 7, all different within a row; in each aligned block of 128 rows (0 to 127, 128 to 255, ...) at most 64 rows name the same one
- gate_weight: bfloat16 [8, 6144, 8192], P('tensor', None, ('dp', 'side')), may hold values from -0.078125 to 0.078125
- up_weight: bfloat16 [8, 6144, 8192], P('tensor', None, ('dp', 'side')), may hold values from -0.078125 to 0.078125
- down_weight: bfloat16 [8, 8192, 6144], P('tensor', ('dp', 'side')), may hold values from -0.0625 to 0.0625
Outputs:
- layer_out: bfloat16 [1024, 6144], P('tensor', ('dp', 'side'))
Inputs may be any that keep to these rules, and one draw needn't show every extreme that they name: `expert_ids`: each row names two different experts; in each aligned block of 128 rows no expert is named by more than 64 rows, and in every draw some expert is named by exactly 64 rows of a block. Row r attends to cached positions 0 to lengths[r] - 1 and to its new key; some rows hold all 192.
All inputs are finite; a program needn't handle non-finite values.
Results may differ from a plain program's by a relative error of at most 0.035.
Values may be sent and summed in bfloat16 or wider, within the bound.
No kernel may reach another device: no remote copies, remote signals or barrier semaphores. Data moves between devices by JAX's collectives and lax.ppermute only.
A program may use at most 128 MiB of HBM per device.

v0:
```python
import jax
import jax.numpy as jnp
from jax import lax
from jax.experimental import pallas as pl
from jax.experimental.pallas import tpu as pltpu
from jax.sharding import PartitionSpec as P

HEAD_DIM = 128
EXPERTS = 8
eps = 1e-05
F32 = jnp.float32
BF16 = jnp.bfloat16
VMEM_LIMIT = 48 * 1024 * 1024

SHIFT_X = [[(4 * x + y, 4 * ((x + d) % 4) + y) for x in range(4) for y in range(4)] for d in range(4)]
SHIFT_Y = [[(4 * x + y, 4 * x + (y + d) % 4) for x in range(4) for y in range(4)] for d in range(4)]
SWAP = [(0, 1), (1, 0)]


def swap_cores(a):
    return lax.ppermute(a, "side", SWAP)


def chip_at(pos, dx, dy):
    return ((pos[0] + dx) & 3) * 4 + ((pos[1] + dy) & 3)


def outproj_kernel(pos, g0, g1, g2, g3, w, out):
    for dy, ref in enumerate((g0, g1, g2, g3)):
        sums = jnp.dot(ref[...].reshape(128, 768), w[...], preferred_element_type=F32).astype(BF16)
        for dx in range(4):
            chip = chip_at(pos, -dx, -dy)
            row = pl.multiple_of((chip & 1) * 32, 32)
            out[chip // 2, pl.ds(row, 32), :] = sums[dx * 32 : dx * 32 + 32]


def norm_kernel(pos, a0, a1, a2, a3, b0, b1, b2, b3, gain, out):
    for h, refs in ((0, (a0, a1, a2, a3)), (1, (b0, b1, b2, b3))):

        def rows_of(n, _, h=h, refs=refs):
            rows = pl.ds(pl.multiple_of(n * 32, 32), 32)
            squares = jnp.zeros((32, 384), F32)
            for i in range(4):
                for j in range(4):
                    v = refs[i][j, rows, :].astype(F32)
                    squares = squares + v * v
            mean = jnp.sum(squares, axis=1, keepdims=True) * (1.0 / 6144.0)
            scale = lax.rsqrt(mean + eps)
            to = pl.ds(pl.multiple_of(h * 128 + n * 32, 32), 32)
            for i in range(4):
                for j in range(4):
                    chip = chip_at(pos, -j, -i) if h == 0 else chip_at(pos, -i, -j)
                    columns = pl.ds(pl.multiple_of(chip * 384, 128), 384)
                    v = refs[i][j, rows, :].astype(F32)
                    out[to, columns] = (v * scale * gain[chip]).astype(BF16)
            return 0

        lax.fori_loop(0, 4, rows_of, 0)


def down_kernel(pos, inner, down_w, near, far, w, sems):
    def copy(dx, dy):
        columns = pl.ds(pl.multiple_of(chip_at(pos, dx, dy) * 384, 128), 384)
        n = dx * 4 + dy
        return pltpu.make_async_copy(down_w.at[:, columns], w.at[n], sems.at[n])

    def issue(n, _):
        copy(n // 4, n % 4).start()
        return 0

    def arrive(n, _):
        copy(n // 4, n % 4).wait()
        return 0

    lax.fori_loop(0, 16, issue, 0)
    lax.fori_loop(0, 16, arrive, 0)
    for out, base, step in ((near, 1, 2), (far, 2, -2)):

        def work(n, _, out=out, base=base, step=step):
            k, i = n // 4, n % 4
            shift = base + step * k
            first = jnp.dot(inner[0:128, :], w[i * 4 + shift], preferred_element_type=F32)
            second = jnp.dot(inner[128:256, :], w[shift * 4 + i], preferred_element_type=F32)
            out[k, 0, i] = first.astype(BF16)
            out[k, 1, i] = second.astype(BF16)
            return 0

        lax.fori_loop(0, 8, work, 0)


def down_call(pos, inner, down_w):
    vmem = pl.BlockSpec(memory_space=pltpu.VMEM)
    return pl.pallas_call(
        down_kernel,
        in_specs=[pl.BlockSpec(memory_space=pltpu.SMEM), vmem, pl.BlockSpec(memory_space=pl.ANY)],
        out_specs=[vmem, vmem],
        out_shape=[jax.ShapeDtypeStruct((2, 2, 4, 128, 384), BF16)] * 2,
        scratch_shapes=[pltpu.VMEM((16, 256, 384), BF16), pltpu.SemaphoreType.DMA((16,))],
        compiler_params=pltpu.CompilerParams(vmem_limit_bytes=VMEM_LIMIT),
        name="expert_down",
    )(pos, inner, down_w)


def attend(q_new, k_new, v_new, k_cache, v_cache, lengths):
    rows_dev = q_new.shape[0]
    kv_local = k_new.shape[1] // HEAD_DIM
    heads_local = q_new.shape[1] // HEAD_DIM
    group_size = heads_local // kv_local
    cache_len = k_cache.shape[1]
    inv_root = HEAD_DIM ** (-0.5)
    queries = q_new.reshape(rows_dev, kv_local, group_size, HEAD_DIM)
    cache_keys = k_cache.reshape(rows_dev, cache_len, kv_local, HEAD_DIM)
    cache_values = v_cache.reshape(rows_dev, cache_len, kv_local, HEAD_DIM)
    own_keys = k_new.reshape(rows_dev, kv_local, HEAD_DIM)
    own_values = v_new.reshape(rows_dev, kv_local, HEAD_DIM).astype(F32)
    cache_scores = (
        jnp.einsum("rkgd,rckd->rkgc", queries, cache_keys, preferred_element_type=F32) * inv_root
    )
    own_scores = (
        jnp.einsum("rkgd,rkd->rkg", queries, own_keys, preferred_element_type=F32) * inv_root
    )
    live_mask = (jnp.arange(cache_len, dtype=jnp.int32)[None, :] < lengths[:, None])[
        :, None, None, :
    ]
    cache_scores = jnp.where(live_mask, cache_scores, -1e30)
    peak = jnp.maximum(jnp.max(cache_scores, axis=3), own_scores)
    cache_exp = jnp.exp(cache_scores - peak[..., None])
    own_exp = jnp.exp(own_scores - peak)
    denominator = jnp.sum(cache_exp, axis=3) + own_exp
    cache_weights = (cache_exp / denominator[..., None]).astype(BF16)
    own_weights = (own_exp / denominator).astype(BF16).astype(F32)
    mixed_heads = jnp.einsum(
        "rkgc,rckd->rkgd", cache_weights, cache_values, preferred_element_type=F32
    )
    mixed_heads = mixed_heads + own_weights[..., None] * own_values[:, :, None, :]
    return mixed_heads.reshape(rows_dev, heads_local * HEAD_DIM).astype(BF16)


def ranks_of(member):
    n = member.shape[0]
    lower = (
        lax.broadcasted_iota(jnp.int32, (n, n), 0) >= lax.broadcasted_iota(jnp.int32, (n, n), 1)
    ).astype(BF16)
    counts = jnp.dot(lower, member.astype(BF16), preferred_element_type=F32).astype(jnp.int32)
    return jnp.where(member, counts - 1, -1)


def shards(
    q_new,
    k_new,
    v_new,
    k_cache,
    v_cache,
    lengths,
    attn_out_weight,
    residual,
    norm_gain,
    router_weight,
    expert_ids,
    gate_weight,
    up_weight,
    down_weight,
):
    chip = lax.axis_index("dp")
    core = lax.axis_index("side")
    plane = lax.axis_index("tensor")
    pos = jnp.stack([chip // 4, chip % 4, core]).astype(jnp.int32)
    first_core = core == 0

    def by_core(own, other, axis):
        return jnp.where(
            first_core,
            jnp.concatenate([own, other], axis=axis),
            jnp.concatenate([other, own], axis=axis),
        )

    def half(a):
        return jnp.where(first_core, a[:, :192], a[:, 192:])

    attention = attend(q_new, k_new, v_new, k_cache, v_cache, lengths)
    labels = jnp.arange(EXPERTS, dtype=jnp.int32)
    block_ids = lax.dynamic_slice_in_dim(expert_ids, plane * 128, 128, 0)
    member = jnp.any(block_ids[:, :, None] == labels, axis=1)
    ranks = ranks_of(member).T
    ranks_by_core = ranks.reshape(8, 2, 2, 32).transpose(0, 2, 1, 3).reshape(8, 128)
    slots = jnp.arange(32, dtype=jnp.int32)

    def pick(ranks, side):
        return (ranks[:, None, :] - side * 32 == slots[:, None]).astype(BF16).reshape(256, 128)

    pick_routed = pick(ranks_by_core, core)
    pick_own, pick_other = pick(ranks, core), pick(ranks, 1 - core)
    ids_by_block = expert_ids.reshape(8, 128, 2)
    named = jnp.any(ids_by_block == plane, axis=2)
    ranks_mine = ranks_of(named.T).T
    partner_ids = jnp.sum(ids_by_block, axis=2) - plane
    hits = ranks_mine[:, None, :] - core * 32 == slots[:, None]
    partner = jnp.sum(jnp.where(hits, partner_ids[:, None, :], 0), axis=2).reshape(256, 1)
    signs = (labels == plane).astype(F32) - (labels == partner).astype(F32)

    rows_x = [lax.ppermute(attention, "dp", SHIFT_X[d]) for d in (1, 2, 3)]
    rows_x = jnp.stack([attention] + rows_x)
    columns, rows_x = lax.optimization_barrier(
        (jnp.concatenate([attn_out_weight, residual], axis=0), rows_x)
    )
    columns = by_core(columns, swap_cores(columns), 1)
    out_w = columns[:768]
    residual_chip = columns[768:].reshape(2, 2, 32, 384)
    residual_half = jnp.where(first_core, residual_chip[:, 0], residual_chip[:, 1])
    rows_xy = [rows_x] + [lax.ppermute(rows_x, "dp", SHIFT_Y[d]) for d in (1, 2, 3)]
    vmem = pl.BlockSpec(memory_space=pltpu.VMEM)
    head_sums = pl.pallas_call(
        outproj_kernel,
        in_specs=[pl.BlockSpec(memory_space=pltpu.SMEM)] + [vmem] * 5,
        out_specs=vmem,
        out_shape=jax.ShapeDtypeStruct((8, 64, 384), BF16),
        compiler_params=pltpu.CompilerParams(vmem_limit_bytes=VMEM_LIMIT),
        name="out_projection",
    )(pos, *rows_xy, out_w)
    heads_in = lax.all_to_all(head_sums, "tensor", split_axis=0, concat_axis=0, tiled=True)
    hidden = (
        jnp.sum(heads_in.astype(F32), axis=0) + residual_half.reshape(64, 384).astype(F32)
    ).astype(BF16)
    hidden_chip = by_core(hidden, swap_cores(hidden), 0)
    hidden_rows = half(
        hidden_chip.reshape(2, 2, 32, 384).transpose(1, 0, 2, 3).reshape(128, 384)
    )
    routed = jnp.dot(pick_routed, hidden_chip, preferred_element_type=F32).astype(BF16)
    mine = lax.all_to_all(
        routed.reshape(8, 32, 384), "tensor", split_axis=0, concat_axis=0, tiled=True
    ).reshape(256, 384)

    a, b = mine[:128], mine[128:]
    got = lax.optimization_barrier(
        [lax.ppermute(a, "dp", SHIFT_X[d]) for d in (1, 2, 3)]
        + [lax.ppermute(b, "dp", SHIFT_Y[d]) for d in (1, 2, 3)]
    )
    stack_a, stack_b = jnp.stack([a] + got[:3]), jnp.stack([b] + got[3:])
    gate_w, up_w, down_w = gate_weight[0], up_weight[0], down_weight[0]
    a1, a3, b1, b3 = [lax.ppermute(stack_a, "dp", SHIFT_Y[d]) for d in (1, 3)] + [
        lax.ppermute(stack_b, "dp", SHIFT_X[d]) for d in (1, 3)
    ]
    far_a, far_b, a1, b1 = lax.optimization_barrier((stack_a, stack_b, a1, b1))
    a2, b2 = lax.ppermute(far_a, "dp", SHIFT_Y[2]), lax.ppermute(far_b, "dp", SHIFT_X[2])
    normed = pl.pallas_call(
        norm_kernel,
        in_specs=[pl.BlockSpec(memory_space=pltpu.SMEM)] + [vmem] * 9,
        out_specs=vmem,
        out_shape=jax.ShapeDtypeStruct((256, 6144), BF16),
        compiler_params=pltpu.CompilerParams(vmem_limit_bytes=VMEM_LIMIT),
        name="norm",
    )(pos, stack_a, a1, a2, a3, stack_b, b1, b2, b3, norm_gain.reshape(16, 1, 384))
    normed_other = swap_cores(normed)

    def expert_in(rows):
        gate = jnp.dot(rows, gate_w, preferred_element_type=F32)
        up = jnp.dot(rows, up_w, preferred_element_type=F32)
        return (jax.nn.silu(gate) * up).astype(BF16)

    logits = jnp.dot(normed, router_weight, preferred_element_type=F32)
    shares = jax.nn.sigmoid(jnp.sum(logits * signs, axis=1, keepdims=True))
    own = down_call(pos, expert_in(normed), down_w)
    own, normed_other = lax.optimization_barrier((own, normed_other))
    other = down_call(pos, expert_in(normed_other), down_w)

    def add(*terms):
        total = terms[0].astype(F32)
        for term in terms[1:]:
            total = total + term.astype(F32)
        return total

    near = swap_cores(other[0])
    far = swap_cores(other[1])
    parts = [add(own[0][k, h], near[k, h]).astype(BF16) for k in (0, 1) for h in (0, 1)]
    far, *parts = lax.optimization_barrier((far, *parts))
    parts += [add(own[1][0, h], far[0, h]).astype(BF16) for h in (0, 1)]
    got_a = [lax.ppermute(parts[2 * n], "dp", SHIFT_Y[d]) for n, d in enumerate((1, 3, 2))]
    got_b = [lax.ppermute(parts[2 * n + 1], "dp", SHIFT_X[d]) for n, d in enumerate((1, 3, 2))]
    part_a, part_b = add(own[1][1, 0], far[1, 0]), add(own[1][1, 1], far[1, 1])
    row_a, row_b = add(part_a, *got_a), add(part_b, *got_b)
    got = lax.optimization_barrier(
        [lax.ppermute(row_a[d].astype(BF16), "dp", SHIFT_X[d]) for d in (1, 2, 3)]
        + [lax.ppermute(row_b[d].astype(BF16), "dp", SHIFT_Y[d]) for d in (1, 2, 3)]
    )
    expert_out = jnp.concatenate([add(row_a[0], *got[:3]), add(row_b[0], *got[3:])], axis=0)

    parts = (shares * expert_out).astype(BF16)
    back = lax.all_to_all(
        parts.reshape(8, 32, 384), "tensor", split_axis=0, concat_axis=0, tiled=True
    ).reshape(256, 384)
    keep = half(back)
    taken = swap_cores(jnp.where(first_core, back[:, 192:], back[:, :192]))

    def spread(pick, rows):
        return lax.dot_general(pick, rows, (((0,), (0,)), ((), ())), preferred_element_type=F32)

    return (hidden_rows.astype(F32) + spread(pick_own, keep) + spread(pick_other, taken)).astype(
        BF16
    )


def solution(mesh):
    return jax.shard_map(
        shards,
        mesh=mesh,
        in_specs=(
            P(("dp", "side"), "tensor"),
            P(("dp", "side"), "tensor"),
            P(("dp", "side"), "tensor"),
            P(("dp", "side"), None, "tensor"),
            P(("dp", "side"), None, "tensor"),
            P(("dp", "side")),
            P("tensor", ("dp", "side")),
            P("tensor", ("dp", "side")),
            P(),
            P(),
            P(),
            P("tensor", None, ("dp", "side")),
            P("tensor", None, ("dp", "side")),
            P("tensor", ("dp", "side"), None),
        ),
        out_specs=P("tensor", ("dp", "side")),
        check_vma=False,
    )
```

profile of v0, /device:TPU:1, one launch (start us, length us, event | category | flops | bytes accessed | tf_op | source)
XLA Modules:
  0.0 214.3 jit_solution(5175457493956563209)
XLA Ops:
  3.4 2.4 %fusion.53 = (f32[32,6]{1,0:T(8,128)S(1)}, f32[32,6,192]{2,1,0:T(8,128)S(1)}) fusion(bf16[32,6,128]{2,1,0:T(8,128)(2,1)S(1)} %reshape.233, bf16[32,192,128]{2,1,0:T(8,128)(2,1)} %param.17, pred[32,192]{1,0:T(8,128)(4,1)S(1)} %iota_compare_fusion.4), kind=kOutput, calls=%fused_computation.113 | convolution fusion | flops 9547584 | bytes 1776384 | tf_op jit(solution)/shard_map/rkgd,rckd->rkgc/dot_general | solution.py:117
  6.1 2.0 fusion.9
  9.3 3.3 %collective-permute-start.2 = (bf16[32,768]{1,0:T(8,128)(2,1)}, bf16[32,768]{1,0:T(8,128)(2,1)}, u32[]{:S(2)}, u32[]{:S(2)}) collective-permute-start(bf16[32,768]{1,0:T(8,128)(2,1)} %bitcast.134), channel_id=1, source_target_pairs={{0,192},{16,208},{32,224},{48,240},{64,0},{80,16},{96,32},{112,48}... | collective-permute-start | bytes 147464 | tf_op jit(solution)/shard_map/ppermute | solution.py:201
  15.6 1.7 pad_maximum_fusion
  19.1 1.8 collective-permute-start.6
  21.0 2.7 %collective-permute-start.5 = (bf16[4,32,768]{2,1,0:T(8,128)(2,1)S(1)}, bf16[4,32,768]{2,1,0:T(8,128)(2,1)S(1)}, u32[]{:S(2)}, u32[]{:S(2)}) collective-permute-start(bf16[4,32,768]{2,1,0:T(8,128)(2,1)S(1)} %pad_maximum_fusion.4.g0), channel_id=1, source_target_pairs={{0,48},{16,0},{32,16},{48,32},{64,112},{80,64},{96,80},{112,96},{1... | collective-permute-start | bytes 589832 | tf_op jit(solution)/shard_map/ppermute | solution.py:210
  24.8 2.0 maximum_select_fusion
  27.0 5.0 %collective-permute-done.5.g3 = bf16[4,32,768]{2,1,0:T(8,128)(2,1)S(1)} collective-permute-done((bf16[4,32,768]{2,1,0:T(8,128)(2,1)S(1)}, bf16[4,32,768]{2,1,0:T(8,128)(2,1)S(1)}, u32[]{:S(2)}, u32[]{:S(2)}) %collective-permute-start.5) | collective-permute-done | bytes 196640 | tf_op jit(solution)/shard_map/ppermute | solution.py:210
  32.0 4.3 %collective-permute-done.3.g1 = bf16[4,32,768]{2,1,0:T(8,128)(2,1)S(1)} collective-permute-done((bf16[4,32,768]{2,1,0:T(8,128)(2,1)S(1)}, bf16[4,32,768]{2,1,0:T(8,128)(2,1)S(1)}, u32[]{:S(2)}, u32[]{:S(2)}) %collective-permute-start.3) | collective-permute-done | bytes 196640 | tf_op jit(solution)/shard_map/ppermute | solution.py:210
  36.3 1.9 out_projection.1
  38.1 8.2 %all-to-all-start = ((bf16[8,64,384]{2,1,0:T(8,128)(2,1)}), bf16[8,64,384]{2,1,0:T(8,128)(2,1)}, u32[]{:S(2)}, u32[]{:S(2)}) async-start(bf16[8,64,384]{2,1,0:T(8,128)(2,1)} %out_projection.1), calls=%async_computation | async-start | bytes 786432 | tf_op jit(solution)/shard_map/all_to_all | solution.py:220
  47.3 14.2 %all-to-all-done = bf16[8,64,384]{2,1,0:T(8,128)(2,1)} async-done(((bf16[8,64,384]{2,1,0:T(8,128)(2,1)}), bf16[8,64,384]{2,1,0:T(8,128)(2,1)}, u32[]{:S(2)}, u32[]{:S(2)}) %all-to-all-start) | async-done | bytes 393248 | tf_op jit(solution)/shard_map/all_to_all | solution.py:220
  64.6 13.4 %all_to_all.15 = bf16[8,32,384]{2,1,0:T(8,128)(2,1)S(1)} all-to-all(bf16[8,32,384]{2,1,0:T(8,128)(2,1)S(1)} %bitcast.143), channel_id=1, replica_groups=mesh['dp'=16,'tensor'=8,'side'=2] {'tensor'}, dimensions={0} | all-to-all | bytes 393216 | tf_op jit(solution)/shard_map/all_to_all | solution.py:229
  78.0 1.9 collective-permute-start.10
  79.9 1.2 collective-permute-start.9
  82.7 2.3 %collective-permute-done.9 = bf16[128,384]{1,0:T(8,128)(2,1)S(1)} collective-permute-done((bf16[128,384]{1,0:T(8,128)(2,1)S(1)}, bf16[128,384]{1,0:T(8,128)(2,1)S(1)}, u32[]{:S(2)}, u32[]{:S(2)}) %collective-permute-start.9) | collective-permute-done | bytes 98336 | tf_op jit(solution)/shard_map/ppermute | solution.py:235
  84.9 2.6 %collective-permute-done.8 = bf16[128,384]{1,0:T(8,128)(2,1)S(1)} collective-permute-done((bf16[128,384]{1,0:T(8,128)(2,1)S(1)}, bf16[128,384]{1,0:T(8,128)(2,1)S(1)}, u32[]{:S(2)}, u32[]{:S(2)}) %collective-permute-start.8) | collective-permute-done | bytes 98336 | tf_op jit(solution)/shard_map/ppermute | solution.py:235
  88.5 1.3 collective-permute-start.15
  89.9 2.1 collective-permute-start.19
  92.0 2.6 %collective-permute-start.17 = (bf16[4,128,384]{2,1,0:T(8,128)(2,1)S(1)}, bf16[4,128,384]{2,1,0:T(8,128)(2,1)S(1)}, u32[]{:S(2)}, u32[]{:S(2)}) collective-permute-start(bf16[4,128,384]{2,1,0:T(8,128)(2,1)S(1)} %pad_maximum_fusion.1.a0), channel_id=1, source_target_pairs={{0,48},{16,0},{32,16},{48,32},{64,112},{80,64},{96,80},{112,96},{1... | collective-permute-start | bytes 1179656 | tf_op jit(solution)/shard_map/ppermute | solution.py:240
  94.6 3.9 %collective-permute-done.15.b1 = bf16[4,128,384]{2,1,0:T(8,128)(2,1)S(1)} collective-permute-done((bf16[4,128,384]{2,1,0:T(8,128)(2,1)S(1)}, bf16[4,128,384]{2,1,0:T(8,128)(2,1)S(1)}, u32[]{:S(2)}, u32[]{:S(2)}) %collective-permute-start.15) | collective-permute-done | bytes 393248 | tf_op jit(solution)/shard_map/ppermute | solution.py:241
  98.7 3.3 %collective-permute-start.18 = (bf16[4,128,384]{2,1,0:T(8,128)(2,1)S(1)}, bf16[4,128,384]{2,1,0:T(8,128)(2,1)S(1)}, u32[]{:S(2)}, u32[]{:S(2)}) collective-permute-start(bf16[4,128,384]{2,1,0:T(8,128)(2,1)S(1)} %pad_maximum_fusion.2.b0), channel_id=1, source_target_pairs={{0,128},{16,144},{32,160},{48,176},{64,192},{80,208},{96,224},{112... | collective-permute-start | bytes 1179656 | tf_op jit(solution)/shard_map/ppermute | solution.py:244
  102.0 4.7 %collective-permute-done.16.a2 = bf16[4,128,384]{2,1,0:T(8,128)(2,1)S(1)} collective-permute-done((bf16[4,128,384]{2,1,0:T(8,128)(2,1)S(1)}, bf16[4,128,384]{2,1,0:T(8,128)(2,1)S(1)}, u32[]{:S(2)}, u32[]{:S(2)}) %collective-permute-start.16) | collective-permute-done | bytes 393248 | tf_op jit(solution)/shard_map/ppermute | solution.py:244
  107.5 4.1 %norm.1 = bf16[256,6144]{1,0:T(8,128)(2,1)} custom-call(s32[3]{0:T(128)S(1)} %pad_add_fusion.pos, bf16[4,128,384]{2,1,0:T(8,128)(2,1)S(1)} %pad_maximum_fusion.1.a0, bf16[4,128,384]{2,1,0:T(8,128)(2,1)S(1)} %collective-permute-done.14.a1, bf16[4,128,384]{2,1,0:T(8,128)(2,1)S(1)} %collective-permute-done.16.a2, ...), custom_call_target="tpu_custom_call" | custom-call | tf_op jit(solution)/shard_map/norm/pallas_call | solution.py:245
  111.6 4.9 %collective-permute-start.20 = (bf16[256,6144]{1,0:T(8,128)(2,1)}, bf16[256,6144]{1,0:T(8,128)(2,1)S(1)}, u32[]{:S(2)}, u32[]{:S(2)}) collective-permute-start(bf16[256,6144]{1,0:T(8,128)(2,1)} %norm.1), channel_id=1, source_target_pairs={{0,1},{1,0},{2,3},{3,2},{4,5},{5,4},{6,7},{7,6},{8,9},{9,8},{10,11... | collective-permute-start | bytes 9437192 | tf_op jit(solution)/shard_map/ppermute | solution.py:21
  116.5 2.9 %fusion.6 = f32[256,256]{1,0:T(8,128)S(1)} fusion(bf16[256,6144]{1,0:T(8,128)(2,1)} %norm.1, bf16[1,6144,256]{2,1,0:T(8,128)(2,1)S(1)} %copy-done), kind=kOutput, calls=%fused_computation.6 | convolution fusion | flops 805306368 | bytes 6553600 | tf_op jit(solution)/shard_map/dot_general | solution.py:256
  120.4 6.3 %expert_down.2 = (bf16[2,2,4,128,384]{4,3,2,1,0:T(8,128)(2,1)S(1)}, bf16[2,2,4,128,384]{4,3,2,1,0:T(8,128)(2,1)S(1)}) custom-call(s32[3]{0:T(128)S(1)} %pad_add_fusion.pos, bf16[256,256]{1,0:T(8,128)(2,1)S(1)} %multiply_convert_fusion.2.inner, bf16[256,6144]{1,0:T(8,128)(2,1)} %bitcast.137), custom_call_target="tpu_custom_call" | custom-call | tf_op jit(solution)/shard_map/expert_down/pallas_call | solution.py:93
  129.5 7.8 %expert_down.3 = (bf16[2,2,4,128,384]{4,3,2,1,0:T(8,128)(2,1)}, bf16[2,2,4,128,384]{4,3,2,1,0:T(8,128)(2,1)}) custom-call(s32[3]{0:T(128)S(1)} %pad_add_fusion.pos, bf16[256,256]{1,0:T(8,128)(2,1)S(1)} %multiply_convert_fusion.1.inner, bf16[256,6144]{1,0:T(8,128)(2,1)} %bitcast.138), custom_call_target="tpu_custom_call" | custom-call | tf_op jit(solution)/shard_map/expert_down/pallas_call | solution.py:93
  138.4 3.2 %collective-permute-done.22 = bf16[2,2,4,128,384]{4,3,2,1,0:T(8,128)(2,1)} collective-permute-done((bf16[2,2,4,128,384]{4,3,2,1,0:T(8,128)(2,1)}, bf16[2,2,4,128,384]{4,3,2,1,0:T(8,128)(2,1)}, u32[]{:S(2)}, u32[]{:S(2)}) %collective-permute-start.22) | collective-permute-done | bytes 1572896 | tf_op jit(solution)/shard_map/ppermute | solution.py:21
  141.6 3.1 %fusion.24 = (bf16[4,128,384]{2,1,0:T(8,128)(2,1)}, bf16[4,128,384]{2,1,0:T(8,128)(2,1)}, bf16[4,128,384]{2,1,0:T(8,128)(2,1)}, bf16[4,128,384]{2,1,0:T(8,128)(2,1)S(1)}) fusion(bf16[2,2,4,128,384]{4,3,2,1,0:T(8,128)(2,1)} %collective-permute-done.22, bf16[2,2,4,128,384]{4,3,2,1,0:T(8,128)(2,1)} %copy-done.4), kind=kLoop, calls=%fused_computation.43 | loop fusion | flops 3145728 | bytes 4718592 | tf_op jit(solution)/shard_map/convert_element_type | solution.py:274
  144.8 1.3 collective-permute-start.23
  146.2 2.1 collective-permute-start.24
  148.4 2.7 %collective-permute-start.30 = (bf16[4,128,384]{2,1,0:T(8,128)(2,1)}, bf16[4,128,384]{2,1,0:T(8,128)(2,1)}, u32[]{:S(2)}, u32[]{:S(2)}) collective-permute-start(bf16[4,128,384]{2,1,0:T(8,128)(2,1)} %get-tuple-element.58), channel_id=1, source_target_pairs={{0,192},{16,208},{32,224},{48,240},{64,0},{80,16},{96,32},{112,48}... | collective-permute-start | bytes 1179656 | tf_op jit(solution)/shard_map/ppermute | solution.py:278
  151.1 2.2 %fusion.25 = (bf16[4,128,384]{2,1,0:T(8,128)(2,1)}, bf16[4,128,384]{2,1,0:T(8,128)(2,1)}) fusion(bf16[2,2,4,128,384]{4,3,2,1,0:T(8,128)(2,1)} %collective-permute-done.21, bf16[2,2,4,128,384]{4,3,2,1,0:T(8,128)(2,1)S(1)} %copy-done.2), kind=kLoop, calls=%fused_computation.44 | loop fusion | flops 1572864 | bytes 2359296 | tf_op jit(solution)/shard_map/convert_element_type | solution.py:276
  153.3 1.2 collective-permute-start.25
  154.5 3.0 %collective-permute-done.23 = bf16[4,128,384]{2,1,0:T(8,128)(2,1)} collective-permute-done((bf16[4,128,384]{2,1,0:T(8,128)(2,1)S(1)}, bf16[4,128,384]{2,1,0:T(8,128)(2,1)}, u32[]{:S(2)}, u32[]{:S(2)}) %collective-permute-start.23) | collective-permute-done | bytes 393248 | tf_op jit(solution)/shard_map/ppermute | solution.py:277
  157.5 1.7 collective-permute-start.31
  159.5 2.9 %fusion.11 = f32[256]{0:T(256)S(1)} fusion(bf16[256,6144]{1,0:T(8,128)(2,1)} %norm.1, bf16[6144,8]{0,1:T(8,128)(2,1)S(1)} %copy-done.9, s32[256]{0:T(256)S(1)} %eq.144, f32[8]{0:T(128)S(1)} %compare_convert_fusion), kind=kOutput, calls=%fused_computation.17 | convolution fusion | flops 25175808 | bytes 3246112 | tf_op jit(solution)/shard_map/dot_general | solution.py:260
  162.5 4.3 %collective-permute-done.25 = bf16[4,128,384]{2,1,0:T(8,128)(2,1)} collective-permute-done((bf16[4,128,384]{2,1,0:T(8,128)(2,1)}, bf16[4,128,384]{2,1,0:T(8,128)(2,1)}, u32[]{:S(2)}, u32[]{:S(2)}) %collective-permute-start.25) | collective-permute-done | bytes 393248 | tf_op jit(solution)/shard_map/ppermute | solution.py:277
  166.8 2.3 %collective-permute-done.31 = bf16[4,128,384]{2,1,0:T(8,128)(2,1)} collective-permute-done((bf16[4,128,384]{2,1,0:T(8,128)(2,1)}, bf16[4,128,384]{2,1,0:T(8,128)(2,1)}, u32[]{:S(2)}, u32[]{:S(2)}) %collective-permute-start.31) | collective-permute-done | bytes 393248 | tf_op jit(solution)/shard_map/ppermute | solution.py:278
  169.1 3.5 %fusion.49 = (bf16[4,128,384]{2,1,0:T(8,128)(2,1)S(1)}, f32[4,128,384]{2,1,0:T(8,128)}, bf16[4,128,384]{2,1,0:T(8,128)(2,1)S(1)}, f32[4,128,384]{2,1,0:T(8,128)}) fusion(bf16[4,128,384]{2,1,0:T(8,128)(2,1)} %collective-permute-done.25, bf16[4,128,384]{2,1,0:T(8,128)(2,1)} %collective-permute-done.24, bf16[4,128,384]{2,1,0:T(8,128)(2,1)} %collective-permute-done.23, ...), kind=kLoop, calls=%fused_computation.110 | loop fusion | flops 3932160 | bytes 6291456 | tf_op jit(solution)/shard_map/convert.6
  172.6 1.6 collective-permute-start.28
  176.5 9.6 %collective-permute-start.33 = (bf16[128,384]{1,0:T(8,128)(2,1)}, bf16[128,384]{1,0:T(8,128)(2,1)}, u32[]{:S(2)}, u32[]{:S(2)}) collective-permute-start(bf16[128,384]{1,0:T(8,128)(2,1)} %get-tuple-element.78), channel_id=1, source_target_pairs={{0,32},{16,48},{32,0},{48,16},{64,96},{80,112},{96,64},{112,80},{1... | collective-permute-start | bytes 294920 | tf_op jit(solution)/shard_map/ppermute | solution.py:283
  188.4 4.2 %collective-permute-done.32 = bf16[128,384]{1,0:T(8,128)(2,1)} collective-permute-done((bf16[128,384]{1,0:T(8,128)(2,1)}, bf16[128,384]{1,0:T(8,128)(2,1)}, u32[]{:S(2)}, u32[]{:S(2)}) %collective-permute-start.32) | collective-permute-done | bytes 98336 | tf_op jit(solution)/shard_map/ppermute | solution.py:283
  192.6 1.4 fusion.30
  194.8 3.8 %all-to-all-start.2 = ((bf16[8,32,384]{2,1,0:T(8,128)(2,1)}), bf16[8,32,384]{2,1,0:T(8,128)(2,1)S(1)}, u32[]{:S(2)}, u32[]{:S(2)}) async-start(bf16[8,32,384]{2,1,0:T(8,128)(2,1)} %multiply_convert_fusion), calls=%async_computation.2 | async-start | bytes 393216 | tf_op jit(solution)/shard_map/all_to_all | solution.py:288
  199.5 7.8 %all-to-all-done.2 = bf16[8,32,384]{2,1,0:T(8,128)(2,1)S(1)} async-done(((bf16[8,32,384]{2,1,0:T(8,128)(2,1)}), bf16[8,32,384]{2,1,0:T(8,128)(2,1)S(1)}, u32[]{:S(2)}, u32[]{:S(2)}) %all-to-all-start.2) | async-done | bytes 196640 | tf_op jit(solution)/shard_map/all_to_all | solution.py:288
  207.4 4.9 %collective-permute-start.35 = (bf16[256,192]{1,0:T(8,128)(2,1)S(1)}, bf16[256,192]{1,0:T(8,128)(2,1)S(1)}, u32[]{:S(2)}, u32[]{:S(2)}) collective-permute-start(bf16[256,192]{1,0:T(8,128)(2,1)S(1)} %broadcast_select_fusion), channel_id=1, source_target_pairs={{0,1},{1,0},{2,3},{3,2},{4,5},{5,4},{6,7},{7,6},{8,9},{9,8},{10,11... | collective-permute-start | bytes 294920 | tf_op jit(solution)/shard_map/ppermute | solution.py:21
  (126 shorter events, 32.1 us)
Async XLA Ops:
  0.0 116.5 %copy-start = (bf16[1,6144,256]{2,1,0:T(8,128)(2,1)S(1)}, bf16[1,6144,256]{2,1,0:T(8,128)(2,1)}, u32[]{:S(2)}) copy-start(bf16[1,6144,256]{2,1,0:T(8,128)(2,1)} %param.25) | copy-start | bytes 9437188
  0.0 13.7 %copy-start.11 = (bf16[128,192]{0,1:T(8,128)(2,1)S(1)}, bf16[128,192]{0,1:T(8,128)(2,1)}, u32[]{:S(2)}) copy-start(bf16[128,192]{0,1:T(8,128)(2,1)} %param.21) | copy-start | bytes 147460
  9.3 8.9 %collective-permute-start.2 = (bf16[32,768]{1,0:T(8,128)(2,1)}, bf16[32,768]{1,0:T(8,128)(2,1)}, u32[]{:S(2)}, u32[]{:S(2)}) collective-permute-start(bf16[32,768]{1,0:T(8,128)(2,1)} %bitcast.134), channel_id=1, source_target_pairs={{0,192},{16,208},{32,224},{48,240},{64,0},{80,16},{96,32},{112,48}... | collective-permute-start | bytes 147464 | tf_op jit(solution)/shard_map/ppermute | solution.py:201
  12.6 5.6 %collective-permute-start.1 = (bf16[32,768]{1,0:T(8,128)(2,1)}, bf16[32,768]{1,0:T(8,128)(2,1)}, u32[]{:S(2)}, u32[]{:S(2)}) collective-permute-start(bf16[32,768]{1,0:T(8,128)(2,1)} %bitcast.134), channel_id=1, source_target_pairs={{0,128},{16,144},{32,160},{48,176},{64,192},{80,208},{96,224},{112... | collective-permute-start | bytes 147464 | tf_op jit(solution)/shard_map/ppermute | solution.py:201
  13.1 5.1 %collective-permute-start = (bf16[32,768]{1,0:T(8,128)(2,1)}, bf16[32,768]{1,0:T(8,128)(2,1)}, u32[]{:S(2)}, u32[]{:S(2)}) collective-permute-start(bf16[32,768]{1,0:T(8,128)(2,1)} %bitcast.134), channel_id=1, source_target_pairs={{0,64},{16,80},{32,96},{48,112},{64,128},{80,144},{96,160},{112,17... | collective-permute-start | bytes 147464 | tf_op jit(solution)/shard_map/ppermute | solution.py:201
  17.3 29.0 %copy-start.12 = (s32[1024,2]{0,1:T(2,128)S(1)}, s32[1024,2]{0,1:T(2,128)}, u32[]{:S(2)}) copy-start(s32[1024,2]{0,1:T(2,128)} %param.24) | copy-start | bytes 24580
  19.1 5.7 %collective-permute-start.6 = (bf16[896,192]{1,0:T(8,128)(2,1)}, bf16[896,192]{1,0:T(8,128)(2,1)}, u32[]{:S(2)}, u32[]{:S(2)}) collective-permute-start(bf16[896,192]{1,0:T(8,128)(2,1)} %pad_maximum_fusion), channel_id=1, source_target_pairs={{0,1},{1,0},{2,3},{3,2},{4,5},{5,4},{6,7},{7,6},{8,9},{9,8},{10,11... | collective-permute-start | bytes 1032200 | tf_op jit(solution)/shard_map/ppermute | solution.py:21
  21.0 11.0 %collective-permute-start.5 = (bf16[4,32,768]{2,1,0:T(8,128)(2,1)S(1)}, bf16[4,32,768]{2,1,0:T(8,128)(2,1)S(1)}, u32[]{:S(2)}, u32[]{:S(2)}) collective-permute-start(bf16[4,32,768]{2,1,0:T(8,128)(2,1)S(1)} %pad_maximum_fusion.4.g0), channel_id=1, source_target_pairs={{0,48},{16,0},{32,16},{48,32},{64,112},{80,64},{96,80},{112,96},{1... | collective-permute-start | bytes 589832 | tf_op jit(solution)/shard_map/ppermute | solution.py:210
  23.7 8.2 %collective-permute-start.4 = (bf16[4,32,768]{2,1,0:T(8,128)(2,1)S(1)}, bf16[4,32,768]{2,1,0:T(8,128)(2,1)S(1)}, u32[]{:S(2)}, u32[]{:S(2)}) collective-permute-start(bf16[4,32,768]{2,1,0:T(8,128)(2,1)S(1)} %pad_maximum_fusion.4.g0), channel_id=1, source_target_pairs={{0,32},{16,48},{32,0},{48,16},{64,96},{80,112},{96,64},{112,80},{1... | collective-permute-start | bytes 589832 | tf_op jit(solution)/shard_map/ppermute | solution.py:210
  24.1 12.2 %collective-permute-start.3 = (bf16[4,32,768]{2,1,0:T(8,128)(2,1)S(1)}, bf16[4,32,768]{2,1,0:T(8,128)(2,1)S(1)}, u32[]{:S(2)}, u32[]{:S(2)}) collective-permute-start(bf16[4,32,768]{2,1,0:T(8,128)(2,1)S(1)} %pad_maximum_fusion.4.g0), channel_id=1, source_target_pairs={{0,16},{16,32},{32,48},{48,0},{64,80},{80,96},{96,112},{112,64},{1... | collective-permute-start | bytes 589832 | tf_op jit(solution)/shard_map/ppermute | solution.py:210
  26.9 5.1 %copy-start.7 = (bf16[896,384]{1,0:T(8,128)(2,1)}, bf16[896,384]{1,0:T(8,128)(2,1)S(1)}, u32[]{:S(2)}) copy-start(bf16[896,384]{1,0:T(8,128)(2,1)S(1)} %maximum_select_fusion) | copy-start | bytes 2064388
  27.0 80.5 %copy-start.5 = (f32[6144]{0:T(1024)S(1)}, f32[6144]{0:T(1024)}, u32[]{:S(2)}) copy-start(f32[6144]{0:T(1024)} %param.22) | copy-start | bytes 73732
  38.1 23.4 %all-to-all-start = ((bf16[8,64,384]{2,1,0:T(8,128)(2,1)}), bf16[8,64,384]{2,1,0:T(8,128)(2,1)}, u32[]{:S(2)}, u32[]{:S(2)}) async-start(bf16[8,64,384]{2,1,0:T(8,128)(2,1)} %out_projection.1), calls=%async_computation | async-start | bytes 786432 | tf_op jit(solution)/shard_map/all_to_all | solution.py:220
  62.6 1.8 collective-permute-start.7
  78.0 4.1 %collective-permute-start.10 = (bf16[128,384]{1,0:T(8,128)(2,1)S(1)}, bf16[128,384]{1,0:T(8,128)(2,1)S(1)}, u32[]{:S(2)}, u32[]{:S(2)}) collective-permute-start(bf16[128,384]{1,0:T(8,128)(2,1)S(1)} %bitcast.145), channel_id=1, source_target_pairs={{0,192},{16,208},{32,224},{48,240},{64,0},{80,16},{96,32},{112,48}... | collective-permute-start | bytes 294920 | tf_op jit(solution)/shard_map/ppermute | solution.py:235
  79.9 5.0 %collective-permute-start.9 = (bf16[128,384]{1,0:T(8,128)(2,1)S(1)}, bf16[128,384]{1,0:T(8,128)(2,1)S(1)}, u32[]{:S(2)}, u32[]{:S(2)}) collective-permute-start(bf16[128,384]{1,0:T(8,128)(2,1)S(1)} %bitcast.146), channel_id=1, source_target_pairs={{0,128},{16,144},{32,160},{48,176},{64,192},{80,208},{96,224},{112... | collective-permute-start | bytes 294920 | tf_op jit(solution)/shard_map/ppermute | solution.py:235
  81.2 6.4 %collective-permute-start.8 = (bf16[128,384]{1,0:T(8,128)(2,1)S(1)}, bf16[128,384]{1,0:T(8,128)(2,1)S(1)}, u32[]{:S(2)}, u32[]{:S(2)}) collective-permute-start(bf16[128,384]{1,0:T(8,128)(2,1)S(1)} %bitcast.147), channel_id=1, source_target_pairs={{0,64},{16,80},{32,96},{48,112},{64,128},{80,144},{96,160},{112,17... | collective-permute-start | bytes 294920 | tf_op jit(solution)/shard_map/ppermute | solution.py:235
  81.2 6.4 %collective-permute-start.13 = (bf16[128,384]{1,0:T(8,128)(2,1)S(1)}, bf16[128,384]{1,0:T(8,128)(2,1)S(1)}, u32[]{:S(2)}, u32[]{:S(2)}) collective-permute-start(bf16[128,384]{1,0:T(8,128)(2,1)S(1)} %bitcast.149), channel_id=1, source_target_pairs={{0,48},{16,0},{32,16},{48,32},{64,112},{80,64},{96,80},{112,96},{1... | collective-permute-start | bytes 294920 | tf_op jit(solution)/shard_map/ppermute | solution.py:236
  81.2 6.4 %collective-permute-start.12 = (bf16[128,384]{1,0:T(8,128)(2,1)S(1)}, bf16[128,384]{1,0:T(8,128)(2,1)S(1)}, u32[]{:S(2)}, u32[]{:S(2)}) collective-permute-start(bf16[128,384]{1,0:T(8,128)(2,1)S(1)} %bitcast.150), channel_id=1, source_target_pairs={{0,32},{16,48},{32,0},{48,16},{64,96},{80,112},{96,64},{112,80},{1... | collective-permute-start | bytes 294920 | tf_op jit(solution)/shard_map/ppermute | solution.py:236
  82.2 6.3 %collective-permute-start.11 = (bf16[128,384]{1,0:T(8,128)(2,1)S(1)}, bf16[128,384]{1,0:T(8,128)(2,1)S(1)}, u32[]{:S(2)}, u32[]{:S(2)}) collective-permute-start(bf16[128,384]{1,0:T(8,128)(2,1)S(1)} %bitcast.151), channel_id=1, source_target_pairs={{0,16},{16,32},{32,48},{48,0},{64,80},{80,96},{96,112},{112,64},{1... | collective-permute-start | bytes 294920 | tf_op jit(solution)/shard_map/ppermute | solution.py:236
  88.5 10.1 %collective-permute-start.15 = (bf16[4,128,384]{2,1,0:T(8,128)(2,1)S(1)}, bf16[4,128,384]{2,1,0:T(8,128)(2,1)S(1)}, u32[]{:S(2)}, u32[]{:S(2)}) collective-permute-start(bf16[4,128,384]{2,1,0:T(8,128)(2,1)S(1)} %pad_maximum_fusion.2.b0), channel_id=1, source_target_pairs={{0,64},{16,80},{32,96},{48,112},{64,128},{80,144},{96,160},{112,17... | collective-permute-start | bytes 1179656 | tf_op jit(solution)/shard_map/ppermute | solution.py:241
  89.8 8.7 %collective-permute-start.14 = (bf16[4,128,384]{2,1,0:T(8,128)(2,1)S(1)}, bf16[4,128,384]{2,1,0:T(8,128)(2,1)S(1)}, u32[]{:S(2)}, u32[]{:S(2)}) collective-permute-start(bf16[4,128,384]{2,1,0:T(8,128)(2,1)S(1)} %pad_maximum_fusion.1.a0), channel_id=1, source_target_pairs={{0,16},{16,32},{32,48},{48,0},{64,80},{80,96},{96,112},{112,64},{1... | collective-permute-start | bytes 1179656 | tf_op jit(solution)/shard_map/ppermute | solution.py:240
  89.9 12.1 %collective-permute-start.19 = (bf16[4,128,384]{2,1,0:T(8,128)(2,1)S(1)}, bf16[4,128,384]{2,1,0:T(8,128)(2,1)S(1)}, u32[]{:S(2)}, u32[]{:S(2)}) collective-permute-start(bf16[4,128,384]{2,1,0:T(8,128)(2,1)S(1)} %pad_maximum_fusion.2.b0), channel_id=1, source_target_pairs={{0,192},{16,208},{32,224},{48,240},{64,0},{80,16},{96,32},{112,48}... | collective-permute-start | bytes 1179656 | tf_op jit(solution)/shard_map/ppermute | solution.py:241
  92.0 10.0 %collective-permute-start.17 = (bf16[4,128,384]{2,1,0:T(8,128)(2,1)S(1)}, bf16[4,128,384]{2,1,0:T(8,128)(2,1)S(1)}, u32[]{:S(2)}, u32[]{:S(2)}) collective-permute-start(bf16[4,128,384]{2,1,0:T(8,128)(2,1)S(1)} %pad_maximum_fusion.1.a0), channel_id=1, source_target_pairs={{0,48},{16,0},{32,16},{48,32},{64,112},{80,64},{96,80},{112,96},{1... | collective-permute-start | bytes 1179656 | tf_op jit(solution)/shard_map/ppermute | solution.py:240
  98.5 8.1 %collective-permute-start.16 = (bf16[4,128,384]{2,1,0:T(8,128)(2,1)S(1)}, bf16[4,128,384]{2,1,0:T(8,128)(2,1)S(1)}, u32[]{:S(2)}, u32[]{:S(2)}) collective-permute-start(bf16[4,128,384]{2,1,0:T(8,128)(2,1)S(1)} %pad_maximum_fusion.1.a0), channel_id=1, source_target_pairs={{0,32},{16,48},{32,0},{48,16},{64,96},{80,112},{96,64},{112,80},{1... | collective-permute-start | bytes 1179656 | tf_op jit(solution)/shard_map/ppermute | solution.py:244
  98.7 8.8 %collective-permute-start.18 = (bf16[4,128,384]{2,1,0:T(8,128)(2,1)S(1)}, bf16[4,128,384]{2,1,0:T(8,128)(2,1)S(1)}, u32[]{:S(2)}, u32[]{:S(2)}) collective-permute-start(bf16[4,128,384]{2,1,0:T(8,128)(2,1)S(1)} %pad_maximum_fusion.2.b0), channel_id=1, source_target_pairs={{0,128},{16,144},{32,160},{48,176},{64,192},{80,208},{96,224},{112... | collective-permute-start | bytes 1179656 | tf_op jit(solution)/shard_map/ppermute | solution.py:244
  111.6 7.8 %copy-start.6 = (bf16[256,6144]{1,0:T(8,128)(2,1)S(1)}, bf16[256,6144]{1,0:T(8,128)(2,1)}, u32[]{:S(2)}) copy-start(bf16[256,6144]{1,0:T(8,128)(2,1)} %norm.1) | copy-start | bytes 9437188
  111.6 7.8 %copy-start.13 = (bf16[1,6144,256]{2,1,0:T(8,128)(2,1)S(1)}, bf16[1,6144,256]{2,1,0:T(8,128)(2,1)}, u32[]{:S(2)}) copy-start(bf16[1,6144,256]{2,1,0:T(8,128)(2,1)} %param.26) | copy-start | bytes 9437188
  111.6 15.2 %collective-permute-start.20 = (bf16[256,6144]{1,0:T(8,128)(2,1)}, bf16[256,6144]{1,0:T(8,128)(2,1)S(1)}, u32[]{:S(2)}, u32[]{:S(2)}) collective-permute-start(bf16[256,6144]{1,0:T(8,128)(2,1)} %norm.1), channel_id=1, source_target_pairs={{0,1},{1,0},{2,3},{3,2},{4,5},{5,4},{6,7},{7,6},{8,9},{9,8},{10,11... | collective-permute-start | bytes 9437192 | tf_op jit(solution)/shard_map/ppermute | solution.py:21
  137.3 4.4 %collective-permute-start.22 = (bf16[2,2,4,128,384]{4,3,2,1,0:T(8,128)(2,1)}, bf16[2,2,4,128,384]{4,3,2,1,0:T(8,128)(2,1)}, u32[]{:S(2)}, u32[]{:S(2)}) collective-permute-start(bf16[2,2,4,128,384]{4,3,2,1,0:T(8,128)(2,1)} %get-tuple-element.53), channel_id=1, source_target_pairs={{0,1},{1,0},{2,3},{3,2},{4,5},{5,4},{6,7},{7,6},{8,9},{9,8},{10,11... | collective-permute-start | bytes 4718600 | tf_op jit(solution)/shard_map/ppermute | solution.py:21
  138.3 6.5 %collective-permute-start.21 = (bf16[2,2,4,128,384]{4,3,2,1,0:T(8,128)(2,1)}, bf16[2,2,4,128,384]{4,3,2,1,0:T(8,128)(2,1)}, u32[]{:S(2)}, u32[]{:S(2)}) collective-permute-start(bf16[2,2,4,128,384]{4,3,2,1,0:T(8,128)(2,1)} %get-tuple-element.51), channel_id=1, source_target_pairs={{0,1},{1,0},{2,3},{3,2},{4,5},{5,4},{6,7},{7,6},{8,9},{9,8},{10,11... | collective-permute-start | bytes 4718600 | tf_op jit(solution)/shard_map/ppermute | solution.py:21
  138.4 12.7 %copy-start.2 = (bf16[2,2,4,128,384]{4,3,2,1,0:T(8,128)(2,1)S(1)}, bf16[2,2,4,128,384]{4,3,2,1,0:T(8,128)(2,1)}, u32[]{:S(2)}) copy-start(bf16[2,2,4,128,384]{4,3,2,1,0:T(8,128)(2,1)} %copy-done.1) | copy-start | bytes 4718596
  138.4 21.0 %copy-start.9 = (bf16[6144,8]{0,1:T(8,128)(2,1)S(1)}, bf16[6144,8]{0,1:T(8,128)(2,1)}, u32[]{:S(2)}) copy-start(bf16[6144,8]{0,1:T(8,128)(2,1)} %param.23) | copy-start | bytes 294916
  144.8 12.7 %collective-permute-start.23 = (bf16[4,128,384]{2,1,0:T(8,128)(2,1)S(1)}, bf16[4,128,384]{2,1,0:T(8,128)(2,1)}, u32[]{:S(2)}, u32[]{:S(2)}) collective-permute-start(bf16[4,128,384]{2,1,0:T(8,128)(2,1)S(1)} %get-tuple-element.55), channel_id=1, source_target_pairs={{0,16},{16,32},{32,48},{48,0},{64,80},{80,96},{96,112},{112,64},{1... | collective-permute-start | bytes 1179656 | tf_op jit(solution)/shard_map/ppermute | solution.py:277
  146.2 16.2 %collective-permute-start.24 = (bf16[4,128,384]{2,1,0:T(8,128)(2,1)}, bf16[4,128,384]{2,1,0:T(8,128)(2,1)}, u32[]{:S(2)}, u32[]{:S(2)}) collective-permute-start(bf16[4,128,384]{2,1,0:T(8,128)(2,1)} %get-tuple-element.56), channel_id=1, source_target_pairs={{0,48},{16,0},{32,16},{48,32},{64,112},{80,64},{96,80},{112,96},{1... | collective-permute-start | bytes 1179656 | tf_op jit(solution)/shard_map/ppermute | solution.py:277
  148.4 14.1 %collective-permute-start.29 = (bf16[4,128,384]{2,1,0:T(8,128)(2,1)}, bf16[4,128,384]{2,1,0:T(8,128)(2,1)}, u32[]{:S(2)}, u32[]{:S(2)}) collective-permute-start(bf16[4,128,384]{2,1,0:T(8,128)(2,1)} %get-tuple-element.57), channel_id=1, source_target_pairs={{0,64},{16,80},{32,96},{48,112},{64,128},{80,144},{96,160},{112,17... | collective-permute-start | bytes 1179656 | tf_op jit(solution)/shard_map/ppermute | solution.py:278
  148.4 14.1 %collective-permute-start.30 = (bf16[4,128,384]{2,1,0:T(8,128)(2,1)}, bf16[4,128,384]{2,1,0:T(8,128)(2,1)}, u32[]{:S(2)}, u32[]{:S(2)}) collective-permute-start(bf16[4,128,384]{2,1,0:T(8,128)(2,1)} %get-tuple-element.58), channel_id=1, source_target_pairs={{0,192},{16,208},{32,224},{48,240},{64,0},{80,16},{96,32},{112,48}... | collective-permute-start | bytes 1179656 | tf_op jit(solution)/shard_map/ppermute | solution.py:278
  153.3 13.5 %collective-permute-start.25 = (bf16[4,128,384]{2,1,0:T(8,128)(2,1)}, bf16[4,128,384]{2,1,0:T(8,128)(2,1)}, u32[]{:S(2)}, u32[]{:S(2)}) collective-permute-start(bf16[4,128,384]{2,1,0:T(8,128)(2,1)} %get-tuple-element.71), channel_id=1, source_target_pairs={{0,32},{16,48},{32,0},{48,16},{64,96},{80,112},{96,64},{112,80},{1... | collective-permute-start | bytes 1179656 | tf_op jit(solution)/shard_map/ppermute | solution.py:277
  157.5 11.6 %collective-permute-start.31 = (bf16[4,128,384]{2,1,0:T(8,128)(2,1)}, bf16[4,128,384]{2,1,0:T(8,128)(2,1)}, u32[]{:S(2)}, u32[]{:S(2)}) collective-permute-start(bf16[4,128,384]{2,1,0:T(8,128)(2,1)} %get-tuple-element.72), channel_id=1, source_target_pairs={{0,128},{16,144},{32,160},{48,176},{64,192},{80,208},{96,224},{112... | collective-permute-start | bytes 1179656 | tf_op jit(solution)/shard_map/ppermute | solution.py:278
  159.5 9.6 %copy-start.3 = (bf16[2,2,4,128,384]{4,3,2,1,0:T(8,128)(2,1)S(1)}, bf16[2,2,4,128,384]{4,3,2,1,0:T(8,128)(2,1)}, u32[]{:S(2)}) copy-start(bf16[2,2,4,128,384]{4,3,2,1,0:T(8,128)(2,1)} %copy-done.1) | copy-start | bytes 4718596
  172.6 13.5 %collective-permute-start.28 = (bf16[128,384]{1,0:T(8,128)(2,1)S(1)}, bf16[128,384]{1,0:T(8,128)(2,1)S(1)}, u32[]{:S(2)}, u32[]{:S(2)}) collective-permute-start(bf16[128,384]{1,0:T(8,128)(2,1)S(1)} %get-tuple-element.80), channel_id=1, source_target_pairs={{0,192},{16,208},{32,224},{48,240},{64,0},{80,16},{96,32},{112,48}... | collective-permute-start | bytes 294920 | tf_op jit(solution)/shard_map/ppermute | solution.py:282
  174.2 13.5 %collective-permute-start.27 = (bf16[128,384]{1,0:T(8,128)(2,1)S(1)}, bf16[128,384]{1,0:T(8,128)(2,1)}, u32[]{:S(2)}, u32[]{:S(2)}) collective-permute-start(bf16[128,384]{1,0:T(8,128)(2,1)S(1)} %get-tuple-element.81), channel_id=1, source_target_pairs={{0,128},{16,144},{32,160},{48,176},{64,192},{80,208},{96,224},{112... | collective-permute-start | bytes 294920 | tf_op jit(solution)/shard_map/ppermute | solution.py:282
  174.7 13.0 %collective-permute-start.26 = (bf16[128,384]{1,0:T(8,128)(2,1)S(1)}, bf16[128,384]{1,0:T(8,128)(2,1)}, u32[]{:S(2)}, u32[]{:S(2)}) collective-permute-start(bf16[128,384]{1,0:T(8,128)(2,1)S(1)} %get-tuple-element.82), channel_id=1, source_target_pairs={{0,64},{16,80},{32,96},{48,112},{64,128},{80,144},{96,160},{112,17... | collective-permute-start | bytes 294920 | tf_op jit(solution)/shard_map/ppermute | solution.py:282
  175.6 12.1 %collective-permute-start.34 = (bf16[128,384]{1,0:T(8,128)(2,1)}, bf16[128,384]{1,0:T(8,128)(2,1)}, u32[]{:S(2)}, u32[]{:S(2)}) collective-permute-start(bf16[128,384]{1,0:T(8,128)(2,1)} %get-tuple-element.77), channel_id=1, source_target_pairs={{0,48},{16,0},{32,16},{48,32},{64,112},{80,64},{96,80},{112,96},{1... | collective-permute-start | bytes 294920 | tf_op jit(solution)/shard_map/ppermute | solution.py:283
  176.5 12.0 %collective-permute-start.33 = (bf16[128,384]{1,0:T(8,128)(2,1)}, bf16[128,384]{1,0:T(8,128)(2,1)}, u32[]{:S(2)}, u32[]{:S(2)}) collective-permute-start(bf16[128,384]{1,0:T(8,128)(2,1)} %get-tuple-element.78), channel_id=1, source_target_pairs={{0,32},{16,48},{32,0},{48,16},{64,96},{80,112},{96,64},{112,80},{1... | collective-permute-start | bytes 294920 | tf_op jit(solution)/shard_map/ppermute | solution.py:283
  186.7 5.9 %collective-permute-start.32 = (bf16[128,384]{1,0:T(8,128)(2,1)}, bf16[128,384]{1,0:T(8,128)(2,1)}, u32[]{:S(2)}, u32[]{:S(2)}) collective-permute-start(bf16[128,384]{1,0:T(8,128)(2,1)} %get-tuple-element.79), channel_id=1, source_target_pairs={{0,16},{16,32},{32,48},{48,0},{64,80},{80,96},{96,112},{112,64},{1... | collective-permute-start | bytes 294920 | tf_op jit(solution)/shard_map/ppermute | solution.py:283
  194.8 12.5 %all-to-all-start.2 = ((bf16[8,32,384]{2,1,0:T(8,128)(2,1)}), bf16[8,32,384]{2,1,0:T(8,128)(2,1)S(1)}, u32[]{:S(2)}, u32[]{:S(2)}) async-start(bf16[8,32,384]{2,1,0:T(8,128)(2,1)} %multiply_convert_fusion), calls=%async_computation.2 | async-start | bytes 393216 | tf_op jit(solution)/shard_map/all_to_all | solution.py:288
  207.4 6.0 %collective-permute-start.35 = (bf16[256,192]{1,0:T(8,128)(2,1)S(1)}, bf16[256,192]{1,0:T(8,128)(2,1)S(1)}, u32[]{:S(2)}, u32[]{:S(2)}) collective-permute-start(bf16[256,192]{1,0:T(8,128)(2,1)S(1)} %broadcast_select_fusion), channel_id=1, source_target_pairs={{0,1},{1,0},{2,3},{3,2},{4,5},{5,4},{6,7},{7,6},{8,9},{9,8},{10,11... | collective-permute-start | bytes 294920 | tf_op jit(solution)/shard_map/ppermute | solution.py:21
  (4 other events, 4.2 us)
where the time goes:
time: 215 us; the launch traced here: 214 us
  starting transfers between devices  69.6 us (32%)
  waiting for transfers between devices  64.9 us (30%)
  Pallas kernels  20.1 us (9%)
  other arithmetic  20 us (9%)
  matrix products  16.4 us (8%)
  blocking collectives  13.4 us (6%)
  local copies, waits for them, and re-layouts  9.47 us (4%)
    all_to_all x1, waiting for transfers between devices, shards(): lax.all_to_all(head_sums, 'tensor', split_axis=0, concat_axis=0, tiled=True)  14.2 us
    pallas_call x2, Pallas kernels, down_call(): pl.pallas_call(down_kernel, in_specs=[pl.BlockSpec(memory_space=pltpu.SME...  14.1 us
    all_to_all x1, blocking collectives, shards(): lax.all_to_all(routed.reshape(8, 32, 384), 'tensor', split_axis=0, concat...  13.4 us
    ppermute x6, starting transfers between devices, swap_cores(): return lax.ppermute(a, 'side', SWAP)  13.4 us
    ppermute x3, starting transfers between devices, shards(): lax.ppermute(row_b[d].astype(BF16), 'dp', SHIFT_Y[d])  11.3 us
    ppermute x3, waiting for transfers between devices, shards(): lax.ppermute(rows_x, 'dp', SHIFT_Y[d])  9.27 us
    all_to_all x1, starting transfers between devices, shards(): lax.all_to_all(head_sums, 'tensor', split_axis=0, concat_axis=0, tiled=True)  8.19 us
    all_to_all x1, waiting for transfers between devices, shards(): lax.all_to_all(parts.reshape(8, 32, 384), 'tensor', split_axis=0, concat_...  7.78 us
  transfers between devices with their start and end apart: 38, of which 17 were waited for; matrix products, arithmetic and copies ran while one was open for 11% of the time, Pallas kernels for 3%

commit v1 on v0

--- a/solution.py
+++ b/solution.py
@@ -10,7 +10,7 @@
 eps = 1e-05
 F32 = jnp.float32
 BF16 = jnp.bfloat16
-VMEM_LIMIT = 48 * 1024 * 1024
+VMEM_LIMIT = 16 * 1024 * 1024
 
 SHIFT_X = [[(4 * x + y, 4 * ((x + d) % 4) + y) for x in range(4) for y in range(4)] for d in range(4)]
 SHIFT_Y = [[(4 * x + y, 4 * x + (y + d) % 4) for x in range(4) for y in range(4)] for d in range(4)]
@@ -27,11 +27,18 @@
 
 def outproj_kernel(pos, g0, g1, g2, g3, w, out):
     for dy, ref in enumerate((g0, g1, g2, g3)):
-        sums = jnp.dot(ref[...].reshape(128, 768), w[...], preferred_element_type=F32).astype(BF16)
-        for dx in range(4):
+
+        def work(dx, _, dy=dy, ref=ref):
+            sums = jnp.dot(ref[dx], w[...], preferred_element_type=F32)
             chip = chip_at(pos, -dx, -dy)
-            row = pl.multiple_of((chip & 1) * 32, 32)
-            out[chip // 2, pl.ds(row, 32), :] = sums[dx * 32 : dx * 32 + 32]
+            out[chip // 2, pl.ds(pl.multiple_of((chip & 1) * 32, 32), 32), :] = sums.astype(BF16)
+            return 0
+
+        lax.fori_loop(0, 4, work, 0)
+
+
+def at_half(pos, h, i, shift):
+    return chip_at(pos, i, shift) if h == 0 else chip_at(pos, shift, i)
 
 
 def norm_kernel(pos, a0, a1, a2, a3, b0, b1, b2, b3, gain, out):
@@ -39,66 +46,73 @@
 
         def rows_of(n, _, h=h, refs=refs):
             rows = pl.ds(pl.multiple_of(n * 32, 32), 32)
-            squares = jnp.zeros((32, 384), F32)
-            for i in range(4):
-                for j in range(4):
+            to = pl.ds(pl.multiple_of(h * 128 + n * 32, 32), 32)
+
+            def square(j, total):
+                for i in range(4):
                     v = refs[i][j, rows, :].astype(F32)
-                    squares = squares + v * v
+                    total = total + v * v
+                return total
+
+            squares = lax.fori_loop(0, 4, square, jnp.zeros((32, 384), F32))
             mean = jnp.sum(squares, axis=1, keepdims=True) * (1.0 / 6144.0)
             scale = lax.rsqrt(mean + eps)
-            to = pl.ds(pl.multiple_of(h * 128 + n * 32, 32), 32)
-            for i in range(4):
-                for j in range(4):
-                    chip = chip_at(pos, -j, -i) if h == 0 else chip_at(pos, -i, -j)
+
+            def store(j, _):
+                for i in range(4):
+                    chip = at_half(pos, h, -j, -i)
                     columns = pl.ds(pl.multiple_of(chip * 384, 128), 384)
                     v = refs[i][j, rows, :].astype(F32)
                     out[to, columns] = (v * scale * gain[chip]).astype(BF16)
+                return 0
+
+            lax.fori_loop(0, 4, store, 0)
             return 0
 
         lax.fori_loop(0, 4, rows_of, 0)
 
 
-def down_kernel(pos, inner, down_w, near, far, w, sems):
-    def copy(dx, dy):
-        columns = pl.ds(pl.multiple_of(chip_at(pos, dx, dy) * 384, 128), 384)
-        n = dx * 4 + dy
-        return pltpu.make_async_copy(down_w.at[:, columns], w.at[n], sems.at[n])
-
-    def issue(n, _):
-        copy(n // 4, n % 4).start()
+def combine_kernel(h):
+    def kernel(pos, own, other, *outs):
+        def work(n, _):
+            i, rows = n // 4, pl.ds(pl.multiple_of((n % 4) * 32, 32), 32)
+            to = pl.ds(pl.multiple_of(h * 128 + (n % 4) * 32, 32), 32)
+            for k in range(4):
+                columns = pl.ds(pl.multiple_of(at_half(pos, h, i, k) * 384, 128), 384)
+                mine = own[to, columns].astype(F32)
+                total = mine + other[rows, columns].astype(F32)
+                outs[k][i, rows, :] = total.astype(BF16)
+            return 0
+
+        lax.fori_loop(0, 16, work, 0)
+
+    return kernel
+
+
+def rows_kernel(mine, got1, got2, got3, *outs):
+    def work(n, _):
+        rows = pl.ds(pl.multiple_of(n * 32, 32), 32)
+        for i in range(4):
+            total = mine[i, rows, :].astype(F32)
+            for got in (got1, got2, got3):
+                total = total + got[i, rows, :].astype(F32)
+            outs[i][rows, :] = total.astype(outs[i].dtype)
         return 0
 
-    def arrive(n, _):
-        copy(n // 4, n % 4).wait()
-        return 0
-
-    lax.fori_loop(0, 16, issue, 0)
-    lax.fori_loop(0, 16, arrive, 0)
-    for out, base, step in ((near, 1, 2), (far, 2, -2)):
-
-        def work(n, _, out=out, base=base, step=step):
-            k, i = n // 4, n % 4
-            shift = base + step * k
-            first = jnp.dot(inner[0:128, :], w[i * 4 + shift], preferred_element_type=F32)
-            second = jnp.dot(inner[128:256, :], w[shift * 4 + i], preferred_element_type=F32)
-            out[k, 0, i] = first.astype(BF16)
-            out[k, 1, i] = second.astype(BF16)
-            return 0
-
-        lax.fori_loop(0, 8, work, 0)
-
-
-def down_call(pos, inner, down_w):
+    lax.fori_loop(0, 4, work, 0)
+
+
+def local_call(kernel, outs, name, *args, smem=True):
     vmem = pl.BlockSpec(memory_space=pltpu.VMEM)
+    first = [pl.BlockSpec(memory_space=pltpu.SMEM)] if smem else []
     return pl.pallas_call(
-        down_kernel,
-        in_specs=[pl.BlockSpec(memory_space=pltpu.SMEM), vmem, pl.BlockSpec(memory_space=pl.ANY)],
-        out_specs=[vmem, vmem],
-        out_shape=[jax.ShapeDtypeStruct((2, 2, 4, 128, 384), BF16)] * 2,
-        scratch_shapes=[pltpu.VMEM((16, 256, 384), BF16), pltpu.SemaphoreType.DMA((16,))],
+        kernel,
+        in_specs=first + [vmem] * (len(args) - len(first)),
+        out_specs=[vmem] * len(outs),
+        out_shape=[jax.ShapeDtypeStruct(*o) for o in outs],
         compiler_params=pltpu.CompilerParams(vmem_limit_bytes=VMEM_LIMIT),
-        name="expert_down",
-    )(pos, inner, down_w)
+        name=name,
+    )(*args)
 
 
 def attend(q_new, k_new, v_new, k_cache, v_cache, lengths):
@@ -178,6 +192,10 @@
         return jnp.where(first_core, a[:, :192], a[:, 192:])
 
     attention = attend(q_new, k_new, v_new, k_cache, v_cache, lengths)
+    out_w = by_core(attn_out_weight, swap_cores(attn_out_weight), 1)
+    residual_chip = by_core(residual, swap_cores(residual), 1).reshape(2, 2, 32, 384)
+    residual_half = jnp.where(first_core, residual_chip[:, 0], residual_chip[:, 1])
+
     labels = jnp.arange(EXPERTS, dtype=jnp.int32)
     block_ids = lax.dynamic_slice_in_dim(expert_ids, plane * 128, 128, 0)
     member = jnp.any(block_ids[:, :, None] == labels, axis=1)
@@ -200,13 +218,6 @@
 
     rows_x = [lax.ppermute(attention, "dp", SHIFT_X[d]) for d in (1, 2, 3)]
     rows_x = jnp.stack([attention] + rows_x)
-    columns, rows_x = lax.optimization_barrier(
-        (jnp.concatenate([attn_out_weight, residual], axis=0), rows_x)
-    )
-    columns = by_core(columns, swap_cores(columns), 1)
-    out_w = columns[:768]
-    residual_chip = columns[768:].reshape(2, 2, 32, 384)
-    residual_half = jnp.where(first_core, residual_chip[:, 0], residual_chip[:, 1])
     rows_xy = [rows_x] + [lax.ppermute(rows_x, "dp", SHIFT_Y[d]) for d in (1, 2, 3)]
     vmem = pl.BlockSpec(memory_space=pltpu.VMEM)
     head_sums = pl.pallas_call(
@@ -242,14 +253,16 @@
     ]
     far_a, far_b, a1, b1 = lax.optimization_barrier((stack_a, stack_b, a1, b1))
     a2, b2 = lax.ppermute(far_a, "dp", SHIFT_Y[2]), lax.ppermute(far_b, "dp", SHIFT_X[2])
-    normed = pl.pallas_call(
+    gain = norm_gain.reshape(16, 1, 384)
+    normed = local_call(
         norm_kernel,
-        in_specs=[pl.BlockSpec(memory_space=pltpu.SMEM)] + [vmem] * 9,
-        out_specs=vmem,
-        out_shape=jax.ShapeDtypeStruct((256, 6144), BF16),
-        compiler_params=pltpu.CompilerParams(vmem_limit_bytes=VMEM_LIMIT),
-        name="norm",
-    )(pos, stack_a, a1, a2, a3, stack_b, b1, b2, b3, norm_gain.reshape(16, 1, 384))
+        [((256, 6144), BF16)],
+        "norm",
+        pos,
+        *(stack_a, a1, a2, a3),
+        *(stack_b, b1, b2, b3),
+        gain,
+    )[0]
     normed_other = swap_cores(normed)
 
     def expert_in(rows):
@@ -257,32 +270,41 @@
         up = jnp.dot(rows, up_w, preferred_element_type=F32)
         return (jax.nn.silu(gate) * up).astype(BF16)
 
+    def expert_out_of(rows):
+        return jnp.dot(rows, down_w, preferred_element_type=F32).astype(BF16)
+
     logits = jnp.dot(normed, router_weight, preferred_element_type=F32)
     shares = jax.nn.sigmoid(jnp.sum(logits * signs, axis=1, keepdims=True))
-    own = down_call(pos, expert_in(normed), down_w)
-    own, normed_other = lax.optimization_barrier((own, normed_other))
-    other = down_call(pos, expert_in(normed_other), down_w)
-
-    def add(*terms):
-        total = terms[0].astype(F32)
-        for term in terms[1:]:
-            total = total + term.astype(F32)
-        return total
-
-    near = swap_cores(other[0])
-    far = swap_cores(other[1])
-    parts = [add(own[0][k, h], near[k, h]).astype(BF16) for k in (0, 1) for h in (0, 1)]
-    far, *parts = lax.optimization_barrier((far, *parts))
-    parts += [add(own[1][0, h], far[0, h]).astype(BF16) for h in (0, 1)]
-    got_a = [lax.ppermute(parts[2 * n], "dp", SHIFT_Y[d]) for n, d in enumerate((1, 3, 2))]
-    got_b = [lax.ppermute(parts[2 * n + 1], "dp", SHIFT_X[d]) for n, d in enumerate((1, 3, 2))]
-    part_a, part_b = add(own[1][1, 0], far[1, 0]), add(own[1][1, 1], far[1, 1])
-    row_a, row_b = add(part_a, *got_a), add(part_b, *got_b)
-    got = lax.optimization_barrier(
-        [lax.ppermute(row_a[d].astype(BF16), "dp", SHIFT_X[d]) for d in (1, 2, 3)]
-        + [lax.ppermute(row_b[d].astype(BF16), "dp", SHIFT_Y[d]) for d in (1, 2, 3)]
-    )
-    expert_out = jnp.concatenate([add(row_a[0], *got[:3]), add(row_b[0], *got[3:])], axis=0)
+    inner = expert_in(normed)
+    inner, normed_other = lax.optimization_barrier((inner, normed_other))
+    own = expert_out_of(inner)
+    inner_other = expert_in(normed_other)
+    other = [swap_cores(expert_out_of(inner_other[r : r + 128])) for r in (0, 128)]
+
+    expert_out = []
+    for h in (0, 1):
+        near, far = (SHIFT_Y, SHIFT_X) if h == 0 else (SHIFT_X, SHIFT_Y)
+        stack = (4, 128, 384)
+        sums = local_call(
+            combine_kernel(h),
+            [(stack, BF16)] * 4,
+            "combine_cores",
+            pos,
+            own,
+            other[h],
+        )
+        got = [lax.ppermute(sums[d], "dp", near[d]) for d in (1, 3, 2)]
+        rows = local_call(
+            rows_kernel,
+            [((128, 384), F32)] + [((128, 384), BF16)] * 3,
+            "sum_rows",
+            sums[0],
+            *got,
+            smem=False,
+        )
+        got = [lax.ppermute(rows[d], "dp", far[d]) for d in (1, 3, 2)]
+        expert_out.append(rows[0] + sum(g.astype(F32) for g in got))
+    expert_out = jnp.concatenate(expert_out)
 
     parts = (shares * expert_out).astype(BF16)
     back = lax.all_to_all(

time: 215 us -> 197 us (0.916)
  other arithmetic: 20 us -> 9.37 us
  starting transfers between devices: 69.6 us -> 63.8 us
  Pallas kernels: 20.1 us -> 17.3 us
  matrix products: 16.4 us -> 19.1 us
  waiting for transfers between devices: 64.9 us -> 62.4 us
    ppermute x12, waiting for transfers between devices: 14.6 us -> 5.37 us  [the longest x6 3.88 us: shards(): got = [lax.ppermute(sums[d], 'dp', near[d]) for d in (1, 3, 2)]]
    pallas_call x3 -> x5, Pallas kernels: 18.2 us -> 12.6 us  [local_call(): pl.pallas_call(kernel, in_specs=first + [vmem] * (len(args) - len(first))...]
    convert_element_type x2 -> x0, other arithmetic: 5.36 us -> none  [the longest x1 3.15 us: shards(): add(own[0][k, h], near[k, h]).astype(BF16)]
    dot_general x0 -> x3, matrix products: none -> 4.56 us  [expert_out_of(): return jnp.dot(rows, down_w, preferred_element_type=F32).astype(BF16)]
    ppermute x3, waiting for transfers between devices: 0.01 us -> 3.7 us  [shards(): rows_x = [lax.ppermute(attention, 'dp', SHIFT_X[d]) for d in (1, 2, 3)]]
    another operation x1 -> x0, other arithmetic: 3.52 us -> none
    ppermute x12, starting transfers between devices: 22.6 us -> 19.7 us  [the longest x6 10.1 us: shards(): got = [lax.ppermute(sums[d], 'dp', near[d]) for d in (1, 3, 2)]]
    pallas_call x1, Pallas kernels: 1.86 us -> 4.71 us  [shards(): pl.pallas_call(outproj_kernel, in_specs=[pl.BlockSpec(memory_space=pltpu....]
  transfers between devices with their start and end apart: 38 -> 39, of which waited for: 17 -> 22; matrix products, arithmetic and copies ran while one was open for 11% -> 14% of each run, Pallas kernels for 3% -> 5%
where the time goes in v1:
time: 197 us; the launch traced here: 196 us
  starting transfers between devices  63.8 us (32%)
  waiting for transfers between devices  62.4 us (32%)
  matrix products  19.1 us (10%)
  Pallas kernels  17.3 us (9%)
  blocking collectives  13.4 us (7%)
  local copies, waits for them, and re-layouts  10.1 us (5%)
  other arithmetic  9.37 us (5%)
    ppermute x7, starting transfers between devices, swap_cores(): return lax.ppermute(a, 'side', SWAP)  15.9 us
    all_to_all x1, blocking collectives, shards(): lax.all_to_all(routed.reshape(8, 32, 384), 'tensor', split_axis=0, concat...  13.4 us
    pallas_call x5, Pallas kernels, local_call(): pl.pallas_call(kernel, in_specs=first + [vmem] * (len(args) - len(first))...  12.6 us
    all_to_all x1, waiting for transfers between devices, shards(): lax.all_to_all(head_sums, 'tensor', split_axis=0, concat_axis=0, tiled=True)  12.4 us
    ppermute x6, starting transfers between devices, shards(): got = [lax.ppermute(sums[d], 'dp', near[d]) for d in (1, 3, 2)]  10.1 us
    ppermute x3, waiting for transfers between devices, shards(): lax.ppermute(rows_x, 'dp', SHIFT_Y[d])  9.73 us
    ppermute x6, starting transfers between devices, shards(): got = [lax.ppermute(rows[d], 'dp', far[d]) for d in (1, 3, 2)]  9.68 us
    all_to_all x1, starting transfers between devices, shards(): lax.all_to_all(head_sums, 'tensor', split_axis=0, concat_axis=0, tiled=True)  8.19 us
  transfers between devices with their start and end apart: 39, of which 22 were waited for; matrix products, arithmetic and copies ran while one was open for 14% of the time, Pallas kernels for 5%

profile of v1, /device:TPU:1, one launch (start us, length us, event | category | flops | bytes accessed | tf_op | source)
XLA Modules:
  0.0 195.9 jit_solution(11523623217853208290)
XLA Ops:
  0.0 1.3 copy.30
  1.3 3.3 %collective-permute-start.6 = (bf16[768,192]{1,0:T(8,128)(2,1)S(1)}, bf16[768,192]{1,0:T(8,128)(2,1)}, u32[]{:S(2)}, u32[]{:S(2)}) collective-permute-start(bf16[768,192]{1,0:T(8,128)(2,1)S(1)} %copy.30), channel_id=1, source_target_pairs={{0,1},{1,0},{2,3},{3,2},{4,5},{5,4},{6,7},{7,6},{8,9},{9,8},{10,11... | collective-permute-start | bytes 884744 | tf_op jit(solution)/shard_map/ppermute | solution.py:21
  5.3 1.3 convert_element_type.118
  6.6 1.5 reshape.199
  9.1 2.4 %fusion.38 = (f32[32,6]{1,0:T(8,128)S(1)}, f32[32,6,192]{2,1,0:T(8,128)S(1)}) fusion(bf16[32,6,128]{2,1,0:T(8,128)(2,1)} %reshape.199, bf16[32,192,128]{2,1,0:T(8,128)(2,1)} %param.17, pred[32,192]{1,0:T(8,128)(4,1)S(1)} %iota_compare_fusion.4), kind=kOutput, calls=%fused_computation.89 | convolution fusion | flops 9547584 | bytes 1776384 | tf_op jit(solution)/shard_map/rkgd,rckd->rkgc/dot_general | solution.py:131
  11.8 2.0 %fusion.12 = bf16[32,6,128]{2,1,0:T(8,128)(2,1)S(1)} fusion(bf16[32,192,128]{2,1,0:T(8,128)(2,1)} %param.18, f32[32,6,192]{2,1,0:T(8,128)S(1)} %get-tuple-element.73, f32[32,6]{1,0:T(8,128)S(1)} %get-tuple-element.66, f32[32,6]{1,0:T(8,128)S(1)} %multiply_maximum_fusion, f32[32,128]{1,0:T(8,128)} %convert_element_type.118, f32[32,6]{1,0:T(8,128)S(1)} %get-tuple-element.65), kind=kOutput, calls=%fused_computation.18 | convolution fusion | flops 9621504 | bytes 1788160 | tf_op jit(solution)/shard_map/rkgc,rckd->rkgd/dot_general | solution.py:146
  17.0 1.5 convert_element_type.120
  18.8 1.9 collective-permute-done.1
  20.6 1.6 collective-permute-done
  23.1 2.6 %collective-permute-start.5 = (bf16[4,32,768]{2,1,0:T(8,128)(2,1)S(1)}, bf16[4,32,768]{2,1,0:T(8,128)(2,1)S(1)}, u32[]{:S(2)}, u32[]{:S(2)}) collective-permute-start(bf16[4,32,768]{2,1,0:T(8,128)(2,1)S(1)} %pad_maximum_fusion.3.g0), channel_id=1, source_target_pairs={{0,48},{16,0},{32,16},{48,32},{64,112},{80,64},{96,80},{112,96},{1... | collective-permute-start | bytes 589832 | tf_op jit(solution)/shard_map/ppermute | solution.py:221
  26.8 1.7 maximum_select_fusion.w
  29.7 2.8 %collective-permute-done.4.g2 = bf16[4,32,768]{2,1,0:T(8,128)(2,1)S(1)} collective-permute-done((bf16[4,32,768]{2,1,0:T(8,128)(2,1)S(1)}, bf16[4,32,768]{2,1,0:T(8,128)(2,1)S(1)}, u32[]{:S(2)}, u32[]{:S(2)}) %collective-permute-start.4) | collective-permute-done | bytes 196640 | tf_op jit(solution)/shard_map/ppermute | solution.py:221
  32.5 5.7 %collective-permute-done.3.g1 = bf16[4,32,768]{2,1,0:T(8,128)(2,1)S(1)} collective-permute-done((bf16[4,32,768]{2,1,0:T(8,128)(2,1)S(1)}, bf16[4,32,768]{2,1,0:T(8,128)(2,1)S(1)}, u32[]{:S(2)}, u32[]{:S(2)}) %collective-permute-start.3) | collective-permute-done | bytes 196640 | tf_op jit(solution)/shard_map/ppermute | solution.py:221
  38.2 4.7 %out_projection.1 = bf16[8,64,384]{2,1,0:T(8,128)(2,1)} custom-call(s32[3]{0:T(128)S(1)} %pad_add_fusion.pos, bf16[4,32,768]{2,1,0:T(8,128)(2,1)S(1)} %pad_maximum_fusion.3.g0, bf16[4,32,768]{2,1,0:T(8,128)(2,1)S(1)} %collective-permute-done.3.g1, bf16[4,32,768]{2,1,0:T(8,128)(2,1)S(1)} %collective-permute-done.4.g2, ...), custom_call_target="tpu_custom_call" | custom-call | tf_op jit(solution)/shard_map/out_projection/pallas_call | solution.py:223
  43.0 8.2 %all-to-all-start = ((bf16[8,64,384]{2,1,0:T(8,128)(2,1)}), bf16[8,64,384]{2,1,0:T(8,128)(2,1)}, u32[]{:S(2)}, u32[]{:S(2)}) async-start(bf16[8,64,384]{2,1,0:T(8,128)(2,1)} %out_projection.1), calls=%async_computation | async-start | bytes 786432 | tf_op jit(solution)/shard_map/all_to_all | solution.py:231
  53.9 12.4 %all-to-all-done = bf16[8,64,384]{2,1,0:T(8,128)(2,1)} async-done(((bf16[8,64,384]{2,1,0:T(8,128)(2,1)}), bf16[8,64,384]{2,1,0:T(8,128)(2,1)}, u32[]{:S(2)}, u32[]{:S(2)}) %all-to-all-start) | async-done | bytes 393248 | tf_op jit(solution)/shard_map/all_to_all | solution.py:231
  69.5 13.4 %all_to_all.15 = bf16[8,32,384]{2,1,0:T(8,128)(2,1)S(1)} all-to-all(bf16[8,32,384]{2,1,0:T(8,128)(2,1)S(1)} %bitcast.95), channel_id=1, replica_groups=mesh['dp'=16,'tensor'=8,'side'=2] {'tensor'}, dimensions={0} | all-to-all | bytes 393216 | tf_op jit(solution)/shard_map/all_to_all | solution.py:240
  84.7 2.2 %collective-permute-done.11 = bf16[128,384]{1,0:T(8,128)(2,1)S(1)} collective-permute-done((bf16[128,384]{1,0:T(8,128)(2,1)S(1)}, bf16[128,384]{1,0:T(8,128)(2,1)S(1)}, u32[]{:S(2)}, u32[]{:S(2)}) %collective-permute-start.11) | collective-permute-done | bytes 98336 | tf_op jit(solution)/shard_map/ppermute | solution.py:246
  88.1 3.3 %collective-permute-done.9 = bf16[128,384]{1,0:T(8,128)(2,1)S(1)} collective-permute-done((bf16[128,384]{1,0:T(8,128)(2,1)S(1)}, bf16[128,384]{1,0:T(8,128)(2,1)S(1)}, u32[]{:S(2)}, u32[]{:S(2)}) %collective-permute-start.9) | collective-permute-done | bytes 98336 | tf_op jit(solution)/shard_map/ppermute | solution.py:246
  93.1 2.2 %collective-permute-start.20 = (bf16[4,128,384]{2,1,0:T(8,128)(2,1)S(1)}, bf16[4,128,384]{2,1,0:T(8,128)(2,1)S(1)}, u32[]{:S(2)}, u32[]{:S(2)}) collective-permute-start(bf16[4,128,384]{2,1,0:T(8,128)(2,1)S(1)} %pad_maximum_fusion.1.b0), channel_id=1, source_target_pairs={{0,192},{16,208},{32,224},{48,240},{64,0},{80,16},{96,32},{112,48}... | collective-permute-start | bytes 1179656 | tf_op jit(solution)/shard_map/ppermute | solution.py:252
  95.3 2.6 %collective-permute-start.18 = (bf16[4,128,384]{2,1,0:T(8,128)(2,1)S(1)}, bf16[4,128,384]{2,1,0:T(8,128)(2,1)S(1)}, u32[]{:S(2)}, u32[]{:S(2)}) collective-permute-start(bf16[4,128,384]{2,1,0:T(8,128)(2,1)S(1)} %pad_maximum_fusion.a0), channel_id=1, source_target_pairs={{0,48},{16,0},{32,16},{48,32},{64,112},{80,64},{96,80},{112,96},{1... | collective-permute-start | bytes 1179656 | tf_op jit(solution)/shard_map/ppermute | solution.py:251
  97.9 3.7 %collective-permute-done.16.b1 = bf16[4,128,384]{2,1,0:T(8,128)(2,1)S(1)} collective-permute-done((bf16[4,128,384]{2,1,0:T(8,128)(2,1)S(1)}, bf16[4,128,384]{2,1,0:T(8,128)(2,1)S(1)}, u32[]{:S(2)}, u32[]{:S(2)}) %collective-permute-start.16) | collective-permute-done | bytes 393248 | tf_op jit(solution)/shard_map/ppermute | solution.py:252
  102.8 3.4 %collective-permute-start.19 = (bf16[4,128,384]{2,1,0:T(8,128)(2,1)S(1)}, bf16[4,128,384]{2,1,0:T(8,128)(2,1)S(1)}, u32[]{:S(2)}, u32[]{:S(2)}) collective-permute-start(bf16[4,128,384]{2,1,0:T(8,128)(2,1)S(1)} %pad_maximum_fusion.1.b0), channel_id=1, source_target_pairs={{0,128},{16,144},{32,160},{48,176},{64,192},{80,208},{96,224},{112... | collective-permute-start | bytes 1179656 | tf_op jit(solution)/shard_map/ppermute | solution.py:255
  106.2 5.6 %collective-permute-done.17.a2 = bf16[4,128,384]{2,1,0:T(8,128)(2,1)S(1)} collective-permute-done((bf16[4,128,384]{2,1,0:T(8,128)(2,1)S(1)}, bf16[4,128,384]{2,1,0:T(8,128)(2,1)S(1)}, u32[]{:S(2)}, u32[]{:S(2)}) %collective-permute-start.17) | collective-permute-done | bytes 393248 | tf_op jit(solution)/shard_map/ppermute | solution.py:255
  112.8 3.2 %norm.1 = bf16[256,6144]{1,0:T(8,128)(2,1)S(1)} custom-call(s32[3]{0:T(128)S(1)} %pad_add_fusion.pos, bf16[4,128,384]{2,1,0:T(8,128)(2,1)S(1)} %pad_maximum_fusion.a0, bf16[4,128,384]{2,1,0:T(8,128)(2,1)S(1)} %collective-permute-done.15.a1, bf16[4,128,384]{2,1,0:T(8,128)(2,1)S(1)} %collective-permute-done.17.a2, ...), custom_call_target="tpu_custom_call" | custom-call | tf_op jit(solution)/shard_map/norm/pallas_call | solution.py:108
  115.9 3.6 %collective-permute-start.21 = (bf16[256,6144]{1,0:T(8,128)(2,1)S(1)}, bf16[256,6144]{1,0:T(8,128)(2,1)S(1)}, u32[]{:S(2)}, u32[]{:S(2)}) collective-permute-start(bf16[256,6144]{1,0:T(8,128)(2,1)S(1)} %norm.1), channel_id=1, source_target_pairs={{0,1},{1,0},{2,3},{3,2},{4,5},{5,4},{6,7},{7,6},{8,9},{9,8},{10,11... | collective-permute-start | bytes 9437192 | tf_op jit(solution)/shard_map/ppermute | solution.py:21
  121.5 3.3 %collective-permute-done.21 = bf16[256,6144]{1,0:T(8,128)(2,1)S(1)} collective-permute-done((bf16[256,6144]{1,0:T(8,128)(2,1)S(1)}, bf16[256,6144]{1,0:T(8,128)(2,1)S(1)}, u32[]{:S(2)}, u32[]{:S(2)}) %collective-permute-start.21) | collective-permute-done | bytes 3145760 | tf_op jit(solution)/shard_map/ppermute | solution.py:21
  126.8 1.8 convolution_convert_fusion.1
  129.0 1.8 convolution_convert_fusion.2
  132.3 3.1 %combine_cores.3 = (bf16[4,128,384]{2,1,0:T(8,128)(2,1)S(1)}, bf16[4,128,384]{2,1,0:T(8,128)(2,1)}, bf16[4,128,384]{2,1,0:T(8,128)(2,1)}, bf16[4,128,384]{2,1,0:T(8,128)(2,1)}) custom-call(s32[3]{0:T(128)S(1)} %pad_add_fusion.pos, bf16[256,6144]{1,0:T(8,128)(2,1)S(1)} %convolution_convert_fusion.own, bf16[128,6144]{1,0:T(8,128)(2,1)} %collective-permute-done.29.other), custom_call_target="tpu_custom_call" | custom-call | tf_op jit(solution)/shard_map/combine_cores/pallas_call | solution.py:108
  135.4 1.4 collective-permute-start.30
  137.0 1.3 collective-permute-start.31
  138.3 1.8 collective-permute-start.32
  140.0 2.8 %combine_cores.2 = (bf16[4,128,384]{2,1,0:T(8,128)(2,1)S(1)}, bf16[4,128,384]{2,1,0:T(8,128)(2,1)}, bf16[4,128,384]{2,1,0:T(8,128)(2,1)S(1)}, bf16[4,128,384]{2,1,0:T(8,128)(2,1)S(1)}) custom-call(s32[3]{0:T(128)S(1)} %pad_add_fusion.pos, bf16[256,6144]{1,0:T(8,128)(2,1)S(1)} %convolution_convert_fusion.own, bf16[128,6144]{1,0:T(8,128)(2,1)} %collective-permute-done.22.other), custom_call_target="tpu_custom_call" | custom-call | tf_op jit(solution)/shard_map/combine_cores/pallas_call | solution.py:108
  144.6 2.7 %collective-permute-start.24 = (bf16[4,128,384]{2,1,0:T(8,128)(2,1)}, bf16[4,128,384]{2,1,0:T(8,128)(2,1)}, u32[]{:S(2)}, u32[]{:S(2)}) collective-permute-start(bf16[4,128,384]{2,1,0:T(8,128)(2,1)} %copy-done.7), channel_id=1, source_target_pairs={{0,48},{16,0},{32,16},{48,32},{64,112},{80,64},{96,80},{112,96},{1... | collective-permute-start | bytes 1179656 | tf_op jit(solution)/shard_map/ppermute | solution.py:296
  147.4 2.8 %collective-permute-start.25 = (bf16[4,128,384]{2,1,0:T(8,128)(2,1)}, bf16[4,128,384]{2,1,0:T(8,128)(2,1)}, u32[]{:S(2)}, u32[]{:S(2)}) collective-permute-start(bf16[4,128,384]{2,1,0:T(8,128)(2,1)} %copy-done.6), channel_id=1, source_target_pairs={{0,32},{16,48},{32,0},{48,16},{64,96},{80,112},{96,64},{112,80},{1... | collective-permute-start | bytes 1179656 | tf_op jit(solution)/shard_map/ppermute | solution.py:296
  150.2 2.8 %fusion.14 = f32[256]{0:T(256)S(1)} fusion(bf16[256,6144]{1,0:T(8,128)(2,1)} %copy-done.1, bf16[6144,8]{0,1:T(8,128)(2,1)} %param.23, s32[256]{0:T(256)S(1)} %eq.144, f32[8]{0:T(128)S(1)} %compare_convert_fusion), kind=kOutput, calls=%fused_computation.23 | convolution fusion | flops 25175808 | bytes 3246112 | tf_op jit(solution)/shard_map/dot_general | solution.py:276
  153.1 3.2 %collective-permute-done.32.got3 = bf16[4,128,384]{2,1,0:T(8,128)(2,1)} collective-permute-done((bf16[4,128,384]{2,1,0:T(8,128)(2,1)}, bf16[4,128,384]{2,1,0:T(8,128)(2,1)}, u32[]{:S(2)}, u32[]{:S(2)}) %collective-permute-start.32) | collective-permute-done | bytes 393248 | tf_op jit(solution)/shard_map/ppermute | solution.py:296
  156.3 2.1 %sum_rows.3 = (f32[128,384]{1,0:T(8,128)S(1)}, bf16[128,384]{1,0:T(8,128)(2,1)}, bf16[128,384]{1,0:T(8,128)(2,1)}, bf16[128,384]{1,0:T(8,128)(2,1)}) custom-call(bf16[4,128,384]{2,1,0:T(8,128)(2,1)S(1)} %copy-done.3, bf16[4,128,384]{2,1,0:T(8,128)(2,1)} %collective-permute-done.30.got1, bf16[4,128,384]{2,1,0:T(8,128)(2,1)} %collective-permute-done.31.got2, ...), custom_call_target="tpu_custom_call" | custom-call | tf_op jit(solution)/shard_map/sum_rows/pallas_call | solution.py:108
  159.1 2.7 %collective-permute-start.34 = (bf16[128,384]{1,0:T(8,128)(2,1)}, bf16[128,384]{1,0:T(8,128)(2,1)}, u32[]{:S(2)}, u32[]{:S(2)}) collective-permute-start(bf16[128,384]{1,0:T(8,128)(2,1)} %get-tuple-element.59), channel_id=1, source_target_pairs={{0,48},{16,0},{32,16},{48,32},{64,112},{80,64},{96,80},{112,96},{1... | collective-permute-start | bytes 294920 | tf_op jit(solution)/shard_map/ppermute | solution.py:305
  161.8 1.8 collective-permute-start.35
  164.3 1.4 sum_rows.2
  166.0 2.5 %collective-permute-start.27 = (bf16[128,384]{1,0:T(8,128)(2,1)S(1)}, bf16[128,384]{1,0:T(8,128)(2,1)S(1)}, u32[]{:S(2)}, u32[]{:S(2)}) collective-permute-start(bf16[128,384]{1,0:T(8,128)(2,1)S(1)} %get-tuple-element.51), channel_id=1, source_target_pairs={{0,192},{16,208},{32,224},{48,240},{64,0},{80,16},{96,32},{112,48}... | collective-permute-start | bytes 294920 | tf_op jit(solution)/shard_map/ppermute | solution.py:305
  168.5 2.5 %collective-permute-start.28 = (bf16[128,384]{1,0:T(8,128)(2,1)S(1)}, bf16[128,384]{1,0:T(8,128)(2,1)S(1)}, u32[]{:S(2)}, u32[]{:S(2)}) collective-permute-start(bf16[128,384]{1,0:T(8,128)(2,1)S(1)} %get-tuple-element.52), channel_id=1, source_target_pairs={{0,128},{16,144},{32,160},{48,176},{64,192},{80,208},{96,224},{112... | collective-permute-start | bytes 294920 | tf_op jit(solution)/shard_map/ppermute | solution.py:305
  172.2 1.5 collective-permute-done.28
  174.5 3.7 %all-to-all-start.2 = ((bf16[8,32,384]{2,1,0:T(8,128)(2,1)}), bf16[8,32,384]{2,1,0:T(8,128)(2,1)S(1)}, u32[]{:S(2)}, u32[]{:S(2)}) async-start(bf16[8,32,384]{2,1,0:T(8,128)(2,1)} %multiply_convert_fusion), calls=%async_computation.2 | async-start | bytes 393216 | tf_op jit(solution)/shard_map/all_to_all | solution.py:310
  179.1 7.7 %all-to-all-done.2 = bf16[8,32,384]{2,1,0:T(8,128)(2,1)S(1)} async-done(((bf16[8,32,384]{2,1,0:T(8,128)(2,1)}), bf16[8,32,384]{2,1,0:T(8,128)(2,1)S(1)}, u32[]{:S(2)}, u32[]{:S(2)}) %all-to-all-start.2) | async-done | bytes 196640 | tf_op jit(solution)/shard_map/all_to_all | solution.py:310
  186.9 7.0 %collective-permute-start.36 = (bf16[256,192]{1,0:T(8,128)(2,1)S(1)}, bf16[256,192]{1,0:T(8,128)(2,1)S(1)}, u32[]{:S(2)}, u32[]{:S(2)}) collective-permute-start(bf16[256,192]{1,0:T(8,128)(2,1)S(1)} %broadcast_select_fusion), channel_id=1, source_target_pairs={{0,1},{1,0},{2,3},{3,2},{4,5},{5,4},{6,7},{7,6},{8,9},{9,8},{10,11... | collective-permute-start | bytes 294920 | tf_op jit(solution)/shard_map/ppermute | solution.py:21
  (129 shorter events, 35.7 us)
Async XLA Ops:
  0.0 126.8 %copy-start = (bf16[1,256,6144]{2,1,0:T(8,128)(2,1)S(1)}, bf16[1,256,6144]{2,1,0:T(8,128)(2,1)}, u32[]{:S(2)}) copy-start(bf16[1,256,6144]{2,1,0:T(8,128)(2,1)} %param.27) | copy-start | bytes 9437188
  1.3 25.5 %collective-permute-start.6 = (bf16[768,192]{1,0:T(8,128)(2,1)S(1)}, bf16[768,192]{1,0:T(8,128)(2,1)}, u32[]{:S(2)}, u32[]{:S(2)}) collective-permute-start(bf16[768,192]{1,0:T(8,128)(2,1)S(1)} %copy.30), channel_id=1, source_target_pairs={{0,1},{1,0},{2,3},{3,2},{4,5},{5,4},{6,7},{7,6},{8,9},{9,8},{10,11... | collective-permute-start | bytes 884744 | tf_op jit(solution)/shard_map/ppermute | solution.py:21
  11.8 41.1 %copy-start.12 = (s32[1024,2]{0,1:T(2,128)S(1)}, s32[1024,2]{0,1:T(2,128)}, u32[]{:S(2)}) copy-start(s32[1024,2]{0,1:T(2,128)} %param.24) | copy-start | bytes 24580
  15.1 3.7 %collective-permute-start.2 = (bf16[32,768]{1,0:T(8,128)(2,1)}, bf16[32,768]{1,0:T(8,128)(2,1)}, u32[]{:S(2)}, u32[]{:S(2)}) collective-permute-start(bf16[32,768]{1,0:T(8,128)(2,1)} %bitcast.88), channel_id=1, source_target_pairs={{0,192},{16,208},{32,224},{48,240},{64,0},{80,16},{96,32},{112,48}... | collective-permute-start | bytes 147464 | tf_op jit(solution)/shard_map/ppermute | solution.py:219
  15.8 4.8 %collective-permute-start.1 = (bf16[32,768]{1,0:T(8,128)(2,1)}, bf16[32,768]{1,0:T(8,128)(2,1)}, u32[]{:S(2)}, u32[]{:S(2)}) collective-permute-start(bf16[32,768]{1,0:T(8,128)(2,1)} %bitcast.88), channel_id=1, source_target_pairs={{0,128},{16,144},{32,160},{48,176},{64,192},{80,208},{96,224},{112... | collective-permute-start | bytes 147464 | tf_op jit(solution)/shard_map/ppermute | solution.py:219
  16.3 5.8 %collective-permute-start = (bf16[32,768]{1,0:T(8,128)(2,1)}, bf16[32,768]{1,0:T(8,128)(2,1)}, u32[]{:S(2)}, u32[]{:S(2)}) collective-permute-start(bf16[32,768]{1,0:T(8,128)(2,1)} %bitcast.88), channel_id=1, source_target_pairs={{0,64},{16,80},{32,96},{48,112},{64,128},{80,144},{96,160},{112,17... | collective-permute-start | bytes 147464 | tf_op jit(solution)/shard_map/ppermute | solution.py:219
  23.1 6.6 %collective-permute-start.5 = (bf16[4,32,768]{2,1,0:T(8,128)(2,1)S(1)}, bf16[4,32,768]{2,1,0:T(8,128)(2,1)S(1)}, u32[]{:S(2)}, u32[]{:S(2)}) collective-permute-start(bf16[4,32,768]{2,1,0:T(8,128)(2,1)S(1)} %pad_maximum_fusion.3.g0), channel_id=1, source_target_pairs={{0,48},{16,0},{32,16},{48,32},{64,112},{80,64},{96,80},{112,96},{1... | collective-permute-start | bytes 589832 | tf_op jit(solution)/shard_map/ppermute | solution.py:221
  25.7 6.8 %collective-permute-start.4 = (bf16[4,32,768]{2,1,0:T(8,128)(2,1)S(1)}, bf16[4,32,768]{2,1,0:T(8,128)(2,1)S(1)}, u32[]{:S(2)}, u32[]{:S(2)}) collective-permute-start(bf16[4,32,768]{2,1,0:T(8,128)(2,1)S(1)} %pad_maximum_fusion.3.g0), channel_id=1, source_target_pairs={{0,32},{16,48},{32,0},{48,16},{64,96},{80,112},{96,64},{112,80},{1... | collective-permute-start | bytes 589832 | tf_op jit(solution)/shard_map/ppermute | solution.py:221
  26.1 12.2 %collective-permute-start.3 = (bf16[4,32,768]{2,1,0:T(8,128)(2,1)S(1)}, bf16[4,32,768]{2,1,0:T(8,128)(2,1)S(1)}, u32[]{:S(2)}, u32[]{:S(2)}) collective-permute-start(bf16[4,32,768]{2,1,0:T(8,128)(2,1)S(1)} %pad_maximum_fusion.3.g0), channel_id=1, source_target_pairs={{0,16},{16,32},{32,48},{48,0},{64,80},{80,96},{96,112},{112,64},{1... | collective-permute-start | bytes 589832 | tf_op jit(solution)/shard_map/ppermute | solution.py:221
  28.5 84.2 %copy-start.5 = (f32[6144]{0:T(1024)S(1)}, f32[6144]{0:T(1024)}, u32[]{:S(2)}) copy-start(f32[6144]{0:T(1024)} %param.22) | copy-start | bytes 73732
  43.0 23.4 %all-to-all-start = ((bf16[8,64,384]{2,1,0:T(8,128)(2,1)}), bf16[8,64,384]{2,1,0:T(8,128)(2,1)}, u32[]{:S(2)}, u32[]{:S(2)}) async-start(bf16[8,64,384]{2,1,0:T(8,128)(2,1)} %out_projection.1), calls=%async_computation | async-start | bytes 786432 | tf_op jit(solution)/shard_map/all_to_all | solution.py:231
  52.0 1.8 collective-permute-start.7
  67.4 1.8 collective-permute-start.8
  69.3 23.0 %copy-start.8 = (bf16[128,384]{1,0:T(8,128)(2,1)}, bf16[128,384]{1,0:T(8,128)(2,1)S(1)}, u32[]{:S(2)}) copy-start(bf16[128,384]{1,0:T(8,128)(2,1)S(1)} %maximum_select_fusion.2) | copy-start | bytes 294916
  82.9 4.0 %collective-permute-start.11 = (bf16[128,384]{1,0:T(8,128)(2,1)S(1)}, bf16[128,384]{1,0:T(8,128)(2,1)S(1)}, u32[]{:S(2)}, u32[]{:S(2)}) collective-permute-start(bf16[128,384]{1,0:T(8,128)(2,1)S(1)} %bitcast.97), channel_id=1, source_target_pairs={{0,192},{16,208},{32,224},{48,240},{64,0},{80,16},{96,32},{112,48}... | collective-permute-start | bytes 294920 | tf_op jit(solution)/shard_map/ppermute | solution.py:246
  83.0 5.1 %collective-permute-start.10 = (bf16[128,384]{1,0:T(8,128)(2,1)S(1)}, bf16[128,384]{1,0:T(8,128)(2,1)S(1)}, u32[]{:S(2)}, u32[]{:S(2)}) collective-permute-start(bf16[128,384]{1,0:T(8,128)(2,1)S(1)} %bitcast.98), channel_id=1, source_target_pairs={{0,128},{16,144},{32,160},{48,176},{64,192},{80,208},{96,224},{112... | collective-permute-start | bytes 294920 | tf_op jit(solution)/shard_map/ppermute | solution.py:246
  83.6 7.8 %collective-permute-start.9 = (bf16[128,384]{1,0:T(8,128)(2,1)S(1)}, bf16[128,384]{1,0:T(8,128)(2,1)S(1)}, u32[]{:S(2)}, u32[]{:S(2)}) collective-permute-start(bf16[128,384]{1,0:T(8,128)(2,1)S(1)} %bitcast.99), channel_id=1, source_target_pairs={{0,64},{16,80},{32,96},{48,112},{64,128},{80,144},{96,160},{112,17... | collective-permute-start | bytes 294920 | tf_op jit(solution)/shard_map/ppermute | solution.py:246
  84.4 6.9 %collective-permute-start.14 = (bf16[128,384]{1,0:T(8,128)(2,1)S(1)}, bf16[128,384]{1,0:T(8,128)(2,1)S(1)}, u32[]{:S(2)}, u32[]{:S(2)}) collective-permute-start(bf16[128,384]{1,0:T(8,128)(2,1)S(1)} %bitcast.101), channel_id=1, source_target_pairs={{0,48},{16,0},{32,16},{48,32},{64,112},{80,64},{96,80},{112,96},{1... | collective-permute-start | bytes 294920 | tf_op jit(solution)/shard_map/ppermute | solution.py:247
  84.4 6.9 %collective-permute-start.13 = (bf16[128,384]{1,0:T(8,128)(2,1)S(1)}, bf16[128,384]{1,0:T(8,128)(2,1)S(1)}, u32[]{:S(2)}, u32[]{:S(2)}) collective-permute-start(bf16[128,384]{1,0:T(8,128)(2,1)S(1)} %bitcast.102), channel_id=1, source_target_pairs={{0,32},{16,48},{32,0},{48,16},{64,96},{80,112},{96,64},{112,80},{1... | collective-permute-start | bytes 294920 | tf_op jit(solution)/shard_map/ppermute | solution.py:247
  86.9 5.3 %collective-permute-start.12 = (bf16[128,384]{1,0:T(8,128)(2,1)S(1)}, bf16[128,384]{1,0:T(8,128)(2,1)S(1)}, u32[]{:S(2)}, u32[]{:S(2)}) collective-permute-start(bf16[128,384]{1,0:T(8,128)(2,1)S(1)} %bitcast.103), channel_id=1, source_target_pairs={{0,16},{16,32},{32,48},{48,0},{64,80},{80,96},{96,112},{112,64},{1... | collective-permute-start | bytes 294920 | tf_op jit(solution)/shard_map/ppermute | solution.py:247
  92.3 9.2 %collective-permute-start.16 = (bf16[4,128,384]{2,1,0:T(8,128)(2,1)S(1)}, bf16[4,128,384]{2,1,0:T(8,128)(2,1)S(1)}, u32[]{:S(2)}, u32[]{:S(2)}) collective-permute-start(bf16[4,128,384]{2,1,0:T(8,128)(2,1)S(1)} %pad_maximum_fusion.1.b0), channel_id=1, source_target_pairs={{0,64},{16,80},{32,96},{48,112},{64,128},{80,144},{96,160},{112,17... | collective-permute-start | bytes 1179656 | tf_op jit(solution)/shard_map/ppermute | solution.py:252
  93.0 9.8 %collective-permute-start.15 = (bf16[4,128,384]{2,1,0:T(8,128)(2,1)S(1)}, bf16[4,128,384]{2,1,0:T(8,128)(2,1)S(1)}, u32[]{:S(2)}, u32[]{:S(2)}) collective-permute-start(bf16[4,128,384]{2,1,0:T(8,128)(2,1)S(1)} %pad_maximum_fusion.a0), channel_id=1, source_target_pairs={{0,16},{16,32},{32,48},{48,0},{64,80},{80,96},{96,112},{112,64},{1... | collective-permute-start | bytes 1179656 | tf_op jit(solution)/shard_map/ppermute | solution.py:251
  93.1 13.1 %collective-permute-start.20 = (bf16[4,128,384]{2,1,0:T(8,128)(2,1)S(1)}, bf16[4,128,384]{2,1,0:T(8,128)(2,1)S(1)}, u32[]{:S(2)}, u32[]{:S(2)}) collective-permute-start(bf16[4,128,384]{2,1,0:T(8,128)(2,1)S(1)} %pad_maximum_fusion.1.b0), channel_id=1, source_target_pairs={{0,192},{16,208},{32,224},{48,240},{64,0},{80,16},{96,32},{112,48}... | collective-permute-start | bytes 1179656 | tf_op jit(solution)/shard_map/ppermute | solution.py:252
  95.3 10.9 %collective-permute-start.18 = (bf16[4,128,384]{2,1,0:T(8,128)(2,1)S(1)}, bf16[4,128,384]{2,1,0:T(8,128)(2,1)S(1)}, u32[]{:S(2)}, u32[]{:S(2)}) collective-permute-start(bf16[4,128,384]{2,1,0:T(8,128)(2,1)S(1)} %pad_maximum_fusion.a0), channel_id=1, source_target_pairs={{0,48},{16,0},{32,16},{48,32},{64,112},{80,64},{96,80},{112,96},{1... | collective-permute-start | bytes 1179656 | tf_op jit(solution)/shard_map/ppermute | solution.py:251
  102.8 9.1 %collective-permute-start.17 = (bf16[4,128,384]{2,1,0:T(8,128)(2,1)S(1)}, bf16[4,128,384]{2,1,0:T(8,128)(2,1)S(1)}, u32[]{:S(2)}, u32[]{:S(2)}) collective-permute-start(bf16[4,128,384]{2,1,0:T(8,128)(2,1)S(1)} %pad_maximum_fusion.a0), channel_id=1, source_target_pairs={{0,32},{16,48},{32,0},{48,16},{64,96},{80,112},{96,64},{112,80},{1... | collective-permute-start | bytes 1179656 | tf_op jit(solution)/shard_map/ppermute | solution.py:255
  102.8 10.0 %collective-permute-start.19 = (bf16[4,128,384]{2,1,0:T(8,128)(2,1)S(1)}, bf16[4,128,384]{2,1,0:T(8,128)(2,1)S(1)}, u32[]{:S(2)}, u32[]{:S(2)}) collective-permute-start(bf16[4,128,384]{2,1,0:T(8,128)(2,1)S(1)} %pad_maximum_fusion.1.b0), channel_id=1, source_target_pairs={{0,128},{16,144},{32,160},{48,176},{64,192},{80,208},{96,224},{112... | collective-permute-start | bytes 1179656 | tf_op jit(solution)/shard_map/ppermute | solution.py:255
  112.8 6.8 %copy-start.13 = (bf16[1,6144,256]{2,1,0:T(8,128)(2,1)S(1)}, bf16[1,6144,256]{2,1,0:T(8,128)(2,1)}, u32[]{:S(2)}) copy-start(bf16[1,6144,256]{2,1,0:T(8,128)(2,1)} %param.25) | copy-start | bytes 9437188
  115.9 8.9 %collective-permute-start.21 = (bf16[256,6144]{1,0:T(8,128)(2,1)S(1)}, bf16[256,6144]{1,0:T(8,128)(2,1)S(1)}, u32[]{:S(2)}, u32[]{:S(2)}) collective-permute-start(bf16[256,6144]{1,0:T(8,128)(2,1)S(1)} %norm.1), channel_id=1, source_target_pairs={{0,1},{1,0},{2,3},{3,2},{4,5},{5,4},{6,7},{7,6},{8,9},{9,8},{10,11... | collective-permute-start | bytes 9437192 | tf_op jit(solution)/shard_map/ppermute | solution.py:21
  128.6 3.8 %collective-permute-start.29 = (bf16[128,6144]{1,0:T(8,128)(2,1)}, bf16[128,6144]{1,0:T(8,128)(2,1)}, u32[]{:S(2)}, u32[]{:S(2)}) collective-permute-start(bf16[128,6144]{1,0:T(8,128)(2,1)} %convolution_convert_fusion.1), channel_id=1, source_target_pairs={{0,1},{1,0},{2,3},{3,2},{4,5},{5,4},{6,7},{7,6},{8,9},{9,8},{10,11... | collective-permute-start | bytes 4718600 | tf_op jit(solution)/shard_map/ppermute | solution.py:21
  130.7 9.3 %collective-permute-start.22 = (bf16[128,6144]{1,0:T(8,128)(2,1)}, bf16[128,6144]{1,0:T(8,128)(2,1)}, u32[]{:S(2)}, u32[]{:S(2)}) collective-permute-start(bf16[128,6144]{1,0:T(8,128)(2,1)} %convolution_convert_fusion.2), channel_id=1, source_target_pairs={{0,1},{1,0},{2,3},{3,2},{4,5},{5,4},{6,7},{7,6},{8,9},{9,8},{10,11... | collective-permute-start | bytes 4718600 | tf_op jit(solution)/shard_map/ppermute | solution.py:21
  135.4 7.4 %copy-start.2 = (bf16[4,128,384]{2,1,0:T(8,128)(2,1)}, bf16[4,128,384]{2,1,0:T(8,128)(2,1)S(1)}, u32[]{:S(2)}) copy-start(bf16[4,128,384]{2,1,0:T(8,128)(2,1)S(1)} %get-tuple-element.53.mine) | copy-start | bytes 1179652
  135.4 12.0 %collective-permute-start.30 = (bf16[4,128,384]{2,1,0:T(8,128)(2,1)}, bf16[4,128,384]{2,1,0:T(8,128)(2,1)}, u32[]{:S(2)}, u32[]{:S(2)}) collective-permute-start(bf16[4,128,384]{2,1,0:T(8,128)(2,1)} %get-tuple-element.54), channel_id=1, source_target_pairs={{0,64},{16,80},{32,96},{48,112},{64,128},{80,144},{96,160},{112,17... | collective-permute-start | bytes 1179656 | tf_op jit(solution)/shard_map/ppermute | solution.py:296
  137.0 16.1 %collective-permute-start.31 = (bf16[4,128,384]{2,1,0:T(8,128)(2,1)}, bf16[4,128,384]{2,1,0:T(8,128)(2,1)}, u32[]{:S(2)}, u32[]{:S(2)}) collective-permute-start(bf16[4,128,384]{2,1,0:T(8,128)(2,1)} %get-tuple-element.55), channel_id=1, source_target_pairs={{0,192},{16,208},{32,224},{48,240},{64,0},{80,16},{96,32},{112,48}... | collective-permute-start | bytes 1179656 | tf_op jit(solution)/shard_map/ppermute | solution.py:296
  138.3 18.1 %collective-permute-start.32 = (bf16[4,128,384]{2,1,0:T(8,128)(2,1)}, bf16[4,128,384]{2,1,0:T(8,128)(2,1)}, u32[]{:S(2)}, u32[]{:S(2)}) collective-permute-start(bf16[4,128,384]{2,1,0:T(8,128)(2,1)} %get-tuple-element.56), channel_id=1, source_target_pairs={{0,128},{16,144},{32,160},{48,176},{64,192},{80,208},{96,224},{112... | collective-permute-start | bytes 1179656 | tf_op jit(solution)/shard_map/ppermute | solution.py:296
  144.3 17.5 %collective-permute-start.23 = (bf16[4,128,384]{2,1,0:T(8,128)(2,1)}, bf16[4,128,384]{2,1,0:T(8,128)(2,1)}, u32[]{:S(2)}, u32[]{:S(2)}) collective-permute-start(bf16[4,128,384]{2,1,0:T(8,128)(2,1)} %get-tuple-element.46), channel_id=1, source_target_pairs={{0,16},{16,32},{32,48},{48,0},{64,80},{80,96},{96,112},{112,64},{1... | collective-permute-start | bytes 1179656 | tf_op jit(solution)/shard_map/ppermute | solution.py:296
  144.6 11.7 %copy-start.3 = (bf16[4,128,384]{2,1,0:T(8,128)(2,1)S(1)}, bf16[4,128,384]{2,1,0:T(8,128)(2,1)}, u32[]{:S(2)}) copy-start(bf16[4,128,384]{2,1,0:T(8,128)(2,1)} %copy-done.2) | copy-start | bytes 1179652
  144.6 19.0 %collective-permute-start.24 = (bf16[4,128,384]{2,1,0:T(8,128)(2,1)}, bf16[4,128,384]{2,1,0:T(8,128)(2,1)}, u32[]{:S(2)}, u32[]{:S(2)}) collective-permute-start(bf16[4,128,384]{2,1,0:T(8,128)(2,1)} %copy-done.7), channel_id=1, source_target_pairs={{0,48},{16,0},{32,16},{48,32},{64,112},{80,64},{96,80},{112,96},{1... | collective-permute-start | bytes 1179656 | tf_op jit(solution)/shard_map/ppermute | solution.py:296
  147.4 16.9 %collective-permute-start.25 = (bf16[4,128,384]{2,1,0:T(8,128)(2,1)}, bf16[4,128,384]{2,1,0:T(8,128)(2,1)}, u32[]{:S(2)}, u32[]{:S(2)}) collective-permute-start(bf16[4,128,384]{2,1,0:T(8,128)(2,1)} %copy-done.6), channel_id=1, source_target_pairs={{0,32},{16,48},{32,0},{48,16},{64,96},{80,112},{96,64},{112,80},{1... | collective-permute-start | bytes 1179656 | tf_op jit(solution)/shard_map/ppermute | solution.py:296
  159.1 9.4 %collective-permute-start.33 = (bf16[128,384]{1,0:T(8,128)(2,1)}, bf16[128,384]{1,0:T(8,128)(2,1)}, u32[]{:S(2)}, u32[]{:S(2)}) collective-permute-start(bf16[128,384]{1,0:T(8,128)(2,1)} %get-tuple-element.58), channel_id=1, source_target_pairs={{0,16},{16,32},{32,48},{48,0},{64,80},{80,96},{96,112},{112,64},{1... | collective-permute-start | bytes 294920 | tf_op jit(solution)/shard_map/ppermute | solution.py:305
  159.1 11.9 %collective-permute-start.34 = (bf16[128,384]{1,0:T(8,128)(2,1)}, bf16[128,384]{1,0:T(8,128)(2,1)}, u32[]{:S(2)}, u32[]{:S(2)}) collective-permute-start(bf16[128,384]{1,0:T(8,128)(2,1)} %get-tuple-element.59), channel_id=1, source_target_pairs={{0,48},{16,0},{32,16},{48,32},{64,112},{80,64},{96,80},{112,96},{1... | collective-permute-start | bytes 294920 | tf_op jit(solution)/shard_map/ppermute | solution.py:305
  161.8 9.2 %collective-permute-start.35 = (bf16[128,384]{1,0:T(8,128)(2,1)}, bf16[128,384]{1,0:T(8,128)(2,1)}, u32[]{:S(2)}, u32[]{:S(2)}) collective-permute-start(bf16[128,384]{1,0:T(8,128)(2,1)} %get-tuple-element.60), channel_id=1, source_target_pairs={{0,32},{16,48},{32,0},{48,16},{64,96},{80,112},{96,64},{112,80},{1... | collective-permute-start | bytes 294920 | tf_op jit(solution)/shard_map/ppermute | solution.py:305
  165.7 12.4 %copy-start.9 = (bf16[128,384]{1,0:T(8,128)(2,1)S(1)}, bf16[128,384]{1,0:T(8,128)(2,1)}, u32[]{:S(2)}) copy-start(bf16[128,384]{1,0:T(8,128)(2,1)} %copy-done.8) | copy-start | bytes 294916
  165.7 29.2 %copy-start.11 = (pred[256,128]{1,0:T(32,128)(4,1)S(1)}, pred[256,128]{1,0:T(32,128)(4,1)}, u32[]{:S(2)}) copy-start(pred[256,128]{1,0:T(32,128)(4,1)} %get-tuple-element.69) | copy-start | bytes 98308
  165.8 6.4 %collective-permute-start.26 = (bf16[128,384]{1,0:T(8,128)(2,1)S(1)}, bf16[128,384]{1,0:T(8,128)(2,1)S(1)}, u32[]{:S(2)}, u32[]{:S(2)}) collective-permute-start(bf16[128,384]{1,0:T(8,128)(2,1)S(1)} %get-tuple-element.50), channel_id=1, source_target_pairs={{0,64},{16,80},{32,96},{48,112},{64,128},{80,144},{96,160},{112,17... | collective-permute-start | bytes 294920 | tf_op jit(solution)/shard_map/ppermute | solution.py:305
  166.0 6.2 %collective-permute-start.27 = (bf16[128,384]{1,0:T(8,128)(2,1)S(1)}, bf16[128,384]{1,0:T(8,128)(2,1)S(1)}, u32[]{:S(2)}, u32[]{:S(2)}) collective-permute-start(bf16[128,384]{1,0:T(8,128)(2,1)S(1)} %get-tuple-element.51), channel_id=1, source_target_pairs={{0,192},{16,208},{32,224},{48,240},{64,0},{80,16},{96,32},{112,48}... | collective-permute-start | bytes 294920 | tf_op jit(solution)/shard_map/ppermute | solution.py:305
  168.5 5.1 %collective-permute-start.28 = (bf16[128,384]{1,0:T(8,128)(2,1)S(1)}, bf16[128,384]{1,0:T(8,128)(2,1)S(1)}, u32[]{:S(2)}, u32[]{:S(2)}) collective-permute-start(bf16[128,384]{1,0:T(8,128)(2,1)S(1)} %get-tuple-element.52), channel_id=1, source_target_pairs={{0,128},{16,144},{32,160},{48,176},{64,192},{80,208},{96,224},{112... | collective-permute-start | bytes 294920 | tf_op jit(solution)/shard_map/ppermute | solution.py:305
  174.5 12.3 %all-to-all-start.2 = ((bf16[8,32,384]{2,1,0:T(8,128)(2,1)}), bf16[8,32,384]{2,1,0:T(8,128)(2,1)S(1)}, u32[]{:S(2)}, u32[]{:S(2)}) async-start(bf16[8,32,384]{2,1,0:T(8,128)(2,1)} %multiply_convert_fusion), calls=%async_computation.2 | async-start | bytes 393216 | tf_op jit(solution)/shard_map/all_to_all | solution.py:310
  186.9 8.1 %collective-permute-start.36 = (bf16[256,192]{1,0:T(8,128)(2,1)S(1)}, bf16[256,192]{1,0:T(8,128)(2,1)S(1)}, u32[]{:S(2)}, u32[]{:S(2)}) collective-permute-start(bf16[256,192]{1,0:T(8,128)(2,1)S(1)} %broadcast_select_fusion), channel_id=1, source_target_pairs={{0,1},{1,0},{2,3},{3,2},{4,5},{5,4},{6,7},{7,6},{8,9},{9,8},{10,11... | collective-permute-start | bytes 294920 | tf_op jit(solution)/shard_map/ppermute | solution.py:21
  (6 other events, 12.0 us)

commit v2 on v1

--- a/solution.py
+++ b/solution.py
@@ -27,14 +27,11 @@
 
 def outproj_kernel(pos, g0, g1, g2, g3, w, out):
     for dy, ref in enumerate((g0, g1, g2, g3)):
-
-        def work(dx, _, dy=dy, ref=ref):
-            sums = jnp.dot(ref[dx], w[...], preferred_element_type=F32)
+        sums = jnp.dot(ref[...].reshape(128, 768), w[...], preferred_element_type=F32).astype(BF16)
+        for dx in range(4):
             chip = chip_at(pos, -dx, -dy)
-            out[chip // 2, pl.ds(pl.multiple_of((chip & 1) * 32, 32), 32), :] = sums.astype(BF16)
-            return 0
-
-        lax.fori_loop(0, 4, work, 0)
+            row = pl.multiple_of((chip & 1) * 32, 32)
+            out[chip // 2, pl.ds(row, 32), :] = sums[dx * 32 : dx * 32 + 32]
 
 
 def at_half(pos, h, i, shift):
@@ -115,39 +112,58 @@
     )(*args)
 
 
+def attend_kernel(q, k_new, v_new, k, v, lengths, out, q_heads, o_heads):
+    inv_root = HEAD_DIM ** (-0.5)
+    for h in range(8):
+        to = pl.ds(h, 16, stride=8)
+        if h < 6:
+            q_heads[to, :] = q[:, h * 128 : h * 128 + 128].astype(F32)
+        else:
+            q_heads[to, :] = jnp.zeros((16, 128), F32)
+    queries = q_heads[...]
+    own_products = queries.reshape(16, 8, 128) * k_new[...].astype(F32)[:, None, :]
+    own_scores = jnp.sum(own_products, axis=2, keepdims=True) * inv_root
+    narrow = queries.astype(BF16)
+    scores = [
+        lax.dot_general(
+            narrow[r * 8 : r * 8 + 8],
+            k[r],
+            (((1,), (1,)), ((), ())),
+            preferred_element_type=F32,
+        )
+        for r in range(16)
+    ]
+    scores = jnp.concatenate(scores, axis=0).reshape(16, 8, 192) * inv_root
+    live = lax.broadcasted_iota(jnp.int32, (16, 8, 192), 2) < lengths[...].reshape(16, 1, 1)
+    scores = jnp.where(live, scores, -1e30)
+    peak = jnp.maximum(jnp.max(scores, axis=2, keepdims=True), own_scores)
+    weights = jnp.exp(scores - peak)
+    own_weights = jnp.exp(own_scores - peak)
+    scale = 1.0 / (jnp.sum(weights, axis=2, keepdims=True) + own_weights)
+    weights = (weights * scale).astype(BF16).reshape(128, 192)
+    own_weights = (own_weights * scale).astype(BF16).astype(F32)
+    own_part = own_weights * v_new[...].astype(F32)[:, None, :]
+    for r in range(16):
+        mixed = jnp.dot(weights[r * 8 : r * 8 + 8], v[r], preferred_element_type=F32)
+        o_heads[r * 8 : r * 8 + 8, :] = mixed + own_part[r]
+    for h in range(6):
+        out[:, h * 128 : h * 128 + 128] = o_heads[pl.ds(h, 16, stride=8), :].astype(BF16)
+
+
 def attend(q_new, k_new, v_new, k_cache, v_cache, lengths):
-    rows_dev = q_new.shape[0]
-    kv_local = k_new.shape[1] // HEAD_DIM
-    heads_local = q_new.shape[1] // HEAD_DIM
-    group_size = heads_local // kv_local
-    cache_len = k_cache.shape[1]
-    inv_root = HEAD_DIM ** (-0.5)
-    queries = q_new.reshape(rows_dev, kv_local, group_size, HEAD_DIM)
-    cache_keys = k_cache.reshape(rows_dev, cache_len, kv_local, HEAD_DIM)
-    cache_values = v_cache.reshape(rows_dev, cache_len, kv_local, HEAD_DIM)
-    own_keys = k_new.reshape(rows_dev, kv_local, HEAD_DIM)
-    own_values = v_new.reshape(rows_dev, kv_local, HEAD_DIM).astype(F32)
-    cache_scores = (
-        jnp.einsum("rkgd,rckd->rkgc", queries, cache_keys, preferred_element_type=F32) * inv_root
-    )
-    own_scores = (
-        jnp.einsum("rkgd,rkd->rkg", queries, own_keys, preferred_element_type=F32) * inv_root
-    )
-    live_mask = (jnp.arange(cache_len, dtype=jnp.int32)[None, :] < lengths[:, None])[
-        :, None, None, :
-    ]
-    cache_scores = jnp.where(live_mask, cache_scores, -1e30)
-    peak = jnp.maximum(jnp.max(cache_scores, axis=3), own_scores)
-    cache_exp = jnp.exp(cache_scores - peak[..., None])
-    own_exp = jnp.exp(own_scores - peak)
-    denominator = jnp.sum(cache_exp, axis=3) + own_exp
-    cache_weights = (cache_exp / denominator[..., None]).astype(BF16)
-    own_weights = (own_exp / denominator).astype(BF16).astype(F32)
-    mixed_heads = jnp.einsum(
-        "rkgc,rckd->rkgd", cache_weights, cache_values, preferred_element_type=F32
-    )
-    mixed_heads = mixed_heads + own_weights[..., None] * own_values[:, :, None, :]
-    return mixed_heads.reshape(rows_dev, heads_local * HEAD_DIM).astype(BF16)
+    def rows(*rest):
+        return pl.BlockSpec((16, *rest), lambda i: (i,) + (0,) * len(rest))
+
+    return pl.pallas_call(
+        attend_kernel,
+        grid=(2,),
+        in_specs=[rows(768), rows(128), rows(128), rows(192, 128), rows(192, 128), rows(1)],
+        out_specs=rows(768),
+        out_shape=jax.ShapeDtypeStruct((32, 768), BF16),
+        scratch_shapes=[pltpu.VMEM((128, 128), F32)] * 2,
+        compiler_params=pltpu.CompilerParams(vmem_limit_bytes=VMEM_LIMIT),
+        name="attend",
+    )(q_new, k_new, v_new, k_cache, v_cache, lengths.reshape(32, 1))
 
 
 def ranks_of(member):
@@ -192,7 +208,6 @@
         return jnp.where(first_core, a[:, :192], a[:, 192:])
 
     attention = attend(q_new, k_new, v_new, k_cache, v_cache, lengths)
-    out_w = by_core(attn_out_weight, swap_cores(attn_out_weight), 1)
     residual_chip = by_core(residual, swap_cores(residual), 1).reshape(2, 2, 32, 384)
     residual_half = jnp.where(first_core, residual_chip[:, 0], residual_chip[:, 1])
 
@@ -217,6 +232,8 @@
     signs = (labels == plane).astype(F32) - (labels == partner).astype(F32)
 
     rows_x = [lax.ppermute(attention, "dp", SHIFT_X[d]) for d in (1, 2, 3)]
+    columns, rows_x[2] = lax.optimization_barrier((attn_out_weight, rows_x[2]))
+    out_w = by_core(columns, swap_cores(columns), 1)
     rows_x = jnp.stack([attention] + rows_x)
     rows_xy = [rows_x] + [lax.ppermute(rows_x, "dp", SHIFT_Y[d]) for d in (1, 2, 3)]
     vmem = pl.BlockSpec(memory_space=pltpu.VMEM)

time: 197 us -> 197 us (level)
  starting transfers between devices: 63.8 us -> 71.8 us
  matrix products: 19.1 us -> 13.7 us
  other arithmetic: 9.37 us -> 7.19 us
    dot_general x3 -> x0, matrix products: 5.41 us -> none  [the longest x1 2.43 us: attend(): jnp.einsum('rkgd,rckd->rkgc', queries, cache_keys, preferred_element_type...]
    ppermute x3, starting transfers between devices: 1.87 us -> 5.92 us  [shards(): rows_x = [lax.ppermute(attention, 'dp', SHIFT_X[d]) for d in (1, 2, 3)]]
    ppermute x7, starting transfers between devices: 15.9 us -> 19.7 us  [swap_cores(): return lax.ppermute(a, 'side', SWAP)]
    pallas_call x1, Pallas kernels: 4.71 us -> 1.87 us  [shards(): pl.pallas_call(outproj_kernel, in_specs=[pl.BlockSpec(memory_space=pltpu....]
    ppermute x1, starting transfers between devices: 3.44 us -> 0.84 us  [shards(): lax.ppermute(far_b, 'dp', SHIFT_X[2])]
    ppermute x1, waiting for transfers between devices: 5.61 us -> 8.19 us  [shards(): lax.ppermute(far_a, 'dp', SHIFT_Y[2])]
    unnamed x35 -> x45, local copies, waits for them, and re-layouts: 6.49 us -> 8.25 us
  transfers between devices with their start and end apart: 39 -> 39, of which waited for: 22 -> 22; matrix products, arithmetic and copies ran while one was open for 14% -> 8% of each run, Pallas kernels for 5% -> 5%
where the time goes in v2:
time: 197 us
  starting transfers between devices  71.8 us (36%)
  waiting for transfers between devices  62.5 us (32%)
  Pallas kernels  16.2 us (8%)
  matrix products  13.7 us (7%)
  blocking collectives  13.4 us (7%)
  local copies, waits for them, and re-layouts  11.3 us (6%)
  other arithmetic  7.19 us (4%)
    ppermute x7, starting transfers between devices, swap_cores(): return lax.ppermute(a, 'side', SWAP)  19.7 us
    all_to_all x1, blocking collectives, shards(): lax.all_to_all(routed.reshape(8, 32, 384), 'tensor', split_axis=0, concat...  13.4 us
    pallas_call x5, Pallas kernels, local_call(): pl.pallas_call(kernel, in_specs=first + [vmem] * (len(args) - len(first))...  12.7 us
    all_to_all x1, waiting for transfers between devices, shards(): lax.all_to_all(head_sums, 'tensor', split_axis=0, concat_axis=0, tiled=True)  12.1 us
    ppermute x6, starting transfers between devices, shards(): got = [lax.ppermute(rows[d], 'dp', far[d]) for d in (1, 3, 2)]  10.7 us
    ppermute x6, starting transfers between devices, shards(): got = [lax.ppermute(sums[d], 'dp', near[d]) for d in (1, 3, 2)]  10.3 us
    ppermute x3, waiting for transfers between devices, shards(): lax.ppermute(rows_x, 'dp', SHIFT_Y[d])  9.4 us
    unnamed x45, local copies, waits for them, and re-layouts  8.25 us
  transfers between devices with their start and end apart: 39, of which 22 were waited for; matrix products, arithmetic and copies ran while one was open for 8% of the time, Pallas kernels for 5%

profile of v2, /device:TPU:1, one launch (start us, length us, event | category | flops | bytes accessed | tf_op | source)
XLA Modules:
  0.0 196.5 jit_solution(2812797083261133558)
XLA Ops:
  0.9 1.5 copy-done.2
  2.4 1.4 copy-done.3
  6.0 1.6 attend.1
  7.6 3.4 %collective-permute-start.2 = (bf16[32,768]{1,0:T(8,128)(2,1)S(1)}, bf16[32,768]{1,0:T(8,128)(2,1)}, u32[]{:S(2)}, u32[]{:S(2)}) collective-permute-start(bf16[32,768]{1,0:T(8,128)(2,1)S(1)} %attend.1), channel_id=1, source_target_pairs={{0,192},{16,208},{32,224},{48,240},{64,0},{80,16},{96,32},{112,48}... | collective-permute-start | bytes 147464 | tf_op jit(solution)/shard_map/ppermute | solution.py:234
  11.0 1.2 collective-permute-done.2
  13.1 3.0 %collective-permute-start.6 = (bf16[768,192]{1,0:T(8,128)(2,1)}, bf16[768,192]{1,0:T(8,128)(2,1)}, u32[]{:S(2)}, u32[]{:S(2)}) collective-permute-start(bf16[768,192]{1,0:T(8,128)(2,1)} %copy.33), channel_id=1, source_target_pairs={{0,1},{1,0},{2,3},{3,2},{4,5},{5,4},{6,7},{7,6},{8,9},{9,8},{10,11... | collective-permute-start | bytes 884744 | tf_op jit(solution)/shard_map/ppermute | solution.py:21
  17.1 1.5 collective-permute-start
  18.6 2.3 %collective-permute-done.1 = bf16[32,768]{1,0:T(8,128)(2,1)S(1)} collective-permute-done((bf16[32,768]{1,0:T(8,128)(2,1)S(1)}, bf16[32,768]{1,0:T(8,128)(2,1)S(1)}, u32[]{:S(2)}, u32[]{:S(2)}) %collective-permute-start.1) | collective-permute-done | bytes 49184 | tf_op jit(solution)/shard_map/ppermute | solution.py:234
  22.9 2.0 %collective-permute-start.5 = (bf16[4,32,768]{2,1,0:T(8,128)(2,1)S(1)}, bf16[4,32,768]{2,1,0:T(8,128)(2,1)S(1)}, u32[]{:S(2)}, u32[]{:S(2)}) collective-permute-start(bf16[4,32,768]{2,1,0:T(8,128)(2,1)S(1)} %pad_maximum_fusion.3.g0), channel_id=1, source_target_pairs={{0,48},{16,0},{32,16},{48,32},{64,112},{80,64},{96,80},{112,96},{1... | collective-permute-start | bytes 589832 | tf_op jit(solution)/shard_map/ppermute | solution.py:238
  26.0 1.8 maximum_select_fusion.w
  28.7 2.3 %collective-permute-done.4.g2 = bf16[4,32,768]{2,1,0:T(8,128)(2,1)S(1)} collective-permute-done((bf16[4,32,768]{2,1,0:T(8,128)(2,1)S(1)}, bf16[4,32,768]{2,1,0:T(8,128)(2,1)S(1)}, u32[]{:S(2)}, u32[]{:S(2)}) %collective-permute-start.4) | collective-permute-done | bytes 196640 | tf_op jit(solution)/shard_map/ppermute | solution.py:238
  31.0 6.2 %collective-permute-done.3.g1 = bf16[4,32,768]{2,1,0:T(8,128)(2,1)S(1)} collective-permute-done((bf16[4,32,768]{2,1,0:T(8,128)(2,1)S(1)}, bf16[4,32,768]{2,1,0:T(8,128)(2,1)S(1)}, u32[]{:S(2)}, u32[]{:S(2)}) %collective-permute-start.3) | collective-permute-done | bytes 196640 | tf_op jit(solution)/shard_map/ppermute | solution.py:238
  37.3 1.9 out_projection.1
  39.1 8.2 %all-to-all-start = ((bf16[8,64,384]{2,1,0:T(8,128)(2,1)}), bf16[8,64,384]{2,1,0:T(8,128)(2,1)}, u32[]{:S(2)}, u32[]{:S(2)}) async-start(bf16[8,64,384]{2,1,0:T(8,128)(2,1)} %out_projection.1), calls=%async_computation | async-start | bytes 786432 | tf_op jit(solution)/shard_map/all_to_all | solution.py:248
  49.5 12.1 %all-to-all-done = bf16[8,64,384]{2,1,0:T(8,128)(2,1)} async-done(((bf16[8,64,384]{2,1,0:T(8,128)(2,1)}), bf16[8,64,384]{2,1,0:T(8,128)(2,1)}, u32[]{:S(2)}, u32[]{:S(2)}) %all-to-all-start) | async-done | bytes 393248 | tf_op jit(solution)/shard_map/all_to_all | solution.py:248
  62.7 1.5 collective-permute-start.8
  65.7 13.4 %all_to_all.15 = bf16[8,32,384]{2,1,0:T(8,128)(2,1)S(1)} all-to-all(bf16[8,32,384]{2,1,0:T(8,128)(2,1)S(1)} %bitcast.87), channel_id=1, replica_groups=mesh['dp'=16,'tensor'=8,'side'=2] {'tensor'}, dimensions={0} | all-to-all | bytes 393216 | tf_op jit(solution)/shard_map/all_to_all | solution.py:257
  79.1 1.9 collective-permute-start.11
  83.8 2.3 %collective-permute-done.10 = bf16[128,384]{1,0:T(8,128)(2,1)S(1)} collective-permute-done((bf16[128,384]{1,0:T(8,128)(2,1)S(1)}, bf16[128,384]{1,0:T(8,128)(2,1)S(1)}, u32[]{:S(2)}, u32[]{:S(2)}) %collective-permute-start.10) | collective-permute-done | bytes 98336 | tf_op jit(solution)/shard_map/ppermute | solution.py:263
  86.0 3.1 %collective-permute-done.9 = bf16[128,384]{1,0:T(8,128)(2,1)S(1)} collective-permute-done((bf16[128,384]{1,0:T(8,128)(2,1)S(1)}, bf16[128,384]{1,0:T(8,128)(2,1)S(1)}, u32[]{:S(2)}, u32[]{:S(2)}) %collective-permute-start.9) | collective-permute-done | bytes 98336 | tf_op jit(solution)/shard_map/ppermute | solution.py:263
  89.4 1.4 collective-permute-start.16
  90.9 1.4 collective-permute-start.20
  92.4 2.6 %collective-permute-start.18 = (bf16[4,128,384]{2,1,0:T(8,128)(2,1)S(1)}, bf16[4,128,384]{2,1,0:T(8,128)(2,1)S(1)}, u32[]{:S(2)}, u32[]{:S(2)}) collective-permute-start(bf16[4,128,384]{2,1,0:T(8,128)(2,1)S(1)} %pad_maximum_fusion.a0), channel_id=1, source_target_pairs={{0,48},{16,0},{32,16},{48,32},{64,112},{80,64},{96,80},{112,96},{1... | collective-permute-start | bytes 1179656 | tf_op jit(solution)/shard_map/ppermute | solution.py:268
  95.0 3.2 %collective-permute-done.16.b1 = bf16[4,128,384]{2,1,0:T(8,128)(2,1)S(1)} collective-permute-done((bf16[4,128,384]{2,1,0:T(8,128)(2,1)S(1)}, bf16[4,128,384]{2,1,0:T(8,128)(2,1)S(1)}, u32[]{:S(2)}, u32[]{:S(2)}) %collective-permute-start.16) | collective-permute-done | bytes 393248 | tf_op jit(solution)/shard_map/ppermute | solution.py:269
  98.2 2.4 %collective-permute-done.15.a1 = bf16[4,128,384]{2,1,0:T(8,128)(2,1)S(1)} collective-permute-done((bf16[4,128,384]{2,1,0:T(8,128)(2,1)S(1)}, bf16[4,128,384]{2,1,0:T(8,128)(2,1)S(1)}, u32[]{:S(2)}, u32[]{:S(2)}) %collective-permute-start.15) | collective-permute-done | bytes 393248 | tf_op jit(solution)/shard_map/ppermute | solution.py:268
  101.4 8.2 %collective-permute-done.17.a2 = bf16[4,128,384]{2,1,0:T(8,128)(2,1)S(1)} collective-permute-done((bf16[4,128,384]{2,1,0:T(8,128)(2,1)S(1)}, bf16[4,128,384]{2,1,0:T(8,128)(2,1)S(1)}, u32[]{:S(2)}, u32[]{:S(2)}) %collective-permute-start.17) | collective-permute-done | bytes 393248 | tf_op jit(solution)/shard_map/ppermute | solution.py:272
  109.6 3.2 %norm.1 = bf16[256,6144]{1,0:T(8,128)(2,1)S(1)} custom-call(s32[3]{0:T(128)S(1)} %pad_add_fusion.pos, bf16[4,128,384]{2,1,0:T(8,128)(2,1)S(1)} %pad_maximum_fusion.a0, bf16[4,128,384]{2,1,0:T(8,128)(2,1)S(1)} %collective-permute-done.15.a1, bf16[4,128,384]{2,1,0:T(8,128)(2,1)S(1)} %collective-permute-done.17.a2, ...), custom_call_target="tpu_custom_call" | custom-call | tf_op jit(solution)/shard_map/norm/pallas_call | solution.py:105
  112.8 6.8 %collective-permute-start.21 = (bf16[256,6144]{1,0:T(8,128)(2,1)S(1)}, bf16[256,6144]{1,0:T(8,128)(2,1)S(1)}, u32[]{:S(2)}, u32[]{:S(2)}) collective-permute-start(bf16[256,6144]{1,0:T(8,128)(2,1)S(1)} %norm.1), channel_id=1, source_target_pairs={{0,1},{1,0},{2,3},{3,2},{4,5},{5,4},{6,7},{7,6},{8,9},{9,8},{10,11... | collective-permute-start | bytes 9437192 | tf_op jit(solution)/shard_map/ppermute | solution.py:21
  121.6 3.3 %collective-permute-done.21 = bf16[256,6144]{1,0:T(8,128)(2,1)S(1)} collective-permute-done((bf16[256,6144]{1,0:T(8,128)(2,1)S(1)}, bf16[256,6144]{1,0:T(8,128)(2,1)S(1)}, u32[]{:S(2)}, u32[]{:S(2)}) %collective-permute-start.21) | collective-permute-done | bytes 3145760 | tf_op jit(solution)/shard_map/ppermute | solution.py:21
  126.9 1.8 convolution_convert_fusion.1
  129.1 1.8 convolution_convert_fusion.2
  132.4 3.1 %combine_cores.3 = (bf16[4,128,384]{2,1,0:T(8,128)(2,1)S(1)}, bf16[4,128,384]{2,1,0:T(8,128)(2,1)}, bf16[4,128,384]{2,1,0:T(8,128)(2,1)}, bf16[4,128,384]{2,1,0:T(8,128)(2,1)}) custom-call(s32[3]{0:T(128)S(1)} %pad_add_fusion.pos, bf16[256,6144]{1,0:T(8,128)(2,1)S(1)} %convolution_convert_fusion.own, bf16[128,6144]{1,0:T(8,128)(2,1)} %collective-permute-done.29.other), custom_call_target="tpu_custom_call" | custom-call | tf_op jit(solution)/shard_map/combine_cores/pallas_call | solution.py:105
  135.7 2.7 %collective-permute-start.31 = (bf16[4,128,384]{2,1,0:T(8,128)(2,1)}, bf16[4,128,384]{2,1,0:T(8,128)(2,1)}, u32[]{:S(2)}, u32[]{:S(2)}) collective-permute-start(bf16[4,128,384]{2,1,0:T(8,128)(2,1)} %get-tuple-element.59), channel_id=1, source_target_pairs={{0,192},{16,208},{32,224},{48,240},{64,0},{80,16},{96,32},{112,48}... | collective-permute-start | bytes 1179656 | tf_op jit(solution)/shard_map/ppermute | solution.py:313
  138.4 2.0 %collective-permute-start.32 = (bf16[4,128,384]{2,1,0:T(8,128)(2,1)}, bf16[4,128,384]{2,1,0:T(8,128)(2,1)}, u32[]{:S(2)}, u32[]{:S(2)}) collective-permute-start(bf16[4,128,384]{2,1,0:T(8,128)(2,1)} %get-tuple-element.60), channel_id=1, source_target_pairs={{0,128},{16,144},{32,160},{48,176},{64,192},{80,208},{96,224},{112... | collective-permute-start | bytes 1179656 | tf_op jit(solution)/shard_map/ppermute | solution.py:313
  140.5 2.8 %combine_cores.2 = (bf16[4,128,384]{2,1,0:T(8,128)(2,1)S(1)}, bf16[4,128,384]{2,1,0:T(8,128)(2,1)}, bf16[4,128,384]{2,1,0:T(8,128)(2,1)S(1)}, bf16[4,128,384]{2,1,0:T(8,128)(2,1)S(1)}) custom-call(s32[3]{0:T(128)S(1)} %pad_add_fusion.pos, bf16[256,6144]{1,0:T(8,128)(2,1)S(1)} %convolution_convert_fusion.own, bf16[128,6144]{1,0:T(8,128)(2,1)} %collective-permute-done.22.other), custom_call_target="tpu_custom_call" | custom-call | tf_op jit(solution)/shard_map/combine_cores/pallas_call | solution.py:105
  145.2 2.6 %collective-permute-start.24 = (bf16[4,128,384]{2,1,0:T(8,128)(2,1)}, bf16[4,128,384]{2,1,0:T(8,128)(2,1)}, u32[]{:S(2)}, u32[]{:S(2)}) collective-permute-start(bf16[4,128,384]{2,1,0:T(8,128)(2,1)} %copy-done.12), channel_id=1, source_target_pairs={{0,48},{16,0},{32,16},{48,32},{64,112},{80,64},{96,80},{112,96},{1... | collective-permute-start | bytes 1179656 | tf_op jit(solution)/shard_map/ppermute | solution.py:313
  147.8 2.9 %collective-permute-start.25 = (bf16[4,128,384]{2,1,0:T(8,128)(2,1)}, bf16[4,128,384]{2,1,0:T(8,128)(2,1)}, u32[]{:S(2)}, u32[]{:S(2)}) collective-permute-start(bf16[4,128,384]{2,1,0:T(8,128)(2,1)} %copy-done.11), channel_id=1, source_target_pairs={{0,32},{16,48},{32,0},{48,16},{64,96},{80,112},{96,64},{112,80},{1... | collective-permute-start | bytes 1179656 | tf_op jit(solution)/shard_map/ppermute | solution.py:313
  150.7 2.8 %fusion.12 = f32[256]{0:T(256)S(1)} fusion(bf16[256,6144]{1,0:T(8,128)(2,1)} %copy-done.1, bf16[6144,8]{0,1:T(8,128)(2,1)} %param.23, s32[256]{0:T(256)S(1)} %eq.144, f32[8]{0:T(128)S(1)} %compare_convert_fusion), kind=kOutput, calls=%fused_computation.19 | convolution fusion | flops 25175808 | bytes 3246112 | tf_op jit(solution)/shard_map/dot_general | solution.py:293
  153.5 3.2 %collective-permute-done.32.got3 = bf16[4,128,384]{2,1,0:T(8,128)(2,1)} collective-permute-done((bf16[4,128,384]{2,1,0:T(8,128)(2,1)}, bf16[4,128,384]{2,1,0:T(8,128)(2,1)}, u32[]{:S(2)}, u32[]{:S(2)}) %collective-permute-start.32) | collective-permute-done | bytes 393248 | tf_op jit(solution)/shard_map/ppermute | solution.py:313
  156.8 2.1 %sum_rows.3 = (f32[128,384]{1,0:T(8,128)S(1)}, bf16[128,384]{1,0:T(8,128)(2,1)}, bf16[128,384]{1,0:T(8,128)(2,1)}, bf16[128,384]{1,0:T(8,128)(2,1)}) custom-call(bf16[4,128,384]{2,1,0:T(8,128)(2,1)S(1)} %copy-done.5, bf16[4,128,384]{2,1,0:T(8,128)(2,1)} %collective-permute-done.30.got1, bf16[4,128,384]{2,1,0:T(8,128)(2,1)} %collective-permute-done.31.got2, ...), custom_call_target="tpu_custom_call" | custom-call | tf_op jit(solution)/shard_map/sum_rows/pallas_call | solution.py:105
  159.7 2.5 %collective-permute-start.34 = (bf16[128,384]{1,0:T(8,128)(2,1)}, bf16[128,384]{1,0:T(8,128)(2,1)}, u32[]{:S(2)}, u32[]{:S(2)}) collective-permute-start(bf16[128,384]{1,0:T(8,128)(2,1)} %get-tuple-element.63), channel_id=1, source_target_pairs={{0,48},{16,0},{32,16},{48,32},{64,112},{80,64},{96,80},{112,96},{1... | collective-permute-start | bytes 294920 | tf_op jit(solution)/shard_map/ppermute | solution.py:322
  162.3 2.0 %collective-permute-start.35 = (bf16[128,384]{1,0:T(8,128)(2,1)}, bf16[128,384]{1,0:T(8,128)(2,1)}, u32[]{:S(2)}, u32[]{:S(2)}) collective-permute-start(bf16[128,384]{1,0:T(8,128)(2,1)} %get-tuple-element.64), channel_id=1, source_target_pairs={{0,32},{16,48},{32,0},{48,16},{64,96},{80,112},{96,64},{112,80},{1... | collective-permute-start | bytes 294920 | tf_op jit(solution)/shard_map/ppermute | solution.py:322
  165.0 1.4 sum_rows.2
  166.4 2.3 %collective-permute-start.26 = (bf16[128,384]{1,0:T(8,128)(2,1)S(1)}, bf16[128,384]{1,0:T(8,128)(2,1)S(1)}, u32[]{:S(2)}, u32[]{:S(2)}) collective-permute-start(bf16[128,384]{1,0:T(8,128)(2,1)S(1)} %get-tuple-element.54), channel_id=1, source_target_pairs={{0,64},{16,80},{32,96},{48,112},{64,128},{80,144},{96,160},{112,17... | collective-permute-start | bytes 294920 | tf_op jit(solution)/shard_map/ppermute | solution.py:322
  169.5 3.2 %collective-permute-start.28 = (bf16[128,384]{1,0:T(8,128)(2,1)S(1)}, bf16[128,384]{1,0:T(8,128)(2,1)S(1)}, u32[]{:S(2)}, u32[]{:S(2)}) collective-permute-start(bf16[128,384]{1,0:T(8,128)(2,1)S(1)} %get-tuple-element.56), channel_id=1, source_target_pairs={{0,128},{16,144},{32,160},{48,176},{64,192},{80,208},{96,224},{112... | collective-permute-start | bytes 294920 | tf_op jit(solution)/shard_map/ppermute | solution.py:322
  175.6 3.4 %all-to-all-start.2 = ((bf16[8,32,384]{2,1,0:T(8,128)(2,1)}), bf16[8,32,384]{2,1,0:T(8,128)(2,1)S(1)}, u32[]{:S(2)}, u32[]{:S(2)}) async-start(bf16[8,32,384]{2,1,0:T(8,128)(2,1)} %multiply_convert_fusion), calls=%async_computation.2 | async-start | bytes 393216 | tf_op jit(solution)/shard_map/all_to_all | solution.py:327
  180.0 7.6 %all-to-all-done.2 = bf16[8,32,384]{2,1,0:T(8,128)(2,1)S(1)} async-done(((bf16[8,32,384]{2,1,0:T(8,128)(2,1)}), bf16[8,32,384]{2,1,0:T(8,128)(2,1)S(1)}, u32[]{:S(2)}, u32[]{:S(2)}) %all-to-all-start.2) | async-done | bytes 196640 | tf_op jit(solution)/shard_map/all_to_all | solution.py:327
  187.7 6.9 %collective-permute-start.36 = (bf16[256,192]{1,0:T(8,128)(2,1)S(1)}, bf16[256,192]{1,0:T(8,128)(2,1)S(1)}, u32[]{:S(2)}, u32[]{:S(2)}) collective-permute-start(bf16[256,192]{1,0:T(8,128)(2,1)S(1)} %broadcast_select_fusion), channel_id=1, source_target_pairs={{0,1},{1,0},{2,3},{3,2},{4,5},{5,4},{6,7},{7,6},{8,9},{9,8},{10,11... | collective-permute-start | bytes 294920 | tf_op jit(solution)/shard_map/ppermute | solution.py:21
  (132 shorter events, 33.7 us)
Async XLA Ops:
  0.0 126.9 %copy-start = (bf16[1,256,6144]{2,1,0:T(8,128)(2,1)S(1)}, bf16[1,256,6144]{2,1,0:T(8,128)(2,1)}, u32[]{:S(2)}) copy-start(bf16[1,256,6144]{2,1,0:T(8,128)(2,1)} %param.27) | copy-start | bytes 9437188
  7.6 39.7 %copy-start.17 = (bf16[128,192]{0,1:T(8,128)(2,1)S(1)}, bf16[128,192]{0,1:T(8,128)(2,1)}, u32[]{:S(2)}) copy-start(bf16[128,192]{0,1:T(8,128)(2,1)} %param.21) | copy-start | bytes 147460
  7.6 4.6 %collective-permute-start.2 = (bf16[32,768]{1,0:T(8,128)(2,1)S(1)}, bf16[32,768]{1,0:T(8,128)(2,1)}, u32[]{:S(2)}, u32[]{:S(2)}) collective-permute-start(bf16[32,768]{1,0:T(8,128)(2,1)S(1)} %attend.1), channel_id=1, source_target_pairs={{0,192},{16,208},{32,224},{48,240},{64,0},{80,16},{96,32},{112,48}... | collective-permute-start | bytes 147464 | tf_op jit(solution)/shard_map/ppermute | solution.py:234
  13.1 12.9 %collective-permute-start.6 = (bf16[768,192]{1,0:T(8,128)(2,1)}, bf16[768,192]{1,0:T(8,128)(2,1)}, u32[]{:S(2)}, u32[]{:S(2)}) collective-permute-start(bf16[768,192]{1,0:T(8,128)(2,1)} %copy.33), channel_id=1, source_target_pairs={{0,1},{1,0},{2,3},{3,2},{4,5},{5,4},{6,7},{7,6},{8,9},{9,8},{10,11... | collective-permute-start | bytes 884744 | tf_op jit(solution)/shard_map/ppermute | solution.py:21
  16.1 4.9 %collective-permute-start.1 = (bf16[32,768]{1,0:T(8,128)(2,1)S(1)}, bf16[32,768]{1,0:T(8,128)(2,1)S(1)}, u32[]{:S(2)}, u32[]{:S(2)}) collective-permute-start(bf16[32,768]{1,0:T(8,128)(2,1)S(1)} %attend.1), channel_id=1, source_target_pairs={{0,128},{16,144},{32,160},{48,176},{64,192},{80,208},{96,224},{112... | collective-permute-start | bytes 147464 | tf_op jit(solution)/shard_map/ppermute | solution.py:234
  17.1 5.0 %collective-permute-start = (bf16[32,768]{1,0:T(8,128)(2,1)S(1)}, bf16[32,768]{1,0:T(8,128)(2,1)S(1)}, u32[]{:S(2)}, u32[]{:S(2)}) collective-permute-start(bf16[32,768]{1,0:T(8,128)(2,1)S(1)} %attend.1), channel_id=1, source_target_pairs={{0,64},{16,80},{32,96},{48,112},{64,128},{80,144},{96,160},{112,17... | collective-permute-start | bytes 147464 | tf_op jit(solution)/shard_map/ppermute | solution.py:234
  22.9 5.8 %collective-permute-start.5 = (bf16[4,32,768]{2,1,0:T(8,128)(2,1)S(1)}, bf16[4,32,768]{2,1,0:T(8,128)(2,1)S(1)}, u32[]{:S(2)}, u32[]{:S(2)}) collective-permute-start(bf16[4,32,768]{2,1,0:T(8,128)(2,1)S(1)} %pad_maximum_fusion.3.g0), channel_id=1, source_target_pairs={{0,48},{16,0},{32,16},{48,32},{64,112},{80,64},{96,80},{112,96},{1... | collective-permute-start | bytes 589832 | tf_op jit(solution)/shard_map/ppermute | solution.py:238
  24.9 6.1 %collective-permute-start.4 = (bf16[4,32,768]{2,1,0:T(8,128)(2,1)S(1)}, bf16[4,32,768]{2,1,0:T(8,128)(2,1)S(1)}, u32[]{:S(2)}, u32[]{:S(2)}) collective-permute-start(bf16[4,32,768]{2,1,0:T(8,128)(2,1)S(1)} %pad_maximum_fusion.3.g0), channel_id=1, source_target_pairs={{0,32},{16,48},{32,0},{48,16},{64,96},{80,112},{96,64},{112,80},{1... | collective-permute-start | bytes 589832 | tf_op jit(solution)/shard_map/ppermute | solution.py:238
  25.2 12.0 %collective-permute-start.3 = (bf16[4,32,768]{2,1,0:T(8,128)(2,1)S(1)}, bf16[4,32,768]{2,1,0:T(8,128)(2,1)S(1)}, u32[]{:S(2)}, u32[]{:S(2)}) collective-permute-start(bf16[4,32,768]{2,1,0:T(8,128)(2,1)S(1)} %pad_maximum_fusion.3.g0), channel_id=1, source_target_pairs={{0,16},{16,32},{32,48},{48,0},{64,80},{80,96},{96,112},{112,64},{1... | collective-permute-start | bytes 589832 | tf_op jit(solution)/shard_map/ppermute | solution.py:238
  27.8 81.8 %copy-start.8 = (f32[6144]{0:T(1024)S(1)}, f32[6144]{0:T(1024)}, u32[]{:S(2)}) copy-start(f32[6144]{0:T(1024)} %param.22) | copy-start | bytes 73732
  39.1 22.5 %all-to-all-start = ((bf16[8,64,384]{2,1,0:T(8,128)(2,1)}), bf16[8,64,384]{2,1,0:T(8,128)(2,1)}, u32[]{:S(2)}, u32[]{:S(2)}) async-start(bf16[8,64,384]{2,1,0:T(8,128)(2,1)} %out_projection.1), calls=%async_computation | async-start | bytes 786432 | tf_op jit(solution)/shard_map/all_to_all | solution.py:248
  47.4 1.9 collective-permute-start.7
  62.7 2.7 %collective-permute-start.8 = (bf16[64,384]{1,0:T(8,128)(2,1)S(1)}, bf16[64,384]{1,0:T(8,128)(2,1)S(1)}, u32[]{:S(2)}, u32[]{:S(2)}) collective-permute-start(bf16[64,384]{1,0:T(8,128)(2,1)S(1)} %fusion.22), channel_id=1, source_target_pairs={{0,1},{1,0},{2,3},{3,2},{4,5},{5,4},{6,7},{7,6},{8,9},{9,8},{10,11... | collective-permute-start | bytes 147464 | tf_op jit(solution)/shard_map/ppermute | solution.py:21
  65.5 23.9 %copy-start.13 = (bf16[128,384]{1,0:T(8,128)(2,1)}, bf16[128,384]{1,0:T(8,128)(2,1)S(1)}, u32[]{:S(2)}) copy-start(bf16[128,384]{1,0:T(8,128)(2,1)S(1)} %maximum_select_fusion.2) | copy-start | bytes 294916
  79.1 4.0 %collective-permute-start.11 = (bf16[128,384]{1,0:T(8,128)(2,1)S(1)}, bf16[128,384]{1,0:T(8,128)(2,1)S(1)}, u32[]{:S(2)}, u32[]{:S(2)}) collective-permute-start(bf16[128,384]{1,0:T(8,128)(2,1)S(1)} %bitcast.89), channel_id=1, source_target_pairs={{0,192},{16,208},{32,224},{48,240},{64,0},{80,16},{96,32},{112,48}... | collective-permute-start | bytes 294920 | tf_op jit(solution)/shard_map/ppermute | solution.py:263
  81.0 5.1 %collective-permute-start.10 = (bf16[128,384]{1,0:T(8,128)(2,1)S(1)}, bf16[128,384]{1,0:T(8,128)(2,1)S(1)}, u32[]{:S(2)}, u32[]{:S(2)}) collective-permute-start(bf16[128,384]{1,0:T(8,128)(2,1)S(1)} %bitcast.90), channel_id=1, source_target_pairs={{0,128},{16,144},{32,160},{48,176},{64,192},{80,208},{96,224},{112... | collective-permute-start | bytes 294920 | tf_op jit(solution)/shard_map/ppermute | solution.py:263
  81.5 7.6 %collective-permute-start.9 = (bf16[128,384]{1,0:T(8,128)(2,1)S(1)}, bf16[128,384]{1,0:T(8,128)(2,1)S(1)}, u32[]{:S(2)}, u32[]{:S(2)}) collective-permute-start(bf16[128,384]{1,0:T(8,128)(2,1)S(1)} %bitcast.91), channel_id=1, source_target_pairs={{0,64},{16,80},{32,96},{48,112},{64,128},{80,144},{96,160},{112,17... | collective-permute-start | bytes 294920 | tf_op jit(solution)/shard_map/ppermute | solution.py:263
  82.3 6.8 %collective-permute-start.14 = (bf16[128,384]{1,0:T(8,128)(2,1)S(1)}, bf16[128,384]{1,0:T(8,128)(2,1)S(1)}, u32[]{:S(2)}, u32[]{:S(2)}) collective-permute-start(bf16[128,384]{1,0:T(8,128)(2,1)S(1)} %bitcast.93), channel_id=1, source_target_pairs={{0,48},{16,0},{32,16},{48,32},{64,112},{80,64},{96,80},{112,96},{1... | collective-permute-start | bytes 294920 | tf_op jit(solution)/shard_map/ppermute | solution.py:264
  82.3 6.8 %collective-permute-start.13 = (bf16[128,384]{1,0:T(8,128)(2,1)S(1)}, bf16[128,384]{1,0:T(8,128)(2,1)S(1)}, u32[]{:S(2)}, u32[]{:S(2)}) collective-permute-start(bf16[128,384]{1,0:T(8,128)(2,1)S(1)} %bitcast.94), channel_id=1, source_target_pairs={{0,32},{16,48},{32,0},{48,16},{64,96},{80,112},{96,64},{112,80},{1... | collective-permute-start | bytes 294920 | tf_op jit(solution)/shard_map/ppermute | solution.py:264
  83.1 6.2 %collective-permute-start.12 = (bf16[128,384]{1,0:T(8,128)(2,1)S(1)}, bf16[128,384]{1,0:T(8,128)(2,1)S(1)}, u32[]{:S(2)}, u32[]{:S(2)}) collective-permute-start(bf16[128,384]{1,0:T(8,128)(2,1)S(1)} %bitcast.95), channel_id=1, source_target_pairs={{0,16},{16,32},{32,48},{48,0},{64,80},{80,96},{96,112},{112,64},{1... | collective-permute-start | bytes 294920 | tf_op jit(solution)/shard_map/ppermute | solution.py:264
  89.4 8.8 %collective-permute-start.16 = (bf16[4,128,384]{2,1,0:T(8,128)(2,1)S(1)}, bf16[4,128,384]{2,1,0:T(8,128)(2,1)S(1)}, u32[]{:S(2)}, u32[]{:S(2)}) collective-permute-start(bf16[4,128,384]{2,1,0:T(8,128)(2,1)S(1)} %pad_maximum_fusion.1.b0), channel_id=1, source_target_pairs={{0,64},{16,80},{32,96},{48,112},{64,128},{80,144},{96,160},{112,17... | collective-permute-start | bytes 1179656 | tf_op jit(solution)/shard_map/ppermute | solution.py:269
  90.9 9.7 %collective-permute-start.15 = (bf16[4,128,384]{2,1,0:T(8,128)(2,1)S(1)}, bf16[4,128,384]{2,1,0:T(8,128)(2,1)S(1)}, u32[]{:S(2)}, u32[]{:S(2)}) collective-permute-start(bf16[4,128,384]{2,1,0:T(8,128)(2,1)S(1)} %pad_maximum_fusion.a0), channel_id=1, source_target_pairs={{0,16},{16,32},{32,48},{48,0},{64,80},{80,96},{96,112},{112,64},{1... | collective-permute-start | bytes 1179656 | tf_op jit(solution)/shard_map/ppermute | solution.py:268
  90.9 10.5 %collective-permute-start.20 = (bf16[4,128,384]{2,1,0:T(8,128)(2,1)S(1)}, bf16[4,128,384]{2,1,0:T(8,128)(2,1)S(1)}, u32[]{:S(2)}, u32[]{:S(2)}) collective-permute-start(bf16[4,128,384]{2,1,0:T(8,128)(2,1)S(1)} %pad_maximum_fusion.1.b0), channel_id=1, source_target_pairs={{0,192},{16,208},{32,224},{48,240},{64,0},{80,16},{96,32},{112,48}... | collective-permute-start | bytes 1179656 | tf_op jit(solution)/shard_map/ppermute | solution.py:269
  92.4 9.1 %collective-permute-start.18 = (bf16[4,128,384]{2,1,0:T(8,128)(2,1)S(1)}, bf16[4,128,384]{2,1,0:T(8,128)(2,1)S(1)}, u32[]{:S(2)}, u32[]{:S(2)}) collective-permute-start(bf16[4,128,384]{2,1,0:T(8,128)(2,1)S(1)} %pad_maximum_fusion.a0), channel_id=1, source_target_pairs={{0,48},{16,0},{32,16},{48,32},{64,112},{80,64},{96,80},{112,96},{1... | collective-permute-start | bytes 1179656 | tf_op jit(solution)/shard_map/ppermute | solution.py:268
  100.6 9.0 %collective-permute-start.17 = (bf16[4,128,384]{2,1,0:T(8,128)(2,1)S(1)}, bf16[4,128,384]{2,1,0:T(8,128)(2,1)S(1)}, u32[]{:S(2)}, u32[]{:S(2)}) collective-permute-start(bf16[4,128,384]{2,1,0:T(8,128)(2,1)S(1)} %pad_maximum_fusion.a0), channel_id=1, source_target_pairs={{0,32},{16,48},{32,0},{48,16},{64,96},{80,112},{96,64},{112,80},{1... | collective-permute-start | bytes 1179656 | tf_op jit(solution)/shard_map/ppermute | solution.py:272
  100.6 9.0 %collective-permute-start.19 = (bf16[4,128,384]{2,1,0:T(8,128)(2,1)S(1)}, bf16[4,128,384]{2,1,0:T(8,128)(2,1)S(1)}, u32[]{:S(2)}, u32[]{:S(2)}) collective-permute-start(bf16[4,128,384]{2,1,0:T(8,128)(2,1)S(1)} %pad_maximum_fusion.1.b0), channel_id=1, source_target_pairs={{0,128},{16,144},{32,160},{48,176},{64,192},{80,208},{96,224},{112... | collective-permute-start | bytes 1179656 | tf_op jit(solution)/shard_map/ppermute | solution.py:272
  109.6 10.0 %copy-start.19 = (bf16[1,6144,256]{2,1,0:T(8,128)(2,1)S(1)}, bf16[1,6144,256]{2,1,0:T(8,128)(2,1)}, u32[]{:S(2)}) copy-start(bf16[1,6144,256]{2,1,0:T(8,128)(2,1)} %param.25) | copy-start | bytes 9437188
  112.8 7.8 %copy-start.1 = (bf16[256,6144]{1,0:T(8,128)(2,1)}, bf16[256,6144]{1,0:T(8,128)(2,1)S(1)}, u32[]{:S(2)}) copy-start(bf16[256,6144]{1,0:T(8,128)(2,1)S(1)} %norm.1) | copy-start | bytes 9437188
  112.8 12.1 %collective-permute-start.21 = (bf16[256,6144]{1,0:T(8,128)(2,1)S(1)}, bf16[256,6144]{1,0:T(8,128)(2,1)S(1)}, u32[]{:S(2)}, u32[]{:S(2)}) collective-permute-start(bf16[256,6144]{1,0:T(8,128)(2,1)S(1)} %norm.1), channel_id=1, source_target_pairs={{0,1},{1,0},{2,3},{3,2},{4,5},{5,4},{6,7},{7,6},{8,9},{9,8},{10,11... | collective-permute-start | bytes 9437192 | tf_op jit(solution)/shard_map/ppermute | solution.py:21
  128.7 3.8 %collective-permute-start.29 = (bf16[128,6144]{1,0:T(8,128)(2,1)}, bf16[128,6144]{1,0:T(8,128)(2,1)}, u32[]{:S(2)}, u32[]{:S(2)}) collective-permute-start(bf16[128,6144]{1,0:T(8,128)(2,1)} %convolution_convert_fusion.1), channel_id=1, source_target_pairs={{0,1},{1,0},{2,3},{3,2},{4,5},{5,4},{6,7},{7,6},{8,9},{9,8},{10,11... | collective-permute-start | bytes 4718600 | tf_op jit(solution)/shard_map/ppermute | solution.py:21
  130.8 9.6 %collective-permute-start.22 = (bf16[128,6144]{1,0:T(8,128)(2,1)}, bf16[128,6144]{1,0:T(8,128)(2,1)}, u32[]{:S(2)}, u32[]{:S(2)}) collective-permute-start(bf16[128,6144]{1,0:T(8,128)(2,1)} %convolution_convert_fusion.2), channel_id=1, source_target_pairs={{0,1},{1,0},{2,3},{3,2},{4,5},{5,4},{6,7},{7,6},{8,9},{9,8},{10,11... | collective-permute-start | bytes 4718600 | tf_op jit(solution)/shard_map/ppermute | solution.py:21
  135.6 12.2 %collective-permute-start.30 = (bf16[4,128,384]{2,1,0:T(8,128)(2,1)}, bf16[4,128,384]{2,1,0:T(8,128)(2,1)}, u32[]{:S(2)}, u32[]{:S(2)}) collective-permute-start(bf16[4,128,384]{2,1,0:T(8,128)(2,1)} %get-tuple-element.58), channel_id=1, source_target_pairs={{0,64},{16,80},{32,96},{48,112},{64,128},{80,144},{96,160},{112,17... | collective-permute-start | bytes 1179656 | tf_op jit(solution)/shard_map/ppermute | solution.py:313
  135.7 17.8 %collective-permute-start.31 = (bf16[4,128,384]{2,1,0:T(8,128)(2,1)}, bf16[4,128,384]{2,1,0:T(8,128)(2,1)}, u32[]{:S(2)}, u32[]{:S(2)}) collective-permute-start(bf16[4,128,384]{2,1,0:T(8,128)(2,1)} %get-tuple-element.59), channel_id=1, source_target_pairs={{0,192},{16,208},{32,224},{48,240},{64,0},{80,16},{96,32},{112,48}... | collective-permute-start | bytes 1179656 | tf_op jit(solution)/shard_map/ppermute | solution.py:313
  138.4 18.3 %collective-permute-start.32 = (bf16[4,128,384]{2,1,0:T(8,128)(2,1)}, bf16[4,128,384]{2,1,0:T(8,128)(2,1)}, u32[]{:S(2)}, u32[]{:S(2)}) collective-permute-start(bf16[4,128,384]{2,1,0:T(8,128)(2,1)} %get-tuple-element.60), channel_id=1, source_target_pairs={{0,128},{16,144},{32,160},{48,176},{64,192},{80,208},{96,224},{112... | collective-permute-start | bytes 1179656 | tf_op jit(solution)/shard_map/ppermute | solution.py:313
  144.8 17.5 %collective-permute-start.23 = (bf16[4,128,384]{2,1,0:T(8,128)(2,1)}, bf16[4,128,384]{2,1,0:T(8,128)(2,1)}, u32[]{:S(2)}, u32[]{:S(2)}) collective-permute-start(bf16[4,128,384]{2,1,0:T(8,128)(2,1)} %get-tuple-element.50), channel_id=1, source_target_pairs={{0,16},{16,32},{32,48},{48,0},{64,80},{80,96},{96,112},{112,64},{1... | collective-permute-start | bytes 1179656 | tf_op jit(solution)/shard_map/ppermute | solution.py:313
  145.2 11.6 %copy-start.5 = (bf16[4,128,384]{2,1,0:T(8,128)(2,1)S(1)}, bf16[4,128,384]{2,1,0:T(8,128)(2,1)}, u32[]{:S(2)}) copy-start(bf16[4,128,384]{2,1,0:T(8,128)(2,1)} %copy-done.4) | copy-start | bytes 1179652
  145.2 19.2 %collective-permute-start.24 = (bf16[4,128,384]{2,1,0:T(8,128)(2,1)}, bf16[4,128,384]{2,1,0:T(8,128)(2,1)}, u32[]{:S(2)}, u32[]{:S(2)}) collective-permute-start(bf16[4,128,384]{2,1,0:T(8,128)(2,1)} %copy-done.12), channel_id=1, source_target_pairs={{0,48},{16,0},{32,16},{48,32},{64,112},{80,64},{96,80},{112,96},{1... | collective-permute-start | bytes 1179656 | tf_op jit(solution)/shard_map/ppermute | solution.py:313
  147.8 17.1 %collective-permute-start.25 = (bf16[4,128,384]{2,1,0:T(8,128)(2,1)}, bf16[4,128,384]{2,1,0:T(8,128)(2,1)}, u32[]{:S(2)}, u32[]{:S(2)}) collective-permute-start(bf16[4,128,384]{2,1,0:T(8,128)(2,1)} %copy-done.11), channel_id=1, source_target_pairs={{0,32},{16,48},{32,0},{48,16},{64,96},{80,112},{96,64},{112,80},{1... | collective-permute-start | bytes 1179656 | tf_op jit(solution)/shard_map/ppermute | solution.py:313
  159.6 9.9 %collective-permute-start.33 = (bf16[128,384]{1,0:T(8,128)(2,1)}, bf16[128,384]{1,0:T(8,128)(2,1)}, u32[]{:S(2)}, u32[]{:S(2)}) collective-permute-start(bf16[128,384]{1,0:T(8,128)(2,1)} %get-tuple-element.62), channel_id=1, source_target_pairs={{0,16},{16,32},{32,48},{48,0},{64,80},{80,96},{96,112},{112,64},{1... | collective-permute-start | bytes 294920 | tf_op jit(solution)/shard_map/ppermute | solution.py:322
  159.7 13.0 %collective-permute-start.34 = (bf16[128,384]{1,0:T(8,128)(2,1)}, bf16[128,384]{1,0:T(8,128)(2,1)}, u32[]{:S(2)}, u32[]{:S(2)}) collective-permute-start(bf16[128,384]{1,0:T(8,128)(2,1)} %get-tuple-element.63), channel_id=1, source_target_pairs={{0,48},{16,0},{32,16},{48,32},{64,112},{80,64},{96,80},{112,96},{1... | collective-permute-start | bytes 294920 | tf_op jit(solution)/shard_map/ppermute | solution.py:322
  162.3 10.5 %collective-permute-start.35 = (bf16[128,384]{1,0:T(8,128)(2,1)}, bf16[128,384]{1,0:T(8,128)(2,1)}, u32[]{:S(2)}, u32[]{:S(2)}) collective-permute-start(bf16[128,384]{1,0:T(8,128)(2,1)} %get-tuple-element.64), channel_id=1, source_target_pairs={{0,32},{16,48},{32,0},{48,16},{64,96},{80,112},{96,64},{112,80},{1... | collective-permute-start | bytes 294920 | tf_op jit(solution)/shard_map/ppermute | solution.py:322
  166.4 12.6 %copy-start.14 = (bf16[128,384]{1,0:T(8,128)(2,1)S(1)}, bf16[128,384]{1,0:T(8,128)(2,1)}, u32[]{:S(2)}) copy-start(bf16[128,384]{1,0:T(8,128)(2,1)} %copy-done.13) | copy-start | bytes 294916
  166.4 29.2 %copy-start.16 = (pred[256,128]{1,0:T(32,128)(4,1)S(1)}, pred[256,128]{1,0:T(32,128)(4,1)}, u32[]{:S(2)}) copy-start(pred[256,128]{1,0:T(32,128)(4,1)} %get-tuple-element.71) | copy-start | bytes 98308
  166.4 7.4 %collective-permute-start.26 = (bf16[128,384]{1,0:T(8,128)(2,1)S(1)}, bf16[128,384]{1,0:T(8,128)(2,1)S(1)}, u32[]{:S(2)}, u32[]{:S(2)}) collective-permute-start(bf16[128,384]{1,0:T(8,128)(2,1)S(1)} %get-tuple-element.54), channel_id=1, source_target_pairs={{0,64},{16,80},{32,96},{48,112},{64,128},{80,144},{96,160},{112,17... | collective-permute-start | bytes 294920 | tf_op jit(solution)/shard_map/ppermute | solution.py:322
  168.7 5.1 %collective-permute-start.27 = (bf16[128,384]{1,0:T(8,128)(2,1)S(1)}, bf16[128,384]{1,0:T(8,128)(2,1)S(1)}, u32[]{:S(2)}, u32[]{:S(2)}) collective-permute-start(bf16[128,384]{1,0:T(8,128)(2,1)S(1)} %get-tuple-element.55), channel_id=1, source_target_pairs={{0,192},{16,208},{32,224},{48,240},{64,0},{80,16},{96,32},{112,48}... | collective-permute-start | bytes 294920 | tf_op jit(solution)/shard_map/ppermute | solution.py:322
  169.5 5.3 %collective-permute-start.28 = (bf16[128,384]{1,0:T(8,128)(2,1)S(1)}, bf16[128,384]{1,0:T(8,128)(2,1)S(1)}, u32[]{:S(2)}, u32[]{:S(2)}) collective-permute-start(bf16[128,384]{1,0:T(8,128)(2,1)S(1)} %get-tuple-element.56), channel_id=1, source_target_pairs={{0,128},{16,144},{32,160},{48,176},{64,192},{80,208},{96,224},{112... | collective-permute-start | bytes 294920 | tf_op jit(solution)/shard_map/ppermute | solution.py:322
  175.6 11.9 %all-to-all-start.2 = ((bf16[8,32,384]{2,1,0:T(8,128)(2,1)}), bf16[8,32,384]{2,1,0:T(8,128)(2,1)S(1)}, u32[]{:S(2)}, u32[]{:S(2)}) async-start(bf16[8,32,384]{2,1,0:T(8,128)(2,1)} %multiply_convert_fusion), calls=%async_computation.2 | async-start | bytes 393216 | tf_op jit(solution)/shard_map/all_to_all | solution.py:327
  187.7 8.0 %collective-permute-start.36 = (bf16[256,192]{1,0:T(8,128)(2,1)S(1)}, bf16[256,192]{1,0:T(8,128)(2,1)S(1)}, u32[]{:S(2)}, u32[]{:S(2)}) collective-permute-start(bf16[256,192]{1,0:T(8,128)(2,1)S(1)} %broadcast_select_fusion), channel_id=1, source_target_pairs={{0,1},{1,0},{2,3},{3,2},{4,5},{5,4},{6,7},{7,6},{8,9},{9,8},{10,11... | collective-permute-start | bytes 294920 | tf_op jit(solution)/shard_map/ppermute | solution.py:21
  (12 other events, 31.2 us)

commit v3 on v2

--- a/solution.py
+++ b/solution.py
@@ -11,6 +11,7 @@
 F32 = jnp.float32
 BF16 = jnp.bfloat16
 VMEM_LIMIT = 16 * 1024 * 1024
+ALL_VMEM = 60 * 1024 * 1024
 
 SHIFT_X = [[(4 * x + y, 4 * ((x + d) % 4) + y) for x in range(4) for y in range(4)] for d in range(4)]
 SHIFT_Y = [[(4 * x + y, 4 * x + (y + d) % 4) for x in range(4) for y in range(4)] for d in range(4)]
@@ -25,9 +26,17 @@
     return ((pos[0] + dx) & 3) * 4 + ((pos[1] + dy) & 3)
 
 
-def outproj_kernel(pos, g0, g1, g2, g3, w, out):
+def outproj_kernel(pos, g0, g1, g2, g3, w_own, w_other, out, w):
+    core = pos[2]
+    w[pl.ds(pl.multiple_of(core * 192, 64), 192), :] = w_own[...]
+    w[pl.ds(pl.multiple_of((1 - core) * 192, 64), 192), :] = w_other[...]
     for dy, ref in enumerate((g0, g1, g2, g3)):
-        sums = jnp.dot(ref[...].reshape(128, 768), w[...], preferred_element_type=F32).astype(BF16)
+        sums = lax.dot_general(
+            ref[...].reshape(128, 768),
+            w[...],
+            (((1,), (1,)), ((), ())),
+            preferred_element_type=F32,
+        ).astype(BF16)
         for dx in range(4):
             chip = chip_at(pos, -dx, -dy)
             row = pl.multiple_of((chip & 1) * 32, 32)
@@ -76,9 +85,7 @@
             to = pl.ds(pl.multiple_of(h * 128 + (n % 4) * 32, 32), 32)
             for k in range(4):
                 columns = pl.ds(pl.multiple_of(at_half(pos, h, i, k) * 384, 128), 384)
-                mine = own[to, columns].astype(F32)
-                total = mine + other[rows, columns].astype(F32)
-                outs[k][i, rows, :] = total.astype(BF16)
+                outs[k][i, rows, :] = own[to, columns] + other[rows, columns]
             return 0
 
         lax.fori_loop(0, 16, work, 0)
@@ -112,58 +119,97 @@
     )(*args)
 
 
-def attend_kernel(q, k_new, v_new, k, v, lengths, out, q_heads, o_heads):
+def attend_kernel(lengths, q_in, k_in, v_in, keys, values, out, *scratch):
+    q, k_new, v_new, k, v, q_heads, o_heads, sems, block_sems = scratch
     inv_root = HEAD_DIM ** (-0.5)
-    for h in range(8):
-        to = pl.ds(h, 16, stride=8)
-        if h < 6:
-            q_heads[to, :] = q[:, h * 128 : h * 128 + 128].astype(F32)
-        else:
-            q_heads[to, :] = jnp.zeros((16, 128), F32)
-    queries = q_heads[...]
-    own_products = queries.reshape(16, 8, 128) * k_new[...].astype(F32)[:, None, :]
-    own_scores = jnp.sum(own_products, axis=2, keepdims=True) * inv_root
-    narrow = queries.astype(BF16)
-    scores = [
-        lax.dot_general(
-            narrow[r * 8 : r * 8 + 8],
-            k[r],
-            (((1,), (1,)), ((), ())),
-            preferred_element_type=F32,
+    small = [
+        pltpu.make_async_copy(ref, to, sems.at[n])
+        for n, (ref, to) in enumerate(((q_in, q), (k_in, k_new), (v_in, v_new)))
+    ]
+
+    def block_copies(b):
+        rows = pl.ds(pl.multiple_of(b * 16, 16), 16)
+        return (
+            pltpu.make_async_copy(keys.at[rows], k.at[rows], block_sems.at[b, 0]),
+            pltpu.make_async_copy(values.at[rows], v.at[rows], block_sems.at[b, 1]),
         )
-        for r in range(16)
-    ]
-    scores = jnp.concatenate(scores, axis=0).reshape(16, 8, 192) * inv_root
-    live = lax.broadcasted_iota(jnp.int32, (16, 8, 192), 2) < lengths[...].reshape(16, 1, 1)
-    scores = jnp.where(live, scores, -1e30)
-    peak = jnp.maximum(jnp.max(scores, axis=2, keepdims=True), own_scores)
-    weights = jnp.exp(scores - peak)
-    own_weights = jnp.exp(own_scores - peak)
-    scale = 1.0 / (jnp.sum(weights, axis=2, keepdims=True) + own_weights)
-    weights = (weights * scale).astype(BF16).reshape(128, 192)
-    own_weights = (own_weights * scale).astype(BF16).astype(F32)
-    own_part = own_weights * v_new[...].astype(F32)[:, None, :]
-    for r in range(16):
-        mixed = jnp.dot(weights[r * 8 : r * 8 + 8], v[r], preferred_element_type=F32)
-        o_heads[r * 8 : r * 8 + 8, :] = mixed + own_part[r]
-    for h in range(6):
-        out[:, h * 128 : h * 128 + 128] = o_heads[pl.ds(h, 16, stride=8), :].astype(BF16)
+
+    for copy in small:
+        copy.start()
+    for b in range(2):
+        for copy in block_copies(b):
+            copy.start()
+    for copy in small:
+        copy.wait()
+
+    def block(b, _):
+        rows = pl.ds(pl.multiple_of(b * 16, 16), 16)
+        for h in range(8):
+            to = pl.ds(h, 16, stride=8)
+            if h < 6:
+                q_heads[to, :] = q[rows, h * 128 : h * 128 + 128].astype(F32)
+            else:
+                q_heads[to, :] = jnp.zeros((16, 128), F32)
+        queries = q_heads[...]
+        own_products = queries.reshape(16, 8, 128) * k_new[rows, :].astype(F32)[:, None, :]
+        own_scores = jnp.sum(own_products, axis=2, keepdims=True) * inv_root
+        narrow = queries.astype(BF16)
+        position = lax.broadcasted_iota(jnp.int32, (8, 192), 1)
+        key_copy, value_copy = block_copies(b)
+        key_copy.wait()
+        scores = []
+        for r in range(16):
+            products = lax.dot_general(
+                narrow[r * 8 : r * 8 + 8],
+                k[b * 16 + r],
+                (((1,), (1,)), ((), ())),
+                preferred_element_type=F32,
+            )
+            live = position < lengths[b * 16 + r]
+            scores.append(jnp.where(live, products * inv_root, -1e30))
+        scores = jnp.concatenate(scores, axis=0).reshape(16, 8, 192)
+        peak = jnp.maximum(jnp.max(scores, axis=2, keepdims=True), own_scores)
+        weights = jnp.exp(scores - peak)
+        own_weights = jnp.exp(own_scores - peak)
+        scale = 1.0 / (jnp.sum(weights, axis=2, keepdims=True) + own_weights)
+        weights = (weights * scale).astype(BF16).reshape(128, 192)
+        own_weights = (own_weights * scale).astype(BF16).astype(F32)
+        own_part = own_weights * v_new[rows, :].astype(F32)[:, None, :]
+        value_copy.wait()
+        for r in range(16):
+            mixed = jnp.dot(
+                weights[r * 8 : r * 8 + 8], v[b * 16 + r], preferred_element_type=F32
+            )
+            o_heads[r * 8 : r * 8 + 8, :] = mixed + own_part[r]
+        for h in range(6):
+            heads = o_heads[pl.ds(h, 16, stride=8), :]
+            out[rows, h * 128 : h * 128 + 128] = heads.astype(BF16)
+        return 0
+
+    lax.fori_loop(0, 2, block, 0)
 
 
 def attend(q_new, k_new, v_new, k_cache, v_cache, lengths):
-    def rows(*rest):
-        return pl.BlockSpec((16, *rest), lambda i: (i,) + (0,) * len(rest))
-
+    hbm = pl.BlockSpec(memory_space=pltpu.HBM)
     return pl.pallas_call(
         attend_kernel,
-        grid=(2,),
-        in_specs=[rows(768), rows(128), rows(128), rows(192, 128), rows(192, 128), rows(1)],
-        out_specs=rows(768),
+        in_specs=[pl.BlockSpec(memory_space=pltpu.SMEM)] + [hbm] * 5,
+        out_specs=pl.BlockSpec(memory_space=pltpu.VMEM),
         out_shape=jax.ShapeDtypeStruct((32, 768), BF16),
-        scratch_shapes=[pltpu.VMEM((128, 128), F32)] * 2,
-        compiler_params=pltpu.CompilerParams(vmem_limit_bytes=VMEM_LIMIT),
+        scratch_shapes=[
+            pltpu.VMEM((32, 768), BF16),
+            pltpu.VMEM((32, 128), BF16),
+            pltpu.VMEM((32, 128), BF16),
+            pltpu.VMEM((32, 192, 128), BF16),
+            pltpu.VMEM((32, 192, 128), BF16),
+            pltpu.VMEM((128, 128), F32),
+            pltpu.VMEM((128, 128), F32),
+            pltpu.SemaphoreType.DMA((3,)),
+            pltpu.SemaphoreType.DMA((2, 2)),
+        ],
+        compiler_params=pltpu.CompilerParams(vmem_limit_bytes=ALL_VMEM),
         name="attend",
-    )(q_new, k_new, v_new, k_cache, v_cache, lengths.reshape(32, 1))
+    )(lengths, q_new, k_new, v_new, k_cache, v_cache)
 
 
 def ranks_of(member):
@@ -232,19 +278,20 @@
     signs = (labels == plane).astype(F32) - (labels == partner).astype(F32)
 
     rows_x = [lax.ppermute(attention, "dp", SHIFT_X[d]) for d in (1, 2, 3)]
-    columns, rows_x[2] = lax.optimization_barrier((attn_out_weight, rows_x[2]))
-    out_w = by_core(columns, swap_cores(columns), 1)
+    out_w = attn_out_weight.T
+    out_w_other = swap_cores(out_w)
     rows_x = jnp.stack([attention] + rows_x)
     rows_xy = [rows_x] + [lax.ppermute(rows_x, "dp", SHIFT_Y[d]) for d in (1, 2, 3)]
     vmem = pl.BlockSpec(memory_space=pltpu.VMEM)
     head_sums = pl.pallas_call(
         outproj_kernel,
-        in_specs=[pl.BlockSpec(memory_space=pltpu.SMEM)] + [vmem] * 5,
+        in_specs=[pl.BlockSpec(memory_space=pltpu.SMEM)] + [vmem] * 6,
         out_specs=vmem,
         out_shape=jax.ShapeDtypeStruct((8, 64, 384), BF16),
+        scratch_shapes=[pltpu.VMEM((384, 768), BF16)],
         compiler_params=pltpu.CompilerParams(vmem_limit_bytes=VMEM_LIMIT),
         name="out_projection",
-    )(pos, *rows_xy, out_w)
+    )(pos, *rows_xy, out_w, out_w_other)
     heads_in = lax.all_to_all(head_sums, "tensor", split_axis=0, concat_axis=0, tiled=True)
     hidden = (
         jnp.sum(heads_in.astype(F32), axis=0) + residual_half.reshape(64, 384).astype(F32)
@@ -293,8 +340,8 @@
     logits = jnp.dot(normed, router_weight, preferred_element_type=F32)
     shares = jax.nn.sigmoid(jnp.sum(logits * signs, axis=1, keepdims=True))
     inner = expert_in(normed)
-    inner, normed_other = lax.optimization_barrier((inner, normed_other))
     own = expert_out_of(inner)
+    own, normed_other = lax.optimization_barrier((own, normed_other))
     inner_other = expert_in(normed_other)
     other = [swap_cores(expert_out_of(inner_other[r : r + 128])) for r in (0, 128)]
 

time: 197 us -> 200 us (1.015)
  matrix products: 13.7 us -> 26.6 us
  starting transfers between devices: 71.8 us -> 64.7 us
  Pallas kernels: 16.2 us -> 22.1 us
  waiting for transfers between devices: 62.5 us -> 57.8 us
  local copies, waits for them, and re-layouts: 11.3 us -> 7.77 us
    dot_general x3, matrix products: 4.57 us -> 11.6 us  [expert_out_of(): return jnp.dot(rows, down_w, preferred_element_type=F32).astype(BF16)]
    all_to_all x1, waiting for transfers between devices: 12.1 us -> 6.34 us  [shards(): lax.all_to_all(head_sums, 'tensor', split_axis=0, concat_axis=0, tiled=True)]
    dot_general x2, matrix products: 1.97 us -> 5.82 us  [expert_in(): up = jnp.dot(rows, up_w, preferred_element_type=F32)]
    pallas_call x1, Pallas kernels: 1.65 us -> 5.35 us  [attend(): pl.pallas_call(attend_kernel, in_specs=[pl.BlockSpec(memory_space=pltpu.S...]
    ppermute x6, waiting for transfers between devices: 3.84 us -> 7.27 us  [shards(): got = [lax.ppermute(sums[d], 'dp', near[d]) for d in (1, 3, 2)]]
    ppermute x6, starting transfers between devices: 10.7 us -> 8.38 us  [shards(): got = [lax.ppermute(rows[d], 'dp', far[d]) for d in (1, 3, 2)]]
    ppermute x3, waiting for transfers between devices: 4.64 us -> 2.54 us  [shards(): rows_x = [lax.ppermute(attention, 'dp', SHIFT_X[d]) for d in (1, 2, 3)]]
    dot_general x2 -> x1, matrix products: 1.94 us -> 3.96 us  [expert_in(): gate = jnp.dot(rows, gate_w, preferred_element_type=F32)]
  transfers between devices with their start and end apart: 39 -> 39, of which waited for: 22 -> 20; matrix products, arithmetic and copies ran while one was open for 8% -> 12% of each run, Pallas kernels for 5% -> 5%
where the time goes in v3:
time: 200 us; the launch traced here: 199 us
  starting transfers between devices  64.7 us (32%)
  waiting for transfers between devices  57.8 us (29%)
  matrix products  26.6 us (13%)
  Pallas kernels  22.1 us (11%)
  blocking collectives  13.4 us (7%)
  local copies, waits for them, and re-layouts  7.77 us (4%)
  other arithmetic  6.69 us (3%)
    ppermute x7, starting transfers between devices, swap_cores(): return lax.ppermute(a, 'side', SWAP)  17.7 us
    pallas_call x5, Pallas kernels, local_call(): pl.pallas_call(kernel, in_specs=first + [vmem] * (len(args) - len(first))...  14 us
    all_to_all x1, blocking collectives, shards(): lax.all_to_all(routed.reshape(8, 32, 384), 'tensor', split_axis=0, concat...  13.4 us
    dot_general x3, matrix products, expert_out_of(): return jnp.dot(rows, down_w, preferred_element_type=F32).astype(BF16)  11.6 us
    ppermute x3, waiting for transfers between devices, shards(): lax.ppermute(rows_x, 'dp', SHIFT_Y[d])  10.6 us
    ppermute x6, starting transfers between devices, shards(): got = [lax.ppermute(rows[d], 'dp', far[d]) for d in (1, 3, 2)]  8.38 us
    ppermute x6, starting transfers between devices, shards(): got = [lax.ppermute(sums[d], 'dp', near[d]) for d in (1, 3, 2)]  8.37 us
    all_to_all x1, starting transfers between devices, shards(): lax.all_to_all(head_sums, 'tensor', split_axis=0, concat_axis=0, tiled=True)  8.18 us
  transfers between devices with their start and end apart: 39, of which 20 were waited for; matrix products, arithmetic and copies ran while one was open for 12% of the time, Pallas kernels for 5%

profile of v3, /device:TPU:1, one launch (start us, length us, event | category | flops | bytes accessed | tf_op | source)
XLA Modules:
  0.0 199.4 jit_solution(3600677472510935670)
XLA Ops:
  0.0 5.3 %attend.1 = bf16[32,768]{1,0:T(8,128)(2,1)} custom-call(s32[32]{0:T(128)} %lengths.1, bf16[32,768]{1,0:T(8,128)(2,1)} %q_in.1, bf16[32,128]{1,0:T(8,128)(2,1)} %k_in.1, bf16[32,128]{1,0:T(8,128)(2,1)} %v_in.1, bf16[32,192,128]{2,1,0:T(8,128)(2,1)} %keys.1, bf16[32,192,128]{2,1,0:T(8,128)(2,1)} %values.1), custom_call_target="tpu_custom_call" | custom-call | tf_op jit(solution)/shard_map/attend/pallas_call | solution.py:194
  5.4 3.4 %collective-permute-start.2 = (bf16[32,768]{1,0:T(8,128)(2,1)}, bf16[32,768]{1,0:T(8,128)(2,1)S(1)}, u32[]{:S(2)}, u32[]{:S(2)}) collective-permute-start(bf16[32,768]{1,0:T(8,128)(2,1)} %attend.1), channel_id=1, source_target_pairs={{0,192},{16,208},{32,224},{48,240},{64,0},{80,16},{96,32},{112,48}... | collective-permute-start | bytes 147464 | tf_op jit(solution)/shard_map/ppermute | solution.py:280
  9.9 1.5 collective-permute-start.6
  11.4 2.0 %collective-permute-done.1 = bf16[32,768]{1,0:T(8,128)(2,1)S(1)} collective-permute-done((bf16[32,768]{1,0:T(8,128)(2,1)}, bf16[32,768]{1,0:T(8,128)(2,1)S(1)}, u32[]{:S(2)}, u32[]{:S(2)}) %collective-permute-start.1) | collective-permute-done | bytes 49184 | tf_op jit(solution)/shard_map/ppermute | solution.py:280
  14.8 2.8 %collective-permute-start.5 = (bf16[4,32,768]{2,1,0:T(8,128)(2,1)S(1)}, bf16[4,32,768]{2,1,0:T(8,128)(2,1)S(1)}, u32[]{:S(2)}, u32[]{:S(2)}) collective-permute-start(bf16[4,32,768]{2,1,0:T(8,128)(2,1)S(1)} %pad_maximum_fusion.3.g0), channel_id=1, source_target_pairs={{0,48},{16,0},{32,16},{48,32},{64,112},{80,64},{96,80},{112,96},{1... | collective-permute-start | bytes 589832 | tf_op jit(solution)/shard_map/ppermute | solution.py:284
  18.7 3.6 %collective-permute-done.5.g3 = bf16[4,32,768]{2,1,0:T(8,128)(2,1)S(1)} collective-permute-done((bf16[4,32,768]{2,1,0:T(8,128)(2,1)S(1)}, bf16[4,32,768]{2,1,0:T(8,128)(2,1)S(1)}, u32[]{:S(2)}, u32[]{:S(2)}) %collective-permute-start.5) | collective-permute-done | bytes 196640 | tf_op jit(solution)/shard_map/ppermute | solution.py:284
  22.3 1.5 collective-permute-done.4.g2
  23.8 5.5 %collective-permute-done.3.g1 = bf16[4,32,768]{2,1,0:T(8,128)(2,1)} collective-permute-done((bf16[4,32,768]{2,1,0:T(8,128)(2,1)S(1)}, bf16[4,32,768]{2,1,0:T(8,128)(2,1)}, u32[]{:S(2)}, u32[]{:S(2)}) %collective-permute-start.3) | collective-permute-done | bytes 196640 | tf_op jit(solution)/shard_map/ppermute | solution.py:284
  29.3 2.8 %out_projection.1 = bf16[8,64,384]{2,1,0:T(8,128)(2,1)} custom-call(s32[3]{0:T(128)S(1)} %pad_add_fusion.pos, bf16[4,32,768]{2,1,0:T(8,128)(2,1)S(1)} %pad_maximum_fusion.3.g0, bf16[4,32,768]{2,1,0:T(8,128)(2,1)} %collective-permute-done.3.g1, bf16[4,32,768]{2,1,0:T(8,128)(2,1)} %collective-permute-done.4.g2, ...), custom_call_target="tpu_custom_call" | custom-call | tf_op jit(solution)/shard_map/out_projection/pallas_call | solution.py:286
  32.1 8.2 %all-to-all-start = ((bf16[8,64,384]{2,1,0:T(8,128)(2,1)}), bf16[8,64,384]{2,1,0:T(8,128)(2,1)S(1)}, u32[]{:S(2)}, u32[]{:S(2)}) async-start(bf16[8,64,384]{2,1,0:T(8,128)(2,1)} %out_projection.1), calls=%async_computation | async-start | bytes 786432 | tf_op jit(solution)/shard_map/all_to_all | solution.py:295
  40.3 1.5 copy.23
  41.8 1.7 collective-permute-start.7
  46.4 6.3 %all-to-all-done = bf16[8,64,384]{2,1,0:T(8,128)(2,1)S(1)} async-done(((bf16[8,64,384]{2,1,0:T(8,128)(2,1)}), bf16[8,64,384]{2,1,0:T(8,128)(2,1)S(1)}, u32[]{:S(2)}, u32[]{:S(2)}) %all-to-all-start) | async-done | bytes 393248 | tf_op jit(solution)/shard_map/all_to_all | solution.py:295
  53.7 3.3 %collective-permute-start.8 = (bf16[64,384]{1,0:T(8,128)(2,1)S(1)}, bf16[64,384]{1,0:T(8,128)(2,1)S(1)}, u32[]{:S(2)}, u32[]{:S(2)}) collective-permute-start(bf16[64,384]{1,0:T(8,128)(2,1)S(1)} %fusion.27), channel_id=1, source_target_pairs={{0,1},{1,0},{2,3},{3,2},{4,5},{5,4},{6,7},{7,6},{8,9},{9,8},{10,11... | collective-permute-start | bytes 147464 | tf_op jit(solution)/shard_map/ppermute | solution.py:22
  58.3 13.4 %all_to_all.15 = bf16[8,32,384]{2,1,0:T(8,128)(2,1)S(1)} all-to-all(bf16[8,32,384]{2,1,0:T(8,128)(2,1)S(1)} %bitcast.87), channel_id=1, replica_groups=mesh['dp'=16,'tensor'=8,'side'=2] {'tensor'}, dimensions={0} | all-to-all | bytes 393216 | tf_op jit(solution)/shard_map/all_to_all | solution.py:304
  74.0 1.8 collective-permute-done.11
  75.7 2.0 %collective-permute-done.10 = bf16[128,384]{1,0:T(8,128)(2,1)S(1)} collective-permute-done((bf16[128,384]{1,0:T(8,128)(2,1)S(1)}, bf16[128,384]{1,0:T(8,128)(2,1)S(1)}, u32[]{:S(2)}, u32[]{:S(2)}) %collective-permute-start.10) | collective-permute-done | bytes 98336 | tf_op jit(solution)/shard_map/ppermute | solution.py:310
  77.8 3.1 %collective-permute-done.9 = bf16[128,384]{1,0:T(8,128)(2,1)S(1)} collective-permute-done((bf16[128,384]{1,0:T(8,128)(2,1)S(1)}, bf16[128,384]{1,0:T(8,128)(2,1)S(1)}, u32[]{:S(2)}, u32[]{:S(2)}) %collective-permute-start.9) | collective-permute-done | bytes 98336 | tf_op jit(solution)/shard_map/ppermute | solution.py:310
  82.7 2.1 %collective-permute-start.20 = (bf16[4,128,384]{2,1,0:T(8,128)(2,1)S(1)}, bf16[4,128,384]{2,1,0:T(8,128)(2,1)S(1)}, u32[]{:S(2)}, u32[]{:S(2)}) collective-permute-start(bf16[4,128,384]{2,1,0:T(8,128)(2,1)S(1)} %pad_maximum_fusion.1.b0), channel_id=1, source_target_pairs={{0,192},{16,208},{32,224},{48,240},{64,0},{80,16},{96,32},{112,48}... | collective-permute-start | bytes 1179656 | tf_op jit(solution)/shard_map/ppermute | solution.py:316
  84.7 2.6 %collective-permute-start.18 = (bf16[4,128,384]{2,1,0:T(8,128)(2,1)S(1)}, bf16[4,128,384]{2,1,0:T(8,128)(2,1)S(1)}, u32[]{:S(2)}, u32[]{:S(2)}) collective-permute-start(bf16[4,128,384]{2,1,0:T(8,128)(2,1)S(1)} %pad_maximum_fusion.a0), channel_id=1, source_target_pairs={{0,48},{16,0},{32,16},{48,32},{64,112},{80,64},{96,80},{112,96},{1... | collective-permute-start | bytes 1179656 | tf_op jit(solution)/shard_map/ppermute | solution.py:315
  87.3 4.3 %collective-permute-done.16.b1 = bf16[4,128,384]{2,1,0:T(8,128)(2,1)S(1)} collective-permute-done((bf16[4,128,384]{2,1,0:T(8,128)(2,1)S(1)}, bf16[4,128,384]{2,1,0:T(8,128)(2,1)S(1)}, u32[]{:S(2)}, u32[]{:S(2)}) %collective-permute-start.16) | collective-permute-done | bytes 393248 | tf_op jit(solution)/shard_map/ppermute | solution.py:316
  92.3 1.9 collective-permute-start.19
  94.2 7.1 %collective-permute-done.17.a2 = bf16[4,128,384]{2,1,0:T(8,128)(2,1)S(1)} collective-permute-done((bf16[4,128,384]{2,1,0:T(8,128)(2,1)S(1)}, bf16[4,128,384]{2,1,0:T(8,128)(2,1)S(1)}, u32[]{:S(2)}, u32[]{:S(2)}) %collective-permute-start.17) | collective-permute-done | bytes 393248 | tf_op jit(solution)/shard_map/ppermute | solution.py:319
  102.1 4.8 %norm.1 = bf16[256,6144]{1,0:T(8,128)(2,1)} custom-call(s32[3]{0:T(128)S(1)} %pad_add_fusion.pos, bf16[4,128,384]{2,1,0:T(8,128)(2,1)S(1)} %pad_maximum_fusion.a0, bf16[4,128,384]{2,1,0:T(8,128)(2,1)S(1)} %collective-permute-done.15.a1, bf16[4,128,384]{2,1,0:T(8,128)(2,1)S(1)} %collective-permute-done.17.a2, ...), custom_call_target="tpu_custom_call" | custom-call | tf_op jit(solution)/shard_map/norm/pallas_call | solution.py:112
  106.9 4.0 %collective-permute-start.21 = (bf16[256,6144]{1,0:T(8,128)(2,1)}, bf16[256,6144]{1,0:T(8,128)(2,1)}, u32[]{:S(2)}, u32[]{:S(2)}) collective-permute-start(bf16[256,6144]{1,0:T(8,128)(2,1)} %norm.1), channel_id=1, source_target_pairs={{0,1},{1,0},{2,3},{3,2},{4,5},{5,4},{6,7},{7,6},{8,9},{9,8},{10,11... | collective-permute-start | bytes 9437192 | tf_op jit(solution)/shard_map/ppermute | solution.py:22
  110.9 2.9 %fusion.5 = f32[256,256]{1,0:T(8,128)S(1)} fusion(bf16[256,6144]{1,0:T(8,128)(2,1)} %norm.1, bf16[1,6144,256]{2,1,0:T(8,128)(2,1)S(1)} %copy-done.12), kind=kOutput, calls=%fused_computation.8 | convolution fusion | flops 805306368 | bytes 6553600 | tf_op jit(solution)/shard_map/dot_general | solution.py:334
  113.8 8.0 %convolution_convert_fusion.own = bf16[256,6144]{1,0:T(8,128)(2,1)} fusion(bf16[1,256,6144]{2,1,0:T(8,128)(2,1)S(1)} %copy-done, f32[256,256]{1,0:T(8,128)S(1)} %fusion.5, bf16[256,6144]{1,0:T(8,128)(2,1)} %norm.1, bf16[1,6144,256]{2,1,0:T(8,128)(2,1)} %param.25), kind=kOutput, calls=%fused_computation | convolution fusion | flops 1612578816 | bytes 12845056 | tf_op jit(solution)/shard_map/dot_general | solution.py:338
  121.8 4.0 %fusion.7 = f32[256,256]{1,0:T(8,128)S(1)} fusion(bf16[256,6144]{1,0:T(8,128)(2,1)} %collective-permute-done.21, bf16[1,6144,256]{2,1,0:T(8,128)(2,1)} %param.25), kind=kOutput, calls=%fused_computation.10 | convolution fusion | flops 805306368 | bytes 6553600 | tf_op jit(solution)/shard_map/dot_general | solution.py:333
  125.8 2.9 %multiply_convert_fusion.1 = bf16[256,256]{1,0:T(8,128)(2,1)S(1)} fusion(f32[256,256]{1,0:T(8,128)S(1)} %fusion.7, bf16[256,6144]{1,0:T(8,128)(2,1)} %collective-permute-done.21, bf16[1,6144,256]{2,1,0:T(8,128)(2,1)S(1)} %copy-done.13), kind=kOutput, calls=%fused_computation.32 | convolution fusion | flops 805699584 | bytes 6684672 | tf_op jit(solution)/shard_map/dot_general | solution.py:334
  128.7 1.8 convolution_convert_fusion.2
  130.6 1.8 convolution_convert_fusion.1
  132.9 1.4 collective-permute-done.22.other
  134.3 1.9 copy-done.1
  136.2 2.9 %combine_cores.2 = (bf16[4,128,384]{2,1,0:T(8,128)(2,1)S(1)}, bf16[4,128,384]{2,1,0:T(8,128)(2,1)}, bf16[4,128,384]{2,1,0:T(8,128)(2,1)}, bf16[4,128,384]{2,1,0:T(8,128)(2,1)}) custom-call(s32[3]{0:T(128)S(1)} %pad_add_fusion.pos, bf16[256,6144]{1,0:T(8,128)(2,1)S(1)} %copy-done.1, bf16[128,6144]{1,0:T(8,128)(2,1)} %collective-permute-done.22.other), custom_call_target="tpu_custom_call" | custom-call | tf_op jit(solution)/shard_map/combine_cores/pallas_call | solution.py:112
  140.3 2.1 %collective-permute-start.24 = (bf16[4,128,384]{2,1,0:T(8,128)(2,1)}, bf16[4,128,384]{2,1,0:T(8,128)(2,1)}, u32[]{:S(2)}, u32[]{:S(2)}) collective-permute-start(bf16[4,128,384]{2,1,0:T(8,128)(2,1)} %get-tuple-element.47), channel_id=1, source_target_pairs={{0,48},{16,0},{32,16},{48,32},{64,112},{80,64},{96,80},{112,96},{1... | collective-permute-start | bytes 1179656 | tf_op jit(solution)/shard_map/ppermute | solution.py:360
  143.7 2.7 %combine_cores.3 = (bf16[4,128,384]{2,1,0:T(8,128)(2,1)S(1)}, bf16[4,128,384]{2,1,0:T(8,128)(2,1)}, bf16[4,128,384]{2,1,0:T(8,128)(2,1)S(1)}, bf16[4,128,384]{2,1,0:T(8,128)(2,1)S(1)}) custom-call(s32[3]{0:T(128)S(1)} %pad_add_fusion.pos, bf16[256,6144]{1,0:T(8,128)(2,1)S(1)} %copy-done.1, bf16[128,6144]{1,0:T(8,128)(2,1)} %collective-permute-done.29.other), custom_call_target="tpu_custom_call" | custom-call | tf_op jit(solution)/shard_map/combine_cores/pallas_call | solution.py:112
  149.4 1.6 collective-permute-start.31
  153.1 2.8 %fusion.12 = f32[256]{0:T(256)S(1)} fusion(bf16[256,6144]{1,0:T(8,128)(2,1)} %norm.1, bf16[6144,8]{0,1:T(8,128)(2,1)} %param.23, s32[256]{0:T(256)S(1)} %eq.144, f32[8]{0:T(128)S(1)} %compare_convert_fusion), kind=kOutput, calls=%fused_computation.19 | convolution fusion | flops 25175808 | bytes 3246112 | tf_op jit(solution)/shard_map/dot_general | solution.py:340
  156.0 5.4 %collective-permute-done.25.got3 = bf16[4,128,384]{2,1,0:T(8,128)(2,1)} collective-permute-done((bf16[4,128,384]{2,1,0:T(8,128)(2,1)}, bf16[4,128,384]{2,1,0:T(8,128)(2,1)}, u32[]{:S(2)}, u32[]{:S(2)}) %collective-permute-start.25) | collective-permute-done | bytes 393248 | tf_op jit(solution)/shard_map/ppermute | solution.py:360
  161.3 2.1 %sum_rows.2 = (f32[128,384]{1,0:T(8,128)S(1)}, bf16[128,384]{1,0:T(8,128)(2,1)}, bf16[128,384]{1,0:T(8,128)(2,1)}, bf16[128,384]{1,0:T(8,128)(2,1)}) custom-call(bf16[4,128,384]{2,1,0:T(8,128)(2,1)S(1)} %copy-done.3, bf16[4,128,384]{2,1,0:T(8,128)(2,1)} %collective-permute-done.23.got1, bf16[4,128,384]{2,1,0:T(8,128)(2,1)} %collective-permute-done.24.got2, ...), custom_call_target="tpu_custom_call" | custom-call | tf_op jit(solution)/shard_map/sum_rows/pallas_call | solution.py:112
  164.2 2.6 %collective-permute-start.27 = (bf16[128,384]{1,0:T(8,128)(2,1)}, bf16[128,384]{1,0:T(8,128)(2,1)}, u32[]{:S(2)}, u32[]{:S(2)}) collective-permute-start(bf16[128,384]{1,0:T(8,128)(2,1)} %get-tuple-element.51), channel_id=1, source_target_pairs={{0,192},{16,208},{32,224},{48,240},{64,0},{80,16},{96,32},{112,48}... | collective-permute-start | bytes 294920 | tf_op jit(solution)/shard_map/ppermute | solution.py:369
  167.8 1.4 sum_rows.3
  169.3 1.4 collective-permute-start.33
  170.7 1.4 collective-permute-start.34
  172.1 3.0 %collective-permute-start.35 = (bf16[128,384]{1,0:T(8,128)(2,1)S(1)}, bf16[128,384]{1,0:T(8,128)(2,1)S(1)}, u32[]{:S(2)}, u32[]{:S(2)}) collective-permute-start(bf16[128,384]{1,0:T(8,128)(2,1)S(1)} %get-tuple-element.60), channel_id=1, source_target_pairs={{0,32},{16,48},{32,0},{48,16},{64,96},{80,112},{96,64},{112,80},{1... | collective-permute-start | bytes 294920 | tf_op jit(solution)/shard_map/ppermute | solution.py:369
  177.9 4.0 %all-to-all-start.2 = ((bf16[8,32,384]{2,1,0:T(8,128)(2,1)}), bf16[8,32,384]{2,1,0:T(8,128)(2,1)S(1)}, u32[]{:S(2)}, u32[]{:S(2)}) async-start(bf16[8,32,384]{2,1,0:T(8,128)(2,1)} %multiply_convert_fusion), calls=%async_computation.2 | async-start | bytes 393216 | tf_op jit(solution)/shard_map/all_to_all | solution.py:374
  182.9 7.7 %all-to-all-done.2 = bf16[8,32,384]{2,1,0:T(8,128)(2,1)S(1)} async-done(((bf16[8,32,384]{2,1,0:T(8,128)(2,1)}), bf16[8,32,384]{2,1,0:T(8,128)(2,1)S(1)}, u32[]{:S(2)}, u32[]{:S(2)}) %all-to-all-start.2) | async-done | bytes 196640 | tf_op jit(solution)/shard_map/all_to_all | solution.py:374
  190.7 6.8 %collective-permute-start.36 = (bf16[256,192]{1,0:T(8,128)(2,1)S(1)}, bf16[256,192]{1,0:T(8,128)(2,1)S(1)}, u32[]{:S(2)}, u32[]{:S(2)}) collective-permute-start(bf16[256,192]{1,0:T(8,128)(2,1)S(1)} %broadcast_select_fusion), channel_id=1, source_target_pairs={{0,1},{1,0},{2,3},{3,2},{4,5},{5,4},{6,7},{7,6},{8,9},{9,8},{10,11... | collective-permute-start | bytes 294920 | tf_op jit(solution)/shard_map/ppermute | solution.py:22
  (114 shorter events, 30.0 us)
Async XLA Ops:
  0.0 113.8 %copy-start = (bf16[1,256,6144]{2,1,0:T(8,128)(2,1)S(1)}, bf16[1,256,6144]{2,1,0:T(8,128)(2,1)}, u32[]{:S(2)}) copy-start(bf16[1,256,6144]{2,1,0:T(8,128)(2,1)} %param.27) | copy-start | bytes 9437188
  0.0 43.5 %copy-start.11 = (s32[1024,2]{0,1:T(2,128)S(1)}, s32[1024,2]{0,1:T(2,128)}, u32[]{:S(2)}) copy-start(s32[1024,2]{0,1:T(2,128)} %param.24) | copy-start | bytes 24580
  5.4 6.0 %collective-permute-start.2 = (bf16[32,768]{1,0:T(8,128)(2,1)}, bf16[32,768]{1,0:T(8,128)(2,1)S(1)}, u32[]{:S(2)}, u32[]{:S(2)}) collective-permute-start(bf16[32,768]{1,0:T(8,128)(2,1)} %attend.1), channel_id=1, source_target_pairs={{0,192},{16,208},{32,224},{48,240},{64,0},{80,16},{96,32},{112,48}... | collective-permute-start | bytes 147464 | tf_op jit(solution)/shard_map/ppermute | solution.py:280
  8.7 4.7 %collective-permute-start.1 = (bf16[32,768]{1,0:T(8,128)(2,1)}, bf16[32,768]{1,0:T(8,128)(2,1)S(1)}, u32[]{:S(2)}, u32[]{:S(2)}) collective-permute-start(bf16[32,768]{1,0:T(8,128)(2,1)} %attend.1), channel_id=1, source_target_pairs={{0,128},{16,144},{32,160},{48,176},{64,192},{80,208},{96,224},{112... | collective-permute-start | bytes 147464 | tf_op jit(solution)/shard_map/ppermute | solution.py:280
  9.3 4.7 %collective-permute-start = (bf16[32,768]{1,0:T(8,128)(2,1)}, bf16[32,768]{1,0:T(8,128)(2,1)S(1)}, u32[]{:S(2)}, u32[]{:S(2)}) collective-permute-start(bf16[32,768]{1,0:T(8,128)(2,1)} %attend.1), channel_id=1, source_target_pairs={{0,64},{16,80},{32,96},{48,112},{64,128},{80,144},{96,160},{112,17... | collective-permute-start | bytes 147464 | tf_op jit(solution)/shard_map/ppermute | solution.py:280
  9.9 19.4 %collective-permute-start.6 = (bf16[192,768]{1,0:T(8,128)(2,1)}, bf16[192,768]{1,0:T(8,128)(2,1)}, u32[]{:S(2)}, u32[]{:S(2)}) collective-permute-start(bf16[192,768]{1,0:T(8,128)(2,1)} %bitcast.7.w_own), channel_id=1, source_target_pairs={{0,1},{1,0},{2,3},{3,2},{4,5},{5,4},{6,7},{7,6},{8,9},{9,8},{10,11... | collective-permute-start | bytes 884744 | tf_op jit(solution)/shard_map/ppermute | solution.py:22
  14.8 7.5 %collective-permute-start.5 = (bf16[4,32,768]{2,1,0:T(8,128)(2,1)S(1)}, bf16[4,32,768]{2,1,0:T(8,128)(2,1)S(1)}, u32[]{:S(2)}, u32[]{:S(2)}) collective-permute-start(bf16[4,32,768]{2,1,0:T(8,128)(2,1)S(1)} %pad_maximum_fusion.3.g0), channel_id=1, source_target_pairs={{0,48},{16,0},{32,16},{48,32},{64,112},{80,64},{96,80},{112,96},{1... | collective-permute-start | bytes 589832 | tf_op jit(solution)/shard_map/ppermute | solution.py:284
  17.6 6.2 %collective-permute-start.4 = (bf16[4,32,768]{2,1,0:T(8,128)(2,1)S(1)}, bf16[4,32,768]{2,1,0:T(8,128)(2,1)}, u32[]{:S(2)}, u32[]{:S(2)}) collective-permute-start(bf16[4,32,768]{2,1,0:T(8,128)(2,1)S(1)} %pad_maximum_fusion.3.g0), channel_id=1, source_target_pairs={{0,32},{16,48},{32,0},{48,16},{64,96},{80,112},{96,64},{112,80},{1... | collective-permute-start | bytes 589832 | tf_op jit(solution)/shard_map/ppermute | solution.py:284
  17.9 11.4 %collective-permute-start.3 = (bf16[4,32,768]{2,1,0:T(8,128)(2,1)S(1)}, bf16[4,32,768]{2,1,0:T(8,128)(2,1)}, u32[]{:S(2)}, u32[]{:S(2)}) collective-permute-start(bf16[4,32,768]{2,1,0:T(8,128)(2,1)S(1)} %pad_maximum_fusion.3.g0), channel_id=1, source_target_pairs={{0,16},{16,32},{32,48},{48,0},{64,80},{80,96},{96,112},{112,64},{1... | collective-permute-start | bytes 589832 | tf_op jit(solution)/shard_map/ppermute | solution.py:284
  32.1 20.6 %all-to-all-start = ((bf16[8,64,384]{2,1,0:T(8,128)(2,1)}), bf16[8,64,384]{2,1,0:T(8,128)(2,1)S(1)}, u32[]{:S(2)}, u32[]{:S(2)}) async-start(bf16[8,64,384]{2,1,0:T(8,128)(2,1)} %out_projection.1), calls=%async_computation | async-start | bytes 786432 | tf_op jit(solution)/shard_map/all_to_all | solution.py:295
  41.8 2.9 %collective-permute-start.7 = (bf16[128,192]{1,0:T(8,128)(2,1)}, bf16[128,192]{1,0:T(8,128)(2,1)}, u32[]{:S(2)}, u32[]{:S(2)}) collective-permute-start(bf16[128,192]{1,0:T(8,128)(2,1)} %copy.23), channel_id=1, source_target_pairs={{0,1},{1,0},{2,3},{3,2},{4,5},{5,4},{6,7},{7,6},{8,9},{9,8},{10,11... | collective-permute-start | bytes 147464 | tf_op jit(solution)/shard_map/ppermute | solution.py:22
  53.7 4.4 %collective-permute-start.8 = (bf16[64,384]{1,0:T(8,128)(2,1)S(1)}, bf16[64,384]{1,0:T(8,128)(2,1)S(1)}, u32[]{:S(2)}, u32[]{:S(2)}) collective-permute-start(bf16[64,384]{1,0:T(8,128)(2,1)S(1)} %fusion.27), channel_id=1, source_target_pairs={{0,1},{1,0},{2,3},{3,2},{4,5},{5,4},{6,7},{7,6},{8,9},{9,8},{10,11... | collective-permute-start | bytes 147464 | tf_op jit(solution)/shard_map/ppermute | solution.py:22
  58.1 23.6 %copy-start.8 = (bf16[128,384]{1,0:T(8,128)(2,1)}, bf16[128,384]{1,0:T(8,128)(2,1)S(1)}, u32[]{:S(2)}) copy-start(bf16[128,384]{1,0:T(8,128)(2,1)S(1)} %maximum_select_fusion.1) | copy-start | bytes 294916
  71.7 4.0 %collective-permute-start.11 = (bf16[128,384]{1,0:T(8,128)(2,1)S(1)}, bf16[128,384]{1,0:T(8,128)(2,1)S(1)}, u32[]{:S(2)}, u32[]{:S(2)}) collective-permute-start(bf16[128,384]{1,0:T(8,128)(2,1)S(1)} %bitcast.89), channel_id=1, source_target_pairs={{0,192},{16,208},{32,224},{48,240},{64,0},{80,16},{96,32},{112,48}... | collective-permute-start | bytes 294920 | tf_op jit(solution)/shard_map/ppermute | solution.py:310
  72.7 5.1 %collective-permute-start.10 = (bf16[128,384]{1,0:T(8,128)(2,1)S(1)}, bf16[128,384]{1,0:T(8,128)(2,1)S(1)}, u32[]{:S(2)}, u32[]{:S(2)}) collective-permute-start(bf16[128,384]{1,0:T(8,128)(2,1)S(1)} %bitcast.90), channel_id=1, source_target_pairs={{0,128},{16,144},{32,160},{48,176},{64,192},{80,208},{96,224},{112... | collective-permute-start | bytes 294920 | tf_op jit(solution)/shard_map/ppermute | solution.py:310
  73.2 7.7 %collective-permute-start.9 = (bf16[128,384]{1,0:T(8,128)(2,1)S(1)}, bf16[128,384]{1,0:T(8,128)(2,1)S(1)}, u32[]{:S(2)}, u32[]{:S(2)}) collective-permute-start(bf16[128,384]{1,0:T(8,128)(2,1)S(1)} %bitcast.91), channel_id=1, source_target_pairs={{0,64},{16,80},{32,96},{48,112},{64,128},{80,144},{96,160},{112,17... | collective-permute-start | bytes 294920 | tf_op jit(solution)/shard_map/ppermute | solution.py:310
  73.9 6.9 %collective-permute-start.14 = (bf16[128,384]{1,0:T(8,128)(2,1)S(1)}, bf16[128,384]{1,0:T(8,128)(2,1)S(1)}, u32[]{:S(2)}, u32[]{:S(2)}) collective-permute-start(bf16[128,384]{1,0:T(8,128)(2,1)S(1)} %bitcast.93), channel_id=1, source_target_pairs={{0,48},{16,0},{32,16},{48,32},{64,112},{80,64},{96,80},{112,96},{1... | collective-permute-start | bytes 294920 | tf_op jit(solution)/shard_map/ppermute | solution.py:311
  74.0 6.9 %collective-permute-start.13 = (bf16[128,384]{1,0:T(8,128)(2,1)S(1)}, bf16[128,384]{1,0:T(8,128)(2,1)S(1)}, u32[]{:S(2)}, u32[]{:S(2)}) collective-permute-start(bf16[128,384]{1,0:T(8,128)(2,1)S(1)} %bitcast.94), channel_id=1, source_target_pairs={{0,32},{16,48},{32,0},{48,16},{64,96},{80,112},{96,64},{112,80},{1... | collective-permute-start | bytes 294920 | tf_op jit(solution)/shard_map/ppermute | solution.py:311
  75.7 5.9 %collective-permute-start.12 = (bf16[128,384]{1,0:T(8,128)(2,1)S(1)}, bf16[128,384]{1,0:T(8,128)(2,1)S(1)}, u32[]{:S(2)}, u32[]{:S(2)}) collective-permute-start(bf16[128,384]{1,0:T(8,128)(2,1)S(1)} %bitcast.95), channel_id=1, source_target_pairs={{0,16},{16,32},{32,48},{48,0},{64,80},{80,96},{96,112},{112,64},{1... | collective-permute-start | bytes 294920 | tf_op jit(solution)/shard_map/ppermute | solution.py:311
  81.8 9.8 %collective-permute-start.16 = (bf16[4,128,384]{2,1,0:T(8,128)(2,1)S(1)}, bf16[4,128,384]{2,1,0:T(8,128)(2,1)S(1)}, u32[]{:S(2)}, u32[]{:S(2)}) collective-permute-start(bf16[4,128,384]{2,1,0:T(8,128)(2,1)S(1)} %pad_maximum_fusion.1.b0), channel_id=1, source_target_pairs={{0,64},{16,80},{32,96},{48,112},{64,128},{80,144},{96,160},{112,17... | collective-permute-start | bytes 1179656 | tf_op jit(solution)/shard_map/ppermute | solution.py:316
  82.6 9.7 %collective-permute-start.15 = (bf16[4,128,384]{2,1,0:T(8,128)(2,1)S(1)}, bf16[4,128,384]{2,1,0:T(8,128)(2,1)S(1)}, u32[]{:S(2)}, u32[]{:S(2)}) collective-permute-start(bf16[4,128,384]{2,1,0:T(8,128)(2,1)S(1)} %pad_maximum_fusion.a0), channel_id=1, source_target_pairs={{0,16},{16,32},{32,48},{48,0},{64,80},{80,96},{96,112},{112,64},{1... | collective-permute-start | bytes 1179656 | tf_op jit(solution)/shard_map/ppermute | solution.py:315
  82.7 11.6 %collective-permute-start.20 = (bf16[4,128,384]{2,1,0:T(8,128)(2,1)S(1)}, bf16[4,128,384]{2,1,0:T(8,128)(2,1)S(1)}, u32[]{:S(2)}, u32[]{:S(2)}) collective-permute-start(bf16[4,128,384]{2,1,0:T(8,128)(2,1)S(1)} %pad_maximum_fusion.1.b0), channel_id=1, source_target_pairs={{0,192},{16,208},{32,224},{48,240},{64,0},{80,16},{96,32},{112,48}... | collective-permute-start | bytes 1179656 | tf_op jit(solution)/shard_map/ppermute | solution.py:316
  84.7 9.5 %collective-permute-start.18 = (bf16[4,128,384]{2,1,0:T(8,128)(2,1)S(1)}, bf16[4,128,384]{2,1,0:T(8,128)(2,1)S(1)}, u32[]{:S(2)}, u32[]{:S(2)}) collective-permute-start(bf16[4,128,384]{2,1,0:T(8,128)(2,1)S(1)} %pad_maximum_fusion.a0), channel_id=1, source_target_pairs={{0,48},{16,0},{32,16},{48,32},{64,112},{80,64},{96,80},{112,96},{1... | collective-permute-start | bytes 1179656 | tf_op jit(solution)/shard_map/ppermute | solution.py:315
  92.3 9.0 %collective-permute-start.17 = (bf16[4,128,384]{2,1,0:T(8,128)(2,1)S(1)}, bf16[4,128,384]{2,1,0:T(8,128)(2,1)S(1)}, u32[]{:S(2)}, u32[]{:S(2)}) collective-permute-start(bf16[4,128,384]{2,1,0:T(8,128)(2,1)S(1)} %pad_maximum_fusion.a0), channel_id=1, source_target_pairs={{0,32},{16,48},{32,0},{48,16},{64,96},{80,112},{96,64},{112,80},{1... | collective-permute-start | bytes 1179656 | tf_op jit(solution)/shard_map/ppermute | solution.py:319
  92.3 9.0 %collective-permute-start.19 = (bf16[4,128,384]{2,1,0:T(8,128)(2,1)S(1)}, bf16[4,128,384]{2,1,0:T(8,128)(2,1)S(1)}, u32[]{:S(2)}, u32[]{:S(2)}) collective-permute-start(bf16[4,128,384]{2,1,0:T(8,128)(2,1)S(1)} %pad_maximum_fusion.1.b0), channel_id=1, source_target_pairs={{0,128},{16,144},{32,160},{48,176},{64,192},{80,208},{96,224},{112... | collective-permute-start | bytes 1179656 | tf_op jit(solution)/shard_map/ppermute | solution.py:319
  102.1 8.8 %copy-start.12 = (bf16[1,6144,256]{2,1,0:T(8,128)(2,1)S(1)}, bf16[1,6144,256]{2,1,0:T(8,128)(2,1)}, u32[]{:S(2)}) copy-start(bf16[1,6144,256]{2,1,0:T(8,128)(2,1)} %param.26) | copy-start | bytes 9437188
  106.9 15.0 %collective-permute-start.21 = (bf16[256,6144]{1,0:T(8,128)(2,1)}, bf16[256,6144]{1,0:T(8,128)(2,1)}, u32[]{:S(2)}, u32[]{:S(2)}) collective-permute-start(bf16[256,6144]{1,0:T(8,128)(2,1)} %norm.1), channel_id=1, source_target_pairs={{0,1},{1,0},{2,3},{3,2},{4,5},{5,4},{6,7},{7,6},{8,9},{9,8},{10,11... | collective-permute-start | bytes 9437192 | tf_op jit(solution)/shard_map/ppermute | solution.py:22
  121.8 4.0 %copy-start.13 = (bf16[1,6144,256]{2,1,0:T(8,128)(2,1)S(1)}, bf16[1,6144,256]{2,1,0:T(8,128)(2,1)}, u32[]{:S(2)}) copy-start(bf16[1,6144,256]{2,1,0:T(8,128)(2,1)} %param.26) | copy-start | bytes 9437188
  130.6 3.8 %collective-permute-start.22 = (bf16[128,6144]{1,0:T(8,128)(2,1)}, bf16[128,6144]{1,0:T(8,128)(2,1)}, u32[]{:S(2)}, u32[]{:S(2)}) collective-permute-start(bf16[128,6144]{1,0:T(8,128)(2,1)} %convolution_convert_fusion.2), channel_id=1, source_target_pairs={{0,1},{1,0},{2,3},{3,2},{4,5},{5,4},{6,7},{7,6},{8,9},{9,8},{10,11... | collective-permute-start | bytes 4718600 | tf_op jit(solution)/shard_map/ppermute | solution.py:22
  132.3 11.4 %collective-permute-start.29 = (bf16[128,6144]{1,0:T(8,128)(2,1)}, bf16[128,6144]{1,0:T(8,128)(2,1)}, u32[]{:S(2)}, u32[]{:S(2)}) collective-permute-start(bf16[128,6144]{1,0:T(8,128)(2,1)} %convolution_convert_fusion.1), channel_id=1, source_target_pairs={{0,1},{1,0},{2,3},{3,2},{4,5},{5,4},{6,7},{7,6},{8,9},{9,8},{10,11... | collective-permute-start | bytes 4718600 | tf_op jit(solution)/shard_map/ppermute | solution.py:22
  139.1 7.2 %copy-start.2 = (bf16[4,128,384]{2,1,0:T(8,128)(2,1)}, bf16[4,128,384]{2,1,0:T(8,128)(2,1)S(1)}, u32[]{:S(2)}) copy-start(bf16[4,128,384]{2,1,0:T(8,128)(2,1)S(1)} %get-tuple-element.45.mine) | copy-start | bytes 1179652
  139.1 12.8 %collective-permute-start.23 = (bf16[4,128,384]{2,1,0:T(8,128)(2,1)}, bf16[4,128,384]{2,1,0:T(8,128)(2,1)}, u32[]{:S(2)}, u32[]{:S(2)}) collective-permute-start(bf16[4,128,384]{2,1,0:T(8,128)(2,1)} %get-tuple-element.46), channel_id=1, source_target_pairs={{0,16},{16,32},{32,48},{48,0},{64,80},{80,96},{96,112},{112,64},{1... | collective-permute-start | bytes 1179656 | tf_op jit(solution)/shard_map/ppermute | solution.py:360
  140.3 15.6 %collective-permute-start.24 = (bf16[4,128,384]{2,1,0:T(8,128)(2,1)}, bf16[4,128,384]{2,1,0:T(8,128)(2,1)}, u32[]{:S(2)}, u32[]{:S(2)}) collective-permute-start(bf16[4,128,384]{2,1,0:T(8,128)(2,1)} %get-tuple-element.47), channel_id=1, source_target_pairs={{0,48},{16,0},{32,16},{48,32},{64,112},{80,64},{96,80},{112,96},{1... | collective-permute-start | bytes 1179656 | tf_op jit(solution)/shard_map/ppermute | solution.py:360
  142.5 18.9 %collective-permute-start.25 = (bf16[4,128,384]{2,1,0:T(8,128)(2,1)}, bf16[4,128,384]{2,1,0:T(8,128)(2,1)}, u32[]{:S(2)}, u32[]{:S(2)}) collective-permute-start(bf16[4,128,384]{2,1,0:T(8,128)(2,1)} %get-tuple-element.48), channel_id=1, source_target_pairs={{0,32},{16,48},{32,0},{48,16},{64,96},{80,112},{96,64},{112,80},{1... | collective-permute-start | bytes 1179656 | tf_op jit(solution)/shard_map/ppermute | solution.py:360
  147.9 18.9 %collective-permute-start.30 = (bf16[4,128,384]{2,1,0:T(8,128)(2,1)}, bf16[4,128,384]{2,1,0:T(8,128)(2,1)}, u32[]{:S(2)}, u32[]{:S(2)}) collective-permute-start(bf16[4,128,384]{2,1,0:T(8,128)(2,1)} %get-tuple-element.54), channel_id=1, source_target_pairs={{0,64},{16,80},{32,96},{48,112},{64,128},{80,144},{96,160},{112,17... | collective-permute-start | bytes 1179656 | tf_op jit(solution)/shard_map/ppermute | solution.py:360
  149.4 11.9 %copy-start.3 = (bf16[4,128,384]{2,1,0:T(8,128)(2,1)S(1)}, bf16[4,128,384]{2,1,0:T(8,128)(2,1)}, u32[]{:S(2)}) copy-start(bf16[4,128,384]{2,1,0:T(8,128)(2,1)} %copy-done.2) | copy-start | bytes 1179652
  149.4 17.5 %collective-permute-start.31 = (bf16[4,128,384]{2,1,0:T(8,128)(2,1)}, bf16[4,128,384]{2,1,0:T(8,128)(2,1)}, u32[]{:S(2)}, u32[]{:S(2)}) collective-permute-start(bf16[4,128,384]{2,1,0:T(8,128)(2,1)} %copy-done.7), channel_id=1, source_target_pairs={{0,192},{16,208},{32,224},{48,240},{64,0},{80,16},{96,32},{112,48}... | collective-permute-start | bytes 1179656 | tf_op jit(solution)/shard_map/ppermute | solution.py:360
  152.0 15.9 %collective-permute-start.32 = (bf16[4,128,384]{2,1,0:T(8,128)(2,1)}, bf16[4,128,384]{2,1,0:T(8,128)(2,1)}, u32[]{:S(2)}, u32[]{:S(2)}) collective-permute-start(bf16[4,128,384]{2,1,0:T(8,128)(2,1)} %copy-done.6), channel_id=1, source_target_pairs={{0,128},{16,144},{32,160},{48,176},{64,192},{80,208},{96,224},{112... | collective-permute-start | bytes 1179656 | tf_op jit(solution)/shard_map/ppermute | solution.py:360
  164.1 7.9 %collective-permute-start.26 = (bf16[128,384]{1,0:T(8,128)(2,1)}, bf16[128,384]{1,0:T(8,128)(2,1)}, u32[]{:S(2)}, u32[]{:S(2)}) collective-permute-start(bf16[128,384]{1,0:T(8,128)(2,1)} %get-tuple-element.50), channel_id=1, source_target_pairs={{0,64},{16,80},{32,96},{48,112},{64,128},{80,144},{96,160},{112,17... | collective-permute-start | bytes 294920 | tf_op jit(solution)/shard_map/ppermute | solution.py:369
  164.2 10.8 %collective-permute-start.27 = (bf16[128,384]{1,0:T(8,128)(2,1)}, bf16[128,384]{1,0:T(8,128)(2,1)}, u32[]{:S(2)}, u32[]{:S(2)}) collective-permute-start(bf16[128,384]{1,0:T(8,128)(2,1)} %get-tuple-element.51), channel_id=1, source_target_pairs={{0,192},{16,208},{32,224},{48,240},{64,0},{80,16},{96,32},{112,48}... | collective-permute-start | bytes 294920 | tf_op jit(solution)/shard_map/ppermute | solution.py:369
  166.8 8.2 %collective-permute-start.28 = (bf16[128,384]{1,0:T(8,128)(2,1)}, bf16[128,384]{1,0:T(8,128)(2,1)}, u32[]{:S(2)}, u32[]{:S(2)}) collective-permute-start(bf16[128,384]{1,0:T(8,128)(2,1)} %get-tuple-element.52), channel_id=1, source_target_pairs={{0,128},{16,144},{32,160},{48,176},{64,192},{80,208},{96,224},{112... | collective-permute-start | bytes 294920 | tf_op jit(solution)/shard_map/ppermute | solution.py:369
  169.3 12.7 %copy-start.9 = (bf16[128,384]{1,0:T(8,128)(2,1)S(1)}, bf16[128,384]{1,0:T(8,128)(2,1)}, u32[]{:S(2)}) copy-start(bf16[128,384]{1,0:T(8,128)(2,1)} %copy-done.8) | copy-start | bytes 294916
  169.3 29.3 %copy-start.10 = (pred[256,128]{1,0:T(32,128)(4,1)S(1)}, pred[256,128]{1,0:T(32,128)(4,1)}, u32[]{:S(2)}) copy-start(pred[256,128]{1,0:T(32,128)(4,1)} %get-tuple-element.67) | copy-start | bytes 98308
  169.3 6.8 %collective-permute-start.33 = (bf16[128,384]{1,0:T(8,128)(2,1)S(1)}, bf16[128,384]{1,0:T(8,128)(2,1)S(1)}, u32[]{:S(2)}, u32[]{:S(2)}) collective-permute-start(bf16[128,384]{1,0:T(8,128)(2,1)S(1)} %get-tuple-element.58), channel_id=1, source_target_pairs={{0,16},{16,32},{32,48},{48,0},{64,80},{80,96},{96,112},{112,64},{1... | collective-permute-start | bytes 294920 | tf_op jit(solution)/shard_map/ppermute | solution.py:369
  170.7 5.5 %collective-permute-start.34 = (bf16[128,384]{1,0:T(8,128)(2,1)S(1)}, bf16[128,384]{1,0:T(8,128)(2,1)S(1)}, u32[]{:S(2)}, u32[]{:S(2)}) collective-permute-start(bf16[128,384]{1,0:T(8,128)(2,1)S(1)} %get-tuple-element.59), channel_id=1, source_target_pairs={{0,48},{16,0},{32,16},{48,32},{64,112},{80,64},{96,80},{112,96},{1... | collective-permute-start | bytes 294920 | tf_op jit(solution)/shard_map/ppermute | solution.py:369
  172.1 5.0 %collective-permute-start.35 = (bf16[128,384]{1,0:T(8,128)(2,1)S(1)}, bf16[128,384]{1,0:T(8,128)(2,1)S(1)}, u32[]{:S(2)}, u32[]{:S(2)}) collective-permute-start(bf16[128,384]{1,0:T(8,128)(2,1)S(1)} %get-tuple-element.60), channel_id=1, source_target_pairs={{0,32},{16,48},{32,0},{48,16},{64,96},{80,112},{96,64},{112,80},{1... | collective-permute-start | bytes 294920 | tf_op jit(solution)/shard_map/ppermute | solution.py:369
  177.9 12.6 %all-to-all-start.2 = ((bf16[8,32,384]{2,1,0:T(8,128)(2,1)}), bf16[8,32,384]{2,1,0:T(8,128)(2,1)S(1)}, u32[]{:S(2)}, u32[]{:S(2)}) async-start(bf16[8,32,384]{2,1,0:T(8,128)(2,1)} %multiply_convert_fusion), calls=%async_computation.2 | async-start | bytes 393216 | tf_op jit(solution)/shard_map/all_to_all | solution.py:374
  190.7 7.8 %collective-permute-start.36 = (bf16[256,192]{1,0:T(8,128)(2,1)S(1)}, bf16[256,192]{1,0:T(8,128)(2,1)S(1)}, u32[]{:S(2)}, u32[]{:S(2)}) collective-permute-start(bf16[256,192]{1,0:T(8,128)(2,1)S(1)} %broadcast_select_fusion), channel_id=1, source_target_pairs={{0,1},{1,0},{2,3},{3,2},{4,5},{5,4},{6,7},{7,6},{8,9},{9,8},{10,11... | collective-permute-start | bytes 294920 | tf_op jit(solution)/shard_map/ppermute | solution.py:22
  (5 other events, 4.8 us)

commit v4 on v3

--- a/solution.py
+++ b/solution.py
@@ -340,8 +340,8 @@
     logits = jnp.dot(normed, router_weight, preferred_element_type=F32)
     shares = jax.nn.sigmoid(jnp.sum(logits * signs, axis=1, keepdims=True))
     inner = expert_in(normed)
+    inner, normed_other = lax.optimization_barrier((inner, normed_other))
     own = expert_out_of(inner)
-    own, normed_other = lax.optimization_barrier((own, normed_other))
     inner_other = expert_in(normed_other)
     other = [swap_cores(expert_out_of(inner_other[r : r + 128])) for r in (0, 128)]
 

time: 200 us -> 188 us (0.940)
  matrix products: 26.6 us -> 13.8 us
    dot_general x3, matrix products: 11.6 us -> 4.57 us  [expert_out_of(): return jnp.dot(rows, down_w, preferred_element_type=F32).astype(BF16)]
    dot_general x2, matrix products: 5.82 us -> 2.02 us  [expert_in(): up = jnp.dot(rows, up_w, preferred_element_type=F32)]
    ppermute x6, waiting for transfers between devices: 7.27 us -> 4.07 us  [shards(): got = [lax.ppermute(sums[d], 'dp', near[d]) for d in (1, 3, 2)]]
    ppermute x6, waiting for transfers between devices: 0.93 us -> 3.95 us  [shards(): got = [lax.ppermute(rows[d], 'dp', far[d]) for d in (1, 3, 2)]]
    ppermute x6, starting transfers between devices: 8.38 us -> 10.8 us  [shards(): got = [lax.ppermute(rows[d], 'dp', far[d]) for d in (1, 3, 2)]]
    ppermute x7, waiting for transfers between devices: 2.64 us -> 4.81 us  [swap_cores(): return lax.ppermute(a, 'side', SWAP)]
  transfers between devices with their start and end apart: 39 -> 39, of which waited for: 20 -> 23; matrix products, arithmetic and copies ran while one was open for 12% -> 9% of each run, Pallas kernels for 5% -> 5%
where the time goes in v4:
time: 188 us; the launch traced here: 186 us
  starting transfers between devices  65.4 us (35%)
  waiting for transfers between devices  59.7 us (32%)
  Pallas kernels  20.6 us (11%)
  matrix products  13.8 us (7%)
  blocking collectives  13.4 us (7%)
  other arithmetic  6.68 us (4%)
  local copies, waits for them, and re-layouts  5.87 us (3%)
    ppermute x7, starting transfers between devices, swap_cores(): return lax.ppermute(a, 'side', SWAP)  15.9 us
    all_to_all x1, blocking collectives, shards(): lax.all_to_all(routed.reshape(8, 32, 384), 'tensor', split_axis=0, concat...  13.4 us
    pallas_call x5, Pallas kernels, local_call(): pl.pallas_call(kernel, in_specs=first + [vmem] * (len(args) - len(first))...  12.5 us
    ppermute x6, starting transfers between devices, shards(): got = [lax.ppermute(rows[d], 'dp', far[d]) for d in (1, 3, 2)]  10.8 us
    ppermute x3, waiting for transfers between devices, shards(): lax.ppermute(rows_x, 'dp', SHIFT_Y[d])  10.6 us
    ppermute x6, starting transfers between devices, shards(): got = [lax.ppermute(sums[d], 'dp', near[d]) for d in (1, 3, 2)]  9.1 us
    all_to_all x1, starting transfers between devices, shards(): lax.all_to_all(head_sums, 'tensor', split_axis=0, concat_axis=0, tiled=True)  8.18 us
    all_to_all x1, waiting for transfers between devices, shards(): lax.all_to_all(parts.reshape(8, 32, 384), 'tensor', split_axis=0, concat_...  7.58 us
  transfers between devices with their start and end apart: 39, of which 23 were waited for; matrix products, arithmetic and copies ran while one was open for 9% of the time, Pallas kernels for 5%

profile of v4, /device:TPU:1, one launch (start us, length us, event | category | flops | bytes accessed | tf_op | source)
XLA Modules:
  0.0 185.9 jit_solution(3281591592764545843)
XLA Ops:
  0.0 5.3 %attend.1 = bf16[32,768]{1,0:T(8,128)(2,1)} custom-call(s32[32]{0:T(128)} %lengths.1, bf16[32,768]{1,0:T(8,128)(2,1)} %q_in.1, bf16[32,128]{1,0:T(8,128)(2,1)} %k_in.1, bf16[32,128]{1,0:T(8,128)(2,1)} %v_in.1, bf16[32,192,128]{2,1,0:T(8,128)(2,1)} %keys.1, bf16[32,192,128]{2,1,0:T(8,128)(2,1)} %values.1), custom_call_target="tpu_custom_call" | custom-call | tf_op jit(solution)/shard_map/attend/pallas_call | solution.py:194
  5.4 3.4 %collective-permute-start.2 = (bf16[32,768]{1,0:T(8,128)(2,1)}, bf16[32,768]{1,0:T(8,128)(2,1)S(1)}, u32[]{:S(2)}, u32[]{:S(2)}) collective-permute-start(bf16[32,768]{1,0:T(8,128)(2,1)} %attend.1), channel_id=1, source_target_pairs={{0,192},{16,208},{32,224},{48,240},{64,0},{80,16},{96,32},{112,48}... | collective-permute-start | bytes 147464 | tf_op jit(solution)/shard_map/ppermute | solution.py:280
  9.9 1.5 collective-permute-start.6
  11.4 2.0 %collective-permute-done.1 = bf16[32,768]{1,0:T(8,128)(2,1)S(1)} collective-permute-done((bf16[32,768]{1,0:T(8,128)(2,1)}, bf16[32,768]{1,0:T(8,128)(2,1)S(1)}, u32[]{:S(2)}, u32[]{:S(2)}) %collective-permute-start.1) | collective-permute-done | bytes 49184 | tf_op jit(solution)/shard_map/ppermute | solution.py:280
  14.8 2.8 %collective-permute-start.5 = (bf16[4,32,768]{2,1,0:T(8,128)(2,1)S(1)}, bf16[4,32,768]{2,1,0:T(8,128)(2,1)S(1)}, u32[]{:S(2)}, u32[]{:S(2)}) collective-permute-start(bf16[4,32,768]{2,1,0:T(8,128)(2,1)S(1)} %pad_maximum_fusion.3.g0), channel_id=1, source_target_pairs={{0,48},{16,0},{32,16},{48,32},{64,112},{80,64},{96,80},{112,96},{1... | collective-permute-start | bytes 589832 | tf_op jit(solution)/shard_map/ppermute | solution.py:284
  18.7 3.6 %collective-permute-done.5.g3 = bf16[4,32,768]{2,1,0:T(8,128)(2,1)S(1)} collective-permute-done((bf16[4,32,768]{2,1,0:T(8,128)(2,1)S(1)}, bf16[4,32,768]{2,1,0:T(8,128)(2,1)S(1)}, u32[]{:S(2)}, u32[]{:S(2)}) %collective-permute-start.5) | collective-permute-done | bytes 196640 | tf_op jit(solution)/shard_map/ppermute | solution.py:284
  22.3 1.5 collective-permute-done.4.g2
  23.8 5.5 %collective-permute-done.3.g1 = bf16[4,32,768]{2,1,0:T(8,128)(2,1)} collective-permute-done((bf16[4,32,768]{2,1,0:T(8,128)(2,1)S(1)}, bf16[4,32,768]{2,1,0:T(8,128)(2,1)}, u32[]{:S(2)}, u32[]{:S(2)}) %collective-permute-start.3) | collective-permute-done | bytes 196640 | tf_op jit(solution)/shard_map/ppermute | solution.py:284
  29.3 2.8 %out_projection.1 = bf16[8,64,384]{2,1,0:T(8,128)(2,1)} custom-call(s32[3]{0:T(128)S(1)} %pad_add_fusion.pos, bf16[4,32,768]{2,1,0:T(8,128)(2,1)S(1)} %pad_maximum_fusion.3.g0, bf16[4,32,768]{2,1,0:T(8,128)(2,1)} %collective-permute-done.3.g1, bf16[4,32,768]{2,1,0:T(8,128)(2,1)} %collective-permute-done.4.g2, ...), custom_call_target="tpu_custom_call" | custom-call | tf_op jit(solution)/shard_map/out_projection/pallas_call | solution.py:286
  32.1 8.2 %all-to-all-start = ((bf16[8,64,384]{2,1,0:T(8,128)(2,1)}), bf16[8,64,384]{2,1,0:T(8,128)(2,1)S(1)}, u32[]{:S(2)}, u32[]{:S(2)}) async-start(bf16[8,64,384]{2,1,0:T(8,128)(2,1)} %out_projection.1), calls=%async_computation | async-start | bytes 786432 | tf_op jit(solution)/shard_map/all_to_all | solution.py:295
  40.3 1.5 copy.23
  41.8 1.7 collective-permute-start.7
  43.5 1.2 collective-permute-done.7
  46.4 6.3 %all-to-all-done = bf16[8,64,384]{2,1,0:T(8,128)(2,1)S(1)} async-done(((bf16[8,64,384]{2,1,0:T(8,128)(2,1)}), bf16[8,64,384]{2,1,0:T(8,128)(2,1)S(1)}, u32[]{:S(2)}, u32[]{:S(2)}) %all-to-all-start) | async-done | bytes 393248 | tf_op jit(solution)/shard_map/all_to_all | solution.py:295
  53.7 3.3 %collective-permute-start.8 = (bf16[64,384]{1,0:T(8,128)(2,1)S(1)}, bf16[64,384]{1,0:T(8,128)(2,1)S(1)}, u32[]{:S(2)}, u32[]{:S(2)}) collective-permute-start(bf16[64,384]{1,0:T(8,128)(2,1)S(1)} %fusion.22), channel_id=1, source_target_pairs={{0,1},{1,0},{2,3},{3,2},{4,5},{5,4},{6,7},{7,6},{8,9},{9,8},{10,11... | collective-permute-start | bytes 147464 | tf_op jit(solution)/shard_map/ppermute | solution.py:22
  58.3 13.4 %all_to_all.15 = bf16[8,32,384]{2,1,0:T(8,128)(2,1)S(1)} all-to-all(bf16[8,32,384]{2,1,0:T(8,128)(2,1)S(1)} %bitcast.86), channel_id=1, replica_groups=mesh['dp'=16,'tensor'=8,'side'=2] {'tensor'}, dimensions={0} | all-to-all | bytes 393216 | tf_op jit(solution)/shard_map/all_to_all | solution.py:304
  74.0 1.8 collective-permute-done.11
  75.7 2.0 %collective-permute-done.10 = bf16[128,384]{1,0:T(8,128)(2,1)S(1)} collective-permute-done((bf16[128,384]{1,0:T(8,128)(2,1)S(1)}, bf16[128,384]{1,0:T(8,128)(2,1)S(1)}, u32[]{:S(2)}, u32[]{:S(2)}) %collective-permute-start.10) | collective-permute-done | bytes 98336 | tf_op jit(solution)/shard_map/ppermute | solution.py:310
  77.8 3.1 %collective-permute-done.9 = bf16[128,384]{1,0:T(8,128)(2,1)S(1)} collective-permute-done((bf16[128,384]{1,0:T(8,128)(2,1)S(1)}, bf16[128,384]{1,0:T(8,128)(2,1)S(1)}, u32[]{:S(2)}, u32[]{:S(2)}) %collective-permute-start.9) | collective-permute-done | bytes 98336 | tf_op jit(solution)/shard_map/ppermute | solution.py:310
  82.7 2.1 %collective-permute-start.20 = (bf16[4,128,384]{2,1,0:T(8,128)(2,1)S(1)}, bf16[4,128,384]{2,1,0:T(8,128)(2,1)S(1)}, u32[]{:S(2)}, u32[]{:S(2)}) collective-permute-start(bf16[4,128,384]{2,1,0:T(8,128)(2,1)S(1)} %pad_maximum_fusion.1.b0), channel_id=1, source_target_pairs={{0,192},{16,208},{32,224},{48,240},{64,0},{80,16},{96,32},{112,48}... | collective-permute-start | bytes 1179656 | tf_op jit(solution)/shard_map/ppermute | solution.py:316
  84.7 2.6 %collective-permute-start.18 = (bf16[4,128,384]{2,1,0:T(8,128)(2,1)S(1)}, bf16[4,128,384]{2,1,0:T(8,128)(2,1)S(1)}, u32[]{:S(2)}, u32[]{:S(2)}) collective-permute-start(bf16[4,128,384]{2,1,0:T(8,128)(2,1)S(1)} %pad_maximum_fusion.a0), channel_id=1, source_target_pairs={{0,48},{16,0},{32,16},{48,32},{64,112},{80,64},{96,80},{112,96},{1... | collective-permute-start | bytes 1179656 | tf_op jit(solution)/shard_map/ppermute | solution.py:315
  87.3 4.3 %collective-permute-done.16.b1 = bf16[4,128,384]{2,1,0:T(8,128)(2,1)S(1)} collective-permute-done((bf16[4,128,384]{2,1,0:T(8,128)(2,1)S(1)}, bf16[4,128,384]{2,1,0:T(8,128)(2,1)S(1)}, u32[]{:S(2)}, u32[]{:S(2)}) %collective-permute-start.16) | collective-permute-done | bytes 393248 | tf_op jit(solution)/shard_map/ppermute | solution.py:316
  92.3 1.9 %collective-permute-start.19 = (bf16[4,128,384]{2,1,0:T(8,128)(2,1)S(1)}, bf16[4,128,384]{2,1,0:T(8,128)(2,1)S(1)}, u32[]{:S(2)}, u32[]{:S(2)}) collective-permute-start(bf16[4,128,384]{2,1,0:T(8,128)(2,1)S(1)} %pad_maximum_fusion.1.b0), channel_id=1, source_target_pairs={{0,128},{16,144},{32,160},{48,176},{64,192},{80,208},{96,224},{112... | collective-permute-start | bytes 1179656 | tf_op jit(solution)/shard_map/ppermute | solution.py:319
  94.2 7.1 %collective-permute-done.17.a2 = bf16[4,128,384]{2,1,0:T(8,128)(2,1)S(1)} collective-permute-done((bf16[4,128,384]{2,1,0:T(8,128)(2,1)S(1)}, bf16[4,128,384]{2,1,0:T(8,128)(2,1)S(1)}, u32[]{:S(2)}, u32[]{:S(2)}) %collective-permute-start.17) | collective-permute-done | bytes 393248 | tf_op jit(solution)/shard_map/ppermute | solution.py:319
  102.1 3.2 %norm.1 = bf16[256,6144]{1,0:T(8,128)(2,1)S(1)} custom-call(s32[3]{0:T(128)S(1)} %pad_add_fusion.pos, bf16[4,128,384]{2,1,0:T(8,128)(2,1)S(1)} %pad_maximum_fusion.a0, bf16[4,128,384]{2,1,0:T(8,128)(2,1)S(1)} %collective-permute-done.15.a1, bf16[4,128,384]{2,1,0:T(8,128)(2,1)S(1)} %collective-permute-done.17.a2, ...), custom_call_target="tpu_custom_call" | custom-call | tf_op jit(solution)/shard_map/norm/pallas_call | solution.py:112
  105.3 4.1 %collective-permute-start.21 = (bf16[256,6144]{1,0:T(8,128)(2,1)S(1)}, bf16[256,6144]{1,0:T(8,128)(2,1)S(1)}, u32[]{:S(2)}, u32[]{:S(2)}) collective-permute-start(bf16[256,6144]{1,0:T(8,128)(2,1)S(1)} %norm.1), channel_id=1, source_target_pairs={{0,1},{1,0},{2,3},{3,2},{4,5},{5,4},{6,7},{7,6},{8,9},{9,8},{10,11... | collective-permute-start | bytes 9437192 | tf_op jit(solution)/shard_map/ppermute | solution.py:22
  111.5 3.2 %collective-permute-done.21 = bf16[256,6144]{1,0:T(8,128)(2,1)S(1)} collective-permute-done((bf16[256,6144]{1,0:T(8,128)(2,1)S(1)}, bf16[256,6144]{1,0:T(8,128)(2,1)S(1)}, u32[]{:S(2)}, u32[]{:S(2)}) %collective-permute-start.21) | collective-permute-done | bytes 3145760 | tf_op jit(solution)/shard_map/ppermute | solution.py:22
  116.6 1.8 convolution_convert_fusion.1
  118.8 1.8 convolution_convert_fusion.2
  122.2 3.0 %combine_cores.3 = (bf16[4,128,384]{2,1,0:T(8,128)(2,1)S(1)}, bf16[4,128,384]{2,1,0:T(8,128)(2,1)}, bf16[4,128,384]{2,1,0:T(8,128)(2,1)}, bf16[4,128,384]{2,1,0:T(8,128)(2,1)}) custom-call(s32[3]{0:T(128)S(1)} %pad_add_fusion.pos, bf16[256,6144]{1,0:T(8,128)(2,1)S(1)} %convolution_convert_fusion.own, bf16[128,6144]{1,0:T(8,128)(2,1)} %collective-permute-done.29.other), custom_call_target="tpu_custom_call" | custom-call | tf_op jit(solution)/shard_map/combine_cores/pallas_call | solution.py:112
  125.2 1.2 collective-permute-start.30
  126.5 1.5 collective-permute-start.31
  128.7 2.7 %combine_cores.2 = (bf16[4,128,384]{2,1,0:T(8,128)(2,1)S(1)}, bf16[4,128,384]{2,1,0:T(8,128)(2,1)}, bf16[4,128,384]{2,1,0:T(8,128)(2,1)S(1)}, bf16[4,128,384]{2,1,0:T(8,128)(2,1)S(1)}) custom-call(s32[3]{0:T(128)S(1)} %pad_add_fusion.pos, bf16[256,6144]{1,0:T(8,128)(2,1)S(1)} %convolution_convert_fusion.own, bf16[128,6144]{1,0:T(8,128)(2,1)} %collective-permute-done.22.other), custom_call_target="tpu_custom_call" | custom-call | tf_op jit(solution)/shard_map/combine_cores/pallas_call | solution.py:112
  133.6 2.4 %collective-permute-start.24 = (bf16[4,128,384]{2,1,0:T(8,128)(2,1)}, bf16[4,128,384]{2,1,0:T(8,128)(2,1)}, u32[]{:S(2)}, u32[]{:S(2)}) collective-permute-start(bf16[4,128,384]{2,1,0:T(8,128)(2,1)} %copy-done.7), channel_id=1, source_target_pairs={{0,48},{16,0},{32,16},{48,32},{64,112},{80,64},{96,80},{112,96},{1... | collective-permute-start | bytes 1179656 | tf_op jit(solution)/shard_map/ppermute | solution.py:360
  136.0 1.1 collective-permute-done.30.got1
  137.1 3.0 %collective-permute-start.25 = (bf16[4,128,384]{2,1,0:T(8,128)(2,1)}, bf16[4,128,384]{2,1,0:T(8,128)(2,1)}, u32[]{:S(2)}, u32[]{:S(2)}) collective-permute-start(bf16[4,128,384]{2,1,0:T(8,128)(2,1)} %copy-done.6), channel_id=1, source_target_pairs={{0,32},{16,48},{32,0},{48,16},{64,96},{80,112},{96,64},{112,80},{1... | collective-permute-start | bytes 1179656 | tf_op jit(solution)/shard_map/ppermute | solution.py:360
  140.0 2.8 %fusion.12 = f32[256]{0:T(256)S(1)} fusion(bf16[256,6144]{1,0:T(8,128)(2,1)} %copy-done.1, bf16[6144,8]{0,1:T(8,128)(2,1)} %param.23, s32[256]{0:T(256)S(1)} %eq.144, f32[8]{0:T(128)S(1)} %compare_convert_fusion), kind=kOutput, calls=%fused_computation.19 | convolution fusion | flops 25175808 | bytes 3246112 | tf_op jit(solution)/shard_map/dot_general | solution.py:340
  142.9 3.0 %collective-permute-done.32.got3 = bf16[4,128,384]{2,1,0:T(8,128)(2,1)} collective-permute-done((bf16[4,128,384]{2,1,0:T(8,128)(2,1)}, bf16[4,128,384]{2,1,0:T(8,128)(2,1)}, u32[]{:S(2)}, u32[]{:S(2)}) %collective-permute-start.32) | collective-permute-done | bytes 393248 | tf_op jit(solution)/shard_map/ppermute | solution.py:360
  145.8 2.1 %sum_rows.3 = (f32[128,384]{1,0:T(8,128)S(1)}, bf16[128,384]{1,0:T(8,128)(2,1)}, bf16[128,384]{1,0:T(8,128)(2,1)}, bf16[128,384]{1,0:T(8,128)(2,1)}) custom-call(bf16[4,128,384]{2,1,0:T(8,128)(2,1)S(1)} %copy-done.3, bf16[4,128,384]{2,1,0:T(8,128)(2,1)} %collective-permute-done.30.got1, bf16[4,128,384]{2,1,0:T(8,128)(2,1)} %collective-permute-done.31.got2, ...), custom_call_target="tpu_custom_call" | custom-call | tf_op jit(solution)/shard_map/sum_rows/pallas_call | solution.py:112
  148.6 6.3 %collective-permute-start.33 = (bf16[128,384]{1,0:T(8,128)(2,1)}, bf16[128,384]{1,0:T(8,128)(2,1)}, u32[]{:S(2)}, u32[]{:S(2)}) collective-permute-start(bf16[128,384]{1,0:T(8,128)(2,1)} %get-tuple-element.58), channel_id=1, source_target_pairs={{0,16},{16,32},{32,48},{48,0},{64,80},{80,96},{96,112},{112,64},{1... | collective-permute-start | bytes 294920 | tf_op jit(solution)/shard_map/ppermute | solution.py:369
  154.9 1.8 collective-permute-start.35
  156.8 1.5 sum_rows.2
  158.4 2.7 %collective-permute-start.27 = (bf16[128,384]{1,0:T(8,128)(2,1)S(1)}, bf16[128,384]{1,0:T(8,128)(2,1)S(1)}, u32[]{:S(2)}, u32[]{:S(2)}) collective-permute-start(bf16[128,384]{1,0:T(8,128)(2,1)S(1)} %get-tuple-element.51), channel_id=1, source_target_pairs={{0,192},{16,208},{32,224},{48,240},{64,0},{80,16},{96,32},{112,48}... | collective-permute-start | bytes 294920 | tf_op jit(solution)/shard_map/ppermute | solution.py:369
  161.1 1.1 add_add_fusion
  163.6 2.5 %collective-permute-done.28 = bf16[128,384]{1,0:T(8,128)(2,1)S(1)} collective-permute-done((bf16[128,384]{1,0:T(8,128)(2,1)S(1)}, bf16[128,384]{1,0:T(8,128)(2,1)S(1)}, u32[]{:S(2)}, u32[]{:S(2)}) %collective-permute-start.28) | collective-permute-done | bytes 98336 | tf_op jit(solution)/shard_map/ppermute | solution.py:369
  167.0 3.4 %all-to-all-start.2 = ((bf16[8,32,384]{2,1,0:T(8,128)(2,1)}), bf16[8,32,384]{2,1,0:T(8,128)(2,1)S(1)}, u32[]{:S(2)}, u32[]{:S(2)}) async-start(bf16[8,32,384]{2,1,0:T(8,128)(2,1)} %multiply_convert_fusion), calls=%async_computation.2 | async-start | bytes 393216 | tf_op jit(solution)/shard_map/all_to_all | solution.py:374
  171.3 7.6 %all-to-all-done.2 = bf16[8,32,384]{2,1,0:T(8,128)(2,1)S(1)} async-done(((bf16[8,32,384]{2,1,0:T(8,128)(2,1)}), bf16[8,32,384]{2,1,0:T(8,128)(2,1)S(1)}, u32[]{:S(2)}, u32[]{:S(2)}) %all-to-all-start.2) | async-done | bytes 196640 | tf_op jit(solution)/shard_map/all_to_all | solution.py:374
  179.0 4.9 %collective-permute-start.36 = (bf16[256,192]{1,0:T(8,128)(2,1)S(1)}, bf16[256,192]{1,0:T(8,128)(2,1)S(1)}, u32[]{:S(2)}, u32[]{:S(2)}) collective-permute-start(bf16[256,192]{1,0:T(8,128)(2,1)S(1)} %broadcast_select_fusion), channel_id=1, source_target_pairs={{0,1},{1,0},{2,3},{3,2},{4,5},{5,4},{6,7},{7,6},{8,9},{9,8},{10,11... | collective-permute-start | bytes 294920 | tf_op jit(solution)/shard_map/ppermute | solution.py:22
  (115 shorter events, 28.1 us)
Async XLA Ops:
  0.0 116.6 %copy-start = (bf16[1,256,6144]{2,1,0:T(8,128)(2,1)S(1)}, bf16[1,256,6144]{2,1,0:T(8,128)(2,1)}, u32[]{:S(2)}) copy-start(bf16[1,256,6144]{2,1,0:T(8,128)(2,1)} %param.27) | copy-start | bytes 9437188
  0.0 43.5 %copy-start.11 = (s32[1024,2]{0,1:T(2,128)S(1)}, s32[1024,2]{0,1:T(2,128)}, u32[]{:S(2)}) copy-start(s32[1024,2]{0,1:T(2,128)} %param.24) | copy-start | bytes 24580
  5.4 6.0 %collective-permute-start.2 = (bf16[32,768]{1,0:T(8,128)(2,1)}, bf16[32,768]{1,0:T(8,128)(2,1)S(1)}, u32[]{:S(2)}, u32[]{:S(2)}) collective-permute-start(bf16[32,768]{1,0:T(8,128)(2,1)} %attend.1), channel_id=1, source_target_pairs={{0,192},{16,208},{32,224},{48,240},{64,0},{80,16},{96,32},{112,48}... | collective-permute-start | bytes 147464 | tf_op jit(solution)/shard_map/ppermute | solution.py:280
  8.7 4.7 %collective-permute-start.1 = (bf16[32,768]{1,0:T(8,128)(2,1)}, bf16[32,768]{1,0:T(8,128)(2,1)S(1)}, u32[]{:S(2)}, u32[]{:S(2)}) collective-permute-start(bf16[32,768]{1,0:T(8,128)(2,1)} %attend.1), channel_id=1, source_target_pairs={{0,128},{16,144},{32,160},{48,176},{64,192},{80,208},{96,224},{112... | collective-permute-start | bytes 147464 | tf_op jit(solution)/shard_map/ppermute | solution.py:280
  9.3 4.7 %collective-permute-start = (bf16[32,768]{1,0:T(8,128)(2,1)}, bf16[32,768]{1,0:T(8,128)(2,1)S(1)}, u32[]{:S(2)}, u32[]{:S(2)}) collective-permute-start(bf16[32,768]{1,0:T(8,128)(2,1)} %attend.1), channel_id=1, source_target_pairs={{0,64},{16,80},{32,96},{48,112},{64,128},{80,144},{96,160},{112,17... | collective-permute-start | bytes 147464 | tf_op jit(solution)/shard_map/ppermute | solution.py:280
  9.9 19.4 %collective-permute-start.6 = (bf16[192,768]{1,0:T(8,128)(2,1)}, bf16[192,768]{1,0:T(8,128)(2,1)}, u32[]{:S(2)}, u32[]{:S(2)}) collective-permute-start(bf16[192,768]{1,0:T(8,128)(2,1)} %bitcast.7.w_own), channel_id=1, source_target_pairs={{0,1},{1,0},{2,3},{3,2},{4,5},{5,4},{6,7},{7,6},{8,9},{9,8},{10,11... | collective-permute-start | bytes 884744 | tf_op jit(solution)/shard_map/ppermute | solution.py:22
  14.8 7.5 %collective-permute-start.5 = (bf16[4,32,768]{2,1,0:T(8,128)(2,1)S(1)}, bf16[4,32,768]{2,1,0:T(8,128)(2,1)S(1)}, u32[]{:S(2)}, u32[]{:S(2)}) collective-permute-start(bf16[4,32,768]{2,1,0:T(8,128)(2,1)S(1)} %pad_maximum_fusion.3.g0), channel_id=1, source_target_pairs={{0,48},{16,0},{32,16},{48,32},{64,112},{80,64},{96,80},{112,96},{1... | collective-permute-start | bytes 589832 | tf_op jit(solution)/shard_map/ppermute | solution.py:284
  17.6 6.2 %collective-permute-start.4 = (bf16[4,32,768]{2,1,0:T(8,128)(2,1)S(1)}, bf16[4,32,768]{2,1,0:T(8,128)(2,1)}, u32[]{:S(2)}, u32[]{:S(2)}) collective-permute-start(bf16[4,32,768]{2,1,0:T(8,128)(2,1)S(1)} %pad_maximum_fusion.3.g0), channel_id=1, source_target_pairs={{0,32},{16,48},{32,0},{48,16},{64,96},{80,112},{96,64},{112,80},{1... | collective-permute-start | bytes 589832 | tf_op jit(solution)/shard_map/ppermute | solution.py:284
  17.9 11.4 %collective-permute-start.3 = (bf16[4,32,768]{2,1,0:T(8,128)(2,1)S(1)}, bf16[4,32,768]{2,1,0:T(8,128)(2,1)}, u32[]{:S(2)}, u32[]{:S(2)}) collective-permute-start(bf16[4,32,768]{2,1,0:T(8,128)(2,1)S(1)} %pad_maximum_fusion.3.g0), channel_id=1, source_target_pairs={{0,16},{16,32},{32,48},{48,0},{64,80},{80,96},{96,112},{112,64},{1... | collective-permute-start | bytes 589832 | tf_op jit(solution)/shard_map/ppermute | solution.py:284
  32.1 20.6 %all-to-all-start = ((bf16[8,64,384]{2,1,0:T(8,128)(2,1)}), bf16[8,64,384]{2,1,0:T(8,128)(2,1)S(1)}, u32[]{:S(2)}, u32[]{:S(2)}) async-start(bf16[8,64,384]{2,1,0:T(8,128)(2,1)} %out_projection.1), calls=%async_computation | async-start | bytes 786432 | tf_op jit(solution)/shard_map/all_to_all | solution.py:295
  41.8 2.9 %collective-permute-start.7 = (bf16[128,192]{1,0:T(8,128)(2,1)}, bf16[128,192]{1,0:T(8,128)(2,1)}, u32[]{:S(2)}, u32[]{:S(2)}) collective-permute-start(bf16[128,192]{1,0:T(8,128)(2,1)} %copy.23), channel_id=1, source_target_pairs={{0,1},{1,0},{2,3},{3,2},{4,5},{5,4},{6,7},{7,6},{8,9},{9,8},{10,11... | collective-permute-start | bytes 147464 | tf_op jit(solution)/shard_map/ppermute | solution.py:22
  53.7 4.4 %collective-permute-start.8 = (bf16[64,384]{1,0:T(8,128)(2,1)S(1)}, bf16[64,384]{1,0:T(8,128)(2,1)S(1)}, u32[]{:S(2)}, u32[]{:S(2)}) collective-permute-start(bf16[64,384]{1,0:T(8,128)(2,1)S(1)} %fusion.22), channel_id=1, source_target_pairs={{0,1},{1,0},{2,3},{3,2},{4,5},{5,4},{6,7},{7,6},{8,9},{9,8},{10,11... | collective-permute-start | bytes 147464 | tf_op jit(solution)/shard_map/ppermute | solution.py:22
  58.1 23.6 %copy-start.8 = (bf16[128,384]{1,0:T(8,128)(2,1)}, bf16[128,384]{1,0:T(8,128)(2,1)S(1)}, u32[]{:S(2)}) copy-start(bf16[128,384]{1,0:T(8,128)(2,1)S(1)} %maximum_select_fusion.1) | copy-start | bytes 294916
  71.7 4.0 %collective-permute-start.11 = (bf16[128,384]{1,0:T(8,128)(2,1)S(1)}, bf16[128,384]{1,0:T(8,128)(2,1)S(1)}, u32[]{:S(2)}, u32[]{:S(2)}) collective-permute-start(bf16[128,384]{1,0:T(8,128)(2,1)S(1)} %bitcast.88), channel_id=1, source_target_pairs={{0,192},{16,208},{32,224},{48,240},{64,0},{80,16},{96,32},{112,48}... | collective-permute-start | bytes 294920 | tf_op jit(solution)/shard_map/ppermute | solution.py:310
  72.7 5.1 %collective-permute-start.10 = (bf16[128,384]{1,0:T(8,128)(2,1)S(1)}, bf16[128,384]{1,0:T(8,128)(2,1)S(1)}, u32[]{:S(2)}, u32[]{:S(2)}) collective-permute-start(bf16[128,384]{1,0:T(8,128)(2,1)S(1)} %bitcast.89), channel_id=1, source_target_pairs={{0,128},{16,144},{32,160},{48,176},{64,192},{80,208},{96,224},{112... | collective-permute-start | bytes 294920 | tf_op jit(solution)/shard_map/ppermute | solution.py:310
  73.2 7.7 %collective-permute-start.9 = (bf16[128,384]{1,0:T(8,128)(2,1)S(1)}, bf16[128,384]{1,0:T(8,128)(2,1)S(1)}, u32[]{:S(2)}, u32[]{:S(2)}) collective-permute-start(bf16[128,384]{1,0:T(8,128)(2,1)S(1)} %bitcast.90), channel_id=1, source_target_pairs={{0,64},{16,80},{32,96},{48,112},{64,128},{80,144},{96,160},{112,17... | collective-permute-start | bytes 294920 | tf_op jit(solution)/shard_map/ppermute | solution.py:310
  73.9 6.9 %collective-permute-start.14 = (bf16[128,384]{1,0:T(8,128)(2,1)S(1)}, bf16[128,384]{1,0:T(8,128)(2,1)S(1)}, u32[]{:S(2)}, u32[]{:S(2)}) collective-permute-start(bf16[128,384]{1,0:T(8,128)(2,1)S(1)} %bitcast.92), channel_id=1, source_target_pairs={{0,48},{16,0},{32,16},{48,32},{64,112},{80,64},{96,80},{112,96},{1... | collective-permute-start | bytes 294920 | tf_op jit(solution)/shard_map/ppermute | solution.py:311
  73.9 6.9 %collective-permute-start.13 = (bf16[128,384]{1,0:T(8,128)(2,1)S(1)}, bf16[128,384]{1,0:T(8,128)(2,1)S(1)}, u32[]{:S(2)}, u32[]{:S(2)}) collective-permute-start(bf16[128,384]{1,0:T(8,128)(2,1)S(1)} %bitcast.93), channel_id=1, source_target_pairs={{0,32},{16,48},{32,0},{48,16},{64,96},{80,112},{96,64},{112,80},{1... | collective-permute-start | bytes 294920 | tf_op jit(solution)/shard_map/ppermute | solution.py:311
  75.7 5.9 %collective-permute-start.12 = (bf16[128,384]{1,0:T(8,128)(2,1)S(1)}, bf16[128,384]{1,0:T(8,128)(2,1)S(1)}, u32[]{:S(2)}, u32[]{:S(2)}) collective-permute-start(bf16[128,384]{1,0:T(8,128)(2,1)S(1)} %bitcast.94), channel_id=1, source_target_pairs={{0,16},{16,32},{32,48},{48,0},{64,80},{80,96},{96,112},{112,64},{1... | collective-permute-start | bytes 294920 | tf_op jit(solution)/shard_map/ppermute | solution.py:311
  81.8 9.8 %collective-permute-start.16 = (bf16[4,128,384]{2,1,0:T(8,128)(2,1)S(1)}, bf16[4,128,384]{2,1,0:T(8,128)(2,1)S(1)}, u32[]{:S(2)}, u32[]{:S(2)}) collective-permute-start(bf16[4,128,384]{2,1,0:T(8,128)(2,1)S(1)} %pad_maximum_fusion.1.b0), channel_id=1, source_target_pairs={{0,64},{16,80},{32,96},{48,112},{64,128},{80,144},{96,160},{112,17... | collective-permute-start | bytes 1179656 | tf_op jit(solution)/shard_map/ppermute | solution.py:316
  82.6 9.7 %collective-permute-start.15 = (bf16[4,128,384]{2,1,0:T(8,128)(2,1)S(1)}, bf16[4,128,384]{2,1,0:T(8,128)(2,1)S(1)}, u32[]{:S(2)}, u32[]{:S(2)}) collective-permute-start(bf16[4,128,384]{2,1,0:T(8,128)(2,1)S(1)} %pad_maximum_fusion.a0), channel_id=1, source_target_pairs={{0,16},{16,32},{32,48},{48,0},{64,80},{80,96},{96,112},{112,64},{1... | collective-permute-start | bytes 1179656 | tf_op jit(solution)/shard_map/ppermute | solution.py:315
  82.7 11.6 %collective-permute-start.20 = (bf16[4,128,384]{2,1,0:T(8,128)(2,1)S(1)}, bf16[4,128,384]{2,1,0:T(8,128)(2,1)S(1)}, u32[]{:S(2)}, u32[]{:S(2)}) collective-permute-start(bf16[4,128,384]{2,1,0:T(8,128)(2,1)S(1)} %pad_maximum_fusion.1.b0), channel_id=1, source_target_pairs={{0,192},{16,208},{32,224},{48,240},{64,0},{80,16},{96,32},{112,48}... | collective-permute-start | bytes 1179656 | tf_op jit(solution)/shard_map/ppermute | solution.py:316
  84.7 9.5 %collective-permute-start.18 = (bf16[4,128,384]{2,1,0:T(8,128)(2,1)S(1)}, bf16[4,128,384]{2,1,0:T(8,128)(2,1)S(1)}, u32[]{:S(2)}, u32[]{:S(2)}) collective-permute-start(bf16[4,128,384]{2,1,0:T(8,128)(2,1)S(1)} %pad_maximum_fusion.a0), channel_id=1, source_target_pairs={{0,48},{16,0},{32,16},{48,32},{64,112},{80,64},{96,80},{112,96},{1... | collective-permute-start | bytes 1179656 | tf_op jit(solution)/shard_map/ppermute | solution.py:315
  92.3 9.0 %collective-permute-start.17 = (bf16[4,128,384]{2,1,0:T(8,128)(2,1)S(1)}, bf16[4,128,384]{2,1,0:T(8,128)(2,1)S(1)}, u32[]{:S(2)}, u32[]{:S(2)}) collective-permute-start(bf16[4,128,384]{2,1,0:T(8,128)(2,1)S(1)} %pad_maximum_fusion.a0), channel_id=1, source_target_pairs={{0,32},{16,48},{32,0},{48,16},{64,96},{80,112},{96,64},{112,80},{1... | collective-permute-start | bytes 1179656 | tf_op jit(solution)/shard_map/ppermute | solution.py:319
  92.3 9.0 %collective-permute-start.19 = (bf16[4,128,384]{2,1,0:T(8,128)(2,1)S(1)}, bf16[4,128,384]{2,1,0:T(8,128)(2,1)S(1)}, u32[]{:S(2)}, u32[]{:S(2)}) collective-permute-start(bf16[4,128,384]{2,1,0:T(8,128)(2,1)S(1)} %pad_maximum_fusion.1.b0), channel_id=1, source_target_pairs={{0,128},{16,144},{32,160},{48,176},{64,192},{80,208},{96,224},{112... | collective-permute-start | bytes 1179656 | tf_op jit(solution)/shard_map/ppermute | solution.py:319
  102.1 7.3 %copy-start.12 = (bf16[1,6144,256]{2,1,0:T(8,128)(2,1)S(1)}, bf16[1,6144,256]{2,1,0:T(8,128)(2,1)}, u32[]{:S(2)}) copy-start(bf16[1,6144,256]{2,1,0:T(8,128)(2,1)} %param.25) | copy-start | bytes 9437188
  105.2 5.2 %copy-start.1 = (bf16[256,6144]{1,0:T(8,128)(2,1)}, bf16[256,6144]{1,0:T(8,128)(2,1)S(1)}, u32[]{:S(2)}) copy-start(bf16[256,6144]{1,0:T(8,128)(2,1)S(1)} %norm.1) | copy-start | bytes 9437188
  105.3 9.4 %collective-permute-start.21 = (bf16[256,6144]{1,0:T(8,128)(2,1)S(1)}, bf16[256,6144]{1,0:T(8,128)(2,1)S(1)}, u32[]{:S(2)}, u32[]{:S(2)}) collective-permute-start(bf16[256,6144]{1,0:T(8,128)(2,1)S(1)} %norm.1), channel_id=1, source_target_pairs={{0,1},{1,0},{2,3},{3,2},{4,5},{5,4},{6,7},{7,6},{8,9},{9,8},{10,11... | collective-permute-start | bytes 9437192 | tf_op jit(solution)/shard_map/ppermute | solution.py:22
  118.4 3.8 %collective-permute-start.29 = (bf16[128,6144]{1,0:T(8,128)(2,1)}, bf16[128,6144]{1,0:T(8,128)(2,1)}, u32[]{:S(2)}, u32[]{:S(2)}) collective-permute-start(bf16[128,6144]{1,0:T(8,128)(2,1)} %convolution_convert_fusion.1), channel_id=1, source_target_pairs={{0,1},{1,0},{2,3},{3,2},{4,5},{5,4},{6,7},{7,6},{8,9},{9,8},{10,11... | collective-permute-start | bytes 4718600 | tf_op jit(solution)/shard_map/ppermute | solution.py:22
  120.6 8.2 %collective-permute-start.22 = (bf16[128,6144]{1,0:T(8,128)(2,1)}, bf16[128,6144]{1,0:T(8,128)(2,1)}, u32[]{:S(2)}, u32[]{:S(2)}) collective-permute-start(bf16[128,6144]{1,0:T(8,128)(2,1)} %convolution_convert_fusion.2), channel_id=1, source_target_pairs={{0,1},{1,0},{2,3},{3,2},{4,5},{5,4},{6,7},{7,6},{8,9},{9,8},{10,11... | collective-permute-start | bytes 4718600 | tf_op jit(solution)/shard_map/ppermute | solution.py:22
  125.2 6.2 %copy-start.2 = (bf16[4,128,384]{2,1,0:T(8,128)(2,1)}, bf16[4,128,384]{2,1,0:T(8,128)(2,1)S(1)}, u32[]{:S(2)}) copy-start(bf16[4,128,384]{2,1,0:T(8,128)(2,1)S(1)} %get-tuple-element.53.mine) | copy-start | bytes 1179652
  125.2 11.9 %collective-permute-start.30 = (bf16[4,128,384]{2,1,0:T(8,128)(2,1)}, bf16[4,128,384]{2,1,0:T(8,128)(2,1)}, u32[]{:S(2)}, u32[]{:S(2)}) collective-permute-start(bf16[4,128,384]{2,1,0:T(8,128)(2,1)} %get-tuple-element.54), channel_id=1, source_target_pairs={{0,64},{16,80},{32,96},{48,112},{64,128},{80,144},{96,160},{112,17... | collective-permute-start | bytes 1179656 | tf_op jit(solution)/shard_map/ppermute | solution.py:360
  126.5 16.3 %collective-permute-start.31 = (bf16[4,128,384]{2,1,0:T(8,128)(2,1)}, bf16[4,128,384]{2,1,0:T(8,128)(2,1)}, u32[]{:S(2)}, u32[]{:S(2)}) collective-permute-start(bf16[4,128,384]{2,1,0:T(8,128)(2,1)} %get-tuple-element.55), channel_id=1, source_target_pairs={{0,192},{16,208},{32,224},{48,240},{64,0},{80,16},{96,32},{112,48}... | collective-permute-start | bytes 1179656 | tf_op jit(solution)/shard_map/ppermute | solution.py:360
  128.0 17.8 %collective-permute-start.32 = (bf16[4,128,384]{2,1,0:T(8,128)(2,1)}, bf16[4,128,384]{2,1,0:T(8,128)(2,1)}, u32[]{:S(2)}, u32[]{:S(2)}) collective-permute-start(bf16[4,128,384]{2,1,0:T(8,128)(2,1)} %get-tuple-element.56), channel_id=1, source_target_pairs={{0,128},{16,144},{32,160},{48,176},{64,192},{80,208},{96,224},{112... | collective-permute-start | bytes 1179656 | tf_op jit(solution)/shard_map/ppermute | solution.py:360
  132.9 22.0 %collective-permute-start.23 = (bf16[4,128,384]{2,1,0:T(8,128)(2,1)}, bf16[4,128,384]{2,1,0:T(8,128)(2,1)}, u32[]{:S(2)}, u32[]{:S(2)}) collective-permute-start(bf16[4,128,384]{2,1,0:T(8,128)(2,1)} %get-tuple-element.46), channel_id=1, source_target_pairs={{0,16},{16,32},{32,48},{48,0},{64,80},{80,96},{96,112},{112,64},{1... | collective-permute-start | bytes 1179656 | tf_op jit(solution)/shard_map/ppermute | solution.py:360
  133.6 12.3 %copy-start.3 = (bf16[4,128,384]{2,1,0:T(8,128)(2,1)S(1)}, bf16[4,128,384]{2,1,0:T(8,128)(2,1)}, u32[]{:S(2)}) copy-start(bf16[4,128,384]{2,1,0:T(8,128)(2,1)} %copy-done.2) | copy-start | bytes 1179652
  133.6 23.2 %collective-permute-start.24 = (bf16[4,128,384]{2,1,0:T(8,128)(2,1)}, bf16[4,128,384]{2,1,0:T(8,128)(2,1)}, u32[]{:S(2)}, u32[]{:S(2)}) collective-permute-start(bf16[4,128,384]{2,1,0:T(8,128)(2,1)} %copy-done.7), channel_id=1, source_target_pairs={{0,48},{16,0},{32,16},{48,32},{64,112},{80,64},{96,80},{112,96},{1... | collective-permute-start | bytes 1179656 | tf_op jit(solution)/shard_map/ppermute | solution.py:360
  137.1 19.7 %collective-permute-start.25 = (bf16[4,128,384]{2,1,0:T(8,128)(2,1)}, bf16[4,128,384]{2,1,0:T(8,128)(2,1)}, u32[]{:S(2)}, u32[]{:S(2)}) collective-permute-start(bf16[4,128,384]{2,1,0:T(8,128)(2,1)} %copy-done.6), channel_id=1, source_target_pairs={{0,32},{16,48},{32,0},{48,16},{64,96},{80,112},{96,64},{112,80},{1... | collective-permute-start | bytes 1179656 | tf_op jit(solution)/shard_map/ppermute | solution.py:360
  148.6 12.4 %collective-permute-start.33 = (bf16[128,384]{1,0:T(8,128)(2,1)}, bf16[128,384]{1,0:T(8,128)(2,1)}, u32[]{:S(2)}, u32[]{:S(2)}) collective-permute-start(bf16[128,384]{1,0:T(8,128)(2,1)} %get-tuple-element.58), channel_id=1, source_target_pairs={{0,16},{16,32},{32,48},{48,0},{64,80},{80,96},{96,112},{112,64},{1... | collective-permute-start | bytes 294920 | tf_op jit(solution)/shard_map/ppermute | solution.py:369
  154.9 6.1 %collective-permute-start.34 = (bf16[128,384]{1,0:T(8,128)(2,1)}, bf16[128,384]{1,0:T(8,128)(2,1)}, u32[]{:S(2)}, u32[]{:S(2)}) collective-permute-start(bf16[128,384]{1,0:T(8,128)(2,1)} %get-tuple-element.59), channel_id=1, source_target_pairs={{0,48},{16,0},{32,16},{48,32},{64,112},{80,64},{96,80},{112,96},{1... | collective-permute-start | bytes 294920 | tf_op jit(solution)/shard_map/ppermute | solution.py:369
  154.9 6.2 %collective-permute-start.35 = (bf16[128,384]{1,0:T(8,128)(2,1)}, bf16[128,384]{1,0:T(8,128)(2,1)}, u32[]{:S(2)}, u32[]{:S(2)}) collective-permute-start(bf16[128,384]{1,0:T(8,128)(2,1)} %get-tuple-element.60), channel_id=1, source_target_pairs={{0,32},{16,48},{32,0},{48,16},{64,96},{80,112},{96,64},{112,80},{1... | collective-permute-start | bytes 294920 | tf_op jit(solution)/shard_map/ppermute | solution.py:369
  158.2 12.1 %copy-start.9 = (bf16[128,384]{1,0:T(8,128)(2,1)S(1)}, bf16[128,384]{1,0:T(8,128)(2,1)}, u32[]{:S(2)}) copy-start(bf16[128,384]{1,0:T(8,128)(2,1)} %copy-done.8) | copy-start | bytes 294916
  158.3 26.7 %copy-start.10 = (pred[256,128]{1,0:T(32,128)(4,1)S(1)}, pred[256,128]{1,0:T(32,128)(4,1)}, u32[]{:S(2)}) copy-start(pred[256,128]{1,0:T(32,128)(4,1)} %get-tuple-element.67) | copy-start | bytes 98308
  158.3 4.8 %collective-permute-start.26 = (bf16[128,384]{1,0:T(8,128)(2,1)S(1)}, bf16[128,384]{1,0:T(8,128)(2,1)S(1)}, u32[]{:S(2)}, u32[]{:S(2)}) collective-permute-start(bf16[128,384]{1,0:T(8,128)(2,1)S(1)} %get-tuple-element.50), channel_id=1, source_target_pairs={{0,64},{16,80},{32,96},{48,112},{64,128},{80,144},{96,160},{112,17... | collective-permute-start | bytes 294920 | tf_op jit(solution)/shard_map/ppermute | solution.py:369
  158.4 5.3 %collective-permute-start.27 = (bf16[128,384]{1,0:T(8,128)(2,1)S(1)}, bf16[128,384]{1,0:T(8,128)(2,1)S(1)}, u32[]{:S(2)}, u32[]{:S(2)}) collective-permute-start(bf16[128,384]{1,0:T(8,128)(2,1)S(1)} %get-tuple-element.51), channel_id=1, source_target_pairs={{0,192},{16,208},{32,224},{48,240},{64,0},{80,16},{96,32},{112,48}... | collective-permute-start | bytes 294920 | tf_op jit(solution)/shard_map/ppermute | solution.py:369
  161.0 5.1 %collective-permute-start.28 = (bf16[128,384]{1,0:T(8,128)(2,1)S(1)}, bf16[128,384]{1,0:T(8,128)(2,1)S(1)}, u32[]{:S(2)}, u32[]{:S(2)}) collective-permute-start(bf16[128,384]{1,0:T(8,128)(2,1)S(1)} %get-tuple-element.52), channel_id=1, source_target_pairs={{0,128},{16,144},{32,160},{48,176},{64,192},{80,208},{96,224},{112... | collective-permute-start | bytes 294920 | tf_op jit(solution)/shard_map/ppermute | solution.py:369
  167.0 11.9 %all-to-all-start.2 = ((bf16[8,32,384]{2,1,0:T(8,128)(2,1)}), bf16[8,32,384]{2,1,0:T(8,128)(2,1)S(1)}, u32[]{:S(2)}, u32[]{:S(2)}) async-start(bf16[8,32,384]{2,1,0:T(8,128)(2,1)} %multiply_convert_fusion), calls=%async_computation.2 | async-start | bytes 393216 | tf_op jit(solution)/shard_map/all_to_all | solution.py:374
  179.0 5.9 %collective-permute-start.36 = (bf16[256,192]{1,0:T(8,128)(2,1)S(1)}, bf16[256,192]{1,0:T(8,128)(2,1)S(1)}, u32[]{:S(2)}, u32[]{:S(2)}) collective-permute-start(bf16[256,192]{1,0:T(8,128)(2,1)S(1)} %broadcast_select_fusion), channel_id=1, source_target_pairs={{0,1},{1,0},{2,3},{3,2},{4,5},{5,4},{6,7},{7,6},{8,9},{9,8},{10,11... | collective-permute-start | bytes 294920 | tf_op jit(solution)/shard_map/ppermute | solution.py:22
  (5 other events, 8.1 us)

commit v5 on v4

--- a/solution.py
+++ b/solution.py
@@ -47,12 +47,12 @@
     return chip_at(pos, i, shift) if h == 0 else chip_at(pos, shift, i)
 
 
-def norm_kernel(pos, a0, a1, a2, a3, b0, b1, b2, b3, gain, out):
-    for h, refs in ((0, (a0, a1, a2, a3)), (1, (b0, b1, b2, b3))):
-
-        def rows_of(n, _, h=h, refs=refs):
+def norm_kernel(h):
+    def kernel(pos, s0, s1, s2, s3, gain, out):
+        refs = (s0, s1, s2, s3)
+
+        def rows_of(n, _):
             rows = pl.ds(pl.multiple_of(n * 32, 32), 32)
-            to = pl.ds(pl.multiple_of(h * 128 + n * 32, 32), 32)
 
             def square(j, total):
                 for i in range(4):
@@ -69,7 +69,7 @@
                     chip = at_half(pos, h, -j, -i)
                     columns = pl.ds(pl.multiple_of(chip * 384, 128), 384)
                     v = refs[i][j, rows, :].astype(F32)
-                    out[to, columns] = (v * scale * gain[chip]).astype(BF16)
+                    out[rows, columns] = (v * scale * gain[chip]).astype(BF16)
                 return 0
 
             lax.fori_loop(0, 4, store, 0)
@@ -77,18 +77,18 @@
 
         lax.fori_loop(0, 4, rows_of, 0)
 
+    return kernel
+
 
 def combine_kernel(h):
     def kernel(pos, own, other, *outs):
-        def work(n, _):
-            i, rows = n // 4, pl.ds(pl.multiple_of((n % 4) * 32, 32), 32)
-            to = pl.ds(pl.multiple_of(h * 128 + (n % 4) * 32, 32), 32)
+        def work(i, _):
             for k in range(4):
                 columns = pl.ds(pl.multiple_of(at_half(pos, h, i, k) * 384, 128), 384)
-                outs[k][i, rows, :] = own[to, columns] + other[rows, columns]
+                outs[k][i] = own[h * 128 : h * 128 + 128, columns] + other[:, columns]
             return 0
 
-        lax.fori_loop(0, 16, work, 0)
+        lax.fori_loop(0, 4, work, 0)
 
     return kernel
 
@@ -318,16 +318,12 @@
     far_a, far_b, a1, b1 = lax.optimization_barrier((stack_a, stack_b, a1, b1))
     a2, b2 = lax.ppermute(far_a, "dp", SHIFT_Y[2]), lax.ppermute(far_b, "dp", SHIFT_X[2])
     gain = norm_gain.reshape(16, 1, 384)
-    normed = local_call(
-        norm_kernel,
-        [((256, 6144), BF16)],
-        "norm",
-        pos,
-        *(stack_a, a1, a2, a3),
-        *(stack_b, b1, b2, b3),
-        gain,
-    )[0]
-    normed_other = swap_cores(normed)
+    halves = [
+        local_call(norm_kernel(h), [((128, 6144), BF16)], "norm", pos, *stacks, gain)[0]
+        for h, stacks in ((0, (stack_a, a1, a2, a3)), (1, (stack_b, b1, b2, b3)))
+    ]
+    halves_other = [swap_cores(rows) for rows in halves]
+    normed = jnp.concatenate(halves)
 
     def expert_in(rows):
         gate = jnp.dot(rows, gate_w, preferred_element_type=F32)
@@ -339,11 +335,12 @@
 
     logits = jnp.dot(normed, router_weight, preferred_element_type=F32)
     shares = jax.nn.sigmoid(jnp.sum(logits * signs, axis=1, keepdims=True))
-    inner = expert_in(normed)
-    inner, normed_other = lax.optimization_barrier((inner, normed_other))
+    inner, halves_other[0] = lax.optimization_barrier((expert_in(normed), halves_other[0]))
+    other = []
+    for rows in halves_other:
+        inner_other = lax.optimization_barrier(expert_in(rows))
+        other.append(swap_cores(expert_out_of(inner_other)))
     own = expert_out_of(inner)
-    inner_other = expert_in(normed_other)
-    other = [swap_cores(expert_out_of(inner_other[r : r + 128])) for r in (0, 128)]
 
     expert_out = []
     for h in (0, 1):

time: 188 us -> 202 us (1.074)
  starting transfers between devices: 65.4 us -> 74.1 us
  waiting for transfers between devices: 59.7 us -> 65.5 us
    ppermute x2, waiting for transfers between devices: 0.71 us -> 11.1 us  [shards(): lax.ppermute(stack_a, 'dp', SHIFT_Y[d])]
    ppermute x1, waiting for transfers between devices: 0.01 us -> 7.12 us  [shards(): lax.ppermute(far_b, 'dp', SHIFT_X[2])]
    ppermute x1, waiting for transfers between devices: 7.12 us -> 1.22 us  [shards(): lax.ppermute(far_a, 'dp', SHIFT_Y[2])]
    ppermute x6, starting transfers between devices: 9.1 us -> 14 us  [shards(): got = [lax.ppermute(sums[d], 'dp', near[d]) for d in (1, 3, 2)]]
    ppermute x6, starting transfers between devices: 10.8 us -> 14.7 us  [shards(): got = [lax.ppermute(rows[d], 'dp', far[d]) for d in (1, 3, 2)]]
    ppermute x7 -> x8, waiting for transfers between devices: 4.81 us -> 1.24 us  [swap_cores(): return lax.ppermute(a, 'side', SWAP)]
    ppermute x6, waiting for transfers between devices: 4.07 us -> 0.98 us  [shards(): got = [lax.ppermute(sums[d], 'dp', near[d]) for d in (1, 3, 2)]]
    ppermute x2, waiting for transfers between devices: 4.27 us -> 6.85 us  [shards(): lax.ppermute(stack_b, 'dp', SHIFT_X[d])]
  transfers between devices with their start and end apart: 39 -> 40, of which waited for: 23 -> 21; matrix products, arithmetic and copies ran while one was open for 9% -> 10% of each run, Pallas kernels for 5% -> 5%
where the time goes in v5:
time: 202 us; the launch traced here: 201 us
  starting transfers between devices  74.1 us (37%)
  waiting for transfers between devices  65.5 us (32%)
  Pallas kernels  20.8 us (10%)
  matrix products  14 us (7%)
  blocking collectives  13.4 us (7%)
  other arithmetic  6.68 us (3%)
  local copies, waits for them, and re-layouts  6.03 us (3%)
    ppermute x8, starting transfers between devices, swap_cores(): return lax.ppermute(a, 'side', SWAP)  18.1 us
    ppermute x6, starting transfers between devices, shards(): got = [lax.ppermute(rows[d], 'dp', far[d]) for d in (1, 3, 2)]  14.7 us
    ppermute x6, starting transfers between devices, shards(): got = [lax.ppermute(sums[d], 'dp', near[d]) for d in (1, 3, 2)]  14 us
    all_to_all x1, blocking collectives, shards(): lax.all_to_all(routed.reshape(8, 32, 384), 'tensor', split_axis=0, concat...  13.4 us
    pallas_call x6, Pallas kernels, local_call(): pl.pallas_call(kernel, in_specs=first + [vmem] * (len(args) - len(first))...  12.6 us
    ppermute x2, waiting for transfers between devices, shards(): lax.ppermute(stack_a, 'dp', SHIFT_Y[d])  11.1 us
    ppermute x3, waiting for transfers between devices, shards(): lax.ppermute(rows_x, 'dp', SHIFT_Y[d])  10.6 us
    all_to_all x1, starting transfers between devices, shards(): lax.all_to_all(head_sums, 'tensor', split_axis=0, concat_axis=0, tiled=True)  8.18 us
  transfers between devices with their start and end apart: 40, of which 21 were waited for; matrix products, arithmetic and copies ran while one was open for 10% of the time, Pallas kernels for 5%

profile of v5, /device:TPU:1, one launch (start us, length us, event | category | flops | bytes accessed | tf_op | source)
XLA Modules:
  0.0 200.9 jit_solution(13306437325317788684)
XLA Ops:
  0.0 5.3 %attend.1 = bf16[32,768]{1,0:T(8,128)(2,1)} custom-call(s32[32]{0:T(128)} %lengths.1, bf16[32,768]{1,0:T(8,128)(2,1)} %q_in.1, bf16[32,128]{1,0:T(8,128)(2,1)} %k_in.1, bf16[32,128]{1,0:T(8,128)(2,1)} %v_in.1, bf16[32,192,128]{2,1,0:T(8,128)(2,1)} %keys.1, bf16[32,192,128]{2,1,0:T(8,128)(2,1)} %values.1), custom_call_target="tpu_custom_call" | custom-call | tf_op jit(solution)/shard_map/attend/pallas_call | solution.py:194
  5.4 3.4 %collective-permute-start.2 = (bf16[32,768]{1,0:T(8,128)(2,1)}, bf16[32,768]{1,0:T(8,128)(2,1)S(1)}, u32[]{:S(2)}, u32[]{:S(2)}) collective-permute-start(bf16[32,768]{1,0:T(8,128)(2,1)} %attend.1), channel_id=1, source_target_pairs={{0,192},{16,208},{32,224},{48,240},{64,0},{80,16},{96,32},{112,48}... | collective-permute-start | bytes 147464 | tf_op jit(solution)/shard_map/ppermute | solution.py:280
  9.9 1.5 collective-permute-start.6
  11.4 2.0 %collective-permute-done.1 = bf16[32,768]{1,0:T(8,128)(2,1)S(1)} collective-permute-done((bf16[32,768]{1,0:T(8,128)(2,1)}, bf16[32,768]{1,0:T(8,128)(2,1)S(1)}, u32[]{:S(2)}, u32[]{:S(2)}) %collective-permute-start.1) | collective-permute-done | bytes 49184 | tf_op jit(solution)/shard_map/ppermute | solution.py:280
  14.8 2.8 %collective-permute-start.5 = (bf16[4,32,768]{2,1,0:T(8,128)(2,1)S(1)}, bf16[4,32,768]{2,1,0:T(8,128)(2,1)S(1)}, u32[]{:S(2)}, u32[]{:S(2)}) collective-permute-start(bf16[4,32,768]{2,1,0:T(8,128)(2,1)S(1)} %pad_maximum_fusion.7.g0), channel_id=1, source_target_pairs={{0,48},{16,0},{32,16},{48,32},{64,112},{80,64},{96,80},{112,96},{1... | collective-permute-start | bytes 589832 | tf_op jit(solution)/shard_map/ppermute | solution.py:284
  18.7 3.6 %collective-permute-done.5.g3 = bf16[4,32,768]{2,1,0:T(8,128)(2,1)S(1)} collective-permute-done((bf16[4,32,768]{2,1,0:T(8,128)(2,1)S(1)}, bf16[4,32,768]{2,1,0:T(8,128)(2,1)S(1)}, u32[]{:S(2)}, u32[]{:S(2)}) %collective-permute-start.5) | collective-permute-done | bytes 196640 | tf_op jit(solution)/shard_map/ppermute | solution.py:284
  22.3 1.5 collective-permute-done.4.g2
  23.8 5.5 %collective-permute-done.3.g1 = bf16[4,32,768]{2,1,0:T(8,128)(2,1)} collective-permute-done((bf16[4,32,768]{2,1,0:T(8,128)(2,1)S(1)}, bf16[4,32,768]{2,1,0:T(8,128)(2,1)}, u32[]{:S(2)}, u32[]{:S(2)}) %collective-permute-start.3) | collective-permute-done | bytes 196640 | tf_op jit(solution)/shard_map/ppermute | solution.py:284
  29.3 2.8 %out_projection.1 = bf16[8,64,384]{2,1,0:T(8,128)(2,1)} custom-call(s32[3]{0:T(128)S(1)} %pad_add_fusion.pos, bf16[4,32,768]{2,1,0:T(8,128)(2,1)S(1)} %pad_maximum_fusion.7.g0, bf16[4,32,768]{2,1,0:T(8,128)(2,1)} %collective-permute-done.3.g1, bf16[4,32,768]{2,1,0:T(8,128)(2,1)} %collective-permute-done.4.g2, ...), custom_call_target="tpu_custom_call" | custom-call | tf_op jit(solution)/shard_map/out_projection/pallas_call | solution.py:286
  32.1 8.2 %all-to-all-start = ((bf16[8,64,384]{2,1,0:T(8,128)(2,1)}), bf16[8,64,384]{2,1,0:T(8,128)(2,1)S(1)}, u32[]{:S(2)}, u32[]{:S(2)}) async-start(bf16[8,64,384]{2,1,0:T(8,128)(2,1)} %out_projection.1), calls=%async_computation | async-start | bytes 786432 | tf_op jit(solution)/shard_map/all_to_all | solution.py:295
  40.3 1.5 copy.23
  41.8 1.7 collective-permute-start.7
  46.4 6.3 %all-to-all-done = bf16[8,64,384]{2,1,0:T(8,128)(2,1)S(1)} async-done(((bf16[8,64,384]{2,1,0:T(8,128)(2,1)}), bf16[8,64,384]{2,1,0:T(8,128)(2,1)S(1)}, u32[]{:S(2)}, u32[]{:S(2)}) %all-to-all-start) | async-done | bytes 393248 | tf_op jit(solution)/shard_map/all_to_all | solution.py:295
  53.7 3.3 %collective-permute-start.8 = (bf16[64,384]{1,0:T(8,128)(2,1)S(1)}, bf16[64,384]{1,0:T(8,128)(2,1)S(1)}, u32[]{:S(2)}, u32[]{:S(2)}) collective-permute-start(bf16[64,384]{1,0:T(8,128)(2,1)S(1)} %fusion.26), channel_id=1, source_target_pairs={{0,1},{1,0},{2,3},{3,2},{4,5},{5,4},{6,7},{7,6},{8,9},{9,8},{10,11... | collective-permute-start | bytes 147464 | tf_op jit(solution)/shard_map/ppermute | solution.py:22
  58.3 13.4 %all_to_all.15 = bf16[8,32,384]{2,1,0:T(8,128)(2,1)S(1)} all-to-all(bf16[8,32,384]{2,1,0:T(8,128)(2,1)S(1)} %bitcast.94), channel_id=1, replica_groups=mesh['dp'=16,'tensor'=8,'side'=2] {'tensor'}, dimensions={0} | all-to-all | bytes 393216 | tf_op jit(solution)/shard_map/all_to_all | solution.py:304
  74.0 1.8 collective-permute-done.11
  75.7 2.0 collective-permute-done.10
  77.8 3.1 %collective-permute-done.9 = bf16[128,384]{1,0:T(8,128)(2,1)S(1)} collective-permute-done((bf16[128,384]{1,0:T(8,128)(2,1)S(1)}, bf16[128,384]{1,0:T(8,128)(2,1)S(1)}, u32[]{:S(2)}, u32[]{:S(2)}) %collective-permute-start.9) | collective-permute-done | bytes 98336 | tf_op jit(solution)/shard_map/ppermute | solution.py:310
  82.7 2.1 %collective-permute-start.20 = (bf16[4,128,384]{2,1,0:T(8,128)(2,1)S(1)}, bf16[4,128,384]{2,1,0:T(8,128)(2,1)S(1)}, u32[]{:S(2)}, u32[]{:S(2)}) collective-permute-start(bf16[4,128,384]{2,1,0:T(8,128)(2,1)S(1)} %pad_maximum_fusion.5.s0), channel_id=1, source_target_pairs={{0,192},{16,208},{32,224},{48,240},{64,0},{80,16},{96,32},{112,48}... | collective-permute-start | bytes 1179656 | tf_op jit(solution)/shard_map/ppermute | solution.py:316
  84.7 6.9 %collective-permute-done.16.s1 = bf16[4,128,384]{2,1,0:T(8,128)(2,1)S(1)} collective-permute-done((bf16[4,128,384]{2,1,0:T(8,128)(2,1)S(1)}, bf16[4,128,384]{2,1,0:T(8,128)(2,1)S(1)}, u32[]{:S(2)}, u32[]{:S(2)}) %collective-permute-start.16) | collective-permute-done | bytes 393248 | tf_op jit(solution)/shard_map/ppermute | solution.py:316
  92.3 1.9 collective-permute-start.19
  94.2 7.1 %collective-permute-done.19.s2 = bf16[4,128,384]{2,1,0:T(8,128)(2,1)S(1)} collective-permute-done((bf16[4,128,384]{2,1,0:T(8,128)(2,1)S(1)}, bf16[4,128,384]{2,1,0:T(8,128)(2,1)S(1)}, u32[]{:S(2)}, u32[]{:S(2)}) %collective-permute-start.19) | collective-permute-done | bytes 393248 | tf_op jit(solution)/shard_map/ppermute | solution.py:319
  102.1 1.8 norm.3
  103.9 4.1 %collective-permute-start.29 = (bf16[128,6144]{1,0:T(8,128)(2,1)S(1)}, bf16[128,6144]{1,0:T(8,128)(2,1)S(1)}, u32[]{:S(2)}, u32[]{:S(2)}) collective-permute-start(bf16[128,6144]{1,0:T(8,128)(2,1)S(1)} %norm.3), channel_id=1, source_target_pairs={{0,1},{1,0},{2,3},{3,2},{4,5},{5,4},{6,7},{7,6},{8,9},{9,8},{10,11... | collective-permute-start | bytes 4718600 | tf_op jit(solution)/shard_map/ppermute | solution.py:22
  108.3 10.3 %collective-permute-done.18.s3 = bf16[4,128,384]{2,1,0:T(8,128)(2,1)S(1)} collective-permute-done((bf16[4,128,384]{2,1,0:T(8,128)(2,1)S(1)}, bf16[4,128,384]{2,1,0:T(8,128)(2,1)S(1)}, u32[]{:S(2)}, u32[]{:S(2)}) %collective-permute-start.18) | collective-permute-done | bytes 393248 | tf_op jit(solution)/shard_map/ppermute | solution.py:315
  119.9 1.8 norm.2
  121.8 1.3 collective-permute-start.21
  126.4 1.8 convolution_convert_fusion.1
  130.6 1.8 convolution_convert_fusion.2
  133.4 2.8 %combine_cores.3 = (bf16[4,128,384]{2,1,0:T(8,128)(2,1)S(1)}, bf16[4,128,384]{2,1,0:T(8,128)(2,1)}, bf16[4,128,384]{2,1,0:T(8,128)(2,1)}, bf16[4,128,384]{2,1,0:T(8,128)(2,1)}) custom-call(s32[3]{0:T(128)S(1)} %pad_add_fusion.pos, bf16[256,6144]{1,0:T(8,128)(2,1)S(1)} %convolution_convert_fusion.own, bf16[128,6144]{1,0:T(8,128)(2,1)} %collective-permute-done.30.other), custom_call_target="tpu_custom_call" | custom-call | tf_op jit(solution)/shard_map/combine_cores/pallas_call | solution.py:112
  136.2 1.5 collective-permute-start.31
  137.9 1.7 collective-permute-start.32
  139.5 1.2 collective-permute-start.33
  140.8 2.5 %combine_cores.2 = (bf16[4,128,384]{2,1,0:T(8,128)(2,1)S(1)}, bf16[4,128,384]{2,1,0:T(8,128)(2,1)}, bf16[4,128,384]{2,1,0:T(8,128)(2,1)S(1)}, bf16[4,128,384]{2,1,0:T(8,128)(2,1)S(1)}) custom-call(s32[3]{0:T(128)S(1)} %pad_add_fusion.pos, bf16[256,6144]{1,0:T(8,128)(2,1)S(1)} %convolution_convert_fusion.own, bf16[128,6144]{1,0:T(8,128)(2,1)} %collective-permute-done.22.other), custom_call_target="tpu_custom_call" | custom-call | tf_op jit(solution)/shard_map/combine_cores/pallas_call | solution.py:112
  144.7 6.0 %collective-permute-start.23 = (bf16[4,128,384]{2,1,0:T(8,128)(2,1)}, bf16[4,128,384]{2,1,0:T(8,128)(2,1)}, u32[]{:S(2)}, u32[]{:S(2)}) collective-permute-start(bf16[4,128,384]{2,1,0:T(8,128)(2,1)} %get-tuple-element.46), channel_id=1, source_target_pairs={{0,16},{16,32},{32,48},{48,0},{64,80},{80,96},{96,112},{112,64},{1... | collective-permute-start | bytes 1179656 | tf_op jit(solution)/shard_map/ppermute | solution.py:357
  151.1 2.4 %collective-permute-start.24 = (bf16[4,128,384]{2,1,0:T(8,128)(2,1)}, bf16[4,128,384]{2,1,0:T(8,128)(2,1)}, u32[]{:S(2)}, u32[]{:S(2)}) collective-permute-start(bf16[4,128,384]{2,1,0:T(8,128)(2,1)} %copy-done.8), channel_id=1, source_target_pairs={{0,48},{16,0},{32,16},{48,32},{64,112},{80,64},{96,80},{112,96},{1... | collective-permute-start | bytes 1179656 | tf_op jit(solution)/shard_map/ppermute | solution.py:357
  153.4 1.3 collective-permute-start.25
  154.7 2.8 %fusion.16 = f32[256]{0:T(256)S(1)} fusion(bf16[6144,8]{0,1:T(8,128)(2,1)} %param.23, bf16[128,6144]{1,0:T(8,128)(2,1)} %copy-done.1, bf16[128,6144]{1,0:T(8,128)(2,1)} %copy-done.2, s32[256]{0:T(256)S(1)} %eq.144, f32[8]{0:T(128)S(1)} %compare_convert_fusion), kind=kOutput, calls=%fused_computation.24 | convolution fusion | flops 31467264 | bytes 3246112 | tf_op jit(solution)/shard_map/dot_general | solution.py:336
  158.0 2.2 %sum_rows.3 = (f32[128,384]{1,0:T(8,128)S(1)}, bf16[128,384]{1,0:T(8,128)(2,1)}, bf16[128,384]{1,0:T(8,128)(2,1)}, bf16[128,384]{1,0:T(8,128)(2,1)}) custom-call(bf16[4,128,384]{2,1,0:T(8,128)(2,1)S(1)} %copy-done.4, bf16[4,128,384]{2,1,0:T(8,128)(2,1)} %collective-permute-done.31.got1, bf16[4,128,384]{2,1,0:T(8,128)(2,1)} %collective-permute-done.32.got2, ...), custom_call_target="tpu_custom_call" | custom-call | tf_op jit(solution)/shard_map/sum_rows/pallas_call | solution.py:112
  160.8 6.0 %collective-permute-start.34 = (bf16[128,384]{1,0:T(8,128)(2,1)}, bf16[128,384]{1,0:T(8,128)(2,1)}, u32[]{:S(2)}, u32[]{:S(2)}) collective-permute-start(bf16[128,384]{1,0:T(8,128)(2,1)} %get-tuple-element.58), channel_id=1, source_target_pairs={{0,16},{16,32},{32,48},{48,0},{64,80},{80,96},{96,112},{112,64},{1... | collective-permute-start | bytes 294920 | tf_op jit(solution)/shard_map/ppermute | solution.py:366
  166.8 2.1 %collective-permute-start.35 = (bf16[128,384]{1,0:T(8,128)(2,1)}, bf16[128,384]{1,0:T(8,128)(2,1)}, u32[]{:S(2)}, u32[]{:S(2)}) collective-permute-start(bf16[128,384]{1,0:T(8,128)(2,1)} %get-tuple-element.59), channel_id=1, source_target_pairs={{0,48},{16,0},{32,16},{48,32},{64,112},{80,64},{96,80},{112,96},{1... | collective-permute-start | bytes 294920 | tf_op jit(solution)/shard_map/ppermute | solution.py:366
  170.8 1.4 sum_rows.2
  173.0 2.0 %collective-permute-start.27 = (bf16[128,384]{1,0:T(8,128)(2,1)S(1)}, bf16[128,384]{1,0:T(8,128)(2,1)S(1)}, u32[]{:S(2)}, u32[]{:S(2)}) collective-permute-start(bf16[128,384]{1,0:T(8,128)(2,1)S(1)} %get-tuple-element.51), channel_id=1, source_target_pairs={{0,192},{16,208},{32,224},{48,240},{64,0},{80,16},{96,32},{112,48}... | collective-permute-start | bytes 294920 | tf_op jit(solution)/shard_map/ppermute | solution.py:366
  175.4 2.6 %collective-permute-start.28 = (bf16[128,384]{1,0:T(8,128)(2,1)S(1)}, bf16[128,384]{1,0:T(8,128)(2,1)S(1)}, u32[]{:S(2)}, u32[]{:S(2)}) collective-permute-start(bf16[128,384]{1,0:T(8,128)(2,1)S(1)} %get-tuple-element.52), channel_id=1, source_target_pairs={{0,128},{16,144},{32,160},{48,176},{64,192},{80,208},{96,224},{112... | collective-permute-start | bytes 294920 | tf_op jit(solution)/shard_map/ppermute | solution.py:366
  179.1 1.7 collective-permute-done.28
  181.7 3.4 %all-to-all-start.2 = ((bf16[8,32,384]{2,1,0:T(8,128)(2,1)}), bf16[8,32,384]{2,1,0:T(8,128)(2,1)S(1)}, u32[]{:S(2)}, u32[]{:S(2)}) async-start(bf16[8,32,384]{2,1,0:T(8,128)(2,1)} %multiply_convert_fusion), calls=%async_computation.2 | async-start | bytes 393216 | tf_op jit(solution)/shard_map/all_to_all | solution.py:371
  186.1 7.7 %all-to-all-done.2 = bf16[8,32,384]{2,1,0:T(8,128)(2,1)S(1)} async-done(((bf16[8,32,384]{2,1,0:T(8,128)(2,1)}), bf16[8,32,384]{2,1,0:T(8,128)(2,1)S(1)}, u32[]{:S(2)}, u32[]{:S(2)}) %all-to-all-start.2) | async-done | bytes 196640 | tf_op jit(solution)/shard_map/all_to_all | solution.py:371
  193.9 5.1 %collective-permute-start.37 = (bf16[256,192]{1,0:T(8,128)(2,1)S(1)}, bf16[256,192]{1,0:T(8,128)(2,1)S(1)}, u32[]{:S(2)}, u32[]{:S(2)}) collective-permute-start(bf16[256,192]{1,0:T(8,128)(2,1)S(1)} %broadcast_select_fusion), channel_id=1, source_target_pairs={{0,1},{1,0},{2,3},{3,2},{4,5},{5,4},{6,7},{7,6},{8,9},{9,8},{10,11... | collective-permute-start | bytes 294920 | tf_op jit(solution)/shard_map/ppermute | solution.py:22
  (122 shorter events, 33.3 us)
Async XLA Ops:
  0.0 126.4 %copy-start = (bf16[1,256,6144]{2,1,0:T(8,128)(2,1)S(1)}, bf16[1,256,6144]{2,1,0:T(8,128)(2,1)}, u32[]{:S(2)}) copy-start(bf16[1,256,6144]{2,1,0:T(8,128)(2,1)} %param.27) | copy-start | bytes 9437188
  0.0 43.5 %copy-start.14 = (s32[1024,2]{0,1:T(2,128)S(1)}, s32[1024,2]{0,1:T(2,128)}, u32[]{:S(2)}) copy-start(s32[1024,2]{0,1:T(2,128)} %param.24) | copy-start | bytes 24580
  5.4 6.0 %collective-permute-start.2 = (bf16[32,768]{1,0:T(8,128)(2,1)}, bf16[32,768]{1,0:T(8,128)(2,1)S(1)}, u32[]{:S(2)}, u32[]{:S(2)}) collective-permute-start(bf16[32,768]{1,0:T(8,128)(2,1)} %attend.1), channel_id=1, source_target_pairs={{0,192},{16,208},{32,224},{48,240},{64,0},{80,16},{96,32},{112,48}... | collective-permute-start | bytes 147464 | tf_op jit(solution)/shard_map/ppermute | solution.py:280
  8.7 4.7 %collective-permute-start.1 = (bf16[32,768]{1,0:T(8,128)(2,1)}, bf16[32,768]{1,0:T(8,128)(2,1)S(1)}, u32[]{:S(2)}, u32[]{:S(2)}) collective-permute-start(bf16[32,768]{1,0:T(8,128)(2,1)} %attend.1), channel_id=1, source_target_pairs={{0,128},{16,144},{32,160},{48,176},{64,192},{80,208},{96,224},{112... | collective-permute-start | bytes 147464 | tf_op jit(solution)/shard_map/ppermute | solution.py:280
  9.3 4.7 %collective-permute-start = (bf16[32,768]{1,0:T(8,128)(2,1)}, bf16[32,768]{1,0:T(8,128)(2,1)S(1)}, u32[]{:S(2)}, u32[]{:S(2)}) collective-permute-start(bf16[32,768]{1,0:T(8,128)(2,1)} %attend.1), channel_id=1, source_target_pairs={{0,64},{16,80},{32,96},{48,112},{64,128},{80,144},{96,160},{112,17... | collective-permute-start | bytes 147464 | tf_op jit(solution)/shard_map/ppermute | solution.py:280
  9.9 19.4 %collective-permute-start.6 = (bf16[192,768]{1,0:T(8,128)(2,1)}, bf16[192,768]{1,0:T(8,128)(2,1)}, u32[]{:S(2)}, u32[]{:S(2)}) collective-permute-start(bf16[192,768]{1,0:T(8,128)(2,1)} %bitcast.7.w_own), channel_id=1, source_target_pairs={{0,1},{1,0},{2,3},{3,2},{4,5},{5,4},{6,7},{7,6},{8,9},{9,8},{10,11... | collective-permute-start | bytes 884744 | tf_op jit(solution)/shard_map/ppermute | solution.py:22
  14.8 7.5 %collective-permute-start.5 = (bf16[4,32,768]{2,1,0:T(8,128)(2,1)S(1)}, bf16[4,32,768]{2,1,0:T(8,128)(2,1)S(1)}, u32[]{:S(2)}, u32[]{:S(2)}) collective-permute-start(bf16[4,32,768]{2,1,0:T(8,128)(2,1)S(1)} %pad_maximum_fusion.7.g0), channel_id=1, source_target_pairs={{0,48},{16,0},{32,16},{48,32},{64,112},{80,64},{96,80},{112,96},{1... | collective-permute-start | bytes 589832 | tf_op jit(solution)/shard_map/ppermute | solution.py:284
  17.6 6.2 %collective-permute-start.4 = (bf16[4,32,768]{2,1,0:T(8,128)(2,1)S(1)}, bf16[4,32,768]{2,1,0:T(8,128)(2,1)}, u32[]{:S(2)}, u32[]{:S(2)}) collective-permute-start(bf16[4,32,768]{2,1,0:T(8,128)(2,1)S(1)} %pad_maximum_fusion.7.g0), channel_id=1, source_target_pairs={{0,32},{16,48},{32,0},{48,16},{64,96},{80,112},{96,64},{112,80},{1... | collective-permute-start | bytes 589832 | tf_op jit(solution)/shard_map/ppermute | solution.py:284
  17.9 11.4 %collective-permute-start.3 = (bf16[4,32,768]{2,1,0:T(8,128)(2,1)S(1)}, bf16[4,32,768]{2,1,0:T(8,128)(2,1)}, u32[]{:S(2)}, u32[]{:S(2)}) collective-permute-start(bf16[4,32,768]{2,1,0:T(8,128)(2,1)S(1)} %pad_maximum_fusion.7.g0), channel_id=1, source_target_pairs={{0,16},{16,32},{32,48},{48,0},{64,80},{80,96},{96,112},{112,64},{1... | collective-permute-start | bytes 589832 | tf_op jit(solution)/shard_map/ppermute | solution.py:284
  32.1 20.6 %all-to-all-start = ((bf16[8,64,384]{2,1,0:T(8,128)(2,1)}), bf16[8,64,384]{2,1,0:T(8,128)(2,1)S(1)}, u32[]{:S(2)}, u32[]{:S(2)}) async-start(bf16[8,64,384]{2,1,0:T(8,128)(2,1)} %out_projection.1), calls=%async_computation | async-start | bytes 786432 | tf_op jit(solution)/shard_map/all_to_all | solution.py:295
  41.8 2.9 %collective-permute-start.7 = (bf16[128,192]{1,0:T(8,128)(2,1)}, bf16[128,192]{1,0:T(8,128)(2,1)}, u32[]{:S(2)}, u32[]{:S(2)}) collective-permute-start(bf16[128,192]{1,0:T(8,128)(2,1)} %copy.23), channel_id=1, source_target_pairs={{0,1},{1,0},{2,3},{3,2},{4,5},{5,4},{6,7},{7,6},{8,9},{9,8},{10,11... | collective-permute-start | bytes 147464 | tf_op jit(solution)/shard_map/ppermute | solution.py:22
  53.7 4.4 %collective-permute-start.8 = (bf16[64,384]{1,0:T(8,128)(2,1)S(1)}, bf16[64,384]{1,0:T(8,128)(2,1)S(1)}, u32[]{:S(2)}, u32[]{:S(2)}) collective-permute-start(bf16[64,384]{1,0:T(8,128)(2,1)S(1)} %fusion.26), channel_id=1, source_target_pairs={{0,1},{1,0},{2,3},{3,2},{4,5},{5,4},{6,7},{7,6},{8,9},{9,8},{10,11... | collective-permute-start | bytes 147464 | tf_op jit(solution)/shard_map/ppermute | solution.py:22
  58.1 23.6 %copy-start.11 = (bf16[128,384]{1,0:T(8,128)(2,1)}, bf16[128,384]{1,0:T(8,128)(2,1)S(1)}, u32[]{:S(2)}) copy-start(bf16[128,384]{1,0:T(8,128)(2,1)S(1)} %maximum_select_fusion.1) | copy-start | bytes 294916
  71.7 4.0 %collective-permute-start.11 = (bf16[128,384]{1,0:T(8,128)(2,1)S(1)}, bf16[128,384]{1,0:T(8,128)(2,1)S(1)}, u32[]{:S(2)}, u32[]{:S(2)}) collective-permute-start(bf16[128,384]{1,0:T(8,128)(2,1)S(1)} %bitcast.96), channel_id=1, source_target_pairs={{0,192},{16,208},{32,224},{48,240},{64,0},{80,16},{96,32},{112,48}... | collective-permute-start | bytes 294920 | tf_op jit(solution)/shard_map/ppermute | solution.py:310
  72.7 5.1 %collective-permute-start.10 = (bf16[128,384]{1,0:T(8,128)(2,1)S(1)}, bf16[128,384]{1,0:T(8,128)(2,1)S(1)}, u32[]{:S(2)}, u32[]{:S(2)}) collective-permute-start(bf16[128,384]{1,0:T(8,128)(2,1)S(1)} %bitcast.97), channel_id=1, source_target_pairs={{0,128},{16,144},{32,160},{48,176},{64,192},{80,208},{96,224},{112... | collective-permute-start | bytes 294920 | tf_op jit(solution)/shard_map/ppermute | solution.py:310
  73.2 7.7 %collective-permute-start.9 = (bf16[128,384]{1,0:T(8,128)(2,1)S(1)}, bf16[128,384]{1,0:T(8,128)(2,1)S(1)}, u32[]{:S(2)}, u32[]{:S(2)}) collective-permute-start(bf16[128,384]{1,0:T(8,128)(2,1)S(1)} %bitcast.98), channel_id=1, source_target_pairs={{0,64},{16,80},{32,96},{48,112},{64,128},{80,144},{96,160},{112,17... | collective-permute-start | bytes 294920 | tf_op jit(solution)/shard_map/ppermute | solution.py:310
  73.9 6.9 %collective-permute-start.14 = (bf16[128,384]{1,0:T(8,128)(2,1)S(1)}, bf16[128,384]{1,0:T(8,128)(2,1)S(1)}, u32[]{:S(2)}, u32[]{:S(2)}) collective-permute-start(bf16[128,384]{1,0:T(8,128)(2,1)S(1)} %bitcast.100), channel_id=1, source_target_pairs={{0,48},{16,0},{32,16},{48,32},{64,112},{80,64},{96,80},{112,96},{1... | collective-permute-start | bytes 294920 | tf_op jit(solution)/shard_map/ppermute | solution.py:311
  74.0 6.9 %collective-permute-start.13 = (bf16[128,384]{1,0:T(8,128)(2,1)S(1)}, bf16[128,384]{1,0:T(8,128)(2,1)S(1)}, u32[]{:S(2)}, u32[]{:S(2)}) collective-permute-start(bf16[128,384]{1,0:T(8,128)(2,1)S(1)} %bitcast.101), channel_id=1, source_target_pairs={{0,32},{16,48},{32,0},{48,16},{64,96},{80,112},{96,64},{112,80},{1... | collective-permute-start | bytes 294920 | tf_op jit(solution)/shard_map/ppermute | solution.py:311
  75.7 5.9 %collective-permute-start.12 = (bf16[128,384]{1,0:T(8,128)(2,1)S(1)}, bf16[128,384]{1,0:T(8,128)(2,1)S(1)}, u32[]{:S(2)}, u32[]{:S(2)}) collective-permute-start(bf16[128,384]{1,0:T(8,128)(2,1)S(1)} %bitcast.102), channel_id=1, source_target_pairs={{0,16},{16,32},{32,48},{48,0},{64,80},{80,96},{96,112},{112,64},{1... | collective-permute-start | bytes 294920 | tf_op jit(solution)/shard_map/ppermute | solution.py:311
  81.8 9.8 %collective-permute-start.16 = (bf16[4,128,384]{2,1,0:T(8,128)(2,1)S(1)}, bf16[4,128,384]{2,1,0:T(8,128)(2,1)S(1)}, u32[]{:S(2)}, u32[]{:S(2)}) collective-permute-start(bf16[4,128,384]{2,1,0:T(8,128)(2,1)S(1)} %pad_maximum_fusion.5.s0), channel_id=1, source_target_pairs={{0,64},{16,80},{32,96},{48,112},{64,128},{80,144},{96,160},{112,17... | collective-permute-start | bytes 1179656 | tf_op jit(solution)/shard_map/ppermute | solution.py:316
  82.6 9.7 %collective-permute-start.15 = (bf16[4,128,384]{2,1,0:T(8,128)(2,1)S(1)}, bf16[4,128,384]{2,1,0:T(8,128)(2,1)S(1)}, u32[]{:S(2)}, u32[]{:S(2)}) collective-permute-start(bf16[4,128,384]{2,1,0:T(8,128)(2,1)S(1)} %pad_maximum_fusion.4.s0), channel_id=1, source_target_pairs={{0,16},{16,32},{32,48},{48,0},{64,80},{80,96},{96,112},{112,64},{1... | collective-permute-start | bytes 1179656 | tf_op jit(solution)/shard_map/ppermute | solution.py:315
  82.7 11.6 %collective-permute-start.20 = (bf16[4,128,384]{2,1,0:T(8,128)(2,1)S(1)}, bf16[4,128,384]{2,1,0:T(8,128)(2,1)S(1)}, u32[]{:S(2)}, u32[]{:S(2)}) collective-permute-start(bf16[4,128,384]{2,1,0:T(8,128)(2,1)S(1)} %pad_maximum_fusion.5.s0), channel_id=1, source_target_pairs={{0,192},{16,208},{32,224},{48,240},{64,0},{80,16},{96,32},{112,48}... | collective-permute-start | bytes 1179656 | tf_op jit(solution)/shard_map/ppermute | solution.py:316
  92.3 9.0 %collective-permute-start.19 = (bf16[4,128,384]{2,1,0:T(8,128)(2,1)S(1)}, bf16[4,128,384]{2,1,0:T(8,128)(2,1)S(1)}, u32[]{:S(2)}, u32[]{:S(2)}) collective-permute-start(bf16[4,128,384]{2,1,0:T(8,128)(2,1)S(1)} %pad_maximum_fusion.5.s0), channel_id=1, source_target_pairs={{0,128},{16,144},{32,160},{48,176},{64,192},{80,208},{96,224},{112... | collective-permute-start | bytes 1179656 | tf_op jit(solution)/shard_map/ppermute | solution.py:319
  102.1 21.0 %copy-start.9 = (bf16[1,6144,256]{2,1,0:T(8,128)(2,1)S(1)}, bf16[1,6144,256]{2,1,0:T(8,128)(2,1)}, u32[]{:S(2)}) copy-start(bf16[1,6144,256]{2,1,0:T(8,128)(2,1)} %param.25) | copy-start | bytes 9437188
  103.9 20.1 %copy-start.1 = (bf16[128,6144]{1,0:T(8,128)(2,1)}, bf16[128,6144]{1,0:T(8,128)(2,1)S(1)}, u32[]{:S(2)}) copy-start(bf16[128,6144]{1,0:T(8,128)(2,1)S(1)} %norm.3) | copy-start | bytes 4718596
  103.9 21.3 %collective-permute-start.29 = (bf16[128,6144]{1,0:T(8,128)(2,1)S(1)}, bf16[128,6144]{1,0:T(8,128)(2,1)S(1)}, u32[]{:S(2)}, u32[]{:S(2)}) collective-permute-start(bf16[128,6144]{1,0:T(8,128)(2,1)S(1)} %norm.3), channel_id=1, source_target_pairs={{0,1},{1,0},{2,3},{3,2},{4,5},{5,4},{6,7},{7,6},{8,9},{9,8},{10,11... | collective-permute-start | bytes 4718600 | tf_op jit(solution)/shard_map/ppermute | solution.py:22
  108.0 10.7 %collective-permute-start.18 = (bf16[4,128,384]{2,1,0:T(8,128)(2,1)S(1)}, bf16[4,128,384]{2,1,0:T(8,128)(2,1)S(1)}, u32[]{:S(2)}, u32[]{:S(2)}) collective-permute-start(bf16[4,128,384]{2,1,0:T(8,128)(2,1)S(1)} %pad_maximum_fusion.4.s0), channel_id=1, source_target_pairs={{0,48},{16,0},{32,16},{48,32},{64,112},{80,64},{96,80},{112,96},{1... | collective-permute-start | bytes 1179656 | tf_op jit(solution)/shard_map/ppermute | solution.py:315
  108.1 11.8 %collective-permute-start.17 = (bf16[4,128,384]{2,1,0:T(8,128)(2,1)S(1)}, bf16[4,128,384]{2,1,0:T(8,128)(2,1)S(1)}, u32[]{:S(2)}, u32[]{:S(2)}) collective-permute-start(bf16[4,128,384]{2,1,0:T(8,128)(2,1)S(1)} %pad_maximum_fusion.4.s0), channel_id=1, source_target_pairs={{0,32},{16,48},{32,0},{48,16},{64,96},{80,112},{96,64},{112,80},{1... | collective-permute-start | bytes 1179656 | tf_op jit(solution)/shard_map/ppermute | solution.py:319
  121.8 7.6 %collective-permute-start.21 = (bf16[128,6144]{1,0:T(8,128)(2,1)S(1)}, bf16[128,6144]{1,0:T(8,128)(2,1)S(1)}, u32[]{:S(2)}, u32[]{:S(2)}) collective-permute-start(bf16[128,6144]{1,0:T(8,128)(2,1)S(1)} %norm.2), channel_id=1, source_target_pairs={{0,1},{1,0},{2,3},{3,2},{4,5},{5,4},{6,7},{7,6},{8,9},{9,8},{10,11... | collective-permute-start | bytes 4718600 | tf_op jit(solution)/shard_map/ppermute | solution.py:22
  128.2 5.2 %collective-permute-start.30 = (bf16[128,6144]{1,0:T(8,128)(2,1)}, bf16[128,6144]{1,0:T(8,128)(2,1)}, u32[]{:S(2)}, u32[]{:S(2)}) collective-permute-start(bf16[128,6144]{1,0:T(8,128)(2,1)} %convolution_convert_fusion.1), channel_id=1, source_target_pairs={{0,1},{1,0},{2,3},{3,2},{4,5},{5,4},{6,7},{7,6},{8,9},{9,8},{10,11... | collective-permute-start | bytes 4718600 | tf_op jit(solution)/shard_map/ppermute | solution.py:22
  132.3 8.4 %collective-permute-start.22 = (bf16[128,6144]{1,0:T(8,128)(2,1)}, bf16[128,6144]{1,0:T(8,128)(2,1)}, u32[]{:S(2)}, u32[]{:S(2)}) collective-permute-start(bf16[128,6144]{1,0:T(8,128)(2,1)} %convolution_convert_fusion.2), channel_id=1, source_target_pairs={{0,1},{1,0},{2,3},{3,2},{4,5},{5,4},{6,7},{7,6},{8,9},{9,8},{10,11... | collective-permute-start | bytes 4718600 | tf_op jit(solution)/shard_map/ppermute | solution.py:22
  136.2 7.0 %copy-start.3 = (bf16[4,128,384]{2,1,0:T(8,128)(2,1)}, bf16[4,128,384]{2,1,0:T(8,128)(2,1)S(1)}, u32[]{:S(2)}) copy-start(bf16[4,128,384]{2,1,0:T(8,128)(2,1)S(1)} %get-tuple-element.53.mine) | copy-start | bytes 1179652
  136.2 17.2 %collective-permute-start.31 = (bf16[4,128,384]{2,1,0:T(8,128)(2,1)}, bf16[4,128,384]{2,1,0:T(8,128)(2,1)}, u32[]{:S(2)}, u32[]{:S(2)}) collective-permute-start(bf16[4,128,384]{2,1,0:T(8,128)(2,1)} %get-tuple-element.54), channel_id=1, source_target_pairs={{0,64},{16,80},{32,96},{48,112},{64,128},{80,144},{96,160},{112,17... | collective-permute-start | bytes 1179656 | tf_op jit(solution)/shard_map/ppermute | solution.py:357
  137.9 19.7 %collective-permute-start.32 = (bf16[4,128,384]{2,1,0:T(8,128)(2,1)}, bf16[4,128,384]{2,1,0:T(8,128)(2,1)}, u32[]{:S(2)}, u32[]{:S(2)}) collective-permute-start(bf16[4,128,384]{2,1,0:T(8,128)(2,1)} %get-tuple-element.55), channel_id=1, source_target_pairs={{0,192},{16,208},{32,224},{48,240},{64,0},{80,16},{96,32},{112,48}... | collective-permute-start | bytes 1179656 | tf_op jit(solution)/shard_map/ppermute | solution.py:357
  139.5 18.5 %collective-permute-start.33 = (bf16[4,128,384]{2,1,0:T(8,128)(2,1)}, bf16[4,128,384]{2,1,0:T(8,128)(2,1)}, u32[]{:S(2)}, u32[]{:S(2)}) collective-permute-start(bf16[4,128,384]{2,1,0:T(8,128)(2,1)} %get-tuple-element.56), channel_id=1, source_target_pairs={{0,128},{16,144},{32,160},{48,176},{64,192},{80,208},{96,224},{112... | collective-permute-start | bytes 1179656 | tf_op jit(solution)/shard_map/ppermute | solution.py:357
  144.7 24.2 %collective-permute-start.23 = (bf16[4,128,384]{2,1,0:T(8,128)(2,1)}, bf16[4,128,384]{2,1,0:T(8,128)(2,1)}, u32[]{:S(2)}, u32[]{:S(2)}) collective-permute-start(bf16[4,128,384]{2,1,0:T(8,128)(2,1)} %get-tuple-element.46), channel_id=1, source_target_pairs={{0,16},{16,32},{32,48},{48,0},{64,80},{80,96},{96,112},{112,64},{1... | collective-permute-start | bytes 1179656 | tf_op jit(solution)/shard_map/ppermute | solution.py:357
  151.1 19.2 %collective-permute-start.24 = (bf16[4,128,384]{2,1,0:T(8,128)(2,1)}, bf16[4,128,384]{2,1,0:T(8,128)(2,1)}, u32[]{:S(2)}, u32[]{:S(2)}) collective-permute-start(bf16[4,128,384]{2,1,0:T(8,128)(2,1)} %copy-done.8), channel_id=1, source_target_pairs={{0,48},{16,0},{32,16},{48,32},{64,112},{80,64},{96,80},{112,96},{1... | collective-permute-start | bytes 1179656 | tf_op jit(solution)/shard_map/ppermute | solution.py:357
  153.4 17.3 %collective-permute-start.25 = (bf16[4,128,384]{2,1,0:T(8,128)(2,1)}, bf16[4,128,384]{2,1,0:T(8,128)(2,1)}, u32[]{:S(2)}, u32[]{:S(2)}) collective-permute-start(bf16[4,128,384]{2,1,0:T(8,128)(2,1)} %copy-done.7), channel_id=1, source_target_pairs={{0,32},{16,48},{32,0},{48,16},{64,96},{80,112},{96,64},{112,80},{1... | collective-permute-start | bytes 1179656 | tf_op jit(solution)/shard_map/ppermute | solution.py:357
  160.8 14.6 %collective-permute-start.34 = (bf16[128,384]{1,0:T(8,128)(2,1)}, bf16[128,384]{1,0:T(8,128)(2,1)}, u32[]{:S(2)}, u32[]{:S(2)}) collective-permute-start(bf16[128,384]{1,0:T(8,128)(2,1)} %get-tuple-element.58), channel_id=1, source_target_pairs={{0,16},{16,32},{32,48},{48,0},{64,80},{80,96},{96,112},{112,64},{1... | collective-permute-start | bytes 294920 | tf_op jit(solution)/shard_map/ppermute | solution.py:366
  166.8 11.1 %collective-permute-start.35 = (bf16[128,384]{1,0:T(8,128)(2,1)}, bf16[128,384]{1,0:T(8,128)(2,1)}, u32[]{:S(2)}, u32[]{:S(2)}) collective-permute-start(bf16[128,384]{1,0:T(8,128)(2,1)} %get-tuple-element.59), channel_id=1, source_target_pairs={{0,48},{16,0},{32,16},{48,32},{64,112},{80,64},{96,80},{112,96},{1... | collective-permute-start | bytes 294920 | tf_op jit(solution)/shard_map/ppermute | solution.py:366
  169.0 9.0 %collective-permute-start.36 = (bf16[128,384]{1,0:T(8,128)(2,1)}, bf16[128,384]{1,0:T(8,128)(2,1)}, u32[]{:S(2)}, u32[]{:S(2)}) collective-permute-start(bf16[128,384]{1,0:T(8,128)(2,1)} %get-tuple-element.60), channel_id=1, source_target_pairs={{0,32},{16,48},{32,0},{48,16},{64,96},{80,112},{96,64},{112,80},{1... | collective-permute-start | bytes 294920 | tf_op jit(solution)/shard_map/ppermute | solution.py:366
  172.2 12.9 %copy-start.12 = (bf16[128,384]{1,0:T(8,128)(2,1)S(1)}, bf16[128,384]{1,0:T(8,128)(2,1)}, u32[]{:S(2)}) copy-start(bf16[128,384]{1,0:T(8,128)(2,1)} %copy-done.11) | copy-start | bytes 294916
  172.2 27.8 %copy-start.13 = (pred[256,128]{1,0:T(32,128)(4,1)S(1)}, pred[256,128]{1,0:T(32,128)(4,1)}, u32[]{:S(2)}) copy-start(pred[256,128]{1,0:T(32,128)(4,1)} %get-tuple-element.67) | copy-start | bytes 98308
  172.2 6.9 %collective-permute-start.26 = (bf16[128,384]{1,0:T(8,128)(2,1)S(1)}, bf16[128,384]{1,0:T(8,128)(2,1)S(1)}, u32[]{:S(2)}, u32[]{:S(2)}) collective-permute-start(bf16[128,384]{1,0:T(8,128)(2,1)S(1)} %get-tuple-element.50), channel_id=1, source_target_pairs={{0,64},{16,80},{32,96},{48,112},{64,128},{80,144},{96,160},{112,17... | collective-permute-start | bytes 294920 | tf_op jit(solution)/shard_map/ppermute | solution.py:366
  173.0 6.1 %collective-permute-start.27 = (bf16[128,384]{1,0:T(8,128)(2,1)S(1)}, bf16[128,384]{1,0:T(8,128)(2,1)S(1)}, u32[]{:S(2)}, u32[]{:S(2)}) collective-permute-start(bf16[128,384]{1,0:T(8,128)(2,1)S(1)} %get-tuple-element.51), channel_id=1, source_target_pairs={{0,192},{16,208},{32,224},{48,240},{64,0},{80,16},{96,32},{112,48}... | collective-permute-start | bytes 294920 | tf_op jit(solution)/shard_map/ppermute | solution.py:366
  175.4 5.5 %collective-permute-start.28 = (bf16[128,384]{1,0:T(8,128)(2,1)S(1)}, bf16[128,384]{1,0:T(8,128)(2,1)S(1)}, u32[]{:S(2)}, u32[]{:S(2)}) collective-permute-start(bf16[128,384]{1,0:T(8,128)(2,1)S(1)} %get-tuple-element.52), channel_id=1, source_target_pairs={{0,128},{16,144},{32,160},{48,176},{64,192},{80,208},{96,224},{112... | collective-permute-start | bytes 294920 | tf_op jit(solution)/shard_map/ppermute | solution.py:366
  181.7 12.0 %all-to-all-start.2 = ((bf16[8,32,384]{2,1,0:T(8,128)(2,1)}), bf16[8,32,384]{2,1,0:T(8,128)(2,1)S(1)}, u32[]{:S(2)}, u32[]{:S(2)}) async-start(bf16[8,32,384]{2,1,0:T(8,128)(2,1)} %multiply_convert_fusion), calls=%async_computation.2 | async-start | bytes 393216 | tf_op jit(solution)/shard_map/all_to_all | solution.py:371
  193.9 6.2 %collective-permute-start.37 = (bf16[256,192]{1,0:T(8,128)(2,1)S(1)}, bf16[256,192]{1,0:T(8,128)(2,1)S(1)}, u32[]{:S(2)}, u32[]{:S(2)}) collective-permute-start(bf16[256,192]{1,0:T(8,128)(2,1)S(1)} %broadcast_select_fusion), channel_id=1, source_target_pairs={{0,1},{1,0},{2,3},{3,2},{4,5},{5,4},{6,7},{7,6},{8,9},{9,8},{10,11... | collective-permute-start | bytes 294920 | tf_op jit(solution)/shard_map/ppermute | solution.py:22
  (7 other events, 14.6 us)

commit v6 on v5

--- a/solution.py
+++ b/solution.py
@@ -317,6 +317,7 @@
     ]
     far_a, far_b, a1, b1 = lax.optimization_barrier((stack_a, stack_b, a1, b1))
     a2, b2 = lax.ppermute(far_a, "dp", SHIFT_Y[2]), lax.ppermute(far_b, "dp", SHIFT_X[2])
+    a2, b2, a3, b3 = lax.optimization_barrier((a2, b2, a3, b3))
     gain = norm_gain.reshape(16, 1, 384)
     halves = [
         local_call(norm_kernel(h), [((128, 6144), BF16)], "norm", pos, *stacks, gain)[0]

time: 202 us -> 186 us (0.921)
  starting transfers between devices: 74.1 us -> 65.1 us
  waiting for transfers between devices: 65.5 us -> 56.7 us
    ppermute x2, waiting for transfers between devices: 11.1 us -> 0.71 us  [shards(): lax.ppermute(stack_a, 'dp', SHIFT_Y[d])]
    ppermute x1, waiting for transfers between devices: 7.12 us -> 0.01 us  [shards(): lax.ppermute(far_b, 'dp', SHIFT_X[2])]
    ppermute x1, waiting for transfers between devices: 1.22 us -> 7.12 us  [shards(): lax.ppermute(far_a, 'dp', SHIFT_Y[2])]
    ppermute x6, starting transfers between devices: 14 us -> 9.14 us  [shards(): got = [lax.ppermute(sums[d], 'dp', near[d]) for d in (1, 3, 2)]]
    ppermute x6, starting transfers between devices: 14.7 us -> 10.8 us  [shards(): got = [lax.ppermute(rows[d], 'dp', far[d]) for d in (1, 3, 2)]]
    ppermute x6, waiting for transfers between devices: 0.98 us -> 4.61 us  [shards(): got = [lax.ppermute(sums[d], 'dp', near[d]) for d in (1, 3, 2)]]
    ppermute x2, waiting for transfers between devices: 6.85 us -> 4.27 us  [shards(): lax.ppermute(stack_b, 'dp', SHIFT_X[d])]
    ppermute x2, starting transfers between devices: 0.13 us -> 2.67 us  [shards(): lax.ppermute(stack_a, 'dp', SHIFT_Y[d])]
  transfers between devices with their start and end apart: 40 -> 40, of which waited for: 21 -> 20; matrix products, arithmetic and copies ran while one was open for 10% -> 11% of each run, Pallas kernels for 5% -> 6%
where the time goes in v6:
time: 186 us; the launch traced here: 184 us
  starting transfers between devices  65.1 us (35%)
  waiting for transfers between devices  56.7 us (30%)
  Pallas kernels  20.8 us (11%)
  matrix products  14.1 us (8%)
  blocking collectives  13.4 us (7%)
  local copies, waits for them, and re-layouts  7.2 us (4%)
  other arithmetic  6.68 us (4%)
    ppermute x8, starting transfers between devices, swap_cores(): return lax.ppermute(a, 'side', SWAP)  15.6 us
    all_to_all x1, blocking collectives, shards(): lax.all_to_all(routed.reshape(8, 32, 384), 'tensor', split_axis=0, concat...  13.4 us
    pallas_call x6, Pallas kernels, local_call(): pl.pallas_call(kernel, in_specs=first + [vmem] * (len(args) - len(first))...  12.6 us
    ppermute x6, starting transfers between devices, shards(): got = [lax.ppermute(rows[d], 'dp', far[d]) for d in (1, 3, 2)]  10.8 us
    ppermute x3, waiting for transfers between devices, shards(): lax.ppermute(rows_x, 'dp', SHIFT_Y[d])  10.6 us
    ppermute x6, starting transfers between devices, shards(): got = [lax.ppermute(sums[d], 'dp', near[d]) for d in (1, 3, 2)]  9.14 us
    all_to_all x1, starting transfers between devices, shards(): lax.all_to_all(head_sums, 'tensor', split_axis=0, concat_axis=0, tiled=True)  8.18 us
    all_to_all x1, waiting for transfers between devices, shards(): lax.all_to_all(parts.reshape(8, 32, 384), 'tensor', split_axis=0, concat_...  7.59 us
  transfers between devices with their start and end apart: 40, of which 20 were waited for; matrix products, arithmetic and copies ran while one was open for 11% of the time, Pallas kernels for 6%

profile of v6, /device:TPU:1, one launch (start us, length us, event | category | flops | bytes accessed | tf_op | source)
XLA Modules:
  0.0 184.3 jit_solution(1552592556647755628)
XLA Ops:
  0.0 5.3 %attend.1 = bf16[32,768]{1,0:T(8,128)(2,1)} custom-call(s32[32]{0:T(128)} %lengths.1, bf16[32,768]{1,0:T(8,128)(2,1)} %q_in.1, bf16[32,128]{1,0:T(8,128)(2,1)} %k_in.1, bf16[32,128]{1,0:T(8,128)(2,1)} %v_in.1, bf16[32,192,128]{2,1,0:T(8,128)(2,1)} %keys.1, bf16[32,192,128]{2,1,0:T(8,128)(2,1)} %values.1), custom_call_target="tpu_custom_call" | custom-call | tf_op jit(solution)/shard_map/attend/pallas_call | solution.py:194
  5.4 3.4 %collective-permute-start.2 = (bf16[32,768]{1,0:T(8,128)(2,1)}, bf16[32,768]{1,0:T(8,128)(2,1)S(1)}, u32[]{:S(2)}, u32[]{:S(2)}) collective-permute-start(bf16[32,768]{1,0:T(8,128)(2,1)} %attend.1), channel_id=1, source_target_pairs={{0,192},{16,208},{32,224},{48,240},{64,0},{80,16},{96,32},{112,48}... | collective-permute-start | bytes 147464 | tf_op jit(solution)/shard_map/ppermute | solution.py:280
  9.9 1.5 collective-permute-start.6
  11.4 2.0 %collective-permute-done.1 = bf16[32,768]{1,0:T(8,128)(2,1)S(1)} collective-permute-done((bf16[32,768]{1,0:T(8,128)(2,1)}, bf16[32,768]{1,0:T(8,128)(2,1)S(1)}, u32[]{:S(2)}, u32[]{:S(2)}) %collective-permute-start.1) | collective-permute-done | bytes 49184 | tf_op jit(solution)/shard_map/ppermute | solution.py:280
  14.8 2.8 %collective-permute-start.5 = (bf16[4,32,768]{2,1,0:T(8,128)(2,1)S(1)}, bf16[4,32,768]{2,1,0:T(8,128)(2,1)S(1)}, u32[]{:S(2)}, u32[]{:S(2)}) collective-permute-start(bf16[4,32,768]{2,1,0:T(8,128)(2,1)S(1)} %pad_maximum_fusion.7.g0), channel_id=1, source_target_pairs={{0,48},{16,0},{32,16},{48,32},{64,112},{80,64},{96,80},{112,96},{1... | collective-permute-start | bytes 589832 | tf_op jit(solution)/shard_map/ppermute | solution.py:284
  18.7 3.6 %collective-permute-done.5.g3 = bf16[4,32,768]{2,1,0:T(8,128)(2,1)S(1)} collective-permute-done((bf16[4,32,768]{2,1,0:T(8,128)(2,1)S(1)}, bf16[4,32,768]{2,1,0:T(8,128)(2,1)S(1)}, u32[]{:S(2)}, u32[]{:S(2)}) %collective-permute-start.5) | collective-permute-done | bytes 196640 | tf_op jit(solution)/shard_map/ppermute | solution.py:284
  22.3 1.5 collective-permute-done.4.g2
  23.8 5.5 %collective-permute-done.3.g1 = bf16[4,32,768]{2,1,0:T(8,128)(2,1)} collective-permute-done((bf16[4,32,768]{2,1,0:T(8,128)(2,1)S(1)}, bf16[4,32,768]{2,1,0:T(8,128)(2,1)}, u32[]{:S(2)}, u32[]{:S(2)}) %collective-permute-start.3) | collective-permute-done | bytes 196640 | tf_op jit(solution)/shard_map/ppermute | solution.py:284
  29.3 2.8 %out_projection.1 = bf16[8,64,384]{2,1,0:T(8,128)(2,1)} custom-call(s32[3]{0:T(128)S(1)} %pad_add_fusion.pos, bf16[4,32,768]{2,1,0:T(8,128)(2,1)S(1)} %pad_maximum_fusion.7.g0, bf16[4,32,768]{2,1,0:T(8,128)(2,1)} %collective-permute-done.3.g1, bf16[4,32,768]{2,1,0:T(8,128)(2,1)} %collective-permute-done.4.g2, ...), custom_call_target="tpu_custom_call" | custom-call | tf_op jit(solution)/shard_map/out_projection/pallas_call | solution.py:286
  32.1 8.2 %all-to-all-start = ((bf16[8,64,384]{2,1,0:T(8,128)(2,1)}), bf16[8,64,384]{2,1,0:T(8,128)(2,1)S(1)}, u32[]{:S(2)}, u32[]{:S(2)}) async-start(bf16[8,64,384]{2,1,0:T(8,128)(2,1)} %out_projection.1), calls=%async_computation | async-start | bytes 786432 | tf_op jit(solution)/shard_map/all_to_all | solution.py:295
  40.3 1.5 copy.23
  41.8 1.7 collective-permute-start.7
  43.5 1.2 collective-permute-done.7
  46.4 6.3 %all-to-all-done = bf16[8,64,384]{2,1,0:T(8,128)(2,1)S(1)} async-done(((bf16[8,64,384]{2,1,0:T(8,128)(2,1)}), bf16[8,64,384]{2,1,0:T(8,128)(2,1)S(1)}, u32[]{:S(2)}, u32[]{:S(2)}) %all-to-all-start) | async-done | bytes 393248 | tf_op jit(solution)/shard_map/all_to_all | solution.py:295
  53.7 3.3 %collective-permute-start.8 = (bf16[64,384]{1,0:T(8,128)(2,1)S(1)}, bf16[64,384]{1,0:T(8,128)(2,1)S(1)}, u32[]{:S(2)}, u32[]{:S(2)}) collective-permute-start(bf16[64,384]{1,0:T(8,128)(2,1)S(1)} %fusion.32), channel_id=1, source_target_pairs={{0,1},{1,0},{2,3},{3,2},{4,5},{5,4},{6,7},{7,6},{8,9},{9,8},{10,11... | collective-permute-start | bytes 147464 | tf_op jit(solution)/shard_map/ppermute | solution.py:22
  58.3 13.4 %all_to_all.15 = bf16[8,32,384]{2,1,0:T(8,128)(2,1)S(1)} all-to-all(bf16[8,32,384]{2,1,0:T(8,128)(2,1)S(1)} %bitcast.96), channel_id=1, replica_groups=mesh['dp'=16,'tensor'=8,'side'=2] {'tensor'}, dimensions={0} | all-to-all | bytes 393216 | tf_op jit(solution)/shard_map/all_to_all | solution.py:304
  74.0 1.8 collective-permute-done.11
  75.7 2.0 %collective-permute-done.10 = bf16[128,384]{1,0:T(8,128)(2,1)S(1)} collective-permute-done((bf16[128,384]{1,0:T(8,128)(2,1)S(1)}, bf16[128,384]{1,0:T(8,128)(2,1)S(1)}, u32[]{:S(2)}, u32[]{:S(2)}) %collective-permute-start.10) | collective-permute-done | bytes 98336 | tf_op jit(solution)/shard_map/ppermute | solution.py:310
  77.8 3.1 %collective-permute-done.9 = bf16[128,384]{1,0:T(8,128)(2,1)S(1)} collective-permute-done((bf16[128,384]{1,0:T(8,128)(2,1)S(1)}, bf16[128,384]{1,0:T(8,128)(2,1)S(1)}, u32[]{:S(2)}, u32[]{:S(2)}) %collective-permute-start.9) | collective-permute-done | bytes 98336 | tf_op jit(solution)/shard_map/ppermute | solution.py:310
  82.7 2.1 %collective-permute-start.20 = (bf16[4,128,384]{2,1,0:T(8,128)(2,1)S(1)}, bf16[4,128,384]{2,1,0:T(8,128)(2,1)S(1)}, u32[]{:S(2)}, u32[]{:S(2)}) collective-permute-start(bf16[4,128,384]{2,1,0:T(8,128)(2,1)S(1)} %pad_maximum_fusion.5.s0), channel_id=1, source_target_pairs={{0,192},{16,208},{32,224},{48,240},{64,0},{80,16},{96,32},{112,48}... | collective-permute-start | bytes 1179656 | tf_op jit(solution)/shard_map/ppermute | solution.py:316
  84.7 2.6 %collective-permute-start.19 = (bf16[4,128,384]{2,1,0:T(8,128)(2,1)S(1)}, bf16[4,128,384]{2,1,0:T(8,128)(2,1)S(1)}, u32[]{:S(2)}, u32[]{:S(2)}) collective-permute-start(bf16[4,128,384]{2,1,0:T(8,128)(2,1)S(1)} %pad_maximum_fusion.4.s0), channel_id=1, source_target_pairs={{0,48},{16,0},{32,16},{48,32},{64,112},{80,64},{96,80},{112,96},{1... | collective-permute-start | bytes 1179656 | tf_op jit(solution)/shard_map/ppermute | solution.py:315
  87.3 4.3 %collective-permute-done.16.s1 = bf16[4,128,384]{2,1,0:T(8,128)(2,1)S(1)} collective-permute-done((bf16[4,128,384]{2,1,0:T(8,128)(2,1)S(1)}, bf16[4,128,384]{2,1,0:T(8,128)(2,1)S(1)}, u32[]{:S(2)}, u32[]{:S(2)}) %collective-permute-start.16) | collective-permute-done | bytes 393248 | tf_op jit(solution)/shard_map/ppermute | solution.py:316
  92.3 1.9 %collective-permute-start.18 = (bf16[4,128,384]{2,1,0:T(8,128)(2,1)S(1)}, bf16[4,128,384]{2,1,0:T(8,128)(2,1)S(1)}, u32[]{:S(2)}, u32[]{:S(2)}) collective-permute-start(bf16[4,128,384]{2,1,0:T(8,128)(2,1)S(1)} %pad_maximum_fusion.5.s0), channel_id=1, source_target_pairs={{0,128},{16,144},{32,160},{48,176},{64,192},{80,208},{96,224},{112... | collective-permute-start | bytes 1179656 | tf_op jit(solution)/shard_map/ppermute | solution.py:319
  94.2 7.1 %collective-permute-done.17.s2 = bf16[4,128,384]{2,1,0:T(8,128)(2,1)S(1)} collective-permute-done((bf16[4,128,384]{2,1,0:T(8,128)(2,1)S(1)}, bf16[4,128,384]{2,1,0:T(8,128)(2,1)S(1)}, u32[]{:S(2)}, u32[]{:S(2)}) %collective-permute-start.17) | collective-permute-done | bytes 393248 | tf_op jit(solution)/shard_map/ppermute | solution.py:319
  102.1 1.8 norm.3
  103.9 4.1 %collective-permute-start.29 = (bf16[128,6144]{1,0:T(8,128)(2,1)S(1)}, bf16[128,6144]{1,0:T(8,128)(2,1)S(1)}, u32[]{:S(2)}, u32[]{:S(2)}) collective-permute-start(bf16[128,6144]{1,0:T(8,128)(2,1)S(1)} %norm.3), channel_id=1, source_target_pairs={{0,1},{1,0},{2,3},{3,2},{4,5},{5,4},{6,7},{7,6},{8,9},{9,8},{10,11... | collective-permute-start | bytes 4718600 | tf_op jit(solution)/shard_map/ppermute | solution.py:22
  108.0 1.8 norm.2
  111.0 1.3 copy-done.10
  114.5 1.8 convolution_convert_fusion.1
  117.5 1.8 convolution_convert_fusion.2
  120.8 2.8 %combine_cores.3 = (bf16[4,128,384]{2,1,0:T(8,128)(2,1)S(1)}, bf16[4,128,384]{2,1,0:T(8,128)(2,1)}, bf16[4,128,384]{2,1,0:T(8,128)(2,1)}, bf16[4,128,384]{2,1,0:T(8,128)(2,1)}) custom-call(s32[3]{0:T(128)S(1)} %pad_add_fusion.pos, bf16[256,6144]{1,0:T(8,128)(2,1)S(1)} %convolution_convert_fusion.own, bf16[128,6144]{1,0:T(8,128)(2,1)} %collective-permute-done.30.other), custom_call_target="tpu_custom_call" | custom-call | tf_op jit(solution)/shard_map/combine_cores/pallas_call | solution.py:112
  123.6 1.2 collective-permute-start.31
  125.0 1.5 collective-permute-start.32
  127.2 2.5 %combine_cores.2 = (bf16[4,128,384]{2,1,0:T(8,128)(2,1)S(1)}, bf16[4,128,384]{2,1,0:T(8,128)(2,1)}, bf16[4,128,384]{2,1,0:T(8,128)(2,1)S(1)}, bf16[4,128,384]{2,1,0:T(8,128)(2,1)S(1)}) custom-call(s32[3]{0:T(128)S(1)} %pad_add_fusion.pos, bf16[256,6144]{1,0:T(8,128)(2,1)S(1)} %convolution_convert_fusion.own, bf16[128,6144]{1,0:T(8,128)(2,1)} %collective-permute-done.22.other), custom_call_target="tpu_custom_call" | custom-call | tf_op jit(solution)/shard_map/combine_cores/pallas_call | solution.py:112
  131.8 2.4 %collective-permute-start.24 = (bf16[4,128,384]{2,1,0:T(8,128)(2,1)}, bf16[4,128,384]{2,1,0:T(8,128)(2,1)}, u32[]{:S(2)}, u32[]{:S(2)}) collective-permute-start(bf16[4,128,384]{2,1,0:T(8,128)(2,1)} %copy-done.8), channel_id=1, source_target_pairs={{0,48},{16,0},{32,16},{48,32},{64,112},{80,64},{96,80},{112,96},{1... | collective-permute-start | bytes 1179656 | tf_op jit(solution)/shard_map/ppermute | solution.py:358
  134.2 1.7 collective-permute-done.31.got1
  135.9 3.0 %collective-permute-start.25 = (bf16[4,128,384]{2,1,0:T(8,128)(2,1)}, bf16[4,128,384]{2,1,0:T(8,128)(2,1)}, u32[]{:S(2)}, u32[]{:S(2)}) collective-permute-start(bf16[4,128,384]{2,1,0:T(8,128)(2,1)} %copy-done.7), channel_id=1, source_target_pairs={{0,32},{16,48},{32,0},{48,16},{64,96},{80,112},{96,64},{112,80},{1... | collective-permute-start | bytes 1179656 | tf_op jit(solution)/shard_map/ppermute | solution.py:358
  138.9 2.8 %fusion.22 = f32[256]{0:T(256)S(1)} fusion(bf16[6144,8]{0,1:T(8,128)(2,1)} %param.23, bf16[128,6144]{1,0:T(8,128)(2,1)} %copy-done.1, bf16[128,6144]{1,0:T(8,128)(2,1)} %copy-done.2, s32[256]{0:T(256)S(1)} %eq.144, f32[8]{0:T(128)S(1)} %compare_convert_fusion), kind=kOutput, calls=%fused_computation.26 | convolution fusion | flops 31467264 | bytes 3246112 | tf_op jit(solution)/shard_map/dot_general | solution.py:337
  141.7 2.9 %collective-permute-done.33.got3 = bf16[4,128,384]{2,1,0:T(8,128)(2,1)} collective-permute-done((bf16[4,128,384]{2,1,0:T(8,128)(2,1)}, bf16[4,128,384]{2,1,0:T(8,128)(2,1)}, u32[]{:S(2)}, u32[]{:S(2)}) %collective-permute-start.33) | collective-permute-done | bytes 393248 | tf_op jit(solution)/shard_map/ppermute | solution.py:358
  144.7 2.2 %sum_rows.3 = (f32[128,384]{1,0:T(8,128)S(1)}, bf16[128,384]{1,0:T(8,128)(2,1)}, bf16[128,384]{1,0:T(8,128)(2,1)}, bf16[128,384]{1,0:T(8,128)(2,1)}) custom-call(bf16[4,128,384]{2,1,0:T(8,128)(2,1)S(1)} %copy-done.4, bf16[4,128,384]{2,1,0:T(8,128)(2,1)} %collective-permute-done.31.got1, bf16[4,128,384]{2,1,0:T(8,128)(2,1)} %collective-permute-done.32.got2, ...), custom_call_target="tpu_custom_call" | custom-call | tf_op jit(solution)/shard_map/sum_rows/pallas_call | solution.py:112
  147.5 6.3 %collective-permute-start.34 = (bf16[128,384]{1,0:T(8,128)(2,1)}, bf16[128,384]{1,0:T(8,128)(2,1)}, u32[]{:S(2)}, u32[]{:S(2)}) collective-permute-start(bf16[128,384]{1,0:T(8,128)(2,1)} %get-tuple-element.66), channel_id=1, source_target_pairs={{0,16},{16,32},{32,48},{48,0},{64,80},{80,96},{96,112},{112,64},{1... | collective-permute-start | bytes 294920 | tf_op jit(solution)/shard_map/ppermute | solution.py:367
  153.8 1.8 collective-permute-start.36
  155.6 1.5 sum_rows.2
  157.2 2.7 %collective-permute-start.27 = (bf16[128,384]{1,0:T(8,128)(2,1)S(1)}, bf16[128,384]{1,0:T(8,128)(2,1)S(1)}, u32[]{:S(2)}, u32[]{:S(2)}) collective-permute-start(bf16[128,384]{1,0:T(8,128)(2,1)S(1)} %get-tuple-element.59), channel_id=1, source_target_pairs={{0,192},{16,208},{32,224},{48,240},{64,0},{80,16},{96,32},{112,48}... | collective-permute-start | bytes 294920 | tf_op jit(solution)/shard_map/ppermute | solution.py:367
  162.4 2.6 %collective-permute-done.28 = bf16[128,384]{1,0:T(8,128)(2,1)S(1)} collective-permute-done((bf16[128,384]{1,0:T(8,128)(2,1)S(1)}, bf16[128,384]{1,0:T(8,128)(2,1)S(1)}, u32[]{:S(2)}, u32[]{:S(2)}) %collective-permute-start.28) | collective-permute-done | bytes 98336 | tf_op jit(solution)/shard_map/ppermute | solution.py:367
  165.8 3.4 %all-to-all-start.2 = ((bf16[8,32,384]{2,1,0:T(8,128)(2,1)}), bf16[8,32,384]{2,1,0:T(8,128)(2,1)S(1)}, u32[]{:S(2)}, u32[]{:S(2)}) async-start(bf16[8,32,384]{2,1,0:T(8,128)(2,1)} %multiply_convert_fusion), calls=%async_computation.2 | async-start | bytes 393216 | tf_op jit(solution)/shard_map/all_to_all | solution.py:372
  170.2 7.6 %all-to-all-done.2 = bf16[8,32,384]{2,1,0:T(8,128)(2,1)S(1)} async-done(((bf16[8,32,384]{2,1,0:T(8,128)(2,1)}), bf16[8,32,384]{2,1,0:T(8,128)(2,1)S(1)}, u32[]{:S(2)}, u32[]{:S(2)}) %all-to-all-start.2) | async-done | bytes 196640 | tf_op jit(solution)/shard_map/all_to_all | solution.py:372
  177.9 4.5 %collective-permute-start.37 = (bf16[256,192]{1,0:T(8,128)(2,1)S(1)}, bf16[256,192]{1,0:T(8,128)(2,1)S(1)}, u32[]{:S(2)}, u32[]{:S(2)}) collective-permute-start(bf16[256,192]{1,0:T(8,128)(2,1)S(1)} %broadcast_select_fusion), channel_id=1, source_target_pairs={{0,1},{1,0},{2,3},{3,2},{4,5},{5,4},{6,7},{7,6},{8,9},{9,8},{10,11... | collective-permute-start | bytes 294920 | tf_op jit(solution)/shard_map/ppermute | solution.py:22
  (122 shorter events, 29.1 us)
Async XLA Ops:
  0.0 114.5 %copy-start = (bf16[1,256,6144]{2,1,0:T(8,128)(2,1)S(1)}, bf16[1,256,6144]{2,1,0:T(8,128)(2,1)}, u32[]{:S(2)}) copy-start(bf16[1,256,6144]{2,1,0:T(8,128)(2,1)} %param.27) | copy-start | bytes 9437188
  0.0 43.5 %copy-start.14 = (s32[1024,2]{0,1:T(2,128)S(1)}, s32[1024,2]{0,1:T(2,128)}, u32[]{:S(2)}) copy-start(s32[1024,2]{0,1:T(2,128)} %param.24) | copy-start | bytes 24580
  5.4 6.0 %collective-permute-start.2 = (bf16[32,768]{1,0:T(8,128)(2,1)}, bf16[32,768]{1,0:T(8,128)(2,1)S(1)}, u32[]{:S(2)}, u32[]{:S(2)}) collective-permute-start(bf16[32,768]{1,0:T(8,128)(2,1)} %attend.1), channel_id=1, source_target_pairs={{0,192},{16,208},{32,224},{48,240},{64,0},{80,16},{96,32},{112,48}... | collective-permute-start | bytes 147464 | tf_op jit(solution)/shard_map/ppermute | solution.py:280
  8.7 4.7 %collective-permute-start.1 = (bf16[32,768]{1,0:T(8,128)(2,1)}, bf16[32,768]{1,0:T(8,128)(2,1)S(1)}, u32[]{:S(2)}, u32[]{:S(2)}) collective-permute-start(bf16[32,768]{1,0:T(8,128)(2,1)} %attend.1), channel_id=1, source_target_pairs={{0,128},{16,144},{32,160},{48,176},{64,192},{80,208},{96,224},{112... | collective-permute-start | bytes 147464 | tf_op jit(solution)/shard_map/ppermute | solution.py:280
  9.3 4.7 %collective-permute-start = (bf16[32,768]{1,0:T(8,128)(2,1)}, bf16[32,768]{1,0:T(8,128)(2,1)S(1)}, u32[]{:S(2)}, u32[]{:S(2)}) collective-permute-start(bf16[32,768]{1,0:T(8,128)(2,1)} %attend.1), channel_id=1, source_target_pairs={{0,64},{16,80},{32,96},{48,112},{64,128},{80,144},{96,160},{112,17... | collective-permute-start | bytes 147464 | tf_op jit(solution)/shard_map/ppermute | solution.py:280
  9.9 19.4 %collective-permute-start.6 = (bf16[192,768]{1,0:T(8,128)(2,1)}, bf16[192,768]{1,0:T(8,128)(2,1)}, u32[]{:S(2)}, u32[]{:S(2)}) collective-permute-start(bf16[192,768]{1,0:T(8,128)(2,1)} %bitcast.7.w_own), channel_id=1, source_target_pairs={{0,1},{1,0},{2,3},{3,2},{4,5},{5,4},{6,7},{7,6},{8,9},{9,8},{10,11... | collective-permute-start | bytes 884744 | tf_op jit(solution)/shard_map/ppermute | solution.py:22
  14.8 7.5 %collective-permute-start.5 = (bf16[4,32,768]{2,1,0:T(8,128)(2,1)S(1)}, bf16[4,32,768]{2,1,0:T(8,128)(2,1)S(1)}, u32[]{:S(2)}, u32[]{:S(2)}) collective-permute-start(bf16[4,32,768]{2,1,0:T(8,128)(2,1)S(1)} %pad_maximum_fusion.7.g0), channel_id=1, source_target_pairs={{0,48},{16,0},{32,16},{48,32},{64,112},{80,64},{96,80},{112,96},{1... | collective-permute-start | bytes 589832 | tf_op jit(solution)/shard_map/ppermute | solution.py:284
  17.6 6.2 %collective-permute-start.4 = (bf16[4,32,768]{2,1,0:T(8,128)(2,1)S(1)}, bf16[4,32,768]{2,1,0:T(8,128)(2,1)}, u32[]{:S(2)}, u32[]{:S(2)}) collective-permute-start(bf16[4,32,768]{2,1,0:T(8,128)(2,1)S(1)} %pad_maximum_fusion.7.g0), channel_id=1, source_target_pairs={{0,32},{16,48},{32,0},{48,16},{64,96},{80,112},{96,64},{112,80},{1... | collective-permute-start | bytes 589832 | tf_op jit(solution)/shard_map/ppermute | solution.py:284
  17.9 11.4 %collective-permute-start.3 = (bf16[4,32,768]{2,1,0:T(8,128)(2,1)S(1)}, bf16[4,32,768]{2,1,0:T(8,128)(2,1)}, u32[]{:S(2)}, u32[]{:S(2)}) collective-permute-start(bf16[4,32,768]{2,1,0:T(8,128)(2,1)S(1)} %pad_maximum_fusion.7.g0), channel_id=1, source_target_pairs={{0,16},{16,32},{32,48},{48,0},{64,80},{80,96},{96,112},{112,64},{1... | collective-permute-start | bytes 589832 | tf_op jit(solution)/shard_map/ppermute | solution.py:284
  32.1 20.6 %all-to-all-start = ((bf16[8,64,384]{2,1,0:T(8,128)(2,1)}), bf16[8,64,384]{2,1,0:T(8,128)(2,1)S(1)}, u32[]{:S(2)}, u32[]{:S(2)}) async-start(bf16[8,64,384]{2,1,0:T(8,128)(2,1)} %out_projection.1), calls=%async_computation | async-start | bytes 786432 | tf_op jit(solution)/shard_map/all_to_all | solution.py:295
  41.8 2.9 %collective-permute-start.7 = (bf16[128,192]{1,0:T(8,128)(2,1)}, bf16[128,192]{1,0:T(8,128)(2,1)}, u32[]{:S(2)}, u32[]{:S(2)}) collective-permute-start(bf16[128,192]{1,0:T(8,128)(2,1)} %copy.23), channel_id=1, source_target_pairs={{0,1},{1,0},{2,3},{3,2},{4,5},{5,4},{6,7},{7,6},{8,9},{9,8},{10,11... | collective-permute-start | bytes 147464 | tf_op jit(solution)/shard_map/ppermute | solution.py:22
  53.7 4.4 %collective-permute-start.8 = (bf16[64,384]{1,0:T(8,128)(2,1)S(1)}, bf16[64,384]{1,0:T(8,128)(2,1)S(1)}, u32[]{:S(2)}, u32[]{:S(2)}) collective-permute-start(bf16[64,384]{1,0:T(8,128)(2,1)S(1)} %fusion.32), channel_id=1, source_target_pairs={{0,1},{1,0},{2,3},{3,2},{4,5},{5,4},{6,7},{7,6},{8,9},{9,8},{10,11... | collective-permute-start | bytes 147464 | tf_op jit(solution)/shard_map/ppermute | solution.py:22
  58.1 23.6 %copy-start.11 = (bf16[128,384]{1,0:T(8,128)(2,1)}, bf16[128,384]{1,0:T(8,128)(2,1)S(1)}, u32[]{:S(2)}) copy-start(bf16[128,384]{1,0:T(8,128)(2,1)S(1)} %maximum_select_fusion.1) | copy-start | bytes 294916
  71.7 4.0 %collective-permute-start.11 = (bf16[128,384]{1,0:T(8,128)(2,1)S(1)}, bf16[128,384]{1,0:T(8,128)(2,1)S(1)}, u32[]{:S(2)}, u32[]{:S(2)}) collective-permute-start(bf16[128,384]{1,0:T(8,128)(2,1)S(1)} %bitcast.98), channel_id=1, source_target_pairs={{0,192},{16,208},{32,224},{48,240},{64,0},{80,16},{96,32},{112,48}... | collective-permute-start | bytes 294920 | tf_op jit(solution)/shard_map/ppermute | solution.py:310
  72.7 5.1 %collective-permute-start.10 = (bf16[128,384]{1,0:T(8,128)(2,1)S(1)}, bf16[128,384]{1,0:T(8,128)(2,1)S(1)}, u32[]{:S(2)}, u32[]{:S(2)}) collective-permute-start(bf16[128,384]{1,0:T(8,128)(2,1)S(1)} %bitcast.99), channel_id=1, source_target_pairs={{0,128},{16,144},{32,160},{48,176},{64,192},{80,208},{96,224},{112... | collective-permute-start | bytes 294920 | tf_op jit(solution)/shard_map/ppermute | solution.py:310
  73.2 7.7 %collective-permute-start.9 = (bf16[128,384]{1,0:T(8,128)(2,1)S(1)}, bf16[128,384]{1,0:T(8,128)(2,1)S(1)}, u32[]{:S(2)}, u32[]{:S(2)}) collective-permute-start(bf16[128,384]{1,0:T(8,128)(2,1)S(1)} %bitcast.100), channel_id=1, source_target_pairs={{0,64},{16,80},{32,96},{48,112},{64,128},{80,144},{96,160},{112,17... | collective-permute-start | bytes 294920 | tf_op jit(solution)/shard_map/ppermute | solution.py:310
  73.9 6.9 %collective-permute-start.14 = (bf16[128,384]{1,0:T(8,128)(2,1)S(1)}, bf16[128,384]{1,0:T(8,128)(2,1)S(1)}, u32[]{:S(2)}, u32[]{:S(2)}) collective-permute-start(bf16[128,384]{1,0:T(8,128)(2,1)S(1)} %bitcast.102), channel_id=1, source_target_pairs={{0,48},{16,0},{32,16},{48,32},{64,112},{80,64},{96,80},{112,96},{1... | collective-permute-start | bytes 294920 | tf_op jit(solution)/shard_map/ppermute | solution.py:311
  74.0 6.9 %collective-permute-start.13 = (bf16[128,384]{1,0:T(8,128)(2,1)S(1)}, bf16[128,384]{1,0:T(8,128)(2,1)S(1)}, u32[]{:S(2)}, u32[]{:S(2)}) collective-permute-start(bf16[128,384]{1,0:T(8,128)(2,1)S(1)} %bitcast.103), channel_id=1, source_target_pairs={{0,32},{16,48},{32,0},{48,16},{64,96},{80,112},{96,64},{112,80},{1... | collective-permute-start | bytes 294920 | tf_op jit(solution)/shard_map/ppermute | solution.py:311
  75.7 5.9 %collective-permute-start.12 = (bf16[128,384]{1,0:T(8,128)(2,1)S(1)}, bf16[128,384]{1,0:T(8,128)(2,1)S(1)}, u32[]{:S(2)}, u32[]{:S(2)}) collective-permute-start(bf16[128,384]{1,0:T(8,128)(2,1)S(1)} %bitcast.104), channel_id=1, source_target_pairs={{0,16},{16,32},{32,48},{48,0},{64,80},{80,96},{96,112},{112,64},{1... | collective-permute-start | bytes 294920 | tf_op jit(solution)/shard_map/ppermute | solution.py:311
  81.8 9.8 %collective-permute-start.16 = (bf16[4,128,384]{2,1,0:T(8,128)(2,1)S(1)}, bf16[4,128,384]{2,1,0:T(8,128)(2,1)S(1)}, u32[]{:S(2)}, u32[]{:S(2)}) collective-permute-start(bf16[4,128,384]{2,1,0:T(8,128)(2,1)S(1)} %pad_maximum_fusion.5.s0), channel_id=1, source_target_pairs={{0,64},{16,80},{32,96},{48,112},{64,128},{80,144},{96,160},{112,17... | collective-permute-start | bytes 1179656 | tf_op jit(solution)/shard_map/ppermute | solution.py:316
  82.6 9.7 %collective-permute-start.15 = (bf16[4,128,384]{2,1,0:T(8,128)(2,1)S(1)}, bf16[4,128,384]{2,1,0:T(8,128)(2,1)S(1)}, u32[]{:S(2)}, u32[]{:S(2)}) collective-permute-start(bf16[4,128,384]{2,1,0:T(8,128)(2,1)S(1)} %pad_maximum_fusion.4.s0), channel_id=1, source_target_pairs={{0,16},{16,32},{32,48},{48,0},{64,80},{80,96},{96,112},{112,64},{1... | collective-permute-start | bytes 1179656 | tf_op jit(solution)/shard_map/ppermute | solution.py:315
  82.7 11.6 %collective-permute-start.20 = (bf16[4,128,384]{2,1,0:T(8,128)(2,1)S(1)}, bf16[4,128,384]{2,1,0:T(8,128)(2,1)S(1)}, u32[]{:S(2)}, u32[]{:S(2)}) collective-permute-start(bf16[4,128,384]{2,1,0:T(8,128)(2,1)S(1)} %pad_maximum_fusion.5.s0), channel_id=1, source_target_pairs={{0,192},{16,208},{32,224},{48,240},{64,0},{80,16},{96,32},{112,48}... | collective-permute-start | bytes 1179656 | tf_op jit(solution)/shard_map/ppermute | solution.py:316
  84.7 9.5 %collective-permute-start.19 = (bf16[4,128,384]{2,1,0:T(8,128)(2,1)S(1)}, bf16[4,128,384]{2,1,0:T(8,128)(2,1)S(1)}, u32[]{:S(2)}, u32[]{:S(2)}) collective-permute-start(bf16[4,128,384]{2,1,0:T(8,128)(2,1)S(1)} %pad_maximum_fusion.4.s0), channel_id=1, source_target_pairs={{0,48},{16,0},{32,16},{48,32},{64,112},{80,64},{96,80},{112,96},{1... | collective-permute-start | bytes 1179656 | tf_op jit(solution)/shard_map/ppermute | solution.py:315
  92.3 9.0 %collective-permute-start.17 = (bf16[4,128,384]{2,1,0:T(8,128)(2,1)S(1)}, bf16[4,128,384]{2,1,0:T(8,128)(2,1)S(1)}, u32[]{:S(2)}, u32[]{:S(2)}) collective-permute-start(bf16[4,128,384]{2,1,0:T(8,128)(2,1)S(1)} %pad_maximum_fusion.4.s0), channel_id=1, source_target_pairs={{0,32},{16,48},{32,0},{48,16},{64,96},{80,112},{96,64},{112,80},{1... | collective-permute-start | bytes 1179656 | tf_op jit(solution)/shard_map/ppermute | solution.py:319
  92.3 9.0 %collective-permute-start.18 = (bf16[4,128,384]{2,1,0:T(8,128)(2,1)S(1)}, bf16[4,128,384]{2,1,0:T(8,128)(2,1)S(1)}, u32[]{:S(2)}, u32[]{:S(2)}) collective-permute-start(bf16[4,128,384]{2,1,0:T(8,128)(2,1)S(1)} %pad_maximum_fusion.5.s0), channel_id=1, source_target_pairs={{0,128},{16,144},{32,160},{48,176},{64,192},{80,208},{96,224},{112... | collective-permute-start | bytes 1179656 | tf_op jit(solution)/shard_map/ppermute | solution.py:319
  102.1 7.9 %copy-start.9 = (bf16[1,6144,256]{2,1,0:T(8,128)(2,1)S(1)}, bf16[1,6144,256]{2,1,0:T(8,128)(2,1)}, u32[]{:S(2)}) copy-start(bf16[1,6144,256]{2,1,0:T(8,128)(2,1)} %param.25) | copy-start | bytes 9437188
  103.9 7.0 %copy-start.1 = (bf16[128,6144]{1,0:T(8,128)(2,1)}, bf16[128,6144]{1,0:T(8,128)(2,1)S(1)}, u32[]{:S(2)}) copy-start(bf16[128,6144]{1,0:T(8,128)(2,1)S(1)} %norm.3) | copy-start | bytes 4718596
  103.9 9.4 %collective-permute-start.29 = (bf16[128,6144]{1,0:T(8,128)(2,1)S(1)}, bf16[128,6144]{1,0:T(8,128)(2,1)S(1)}, u32[]{:S(2)}, u32[]{:S(2)}) collective-permute-start(bf16[128,6144]{1,0:T(8,128)(2,1)S(1)} %norm.3), channel_id=1, source_target_pairs={{0,1},{1,0},{2,3},{3,2},{4,5},{5,4},{6,7},{7,6},{8,9},{9,8},{10,11... | collective-permute-start | bytes 4718600 | tf_op jit(solution)/shard_map/ppermute | solution.py:22
  109.9 6.4 %collective-permute-start.21 = (bf16[128,6144]{1,0:T(8,128)(2,1)S(1)}, bf16[128,6144]{1,0:T(8,128)(2,1)S(1)}, u32[]{:S(2)}, u32[]{:S(2)}) collective-permute-start(bf16[128,6144]{1,0:T(8,128)(2,1)S(1)} %norm.2), channel_id=1, source_target_pairs={{0,1},{1,0},{2,3},{3,2},{4,5},{5,4},{6,7},{7,6},{8,9},{9,8},{10,11... | collective-permute-start | bytes 4718600 | tf_op jit(solution)/shard_map/ppermute | solution.py:22
  116.3 4.5 %collective-permute-start.30 = (bf16[128,6144]{1,0:T(8,128)(2,1)}, bf16[128,6144]{1,0:T(8,128)(2,1)}, u32[]{:S(2)}, u32[]{:S(2)}) collective-permute-start(bf16[128,6144]{1,0:T(8,128)(2,1)} %convolution_convert_fusion.1), channel_id=1, source_target_pairs={{0,1},{1,0},{2,3},{3,2},{4,5},{5,4},{6,7},{7,6},{8,9},{9,8},{10,11... | collective-permute-start | bytes 4718600 | tf_op jit(solution)/shard_map/ppermute | solution.py:22
  119.3 7.9 %collective-permute-start.22 = (bf16[128,6144]{1,0:T(8,128)(2,1)}, bf16[128,6144]{1,0:T(8,128)(2,1)}, u32[]{:S(2)}, u32[]{:S(2)}) collective-permute-start(bf16[128,6144]{1,0:T(8,128)(2,1)} %convolution_convert_fusion.2), channel_id=1, source_target_pairs={{0,1},{1,0},{2,3},{3,2},{4,5},{5,4},{6,7},{7,6},{8,9},{9,8},{10,11... | collective-permute-start | bytes 4718600 | tf_op jit(solution)/shard_map/ppermute | solution.py:22
  123.6 12.2 %collective-permute-start.31 = (bf16[4,128,384]{2,1,0:T(8,128)(2,1)}, bf16[4,128,384]{2,1,0:T(8,128)(2,1)}, u32[]{:S(2)}, u32[]{:S(2)}) collective-permute-start(bf16[4,128,384]{2,1,0:T(8,128)(2,1)} %get-tuple-element.62), channel_id=1, source_target_pairs={{0,64},{16,80},{32,96},{48,112},{64,128},{80,144},{96,160},{112,17... | collective-permute-start | bytes 1179656 | tf_op jit(solution)/shard_map/ppermute | solution.py:358
  125.0 16.7 %collective-permute-start.32 = (bf16[4,128,384]{2,1,0:T(8,128)(2,1)}, bf16[4,128,384]{2,1,0:T(8,128)(2,1)}, u32[]{:S(2)}, u32[]{:S(2)}) collective-permute-start(bf16[4,128,384]{2,1,0:T(8,128)(2,1)} %get-tuple-element.63), channel_id=1, source_target_pairs={{0,192},{16,208},{32,224},{48,240},{64,0},{80,16},{96,32},{112,48}... | collective-permute-start | bytes 1179656 | tf_op jit(solution)/shard_map/ppermute | solution.py:358
  126.5 18.2 %collective-permute-start.33 = (bf16[4,128,384]{2,1,0:T(8,128)(2,1)}, bf16[4,128,384]{2,1,0:T(8,128)(2,1)}, u32[]{:S(2)}, u32[]{:S(2)}) collective-permute-start(bf16[4,128,384]{2,1,0:T(8,128)(2,1)} %get-tuple-element.64), channel_id=1, source_target_pairs={{0,128},{16,144},{32,160},{48,176},{64,192},{80,208},{96,224},{112... | collective-permute-start | bytes 1179656 | tf_op jit(solution)/shard_map/ppermute | solution.py:358
  131.2 22.6 %collective-permute-start.23 = (bf16[4,128,384]{2,1,0:T(8,128)(2,1)}, bf16[4,128,384]{2,1,0:T(8,128)(2,1)}, u32[]{:S(2)}, u32[]{:S(2)}) collective-permute-start(bf16[4,128,384]{2,1,0:T(8,128)(2,1)} %get-tuple-element.54), channel_id=1, source_target_pairs={{0,16},{16,32},{32,48},{48,0},{64,80},{80,96},{96,112},{112,64},{1... | collective-permute-start | bytes 1179656 | tf_op jit(solution)/shard_map/ppermute | solution.py:358
  131.8 12.8 %copy-start.4 = (bf16[4,128,384]{2,1,0:T(8,128)(2,1)S(1)}, bf16[4,128,384]{2,1,0:T(8,128)(2,1)}, u32[]{:S(2)}) copy-start(bf16[4,128,384]{2,1,0:T(8,128)(2,1)} %copy-done.3) | copy-start | bytes 1179652
  131.8 23.8 %collective-permute-start.24 = (bf16[4,128,384]{2,1,0:T(8,128)(2,1)}, bf16[4,128,384]{2,1,0:T(8,128)(2,1)}, u32[]{:S(2)}, u32[]{:S(2)}) collective-permute-start(bf16[4,128,384]{2,1,0:T(8,128)(2,1)} %copy-done.8), channel_id=1, source_target_pairs={{0,48},{16,0},{32,16},{48,32},{64,112},{80,64},{96,80},{112,96},{1... | collective-permute-start | bytes 1179656 | tf_op jit(solution)/shard_map/ppermute | solution.py:358
  135.9 19.7 %collective-permute-start.25 = (bf16[4,128,384]{2,1,0:T(8,128)(2,1)}, bf16[4,128,384]{2,1,0:T(8,128)(2,1)}, u32[]{:S(2)}, u32[]{:S(2)}) collective-permute-start(bf16[4,128,384]{2,1,0:T(8,128)(2,1)} %copy-done.7), channel_id=1, source_target_pairs={{0,32},{16,48},{32,0},{48,16},{64,96},{80,112},{96,64},{112,80},{1... | collective-permute-start | bytes 1179656 | tf_op jit(solution)/shard_map/ppermute | solution.py:358
  147.5 12.4 %collective-permute-start.34 = (bf16[128,384]{1,0:T(8,128)(2,1)}, bf16[128,384]{1,0:T(8,128)(2,1)}, u32[]{:S(2)}, u32[]{:S(2)}) collective-permute-start(bf16[128,384]{1,0:T(8,128)(2,1)} %get-tuple-element.66), channel_id=1, source_target_pairs={{0,16},{16,32},{32,48},{48,0},{64,80},{80,96},{96,112},{112,64},{1... | collective-permute-start | bytes 294920 | tf_op jit(solution)/shard_map/ppermute | solution.py:367
  153.8 6.1 %collective-permute-start.35 = (bf16[128,384]{1,0:T(8,128)(2,1)}, bf16[128,384]{1,0:T(8,128)(2,1)}, u32[]{:S(2)}, u32[]{:S(2)}) collective-permute-start(bf16[128,384]{1,0:T(8,128)(2,1)} %get-tuple-element.67), channel_id=1, source_target_pairs={{0,48},{16,0},{32,16},{48,32},{64,112},{80,64},{96,80},{112,96},{1... | collective-permute-start | bytes 294920 | tf_op jit(solution)/shard_map/ppermute | solution.py:367
  153.8 6.1 %collective-permute-start.36 = (bf16[128,384]{1,0:T(8,128)(2,1)}, bf16[128,384]{1,0:T(8,128)(2,1)}, u32[]{:S(2)}, u32[]{:S(2)}) collective-permute-start(bf16[128,384]{1,0:T(8,128)(2,1)} %get-tuple-element.68), channel_id=1, source_target_pairs={{0,32},{16,48},{32,0},{48,16},{64,96},{80,112},{96,64},{112,80},{1... | collective-permute-start | bytes 294920 | tf_op jit(solution)/shard_map/ppermute | solution.py:367
  157.1 12.1 %copy-start.12 = (bf16[128,384]{1,0:T(8,128)(2,1)S(1)}, bf16[128,384]{1,0:T(8,128)(2,1)}, u32[]{:S(2)}) copy-start(bf16[128,384]{1,0:T(8,128)(2,1)} %copy-done.11) | copy-start | bytes 294916
  157.1 26.3 %copy-start.13 = (pred[256,128]{1,0:T(32,128)(4,1)S(1)}, pred[256,128]{1,0:T(32,128)(4,1)}, u32[]{:S(2)}) copy-start(pred[256,128]{1,0:T(32,128)(4,1)} %get-tuple-element.75) | copy-start | bytes 98308
  157.1 4.8 %collective-permute-start.26 = (bf16[128,384]{1,0:T(8,128)(2,1)S(1)}, bf16[128,384]{1,0:T(8,128)(2,1)S(1)}, u32[]{:S(2)}, u32[]{:S(2)}) collective-permute-start(bf16[128,384]{1,0:T(8,128)(2,1)S(1)} %get-tuple-element.58), channel_id=1, source_target_pairs={{0,64},{16,80},{32,96},{48,112},{64,128},{80,144},{96,160},{112,17... | collective-permute-start | bytes 294920 | tf_op jit(solution)/shard_map/ppermute | solution.py:367
  157.2 5.1 %collective-permute-start.27 = (bf16[128,384]{1,0:T(8,128)(2,1)S(1)}, bf16[128,384]{1,0:T(8,128)(2,1)S(1)}, u32[]{:S(2)}, u32[]{:S(2)}) collective-permute-start(bf16[128,384]{1,0:T(8,128)(2,1)S(1)} %get-tuple-element.59), channel_id=1, source_target_pairs={{0,192},{16,208},{32,224},{48,240},{64,0},{80,16},{96,32},{112,48}... | collective-permute-start | bytes 294920 | tf_op jit(solution)/shard_map/ppermute | solution.py:367
  159.9 5.1 %collective-permute-start.28 = (bf16[128,384]{1,0:T(8,128)(2,1)S(1)}, bf16[128,384]{1,0:T(8,128)(2,1)S(1)}, u32[]{:S(2)}, u32[]{:S(2)}) collective-permute-start(bf16[128,384]{1,0:T(8,128)(2,1)S(1)} %get-tuple-element.60), channel_id=1, source_target_pairs={{0,128},{16,144},{32,160},{48,176},{64,192},{80,208},{96,224},{112... | collective-permute-start | bytes 294920 | tf_op jit(solution)/shard_map/ppermute | solution.py:367
  165.8 12.0 %all-to-all-start.2 = ((bf16[8,32,384]{2,1,0:T(8,128)(2,1)}), bf16[8,32,384]{2,1,0:T(8,128)(2,1)S(1)}, u32[]{:S(2)}, u32[]{:S(2)}) async-start(bf16[8,32,384]{2,1,0:T(8,128)(2,1)} %multiply_convert_fusion), calls=%async_computation.2 | async-start | bytes 393216 | tf_op jit(solution)/shard_map/all_to_all | solution.py:372
  177.9 5.5 %collective-permute-start.37 = (bf16[256,192]{1,0:T(8,128)(2,1)S(1)}, bf16[256,192]{1,0:T(8,128)(2,1)S(1)}, u32[]{:S(2)}, u32[]{:S(2)}) collective-permute-start(bf16[256,192]{1,0:T(8,128)(2,1)S(1)} %broadcast_select_fusion), channel_id=1, source_target_pairs={{0,1},{1,0},{2,3},{3,2},{4,5},{5,4},{6,7},{7,6},{8,9},{9,8},{10,11... | collective-permute-start | bytes 294920 | tf_op jit(solution)/shard_map/ppermute | solution.py:22
  (7 other events, 12.6 us)

commit v7 on v6

--- a/solution.py
+++ b/solution.py
@@ -127,17 +127,18 @@
         for n, (ref, to) in enumerate(((q_in, q), (k_in, k_new), (v_in, v_new)))
     ]
 
-    def block_copies(b):
-        rows = pl.ds(pl.multiple_of(b * 16, 16), 16)
-        return (
-            pltpu.make_async_copy(keys.at[rows], k.at[rows], block_sems.at[b, 0]),
-            pltpu.make_async_copy(values.at[rows], v.at[rows], block_sems.at[b, 1]),
-        )
+    def block_copies(b, which):
+        ref, to = ((keys, k), (values, v))[which]
+        rows = [pl.ds(pl.multiple_of(b * 16, 16) + n * 4, 4) for n in range(4)]
+        return [
+            pltpu.make_async_copy(ref.at[rows[n]], to.at[rows[n]], block_sems.at[b, which, n])
+            for n in range(4)
+        ]
 
     for copy in small:
         copy.start()
     for b in range(2):
-        for copy in block_copies(b):
+        for copy in block_copies(b, 0) + block_copies(b, 1):
             copy.start()
     for copy in small:
         copy.wait()
@@ -155,8 +156,8 @@
         own_scores = jnp.sum(own_products, axis=2, keepdims=True) * inv_root
         narrow = queries.astype(BF16)
         position = lax.broadcasted_iota(jnp.int32, (8, 192), 1)
-        key_copy, value_copy = block_copies(b)
-        key_copy.wait()
+        for copy in block_copies(b, 0):
+            copy.wait()
         scores = []
         for r in range(16):
             products = lax.dot_general(
@@ -175,7 +176,8 @@
         weights = (weights * scale).astype(BF16).reshape(128, 192)
         own_weights = (own_weights * scale).astype(BF16).astype(F32)
         own_part = own_weights * v_new[rows, :].astype(F32)[:, None, :]
-        value_copy.wait()
+        for copy in block_copies(b, 1):
+            copy.wait()
         for r in range(16):
             mixed = jnp.dot(
                 weights[r * 8 : r * 8 + 8], v[b * 16 + r], preferred_element_type=F32
@@ -205,7 +207,7 @@
             pltpu.VMEM((128, 128), F32),
             pltpu.VMEM((128, 128), F32),
             pltpu.SemaphoreType.DMA((3,)),
-            pltpu.SemaphoreType.DMA((2, 2)),
+            pltpu.SemaphoreType.DMA((2, 2, 4)),
         ],
         compiler_params=pltpu.CompilerParams(vmem_limit_bytes=ALL_VMEM),
         name="attend",

time: 186 us -> 187 us (level)
  no operation moved by 1% of the time
where the time goes in v7:
time: 187 us; the launch traced here: 185 us
  starting transfers between devices  65.1 us (35%)
  waiting for transfers between devices  56.8 us (30%)
  Pallas kernels  21.2 us (11%)
  matrix products  14.1 us (8%)
  blocking collectives  13.4 us (7%)
  local copies, waits for them, and re-layouts  7.2 us (4%)
  other arithmetic  6.68 us (4%)
    ppermute x8, starting transfers between devices, swap_cores(): return lax.ppermute(a, 'side', SWAP)  15.6 us
    all_to_all x1, blocking collectives, shards(): lax.all_to_all(routed.reshape(8, 32, 384), 'tensor', split_axis=0, concat...  13.4 us
    pallas_call x6, Pallas kernels, local_call(): pl.pallas_call(kernel, in_specs=first + [vmem] * (len(args) - len(first))...  12.6 us
    ppermute x6, starting transfers between devices, shards(): got = [lax.ppermute(rows[d], 'dp', far[d]) for d in (1, 3, 2)]  10.8 us
    ppermute x3, waiting for transfers between devices, shards(): lax.ppermute(rows_x, 'dp', SHIFT_Y[d])  10.6 us
    ppermute x6, starting transfers between devices, shards(): got = [lax.ppermute(sums[d], 'dp', near[d]) for d in (1, 3, 2)]  9.07 us
    all_to_all x1, starting transfers between devices, shards(): lax.all_to_all(head_sums, 'tensor', split_axis=0, concat_axis=0, tiled=True)  8.18 us
    all_to_all x1, waiting for transfers between devices, shards(): lax.all_to_all(parts.reshape(8, 32, 384), 'tensor', split_axis=0, concat_...  7.59 us
  transfers between devices with their start and end apart: 40, of which 20 were waited for; matrix products, arithmetic and copies ran while one was open for 11% of the time, Pallas kernels for 6%

profile of v7, /device:TPU:1, one launch (start us, length us, event | category | flops | bytes accessed | tf_op | source)
XLA Modules:
  0.0 184.7 jit_solution(15977184348858463743)
XLA Ops:
  0.0 5.7 %attend.1 = bf16[32,768]{1,0:T(8,128)(2,1)} custom-call(s32[32]{0:T(128)} %lengths.1, bf16[32,768]{1,0:T(8,128)(2,1)} %q_in.1, bf16[32,128]{1,0:T(8,128)(2,1)} %k_in.1, bf16[32,128]{1,0:T(8,128)(2,1)} %v_in.1, bf16[32,192,128]{2,1,0:T(8,128)(2,1)} %keys.1, bf16[32,192,128]{2,1,0:T(8,128)(2,1)} %values.1), custom_call_target="tpu_custom_call" | custom-call | tf_op jit(solution)/shard_map/attend/pallas_call | solution.py:196
  5.8 3.4 %collective-permute-start.2 = (bf16[32,768]{1,0:T(8,128)(2,1)}, bf16[32,768]{1,0:T(8,128)(2,1)S(1)}, u32[]{:S(2)}, u32[]{:S(2)}) collective-permute-start(bf16[32,768]{1,0:T(8,128)(2,1)} %attend.1), channel_id=1, source_target_pairs={{0,192},{16,208},{32,224},{48,240},{64,0},{80,16},{96,32},{112,48}... | collective-permute-start | bytes 147464 | tf_op jit(solution)/shard_map/ppermute | solution.py:282
  10.3 1.5 collective-permute-start.6
  11.8 2.0 %collective-permute-done.1 = bf16[32,768]{1,0:T(8,128)(2,1)S(1)} collective-permute-done((bf16[32,768]{1,0:T(8,128)(2,1)}, bf16[32,768]{1,0:T(8,128)(2,1)S(1)}, u32[]{:S(2)}, u32[]{:S(2)}) %collective-permute-start.1) | collective-permute-done | bytes 49184 | tf_op jit(solution)/shard_map/ppermute | solution.py:282
  15.1 2.8 %collective-permute-start.5 = (bf16[4,32,768]{2,1,0:T(8,128)(2,1)S(1)}, bf16[4,32,768]{2,1,0:T(8,128)(2,1)S(1)}, u32[]{:S(2)}, u32[]{:S(2)}) collective-permute-start(bf16[4,32,768]{2,1,0:T(8,128)(2,1)S(1)} %pad_maximum_fusion.7.g0), channel_id=1, source_target_pairs={{0,48},{16,0},{32,16},{48,32},{64,112},{80,64},{96,80},{112,96},{1... | collective-permute-start | bytes 589832 | tf_op jit(solution)/shard_map/ppermute | solution.py:286
  19.1 3.6 %collective-permute-done.5.g3 = bf16[4,32,768]{2,1,0:T(8,128)(2,1)S(1)} collective-permute-done((bf16[4,32,768]{2,1,0:T(8,128)(2,1)S(1)}, bf16[4,32,768]{2,1,0:T(8,128)(2,1)S(1)}, u32[]{:S(2)}, u32[]{:S(2)}) %collective-permute-start.5) | collective-permute-done | bytes 196640 | tf_op jit(solution)/shard_map/ppermute | solution.py:286
  22.7 1.5 collective-permute-done.4.g2
  24.2 5.5 %collective-permute-done.3.g1 = bf16[4,32,768]{2,1,0:T(8,128)(2,1)} collective-permute-done((bf16[4,32,768]{2,1,0:T(8,128)(2,1)S(1)}, bf16[4,32,768]{2,1,0:T(8,128)(2,1)}, u32[]{:S(2)}, u32[]{:S(2)}) %collective-permute-start.3) | collective-permute-done | bytes 196640 | tf_op jit(solution)/shard_map/ppermute | solution.py:286
  29.7 2.8 %out_projection.1 = bf16[8,64,384]{2,1,0:T(8,128)(2,1)} custom-call(s32[3]{0:T(128)S(1)} %pad_add_fusion.pos, bf16[4,32,768]{2,1,0:T(8,128)(2,1)S(1)} %pad_maximum_fusion.7.g0, bf16[4,32,768]{2,1,0:T(8,128)(2,1)} %collective-permute-done.3.g1, bf16[4,32,768]{2,1,0:T(8,128)(2,1)} %collective-permute-done.4.g2, ...), custom_call_target="tpu_custom_call" | custom-call | tf_op jit(solution)/shard_map/out_projection/pallas_call | solution.py:288
  32.5 8.2 %all-to-all-start = ((bf16[8,64,384]{2,1,0:T(8,128)(2,1)}), bf16[8,64,384]{2,1,0:T(8,128)(2,1)S(1)}, u32[]{:S(2)}, u32[]{:S(2)}) async-start(bf16[8,64,384]{2,1,0:T(8,128)(2,1)} %out_projection.1), calls=%async_computation | async-start | bytes 786432 | tf_op jit(solution)/shard_map/all_to_all | solution.py:297
  40.7 1.5 copy.23
  42.2 1.7 collective-permute-start.7
  43.9 1.2 collective-permute-done.7
  46.8 6.3 %all-to-all-done = bf16[8,64,384]{2,1,0:T(8,128)(2,1)S(1)} async-done(((bf16[8,64,384]{2,1,0:T(8,128)(2,1)}), bf16[8,64,384]{2,1,0:T(8,128)(2,1)S(1)}, u32[]{:S(2)}, u32[]{:S(2)}) %all-to-all-start) | async-done | bytes 393248 | tf_op jit(solution)/shard_map/all_to_all | solution.py:297
  54.1 3.3 %collective-permute-start.8 = (bf16[64,384]{1,0:T(8,128)(2,1)S(1)}, bf16[64,384]{1,0:T(8,128)(2,1)S(1)}, u32[]{:S(2)}, u32[]{:S(2)}) collective-permute-start(bf16[64,384]{1,0:T(8,128)(2,1)S(1)} %fusion.32), channel_id=1, source_target_pairs={{0,1},{1,0},{2,3},{3,2},{4,5},{5,4},{6,7},{7,6},{8,9},{9,8},{10,11... | collective-permute-start | bytes 147464 | tf_op jit(solution)/shard_map/ppermute | solution.py:22
  58.7 13.4 %all_to_all.15 = bf16[8,32,384]{2,1,0:T(8,128)(2,1)S(1)} all-to-all(bf16[8,32,384]{2,1,0:T(8,128)(2,1)S(1)} %bitcast.96), channel_id=1, replica_groups=mesh['dp'=16,'tensor'=8,'side'=2] {'tensor'}, dimensions={0} | all-to-all | bytes 393216 | tf_op jit(solution)/shard_map/all_to_all | solution.py:306
  74.4 1.8 collective-permute-done.11
  76.1 2.0 %collective-permute-done.10 = bf16[128,384]{1,0:T(8,128)(2,1)S(1)} collective-permute-done((bf16[128,384]{1,0:T(8,128)(2,1)S(1)}, bf16[128,384]{1,0:T(8,128)(2,1)S(1)}, u32[]{:S(2)}, u32[]{:S(2)}) %collective-permute-start.10) | collective-permute-done | bytes 98336 | tf_op jit(solution)/shard_map/ppermute | solution.py:312
  78.1 3.1 %collective-permute-done.9 = bf16[128,384]{1,0:T(8,128)(2,1)S(1)} collective-permute-done((bf16[128,384]{1,0:T(8,128)(2,1)S(1)}, bf16[128,384]{1,0:T(8,128)(2,1)S(1)}, u32[]{:S(2)}, u32[]{:S(2)}) %collective-permute-start.9) | collective-permute-done | bytes 98336 | tf_op jit(solution)/shard_map/ppermute | solution.py:312
  83.0 2.1 %collective-permute-start.20 = (bf16[4,128,384]{2,1,0:T(8,128)(2,1)S(1)}, bf16[4,128,384]{2,1,0:T(8,128)(2,1)S(1)}, u32[]{:S(2)}, u32[]{:S(2)}) collective-permute-start(bf16[4,128,384]{2,1,0:T(8,128)(2,1)S(1)} %pad_maximum_fusion.5.s0), channel_id=1, source_target_pairs={{0,192},{16,208},{32,224},{48,240},{64,0},{80,16},{96,32},{112,48}... | collective-permute-start | bytes 1179656 | tf_op jit(solution)/shard_map/ppermute | solution.py:318
  85.1 2.6 %collective-permute-start.19 = (bf16[4,128,384]{2,1,0:T(8,128)(2,1)S(1)}, bf16[4,128,384]{2,1,0:T(8,128)(2,1)S(1)}, u32[]{:S(2)}, u32[]{:S(2)}) collective-permute-start(bf16[4,128,384]{2,1,0:T(8,128)(2,1)S(1)} %pad_maximum_fusion.4.s0), channel_id=1, source_target_pairs={{0,48},{16,0},{32,16},{48,32},{64,112},{80,64},{96,80},{112,96},{1... | collective-permute-start | bytes 1179656 | tf_op jit(solution)/shard_map/ppermute | solution.py:317
  87.7 4.3 %collective-permute-done.16.s1 = bf16[4,128,384]{2,1,0:T(8,128)(2,1)S(1)} collective-permute-done((bf16[4,128,384]{2,1,0:T(8,128)(2,1)S(1)}, bf16[4,128,384]{2,1,0:T(8,128)(2,1)S(1)}, u32[]{:S(2)}, u32[]{:S(2)}) %collective-permute-start.16) | collective-permute-done | bytes 393248 | tf_op jit(solution)/shard_map/ppermute | solution.py:318
  92.7 1.9 %collective-permute-start.18 = (bf16[4,128,384]{2,1,0:T(8,128)(2,1)S(1)}, bf16[4,128,384]{2,1,0:T(8,128)(2,1)S(1)}, u32[]{:S(2)}, u32[]{:S(2)}) collective-permute-start(bf16[4,128,384]{2,1,0:T(8,128)(2,1)S(1)} %pad_maximum_fusion.5.s0), channel_id=1, source_target_pairs={{0,128},{16,144},{32,160},{48,176},{64,192},{80,208},{96,224},{112... | collective-permute-start | bytes 1179656 | tf_op jit(solution)/shard_map/ppermute | solution.py:321
  94.6 7.1 %collective-permute-done.17.s2 = bf16[4,128,384]{2,1,0:T(8,128)(2,1)S(1)} collective-permute-done((bf16[4,128,384]{2,1,0:T(8,128)(2,1)S(1)}, bf16[4,128,384]{2,1,0:T(8,128)(2,1)S(1)}, u32[]{:S(2)}, u32[]{:S(2)}) %collective-permute-start.17) | collective-permute-done | bytes 393248 | tf_op jit(solution)/shard_map/ppermute | solution.py:321
  102.5 1.8 norm.3
  104.3 4.1 %collective-permute-start.29 = (bf16[128,6144]{1,0:T(8,128)(2,1)S(1)}, bf16[128,6144]{1,0:T(8,128)(2,1)S(1)}, u32[]{:S(2)}, u32[]{:S(2)}) collective-permute-start(bf16[128,6144]{1,0:T(8,128)(2,1)S(1)} %norm.3), channel_id=1, source_target_pairs={{0,1},{1,0},{2,3},{3,2},{4,5},{5,4},{6,7},{7,6},{8,9},{9,8},{10,11... | collective-permute-start | bytes 4718600 | tf_op jit(solution)/shard_map/ppermute | solution.py:22
  108.4 1.8 norm.2
  111.4 1.3 copy-done.10
  114.9 1.8 convolution_convert_fusion.1
  117.9 1.8 convolution_convert_fusion.2
  121.2 2.8 %combine_cores.3 = (bf16[4,128,384]{2,1,0:T(8,128)(2,1)S(1)}, bf16[4,128,384]{2,1,0:T(8,128)(2,1)}, bf16[4,128,384]{2,1,0:T(8,128)(2,1)}, bf16[4,128,384]{2,1,0:T(8,128)(2,1)}) custom-call(s32[3]{0:T(128)S(1)} %pad_add_fusion.pos, bf16[256,6144]{1,0:T(8,128)(2,1)S(1)} %convolution_convert_fusion.own, bf16[128,6144]{1,0:T(8,128)(2,1)} %collective-permute-done.30.other), custom_call_target="tpu_custom_call" | custom-call | tf_op jit(solution)/shard_map/combine_cores/pallas_call | solution.py:112
  124.1 1.2 collective-permute-start.31
  125.4 1.5 collective-permute-start.32
  127.6 2.5 %combine_cores.2 = (bf16[4,128,384]{2,1,0:T(8,128)(2,1)S(1)}, bf16[4,128,384]{2,1,0:T(8,128)(2,1)}, bf16[4,128,384]{2,1,0:T(8,128)(2,1)S(1)}, bf16[4,128,384]{2,1,0:T(8,128)(2,1)S(1)}) custom-call(s32[3]{0:T(128)S(1)} %pad_add_fusion.pos, bf16[256,6144]{1,0:T(8,128)(2,1)S(1)} %convolution_convert_fusion.own, bf16[128,6144]{1,0:T(8,128)(2,1)} %collective-permute-done.22.other), custom_call_target="tpu_custom_call" | custom-call | tf_op jit(solution)/shard_map/combine_cores/pallas_call | solution.py:112
  132.2 2.4 %collective-permute-start.24 = (bf16[4,128,384]{2,1,0:T(8,128)(2,1)}, bf16[4,128,384]{2,1,0:T(8,128)(2,1)}, u32[]{:S(2)}, u32[]{:S(2)}) collective-permute-start(bf16[4,128,384]{2,1,0:T(8,128)(2,1)} %copy-done.8), channel_id=1, source_target_pairs={{0,48},{16,0},{32,16},{48,32},{64,112},{80,64},{96,80},{112,96},{1... | collective-permute-start | bytes 1179656 | tf_op jit(solution)/shard_map/ppermute | solution.py:360
  134.6 1.7 collective-permute-done.31.got1
  136.3 2.9 %collective-permute-start.25 = (bf16[4,128,384]{2,1,0:T(8,128)(2,1)}, bf16[4,128,384]{2,1,0:T(8,128)(2,1)}, u32[]{:S(2)}, u32[]{:S(2)}) collective-permute-start(bf16[4,128,384]{2,1,0:T(8,128)(2,1)} %copy-done.7), channel_id=1, source_target_pairs={{0,32},{16,48},{32,0},{48,16},{64,96},{80,112},{96,64},{112,80},{1... | collective-permute-start | bytes 1179656 | tf_op jit(solution)/shard_map/ppermute | solution.py:360
  139.3 2.8 %fusion.22 = f32[256]{0:T(256)S(1)} fusion(bf16[6144,8]{0,1:T(8,128)(2,1)} %param.23, bf16[128,6144]{1,0:T(8,128)(2,1)} %copy-done.1, bf16[128,6144]{1,0:T(8,128)(2,1)} %copy-done.2, s32[256]{0:T(256)S(1)} %eq.144, f32[8]{0:T(128)S(1)} %compare_convert_fusion), kind=kOutput, calls=%fused_computation.26 | convolution fusion | flops 31467264 | bytes 3246112 | tf_op jit(solution)/shard_map/dot_general | solution.py:339
  142.1 3.0 %collective-permute-done.33.got3 = bf16[4,128,384]{2,1,0:T(8,128)(2,1)} collective-permute-done((bf16[4,128,384]{2,1,0:T(8,128)(2,1)}, bf16[4,128,384]{2,1,0:T(8,128)(2,1)}, u32[]{:S(2)}, u32[]{:S(2)}) %collective-permute-start.33) | collective-permute-done | bytes 393248 | tf_op jit(solution)/shard_map/ppermute | solution.py:360
  145.1 2.2 %sum_rows.3 = (f32[128,384]{1,0:T(8,128)S(1)}, bf16[128,384]{1,0:T(8,128)(2,1)}, bf16[128,384]{1,0:T(8,128)(2,1)}, bf16[128,384]{1,0:T(8,128)(2,1)}) custom-call(bf16[4,128,384]{2,1,0:T(8,128)(2,1)S(1)} %copy-done.4, bf16[4,128,384]{2,1,0:T(8,128)(2,1)} %collective-permute-done.31.got1, bf16[4,128,384]{2,1,0:T(8,128)(2,1)} %collective-permute-done.32.got2, ...), custom_call_target="tpu_custom_call" | custom-call | tf_op jit(solution)/shard_map/sum_rows/pallas_call | solution.py:112
  147.9 6.3 %collective-permute-start.34 = (bf16[128,384]{1,0:T(8,128)(2,1)}, bf16[128,384]{1,0:T(8,128)(2,1)}, u32[]{:S(2)}, u32[]{:S(2)}) collective-permute-start(bf16[128,384]{1,0:T(8,128)(2,1)} %get-tuple-element.66), channel_id=1, source_target_pairs={{0,16},{16,32},{32,48},{48,0},{64,80},{80,96},{96,112},{112,64},{1... | collective-permute-start | bytes 294920 | tf_op jit(solution)/shard_map/ppermute | solution.py:369
  154.2 1.8 collective-permute-start.36
  156.0 1.5 sum_rows.2
  157.6 2.7 %collective-permute-start.27 = (bf16[128,384]{1,0:T(8,128)(2,1)S(1)}, bf16[128,384]{1,0:T(8,128)(2,1)S(1)}, u32[]{:S(2)}, u32[]{:S(2)}) collective-permute-start(bf16[128,384]{1,0:T(8,128)(2,1)S(1)} %get-tuple-element.59), channel_id=1, source_target_pairs={{0,192},{16,208},{32,224},{48,240},{64,0},{80,16},{96,32},{112,48}... | collective-permute-start | bytes 294920 | tf_op jit(solution)/shard_map/ppermute | solution.py:369
  162.8 2.6 %collective-permute-done.28 = bf16[128,384]{1,0:T(8,128)(2,1)S(1)} collective-permute-done((bf16[128,384]{1,0:T(8,128)(2,1)S(1)}, bf16[128,384]{1,0:T(8,128)(2,1)S(1)}, u32[]{:S(2)}, u32[]{:S(2)}) %collective-permute-start.28) | collective-permute-done | bytes 98336 | tf_op jit(solution)/shard_map/ppermute | solution.py:369
  166.2 3.4 %all-to-all-start.2 = ((bf16[8,32,384]{2,1,0:T(8,128)(2,1)}), bf16[8,32,384]{2,1,0:T(8,128)(2,1)S(1)}, u32[]{:S(2)}, u32[]{:S(2)}) async-start(bf16[8,32,384]{2,1,0:T(8,128)(2,1)} %multiply_convert_fusion), calls=%async_computation.2 | async-start | bytes 393216 | tf_op jit(solution)/shard_map/all_to_all | solution.py:374
  170.6 7.6 %all-to-all-done.2 = bf16[8,32,384]{2,1,0:T(8,128)(2,1)S(1)} async-done(((bf16[8,32,384]{2,1,0:T(8,128)(2,1)}), bf16[8,32,384]{2,1,0:T(8,128)(2,1)S(1)}, u32[]{:S(2)}, u32[]{:S(2)}) %all-to-all-start.2) | async-done | bytes 196640 | tf_op jit(solution)/shard_map/all_to_all | solution.py:374
  178.3 4.5 %collective-permute-start.37 = (bf16[256,192]{1,0:T(8,128)(2,1)S(1)}, bf16[256,192]{1,0:T(8,128)(2,1)S(1)}, u32[]{:S(2)}, u32[]{:S(2)}) collective-permute-start(bf16[256,192]{1,0:T(8,128)(2,1)S(1)} %broadcast_select_fusion), channel_id=1, source_target_pairs={{0,1},{1,0},{2,3},{3,2},{4,5},{5,4},{6,7},{7,6},{8,9},{9,8},{10,11... | collective-permute-start | bytes 294920 | tf_op jit(solution)/shard_map/ppermute | solution.py:22
  (122 shorter events, 29.1 us)
Async XLA Ops:
  0.0 114.9 %copy-start = (bf16[1,256,6144]{2,1,0:T(8,128)(2,1)S(1)}, bf16[1,256,6144]{2,1,0:T(8,128)(2,1)}, u32[]{:S(2)}) copy-start(bf16[1,256,6144]{2,1,0:T(8,128)(2,1)} %param.27) | copy-start | bytes 9437188
  0.0 43.9 %copy-start.14 = (s32[1024,2]{0,1:T(2,128)S(1)}, s32[1024,2]{0,1:T(2,128)}, u32[]{:S(2)}) copy-start(s32[1024,2]{0,1:T(2,128)} %param.24) | copy-start | bytes 24580
  5.8 6.0 %collective-permute-start.2 = (bf16[32,768]{1,0:T(8,128)(2,1)}, bf16[32,768]{1,0:T(8,128)(2,1)S(1)}, u32[]{:S(2)}, u32[]{:S(2)}) collective-permute-start(bf16[32,768]{1,0:T(8,128)(2,1)} %attend.1), channel_id=1, source_target_pairs={{0,192},{16,208},{32,224},{48,240},{64,0},{80,16},{96,32},{112,48}... | collective-permute-start | bytes 147464 | tf_op jit(solution)/shard_map/ppermute | solution.py:282
  9.1 4.7 %collective-permute-start.1 = (bf16[32,768]{1,0:T(8,128)(2,1)}, bf16[32,768]{1,0:T(8,128)(2,1)S(1)}, u32[]{:S(2)}, u32[]{:S(2)}) collective-permute-start(bf16[32,768]{1,0:T(8,128)(2,1)} %attend.1), channel_id=1, source_target_pairs={{0,128},{16,144},{32,160},{48,176},{64,192},{80,208},{96,224},{112... | collective-permute-start | bytes 147464 | tf_op jit(solution)/shard_map/ppermute | solution.py:282
  9.7 4.7 %collective-permute-start = (bf16[32,768]{1,0:T(8,128)(2,1)}, bf16[32,768]{1,0:T(8,128)(2,1)S(1)}, u32[]{:S(2)}, u32[]{:S(2)}) collective-permute-start(bf16[32,768]{1,0:T(8,128)(2,1)} %attend.1), channel_id=1, source_target_pairs={{0,64},{16,80},{32,96},{48,112},{64,128},{80,144},{96,160},{112,17... | collective-permute-start | bytes 147464 | tf_op jit(solution)/shard_map/ppermute | solution.py:282
  10.3 19.4 %collective-permute-start.6 = (bf16[192,768]{1,0:T(8,128)(2,1)}, bf16[192,768]{1,0:T(8,128)(2,1)}, u32[]{:S(2)}, u32[]{:S(2)}) collective-permute-start(bf16[192,768]{1,0:T(8,128)(2,1)} %bitcast.7.w_own), channel_id=1, source_target_pairs={{0,1},{1,0},{2,3},{3,2},{4,5},{5,4},{6,7},{7,6},{8,9},{9,8},{10,11... | collective-permute-start | bytes 884744 | tf_op jit(solution)/shard_map/ppermute | solution.py:22
  15.1 7.5 %collective-permute-start.5 = (bf16[4,32,768]{2,1,0:T(8,128)(2,1)S(1)}, bf16[4,32,768]{2,1,0:T(8,128)(2,1)S(1)}, u32[]{:S(2)}, u32[]{:S(2)}) collective-permute-start(bf16[4,32,768]{2,1,0:T(8,128)(2,1)S(1)} %pad_maximum_fusion.7.g0), channel_id=1, source_target_pairs={{0,48},{16,0},{32,16},{48,32},{64,112},{80,64},{96,80},{112,96},{1... | collective-permute-start | bytes 589832 | tf_op jit(solution)/shard_map/ppermute | solution.py:286
  18.0 6.2 %collective-permute-start.4 = (bf16[4,32,768]{2,1,0:T(8,128)(2,1)S(1)}, bf16[4,32,768]{2,1,0:T(8,128)(2,1)}, u32[]{:S(2)}, u32[]{:S(2)}) collective-permute-start(bf16[4,32,768]{2,1,0:T(8,128)(2,1)S(1)} %pad_maximum_fusion.7.g0), channel_id=1, source_target_pairs={{0,32},{16,48},{32,0},{48,16},{64,96},{80,112},{96,64},{112,80},{1... | collective-permute-start | bytes 589832 | tf_op jit(solution)/shard_map/ppermute | solution.py:286
  18.3 11.4 %collective-permute-start.3 = (bf16[4,32,768]{2,1,0:T(8,128)(2,1)S(1)}, bf16[4,32,768]{2,1,0:T(8,128)(2,1)}, u32[]{:S(2)}, u32[]{:S(2)}) collective-permute-start(bf16[4,32,768]{2,1,0:T(8,128)(2,1)S(1)} %pad_maximum_fusion.7.g0), channel_id=1, source_target_pairs={{0,16},{16,32},{32,48},{48,0},{64,80},{80,96},{96,112},{112,64},{1... | collective-permute-start | bytes 589832 | tf_op jit(solution)/shard_map/ppermute | solution.py:286
  32.5 20.6 %all-to-all-start = ((bf16[8,64,384]{2,1,0:T(8,128)(2,1)}), bf16[8,64,384]{2,1,0:T(8,128)(2,1)S(1)}, u32[]{:S(2)}, u32[]{:S(2)}) async-start(bf16[8,64,384]{2,1,0:T(8,128)(2,1)} %out_projection.1), calls=%async_computation | async-start | bytes 786432 | tf_op jit(solution)/shard_map/all_to_all | solution.py:297
  42.2 2.9 %collective-permute-start.7 = (bf16[128,192]{1,0:T(8,128)(2,1)}, bf16[128,192]{1,0:T(8,128)(2,1)}, u32[]{:S(2)}, u32[]{:S(2)}) collective-permute-start(bf16[128,192]{1,0:T(8,128)(2,1)} %copy.23), channel_id=1, source_target_pairs={{0,1},{1,0},{2,3},{3,2},{4,5},{5,4},{6,7},{7,6},{8,9},{9,8},{10,11... | collective-permute-start | bytes 147464 | tf_op jit(solution)/shard_map/ppermute | solution.py:22
  54.1 4.4 %collective-permute-start.8 = (bf16[64,384]{1,0:T(8,128)(2,1)S(1)}, bf16[64,384]{1,0:T(8,128)(2,1)S(1)}, u32[]{:S(2)}, u32[]{:S(2)}) collective-permute-start(bf16[64,384]{1,0:T(8,128)(2,1)S(1)} %fusion.32), channel_id=1, source_target_pairs={{0,1},{1,0},{2,3},{3,2},{4,5},{5,4},{6,7},{7,6},{8,9},{9,8},{10,11... | collective-permute-start | bytes 147464 | tf_op jit(solution)/shard_map/ppermute | solution.py:22
  58.5 23.6 %copy-start.11 = (bf16[128,384]{1,0:T(8,128)(2,1)}, bf16[128,384]{1,0:T(8,128)(2,1)S(1)}, u32[]{:S(2)}) copy-start(bf16[128,384]{1,0:T(8,128)(2,1)S(1)} %maximum_select_fusion.1) | copy-start | bytes 294916
  72.1 4.0 %collective-permute-start.11 = (bf16[128,384]{1,0:T(8,128)(2,1)S(1)}, bf16[128,384]{1,0:T(8,128)(2,1)S(1)}, u32[]{:S(2)}, u32[]{:S(2)}) collective-permute-start(bf16[128,384]{1,0:T(8,128)(2,1)S(1)} %bitcast.98), channel_id=1, source_target_pairs={{0,192},{16,208},{32,224},{48,240},{64,0},{80,16},{96,32},{112,48}... | collective-permute-start | bytes 294920 | tf_op jit(solution)/shard_map/ppermute | solution.py:312
  73.1 5.1 %collective-permute-start.10 = (bf16[128,384]{1,0:T(8,128)(2,1)S(1)}, bf16[128,384]{1,0:T(8,128)(2,1)S(1)}, u32[]{:S(2)}, u32[]{:S(2)}) collective-permute-start(bf16[128,384]{1,0:T(8,128)(2,1)S(1)} %bitcast.99), channel_id=1, source_target_pairs={{0,128},{16,144},{32,160},{48,176},{64,192},{80,208},{96,224},{112... | collective-permute-start | bytes 294920 | tf_op jit(solution)/shard_map/ppermute | solution.py:312
  73.6 7.7 %collective-permute-start.9 = (bf16[128,384]{1,0:T(8,128)(2,1)S(1)}, bf16[128,384]{1,0:T(8,128)(2,1)S(1)}, u32[]{:S(2)}, u32[]{:S(2)}) collective-permute-start(bf16[128,384]{1,0:T(8,128)(2,1)S(1)} %bitcast.100), channel_id=1, source_target_pairs={{0,64},{16,80},{32,96},{48,112},{64,128},{80,144},{96,160},{112,17... | collective-permute-start | bytes 294920 | tf_op jit(solution)/shard_map/ppermute | solution.py:312
  74.3 6.9 %collective-permute-start.14 = (bf16[128,384]{1,0:T(8,128)(2,1)S(1)}, bf16[128,384]{1,0:T(8,128)(2,1)S(1)}, u32[]{:S(2)}, u32[]{:S(2)}) collective-permute-start(bf16[128,384]{1,0:T(8,128)(2,1)S(1)} %bitcast.102), channel_id=1, source_target_pairs={{0,48},{16,0},{32,16},{48,32},{64,112},{80,64},{96,80},{112,96},{1... | collective-permute-start | bytes 294920 | tf_op jit(solution)/shard_map/ppermute | solution.py:313
  74.3 6.9 %collective-permute-start.13 = (bf16[128,384]{1,0:T(8,128)(2,1)S(1)}, bf16[128,384]{1,0:T(8,128)(2,1)S(1)}, u32[]{:S(2)}, u32[]{:S(2)}) collective-permute-start(bf16[128,384]{1,0:T(8,128)(2,1)S(1)} %bitcast.103), channel_id=1, source_target_pairs={{0,32},{16,48},{32,0},{48,16},{64,96},{80,112},{96,64},{112,80},{1... | collective-permute-start | bytes 294920 | tf_op jit(solution)/shard_map/ppermute | solution.py:313
  76.1 5.9 %collective-permute-start.12 = (bf16[128,384]{1,0:T(8,128)(2,1)S(1)}, bf16[128,384]{1,0:T(8,128)(2,1)S(1)}, u32[]{:S(2)}, u32[]{:S(2)}) collective-permute-start(bf16[128,384]{1,0:T(8,128)(2,1)S(1)} %bitcast.104), channel_id=1, source_target_pairs={{0,16},{16,32},{32,48},{48,0},{64,80},{80,96},{96,112},{112,64},{1... | collective-permute-start | bytes 294920 | tf_op jit(solution)/shard_map/ppermute | solution.py:313
  82.2 9.8 %collective-permute-start.16 = (bf16[4,128,384]{2,1,0:T(8,128)(2,1)S(1)}, bf16[4,128,384]{2,1,0:T(8,128)(2,1)S(1)}, u32[]{:S(2)}, u32[]{:S(2)}) collective-permute-start(bf16[4,128,384]{2,1,0:T(8,128)(2,1)S(1)} %pad_maximum_fusion.5.s0), channel_id=1, source_target_pairs={{0,64},{16,80},{32,96},{48,112},{64,128},{80,144},{96,160},{112,17... | collective-permute-start | bytes 1179656 | tf_op jit(solution)/shard_map/ppermute | solution.py:318
  83.0 9.7 %collective-permute-start.15 = (bf16[4,128,384]{2,1,0:T(8,128)(2,1)S(1)}, bf16[4,128,384]{2,1,0:T(8,128)(2,1)S(1)}, u32[]{:S(2)}, u32[]{:S(2)}) collective-permute-start(bf16[4,128,384]{2,1,0:T(8,128)(2,1)S(1)} %pad_maximum_fusion.4.s0), channel_id=1, source_target_pairs={{0,16},{16,32},{32,48},{48,0},{64,80},{80,96},{96,112},{112,64},{1... | collective-permute-start | bytes 1179656 | tf_op jit(solution)/shard_map/ppermute | solution.py:317
  83.0 11.6 %collective-permute-start.20 = (bf16[4,128,384]{2,1,0:T(8,128)(2,1)S(1)}, bf16[4,128,384]{2,1,0:T(8,128)(2,1)S(1)}, u32[]{:S(2)}, u32[]{:S(2)}) collective-permute-start(bf16[4,128,384]{2,1,0:T(8,128)(2,1)S(1)} %pad_maximum_fusion.5.s0), channel_id=1, source_target_pairs={{0,192},{16,208},{32,224},{48,240},{64,0},{80,16},{96,32},{112,48}... | collective-permute-start | bytes 1179656 | tf_op jit(solution)/shard_map/ppermute | solution.py:318
  85.1 9.5 %collective-permute-start.19 = (bf16[4,128,384]{2,1,0:T(8,128)(2,1)S(1)}, bf16[4,128,384]{2,1,0:T(8,128)(2,1)S(1)}, u32[]{:S(2)}, u32[]{:S(2)}) collective-permute-start(bf16[4,128,384]{2,1,0:T(8,128)(2,1)S(1)} %pad_maximum_fusion.4.s0), channel_id=1, source_target_pairs={{0,48},{16,0},{32,16},{48,32},{64,112},{80,64},{96,80},{112,96},{1... | collective-permute-start | bytes 1179656 | tf_op jit(solution)/shard_map/ppermute | solution.py:317
  92.7 9.0 %collective-permute-start.17 = (bf16[4,128,384]{2,1,0:T(8,128)(2,1)S(1)}, bf16[4,128,384]{2,1,0:T(8,128)(2,1)S(1)}, u32[]{:S(2)}, u32[]{:S(2)}) collective-permute-start(bf16[4,128,384]{2,1,0:T(8,128)(2,1)S(1)} %pad_maximum_fusion.4.s0), channel_id=1, source_target_pairs={{0,32},{16,48},{32,0},{48,16},{64,96},{80,112},{96,64},{112,80},{1... | collective-permute-start | bytes 1179656 | tf_op jit(solution)/shard_map/ppermute | solution.py:321
  92.7 9.0 %collective-permute-start.18 = (bf16[4,128,384]{2,1,0:T(8,128)(2,1)S(1)}, bf16[4,128,384]{2,1,0:T(8,128)(2,1)S(1)}, u32[]{:S(2)}, u32[]{:S(2)}) collective-permute-start(bf16[4,128,384]{2,1,0:T(8,128)(2,1)S(1)} %pad_maximum_fusion.5.s0), channel_id=1, source_target_pairs={{0,128},{16,144},{32,160},{48,176},{64,192},{80,208},{96,224},{112... | collective-permute-start | bytes 1179656 | tf_op jit(solution)/shard_map/ppermute | solution.py:321
  102.5 7.9 %copy-start.9 = (bf16[1,6144,256]{2,1,0:T(8,128)(2,1)S(1)}, bf16[1,6144,256]{2,1,0:T(8,128)(2,1)}, u32[]{:S(2)}) copy-start(bf16[1,6144,256]{2,1,0:T(8,128)(2,1)} %param.25) | copy-start | bytes 9437188
  104.3 7.0 %copy-start.1 = (bf16[128,6144]{1,0:T(8,128)(2,1)}, bf16[128,6144]{1,0:T(8,128)(2,1)S(1)}, u32[]{:S(2)}) copy-start(bf16[128,6144]{1,0:T(8,128)(2,1)S(1)} %norm.3) | copy-start | bytes 4718596
  104.3 9.4 %collective-permute-start.29 = (bf16[128,6144]{1,0:T(8,128)(2,1)S(1)}, bf16[128,6144]{1,0:T(8,128)(2,1)S(1)}, u32[]{:S(2)}, u32[]{:S(2)}) collective-permute-start(bf16[128,6144]{1,0:T(8,128)(2,1)S(1)} %norm.3), channel_id=1, source_target_pairs={{0,1},{1,0},{2,3},{3,2},{4,5},{5,4},{6,7},{7,6},{8,9},{9,8},{10,11... | collective-permute-start | bytes 4718600 | tf_op jit(solution)/shard_map/ppermute | solution.py:22
  110.3 6.5 %collective-permute-start.21 = (bf16[128,6144]{1,0:T(8,128)(2,1)S(1)}, bf16[128,6144]{1,0:T(8,128)(2,1)S(1)}, u32[]{:S(2)}, u32[]{:S(2)}) collective-permute-start(bf16[128,6144]{1,0:T(8,128)(2,1)S(1)} %norm.2), channel_id=1, source_target_pairs={{0,1},{1,0},{2,3},{3,2},{4,5},{5,4},{6,7},{7,6},{8,9},{9,8},{10,11... | collective-permute-start | bytes 4718600 | tf_op jit(solution)/shard_map/ppermute | solution.py:22
  116.7 4.5 %collective-permute-start.30 = (bf16[128,6144]{1,0:T(8,128)(2,1)}, bf16[128,6144]{1,0:T(8,128)(2,1)}, u32[]{:S(2)}, u32[]{:S(2)}) collective-permute-start(bf16[128,6144]{1,0:T(8,128)(2,1)} %convolution_convert_fusion.1), channel_id=1, source_target_pairs={{0,1},{1,0},{2,3},{3,2},{4,5},{5,4},{6,7},{7,6},{8,9},{9,8},{10,11... | collective-permute-start | bytes 4718600 | tf_op jit(solution)/shard_map/ppermute | solution.py:22
  119.7 7.9 %collective-permute-start.22 = (bf16[128,6144]{1,0:T(8,128)(2,1)}, bf16[128,6144]{1,0:T(8,128)(2,1)}, u32[]{:S(2)}, u32[]{:S(2)}) collective-permute-start(bf16[128,6144]{1,0:T(8,128)(2,1)} %convolution_convert_fusion.2), channel_id=1, source_target_pairs={{0,1},{1,0},{2,3},{3,2},{4,5},{5,4},{6,7},{7,6},{8,9},{9,8},{10,11... | collective-permute-start | bytes 4718600 | tf_op jit(solution)/shard_map/ppermute | solution.py:22
  124.1 12.3 %collective-permute-start.31 = (bf16[4,128,384]{2,1,0:T(8,128)(2,1)}, bf16[4,128,384]{2,1,0:T(8,128)(2,1)}, u32[]{:S(2)}, u32[]{:S(2)}) collective-permute-start(bf16[4,128,384]{2,1,0:T(8,128)(2,1)} %get-tuple-element.62), channel_id=1, source_target_pairs={{0,64},{16,80},{32,96},{48,112},{64,128},{80,144},{96,160},{112,17... | collective-permute-start | bytes 1179656 | tf_op jit(solution)/shard_map/ppermute | solution.py:360
  125.4 16.7 %collective-permute-start.32 = (bf16[4,128,384]{2,1,0:T(8,128)(2,1)}, bf16[4,128,384]{2,1,0:T(8,128)(2,1)}, u32[]{:S(2)}, u32[]{:S(2)}) collective-permute-start(bf16[4,128,384]{2,1,0:T(8,128)(2,1)} %get-tuple-element.63), channel_id=1, source_target_pairs={{0,192},{16,208},{32,224},{48,240},{64,0},{80,16},{96,32},{112,48}... | collective-permute-start | bytes 1179656 | tf_op jit(solution)/shard_map/ppermute | solution.py:360
  126.9 18.2 %collective-permute-start.33 = (bf16[4,128,384]{2,1,0:T(8,128)(2,1)}, bf16[4,128,384]{2,1,0:T(8,128)(2,1)}, u32[]{:S(2)}, u32[]{:S(2)}) collective-permute-start(bf16[4,128,384]{2,1,0:T(8,128)(2,1)} %get-tuple-element.64), channel_id=1, source_target_pairs={{0,128},{16,144},{32,160},{48,176},{64,192},{80,208},{96,224},{112... | collective-permute-start | bytes 1179656 | tf_op jit(solution)/shard_map/ppermute | solution.py:360
  131.6 22.6 %collective-permute-start.23 = (bf16[4,128,384]{2,1,0:T(8,128)(2,1)}, bf16[4,128,384]{2,1,0:T(8,128)(2,1)}, u32[]{:S(2)}, u32[]{:S(2)}) collective-permute-start(bf16[4,128,384]{2,1,0:T(8,128)(2,1)} %get-tuple-element.54), channel_id=1, source_target_pairs={{0,16},{16,32},{32,48},{48,0},{64,80},{80,96},{96,112},{112,64},{1... | collective-permute-start | bytes 1179656 | tf_op jit(solution)/shard_map/ppermute | solution.py:360
  132.2 12.8 %copy-start.4 = (bf16[4,128,384]{2,1,0:T(8,128)(2,1)S(1)}, bf16[4,128,384]{2,1,0:T(8,128)(2,1)}, u32[]{:S(2)}) copy-start(bf16[4,128,384]{2,1,0:T(8,128)(2,1)} %copy-done.3) | copy-start | bytes 1179652
  132.2 23.8 %collective-permute-start.24 = (bf16[4,128,384]{2,1,0:T(8,128)(2,1)}, bf16[4,128,384]{2,1,0:T(8,128)(2,1)}, u32[]{:S(2)}, u32[]{:S(2)}) collective-permute-start(bf16[4,128,384]{2,1,0:T(8,128)(2,1)} %copy-done.8), channel_id=1, source_target_pairs={{0,48},{16,0},{32,16},{48,32},{64,112},{80,64},{96,80},{112,96},{1... | collective-permute-start | bytes 1179656 | tf_op jit(solution)/shard_map/ppermute | solution.py:360
  136.3 19.7 %collective-permute-start.25 = (bf16[4,128,384]{2,1,0:T(8,128)(2,1)}, bf16[4,128,384]{2,1,0:T(8,128)(2,1)}, u32[]{:S(2)}, u32[]{:S(2)}) collective-permute-start(bf16[4,128,384]{2,1,0:T(8,128)(2,1)} %copy-done.7), channel_id=1, source_target_pairs={{0,32},{16,48},{32,0},{48,16},{64,96},{80,112},{96,64},{112,80},{1... | collective-permute-start | bytes 1179656 | tf_op jit(solution)/shard_map/ppermute | solution.py:360
  147.9 12.4 %collective-permute-start.34 = (bf16[128,384]{1,0:T(8,128)(2,1)}, bf16[128,384]{1,0:T(8,128)(2,1)}, u32[]{:S(2)}, u32[]{:S(2)}) collective-permute-start(bf16[128,384]{1,0:T(8,128)(2,1)} %get-tuple-element.66), channel_id=1, source_target_pairs={{0,16},{16,32},{32,48},{48,0},{64,80},{80,96},{96,112},{112,64},{1... | collective-permute-start | bytes 294920 | tf_op jit(solution)/shard_map/ppermute | solution.py:369
  154.2 6.1 %collective-permute-start.35 = (bf16[128,384]{1,0:T(8,128)(2,1)}, bf16[128,384]{1,0:T(8,128)(2,1)}, u32[]{:S(2)}, u32[]{:S(2)}) collective-permute-start(bf16[128,384]{1,0:T(8,128)(2,1)} %get-tuple-element.67), channel_id=1, source_target_pairs={{0,48},{16,0},{32,16},{48,32},{64,112},{80,64},{96,80},{112,96},{1... | collective-permute-start | bytes 294920 | tf_op jit(solution)/shard_map/ppermute | solution.py:369
  154.2 6.1 %collective-permute-start.36 = (bf16[128,384]{1,0:T(8,128)(2,1)}, bf16[128,384]{1,0:T(8,128)(2,1)}, u32[]{:S(2)}, u32[]{:S(2)}) collective-permute-start(bf16[128,384]{1,0:T(8,128)(2,1)} %get-tuple-element.68), channel_id=1, source_target_pairs={{0,32},{16,48},{32,0},{48,16},{64,96},{80,112},{96,64},{112,80},{1... | collective-permute-start | bytes 294920 | tf_op jit(solution)/shard_map/ppermute | solution.py:369
  157.5 12.1 %copy-start.12 = (bf16[128,384]{1,0:T(8,128)(2,1)S(1)}, bf16[128,384]{1,0:T(8,128)(2,1)}, u32[]{:S(2)}) copy-start(bf16[128,384]{1,0:T(8,128)(2,1)} %copy-done.11) | copy-start | bytes 294916
  157.5 26.3 %copy-start.13 = (pred[256,128]{1,0:T(32,128)(4,1)S(1)}, pred[256,128]{1,0:T(32,128)(4,1)}, u32[]{:S(2)}) copy-start(pred[256,128]{1,0:T(32,128)(4,1)} %get-tuple-element.75) | copy-start | bytes 98308
  157.5 4.8 %collective-permute-start.26 = (bf16[128,384]{1,0:T(8,128)(2,1)S(1)}, bf16[128,384]{1,0:T(8,128)(2,1)S(1)}, u32[]{:S(2)}, u32[]{:S(2)}) collective-permute-start(bf16[128,384]{1,0:T(8,128)(2,1)S(1)} %get-tuple-element.58), channel_id=1, source_target_pairs={{0,64},{16,80},{32,96},{48,112},{64,128},{80,144},{96,160},{112,17... | collective-permute-start | bytes 294920 | tf_op jit(solution)/shard_map/ppermute | solution.py:369
  157.6 5.1 %collective-permute-start.27 = (bf16[128,384]{1,0:T(8,128)(2,1)S(1)}, bf16[128,384]{1,0:T(8,128)(2,1)S(1)}, u32[]{:S(2)}, u32[]{:S(2)}) collective-permute-start(bf16[128,384]{1,0:T(8,128)(2,1)S(1)} %get-tuple-element.59), channel_id=1, source_target_pairs={{0,192},{16,208},{32,224},{48,240},{64,0},{80,16},{96,32},{112,48}... | collective-permute-start | bytes 294920 | tf_op jit(solution)/shard_map/ppermute | solution.py:369
  160.3 5.1 %collective-permute-start.28 = (bf16[128,384]{1,0:T(8,128)(2,1)S(1)}, bf16[128,384]{1,0:T(8,128)(2,1)S(1)}, u32[]{:S(2)}, u32[]{:S(2)}) collective-permute-start(bf16[128,384]{1,0:T(8,128)(2,1)S(1)} %get-tuple-element.60), channel_id=1, source_target_pairs={{0,128},{16,144},{32,160},{48,176},{64,192},{80,208},{96,224},{112... | collective-permute-start | bytes 294920 | tf_op jit(solution)/shard_map/ppermute | solution.py:369
  166.2 12.0 %all-to-all-start.2 = ((bf16[8,32,384]{2,1,0:T(8,128)(2,1)}), bf16[8,32,384]{2,1,0:T(8,128)(2,1)S(1)}, u32[]{:S(2)}, u32[]{:S(2)}) async-start(bf16[8,32,384]{2,1,0:T(8,128)(2,1)} %multiply_convert_fusion), calls=%async_computation.2 | async-start | bytes 393216 | tf_op jit(solution)/shard_map/all_to_all | solution.py:374
  178.3 5.5 %collective-permute-start.37 = (bf16[256,192]{1,0:T(8,128)(2,1)S(1)}, bf16[256,192]{1,0:T(8,128)(2,1)S(1)}, u32[]{:S(2)}, u32[]{:S(2)}) collective-permute-start(bf16[256,192]{1,0:T(8,128)(2,1)S(1)} %broadcast_select_fusion), channel_id=1, source_target_pairs={{0,1},{1,0},{2,3},{3,2},{4,5},{5,4},{6,7},{7,6},{8,9},{9,8},{10,11... | collective-permute-start | bytes 294920 | tf_op jit(solution)/shard_map/ppermute | solution.py:22
  (7 other events, 12.6 us)
